TPU v7x, 32 devices: a whole 2x2x4 slice. The times are simulated.
32 devices in a mesh: rep: 2 (over x), shard: 16 (over z, y, core).
Axes of the slice: x: 2, y: 2, z: 4, core: 2. Of those that a mesh axis runs over, the one named last changes fastest.
Arguments:
- tokens: bfloat16 [8192, 1536], P(('rep', 'shard')), may hold values from -6 to 6
- cotangent: bfloat16 [8192, 1536], P(('rep', 'shard')), may hold values from -6 to 6
- mix_gain: bfloat16 [1536], P('shard'), may hold values from 0.25 to 1.75
- branch_proj: bfloat16 [1536, 2048], P('shard'), may hold values from -0.15625 to 0.15625
- lruin_proj: bfloat16 [1536, 2048], P('shard'), may hold values from -0.15625 to 0.15625
- conv_kernel: bfloat16 [4, 2048], P(None, 'shard'), may hold values from -3 to 3
- conv_bias: bfloat16 [2048], P('shard'), may hold values from -3 to 3
- recur_proj: bfloat16 [2048, 2048], P('shard'), may hold values from -0.125 to 0.125
- recur_bias: bfloat16 [2048], P('shard'), may hold values from -4 to 4
- admit_proj: bfloat16 [2048, 2048], P('shard'), may hold values from -0.125 to 0.125
- admit_bias: bfloat16 [2048], P('shard'), may hold values from -4 to 4
- decay_param: bfloat16 [2048], P('shard'), may hold values from 3.5 to 7.5
- out_proj: bfloat16 [2048, 1536], P('shard'), may hold values from -0.5 to 0.5
- ffn_gain: bfloat16 [1536], P('shard'), may hold values from 0.25 to 1.75
- ffn_gate: bfloat16 [1536, 4608], P('shard'), may hold values from -0.15625 to 0.15625
- ffn_up: bfloat16 [1536, 4608], P('shard'), may hold values from -0.15625 to 0.15625
- ffn_down: bfloat16 [4608, 1536], P('shard'), may hold values from -0.1875 to 0.1875
Outputs:
- block_out: bfloat16 [8192, 1536], P(('rep', 'shard'))
- tokens_grad: float32 [8192, 1536], P(('rep', 'shard'))
- mixgain_grad: float32 [1536], P('shard')
- branch_grad: float32 [1536, 2048], P('shard')
- lruin_grad: float32 [1536, 2048], P('shard')
- kernel_grad: float32 [4, 2048], P(None, 'shard')
- convbias_grad: float32 [2048], P('shard')
- recur_grad: float32 [2048, 2048], P('shard')
- recurbias_grad: float32 [2048], P('shard')
- admit_grad: float32 [2048, 2048], P('shard')
- admitbias_grad: float32 [2048], P('shard')
- decay_grad: float32 [2048], P('shard')
- outproj_grad: float32 [2048, 1536], P('shard')
- ffngain_grad: float32 [1536], P('shard')
- ffngate_grad: float32 [1536, 4608], P('shard')
- ffnup_grad: float32 [1536, 4608], P('shard')
- ffndown_grad: float32 [4608, 1536], P('shard')
All inputs are finite; a program needn't handle non-finite values.
Results may differ from a plain program's by a relative error of at most 0.0098.
Values may be sent and summed in bfloat16 or wider, within the bound.
No kernel may reach another device: no remote copies, remote signals or barrier semaphores. Data moves between devices by JAX's collectives and lax.ppermute only.
A program may use at most 384 MiB of HBM per device.

v0:
```python
import jax
import jax.numpy as jnp
from jax import lax
from jax.sharding import PartitionSpec as P

EPS = 1e-06
DECAY_SCALE = 8.0
ROOT_FLOOR = 0.001


def matmul(left, right):
    return jnp.dot(left, right, preferred_element_type=jnp.float32)


def rows_product(left, right):
    return lax.dot_general(
        left, right, (((0,), (0,)), ((), ())), preferred_element_type=jnp.float32
    )


def cols_product(left, right):
    return lax.dot_general(
        left, right, (((1,), (1,)), ((), ())), preferred_element_type=jnp.float32
    )


def rms_norm(values, gain):
    return values * lax.rsqrt(jnp.mean(values * values, axis=-1, keepdims=True) + EPS) * gain


def convolve(values, kernel, bias):
    length = values.shape[0]
    total = jnp.zeros_like(values) + bias
    for offset in range(kernel.shape[0]):
        shifted = jnp.pad(values, ((offset, 0), (0, 0)))[:length]
        total = total + kernel[offset] * shifted
    return total


def combine(earlier, later):
    return (earlier[0] * later[0], later[0] * earlier[1] + later[1])


def recurrence(branch_pre, admitted, recur_pre, admit_pre, recur_bias, admit_bias, decay_param):
    gate_r = jax.nn.sigmoid(recur_pre + recur_bias)
    gate_i = jax.nn.sigmoid(admit_pre + admit_bias)
    decay = jnp.exp(-DECAY_SCALE * gate_r * jax.nn.softplus(-decay_param))
    inflow = jnp.sqrt(jnp.maximum(1.0 - decay * decay, ROOT_FLOOR)) * gate_i * admitted
    factors, states = lax.associative_scan(combine, (decay, inflow), axis=0)
    return states * jax.nn.gelu(branch_pre, approximate=True)


def gated(gate_pre, up_pre):
    return jax.nn.gelu(gate_pre, approximate=True) * up_pre


def widen(value):
    return value.astype(jnp.float32)


def body(
    tokens,
    cotangent,
    mix_gain,
    branch_proj,
    lruin_proj,
    conv_kernel,
    conv_bias,
    recur_proj,
    recur_bias,
    admit_proj,
    admit_bias,
    decay_param,
    out_proj,
    ffn_gain,
    ffn_gate,
    ffn_up,
    ffn_down,
):
    mixer_whole = (
        lax.all_gather(mix_gain, "shard", axis=0, tiled=True),
        lax.all_gather(branch_proj, "shard", axis=0, tiled=True),
        lax.all_gather(lruin_proj, "shard", axis=0, tiled=True),
        lax.all_gather(conv_kernel, "shard", axis=1, tiled=True),
        lax.all_gather(conv_bias, "shard", axis=0, tiled=True),
        lax.all_gather(recur_proj, "shard", axis=0, tiled=True),
        lax.all_gather(recur_bias, "shard", axis=0, tiled=True),
        lax.all_gather(admit_proj, "shard", axis=0, tiled=True),
        lax.all_gather(admit_bias, "shard", axis=0, tiled=True),
        lax.all_gather(decay_param, "shard", axis=0, tiled=True),
        lax.all_gather(out_proj, "shard", axis=0, tiled=True),
    )
    ffn_whole = (
        lax.all_gather(ffn_gain, "shard", axis=0, tiled=True),
        lax.all_gather(ffn_gate, "shard", axis=0, tiled=True),
        lax.all_gather(ffn_up, "shard", axis=0, tiled=True),
        lax.all_gather(ffn_down, "shard", axis=0, tiled=True),
    )
    (
        gain_one,
        branch_whole,
        lruin_whole,
        kernel_whole,
        cbias_whole,
        recur_whole,
        rbias_whole,
        admit_whole,
        abias_whole,
        decay_whole,
        outp_whole,
    ) = mixer_whole
    gain_two, gate_whole, up_whole, down_whole = ffn_whole
    values = widen(tokens)
    normed_f, norm_one_pull = jax.vjp(rms_norm, values, widen(gain_one))
    normed = normed_f.astype(jnp.bfloat16)
    branch_pre = matmul(normed, branch_whole)
    lru_pre = matmul(normed, lruin_whole)
    conv_out, conv_pull = jax.vjp(convolve, lru_pre, widen(kernel_whole), widen(cbias_whole))
    admitted = conv_out.astype(jnp.bfloat16)
    recur_pre = matmul(admitted, recur_whole)
    admit_pre = matmul(admitted, admit_whole)
    mixed_f, lru_pull = jax.vjp(
        recurrence,
        branch_pre,
        widen(admitted),
        recur_pre,
        admit_pre,
        widen(rbias_whole),
        widen(abias_whole),
        widen(decay_whole),
    )
    mixed = mixed_f.astype(jnp.bfloat16)
    middle = values + matmul(mixed, outp_whole)
    normed_two_f, norm_two_pull = jax.vjp(rms_norm, middle, widen(gain_two))
    normed_two = normed_two_f.astype(jnp.bfloat16)
    gate_pre = matmul(normed_two, gate_whole)
    up_pre = matmul(normed_two, up_whole)
    hidden_f, glu_pull = jax.vjp(gated, gate_pre, up_pre)
    hidden = hidden_f.astype(jnp.bfloat16)
    block_out = (middle + matmul(hidden, down_whole)).astype(jnp.bfloat16)
    gain_two, gate_whole, up_whole, down_whole = (
        lax.all_gather(ffn_gain, "shard", axis=0, tiled=True),
        lax.all_gather(ffn_gate, "shard", axis=0, tiled=True),
        lax.all_gather(ffn_up, "shard", axis=0, tiled=True),
        lax.all_gather(ffn_down, "shard", axis=0, tiled=True),
    )
    out_cot = widen(cotangent)
    down_cot = out_cot.astype(jnp.bfloat16)
    grad_down = rows_product(hidden, down_cot)
    hidden_cot = cols_product(down_cot, down_whole)
    gate_cot, up_cot = glu_pull(hidden_cot)
    gate_low = gate_cot.astype(jnp.bfloat16)
    up_low = up_cot.astype(jnp.bfloat16)
    grad_gate = rows_product(normed_two, gate_low)
    grad_up = rows_product(normed_two, up_low)
    normed_two_cot = cols_product(gate_low, gate_whole) + cols_product(up_low, up_whole)
    middle_part, gain_two_grad = norm_two_pull(normed_two_cot)
    middle_cot = out_cot + middle_part
    ffn_shares = (
        lax.psum_scatter(gain_two_grad, "shard", scatter_dimension=0, tiled=True),
        lax.psum_scatter(grad_gate, "shard", scatter_dimension=0, tiled=True),
        lax.psum_scatter(grad_up, "shard", scatter_dimension=0, tiled=True),
        lax.psum_scatter(grad_down, "shard", scatter_dimension=0, tiled=True),
    )
    (
        gain_one,
        branch_whole,
        lruin_whole,
        kernel_whole,
        cbias_whole,
        recur_whole,
        rbias_whole,
        admit_whole,
        abias_whole,
        decay_whole,
        outp_whole,
    ) = (
        lax.all_gather(mix_gain, "shard", axis=0, tiled=True),
        lax.all_gather(branch_proj, "shard", axis=0, tiled=True),
        lax.all_gather(lruin_proj, "shard", axis=0, tiled=True),
        lax.all_gather(conv_kernel, "shard", axis=1, tiled=True),
        lax.all_gather(conv_bias, "shard", axis=0, tiled=True),
        lax.all_gather(recur_proj, "shard", axis=0, tiled=True),
        lax.all_gather(recur_bias, "shard", axis=0, tiled=True),
        lax.all_gather(admit_proj, "shard", axis=0, tiled=True),
        lax.all_gather(admit_bias, "shard", axis=0, tiled=True),
        lax.all_gather(decay_param, "shard", axis=0, tiled=True),
        lax.all_gather(out_proj, "shard", axis=0, tiled=True),
    )
    outp_low = middle_cot.astype(jnp.bfloat16)
    grad_outp = rows_product(mixed, outp_low)
    mixed_cot = cols_product(outp_low, outp_whole)
    branch_cot, admitted_direct, recur_cot, admit_cot, rbias_grad, abias_grad, decay_grad = (
        lru_pull(mixed_cot)
    )
    branch_low = branch_cot.astype(jnp.bfloat16)
    recur_low = recur_cot.astype(jnp.bfloat16)
    admit_low = admit_cot.astype(jnp.bfloat16)
    grad_recur = rows_product(admitted, recur_low)
    grad_admit = rows_product(admitted, admit_low)
    admitted_cot = (
        admitted_direct
        + cols_product(recur_low, recur_whole)
        + cols_product(admit_low, admit_whole)
    )
    lru_cot, kernel_grad, cbias_grad = conv_pull(admitted_cot)
    lru_low = lru_cot.astype(jnp.bfloat16)
    grad_branch = rows_product(normed, branch_low)
    grad_lruin = rows_product(normed, lru_low)
    normed_cot = cols_product(branch_low, branch_whole) + cols_product(lru_low, lruin_whole)
    token_part, gain_one_grad = norm_one_pull(normed_cot)
    tokens_grad = middle_cot + token_part
    mixer_shares = (
        lax.psum_scatter(gain_one_grad, "shard", scatter_dimension=0, tiled=True),
        lax.psum_scatter(grad_branch, "shard", scatter_dimension=0, tiled=True),
        lax.psum_scatter(grad_lruin, "shard", scatter_dimension=0, tiled=True),
        lax.psum_scatter(kernel_grad, "shard", scatter_dimension=1, tiled=True),
        lax.psum_scatter(cbias_grad, "shard", scatter_dimension=0, tiled=True),
        lax.psum_scatter(grad_recur, "shard", scatter_dimension=0, tiled=True),
        lax.psum_scatter(rbias_grad, "shard", scatter_dimension=0, tiled=True),
        lax.psum_scatter(grad_admit, "shard", scatter_dimension=0, tiled=True),
        lax.psum_scatter(abias_grad, "shard", scatter_dimension=0, tiled=True),
        lax.psum_scatter(decay_grad, "shard", scatter_dimension=0, tiled=True),
        lax.psum_scatter(grad_outp, "shard", scatter_dimension=0, tiled=True),
    )
    summed = lax.psum(
        (
            mixer_shares[0],
            mixer_shares[1],
            mixer_shares[2],
            mixer_shares[3],
            mixer_shares[4],
            mixer_shares[5],
            mixer_shares[6],
            mixer_shares[7],
            mixer_shares[8],
            mixer_shares[9],
            mixer_shares[10],
            ffn_shares[0],
            ffn_shares[1],
            ffn_shares[2],
            ffn_shares[3],
        ),
        "rep",
    )
    mixer_shares = summed[:11]
    ffn_shares = summed[11:]
    return (
        block_out,
        tokens_grad,
        mixer_shares[0],
        mixer_shares[1],
        mixer_shares[2],
        mixer_shares[3],
        mixer_shares[4],
        mixer_shares[5],
        mixer_shares[6],
        mixer_shares[7],
        mixer_shares[8],
        mixer_shares[9],
        mixer_shares[10],
        ffn_shares[0],
        ffn_shares[1],
        ffn_shares[2],
        ffn_shares[3],
    )


def solution(mesh):
    in_specs = (
        P(("rep", "shard"), None),
        P(("rep", "shard"), None),
        P("shard"),
        P("shard", None),
        P("shard", None),
        P(None, "shard"),
        P("shard"),
        P("shard", None),
        P("shard"),
        P("shard", None),
        P("shard"),
        P("shard"),
        P("shard", None),
        P("shard"),
        P("shard", None),
        P("shard", None),
        P("shard", None),
    )
    out_specs = (
        P(("rep", "shard"), None),
        P(("rep", "shard"), None),
        P("shard"),
        P("shard", None),
        P("shard", None),
        P(None, "shard"),
        P("shard"),
        P("shard", None),
        P("shard"),
        P("shard", None),
        P("shard"),
        P("shard"),
        P("shard", None),
        P("shard"),
        P("shard", None),
        P("shard", None),
        P("shard", None),
    )
    return jax.shard_map(body, mesh=mesh, in_specs=in_specs, out_specs=out_specs, check_vma=False)
```

profile of v0, /device:TPU:0, one launch (start us, length us, event | category | flops | bytes accessed | tf_op | source)
XLA Modules:
  0.0 2886.7 jit_solution(8654829896797584471)
XLA Ops:
  14.6 36.2 %all-reduce.96 = (bf16[1536]{0:T(1024)(128)(2,1)S(1)}, bf16[1536]{0:T(1024)(128)(2,1)S(1)}) all-reduce(bf16[1536]{0:T(1024)(128)(2,1)S(1)} %dynamic-update-slice, bf16[1536]{0:T(1024)(128)(2,1)S(1)} %dynamic-update-slice.1), channel_id=1, replica_groups=mesh['rep'=2,'shard'=16] {'shard'}, use_global_device_ids=true, to_apply=%add.85 | all-reduce | flops 3072 | bytes 12288
  50.8 17.2 all-gather
  68.0 19.2 all-gather.1
  87.2 17.4 all-gather.3
  105.3 18.9 all-gather.2
  124.1 17.6 all_gather.54
  142.2 4.8 fusion.80
  151.1 7.1 fusion.14
  158.2 68.3 %all-gather.17.cloned.1.call-done = bf16[2048,2048]{1,0:T(8,128)(2,1)} async-done(((bf16[128,2048]{1,0:T(8,128)(2,1)}), bf16[2048,2048]{1,0:T(8,128)(2,1)}) %all-gather.17.cloned.1.call-update) | async-done | bytes 8388624 | tf_op jit(solution)/shard_map/all_gather | solution.py:88
  226.5 10.0 convert_multiply_fusion.5
  242.6 5.4 slice.276
  248.0 5.4 slice.277
  335.7 5.6 slice.331
  366.1 4.7 pad.358
  373.4 8.6 pad.360
  385.6 8.7 pad.359
  394.3 9.0 multiply_convert_fusion.2
  403.3 5.1 multiply_reduce_fusion.7
  410.6 52.2 %all-gather.23.cloned.1.call-done = bf16[1536,4608]{1,0:T(8,128)(2,1)} async-done(((bf16[96,4608]{1,0:T(8,128)(2,1)}), bf16[1536,4608]{1,0:T(8,128)(2,1)}) %all-gather.23.cloned.1.call-update) | async-done | bytes 14155792 | tf_op jit(solution)/shard_map/all_gather | solution.py:95
  462.8 11.3 fusion.115
  474.1 99.8 %all-gather.25.cloned.1.call-done = bf16[1536,4608]{1,0:T(8,128)(2,1)} async-done(((bf16[96,4608]{1,0:T(8,128)(2,1)}), bf16[1536,4608]{1,0:T(8,128)(2,1)}) %all-gather.25.cloned.1.call-update) | async-done | bytes 14155792 | tf_op jit(solution)/shard_map/all_gather | solution.py:96
  573.9 11.2 fusion.116
  585.1 99.9 %all-gather.27.cloned.1.call-done = bf16[4608,1536]{1,0:T(8,128)(2,1)} async-done(((bf16[288,1536]{1,0:T(8,128)(2,1)}), bf16[4608,1536]{1,0:T(8,128)(2,1)}) %all-gather.27.cloned.1.call-update) | async-done | bytes 14155792 | tf_op jit(solution)/shard_map/all_gather | solution.py:97
  685.0 13.8 multiply_convert_fusion
  698.9 10.8 fusion.117
  709.7 11.9 multiply_reduce_fusion.5
  724.3 6.6 fusion.39
  733.4 5.4 slice.332
  742.9 5.4 slice.333
  859.8 4.7 pad.410
  869.1 4.7 pad.432
  878.3 4.6 pad.368
  885.8 6.2 multiply_add_fusion
  894.1 8.6 pad.412
  902.7 8.6 pad.413
  911.3 8.7 pad.434
  919.9 8.7 pad.435
  928.6 8.9 pad.363
  937.5 8.7 pad.414
  946.2 10.7 multiply_reduce_fusion
  960.1 7.3 convolution_add_fusion.4
  967.5 4.6 broadcast_multiply_fusion.2
  976.6 6.5 fusion.74
  984.8 7.5 fusion.46
  993.7 8.0 fusion.76
  1003.1 9.5 fusion.40
  1012.7 9.4 fusion.43
  1023.2 13.1 fusion.119
  1036.4 13.1 fusion.120
  1050.6 13.4 fusion.121
  1065.6 50.6 %reduce-scatter.14.cloned.1.call-done = f32[96,2048]{1,0:T(8,128)} async-done(((f32[1536,2048]{1,0:T(8,128)}), f32[96,2048]{1,0:T(8,128)}) %reduce-scatter.14.cloned.1.call-update) | async-done | bytes 786448 | tf_op jit(solution)/shard_map/reduce_scatter | solution.py:216
  1116.2 137.9 %reduce-scatter.20.cloned.1.call-done = f32[128,1536]{1,0:T(8,128)} async-done(((f32[2048,1536]{1,0:T(8,128)}), f32[128,1536]{1,0:T(8,128)}) %reduce-scatter.20.cloned.1.call-update) | async-done | bytes 786448 | tf_op jit(solution)/shard_map/reduce_scatter | solution.py:224
  1254.0 138.0 %reduce-scatter.12.cloned.1.call-done = f32[96,2048]{1,0:T(8,128)} async-done(((f32[1536,2048]{1,0:T(8,128)}), f32[96,2048]{1,0:T(8,128)}) %reduce-scatter.12.cloned.1.call-update) | async-done | bytes 786448 | tf_op jit(solution)/shard_map/reduce_scatter | solution.py:215
  1392.1 181.7 %reduce-scatter.18.cloned.1.call-done = f32[128,2048]{1,0:T(8,128)} async-done(((f32[2048,2048]{1,0:T(8,128)}), f32[128,2048]{1,0:T(8,128)}) %reduce-scatter.18.cloned.1.call-update) | async-done | bytes 1048592 | tf_op jit(solution)/shard_map/reduce_scatter | solution.py:221
  1573.8 181.7 %reduce-scatter.16.cloned.1.call-done = f32[128,2048]{1,0:T(8,128)} async-done(((f32[2048,2048]{1,0:T(8,128)}), f32[128,2048]{1,0:T(8,128)}) %reduce-scatter.16.cloned.1.call-update) | async-done | bytes 1048592 | tf_op jit(solution)/shard_map/reduce_scatter | solution.py:219
  1755.5 272.3 %reduce-scatter.22.cloned.1.call-done = f32[96,4608]{1,0:T(8,128)} async-done(((f32[1536,4608]{1,0:T(8,128)}), f32[96,4608]{1,0:T(8,128)}) %reduce-scatter.22.cloned.1.call-update) | async-done | bytes 1769488 | tf_op jit(solution)/shard_map/reduce_scatter | solution.py:161
  2027.8 272.4 %reduce-scatter.24.cloned.1.call-done = f32[96,4608]{1,0:T(8,128)} async-done(((f32[1536,4608]{1,0:T(8,128)}), f32[96,4608]{1,0:T(8,128)}) %reduce-scatter.24.cloned.1.call-update) | async-done | bytes 1769488 | tf_op jit(solution)/shard_map/reduce_scatter | solution.py:162
  2300.2 272.4 %reduce-scatter.26.cloned.1.call-done = f32[288,1536]{1,0:T(8,128)} async-done(((f32[4608,1536]{1,0:T(8,128)}), f32[288,1536]{1,0:T(8,128)}) %reduce-scatter.26.cloned.1.call-update) | async-done | bytes 1769488 | tf_op jit(solution)/shard_map/reduce_scatter | solution.py:163
  2574.0 4.7 fusion.118
  2578.7 6.3 fusion.34
  2585.0 59.8 %all-reduce.93 = (f32[1536]{0:T(1024)S(1)}, f32[2048]{0:T(1024)S(1)}, f32[2048]{0:T(1024)S(1)}, f32[2048]{0:T(1024)S(1)}, f32[2048]{0:T(1024)S(1)}, /*index=5*/f32[1536]{0:T(1024)S(1)}) all-reduce(f32[1536]{0:T(1024)S(1)} %get-tuple-element.23, f32[2048]{0:T(1024)S(1)} %get-tuple-element.25, ...), channel_id=2, replica_groups=mesh['rep'=2,'shard'=16] {'shard'}, use_global_device_ids=true, to_apply=%region_5.6.clone | all-reduce | flops 11264 | bytes 90112
  2648.4 8.1 fusion.15
  2657.4 5.7 all-reduce.94
  2663.2 203.9 %all-reduce.99.cloned.1.call-done = (f32[96,2048]{1,0:T(8,128)}, f32[96,2048]{1,0:T(8,128)}, f32[128,2048]{1,0:T(8,128)}, f32[128,2048]{1,0:T(8,128)}, f32[128,1...) async-done(((f32[96,2048]{1,0:T(8,128)}, f32[96,2048]{1,0:T(8,128)}, f32[128,2048]{1,0:T(8,128)}, f32[128,2048]{1,0:T(8,128)}, ...) | async-done | bytes 9764880 | tf_op jit(solution)/shard_map/psum | solution.py:226
  (482 shorter events, 300.4 us)
Async XLA Ops:
  7.2 135.0 %all-gather.13.cloned.1.call-start = ((), (), s32[]{:S(2)}) async-start(), calls=%async_computation.9 | async-start | bytes 6684672 | tf_op jit(solution)/shard_map/all_gather | solution.py:83
  7.9 143.2 %all-gather.15.cloned.1.call-start = ((), (), s32[]{:S(2)}) async-start(), calls=%async_computation.10 | async-start | bytes 8912896 | tf_op jit(solution)/shard_map/all_gather | solution.py:86
  8.7 42.1 %copy-start.105 = (bf16[128]{0:T(256)(128)(2,1)S(1)}, bf16[128]{0:T(256)(128)(2,1)}, u32[]{:S(2)}) copy-start(bf16[128]{0:T(256)(128)(2,1)} %param.23) | copy-start | bytes 772
  8.7 59.3 %copy-start.106 = (bf16[128]{0:T(256)(128)(2,1)S(1)}, bf16[128]{0:T(256)(128)(2,1)}, u32[]{:S(2)}) copy-start(bf16[128]{0:T(256)(128)(2,1)} %param.25) | copy-start | bytes 772
  8.7 78.5 %copy-start.107 = (bf16[128]{0:T(256)(128)(2,1)S(1)}, bf16[128]{0:T(256)(128)(2,1)}, u32[]{:S(2)}) copy-start(bf16[128]{0:T(256)(128)(2,1)} %param.27) | copy-start | bytes 772
  8.7 96.5 %copy-start.108 = (bf16[128]{0:T(256)(128)(2,1)S(1)}, bf16[128]{0:T(256)(128)(2,1)}, u32[]{:S(2)}) copy-start(bf16[128]{0:T(256)(128)(2,1)} %param.28) | copy-start | bytes 772
  8.7 115.4 %copy-start.104 = (bf16[4,128]{1,0:T(4,128)(2,1)S(1)}, bf16[4,128]{1,0:T(4,128)(2,1)}, u32[]{:S(2)}) copy-start(bf16[4,128]{1,0:T(4,128)(2,1)} %param.22) | copy-start | bytes 3076
  8.8 133.0 %copy-start.2 = (bf16[256,1536]{1,0:T(8,128)(2,1)S(1)}, bf16[256,1536]{1,0:T(8,128)(2,1)}, u32[]{:S(2)}) copy-start(bf16[256,1536]{1,0:T(8,128)(2,1)} %param.17) | copy-start | bytes 2359300
  8.8 217.7 %all-gather.17.cloned.1.call-start = ((), (), s32[]{:S(2)}) async-start(), calls=%async_computation.11 | async-start | bytes 8912896 | tf_op jit(solution)/shard_map/all_gather | solution.py:88
  9.5 384.8 %all-gather.19.cloned.1.call-start = ((), (), s32[]{:S(2)}) async-start(), calls=%async_computation.12 | async-start | bytes 6684672 | tf_op jit(solution)/shard_map/all_gather | solution.py:82
  10.1 393.2 %all-gather.21.cloned.1.call-start = ((), (), s32[]{:S(2)}) async-start(), calls=%async_computation.13 | async-start | bytes 6684672 | tf_op jit(solution)/shard_map/all_gather | solution.py:91
  10.7 452.1 %all-gather.23.cloned.1.call-start = ((), (), s32[]{:S(2)}) async-start(), calls=%async_computation.14 | async-start | bytes 15040512 | tf_op jit(solution)/shard_map/all_gather | solution.py:95
  11.2 562.7 %all-gather.25.cloned.1.call-start = ((), (), s32[]{:S(2)}) async-start(), calls=%async_computation.15 | async-start | bytes 15040512 | tf_op jit(solution)/shard_map/all_gather | solution.py:96
  12.0 673.0 %all-gather.27.cloned.1.call-start = ((), (), s32[]{:S(2)}) async-start(), calls=%async_computation.16 | async-start | bytes 15040512 | tf_op jit(solution)/shard_map/all_gather | solution.py:97
  12.7 1103.4 %reduce-scatter.14.cloned.1.call-start = ((), (), s32[]{:S(2)}) async-start(), calls=%async_computation.18 | async-start | bytes 13369344 | tf_op jit(solution)/shard_map/reduce_scatter | solution.py:216
  68.0 79.0 %copy-start.80 = (f32[16,1,128]{2,1,0:T(1,128)}, f32[16,1,128]{2,1,0:T(1,128)S(1)}, u32[]{:S(2)}) copy-start(f32[16,1,128]{2,1,0:T(1,128)S(1)} %convert_element_type.99) | copy-start | bytes 24580
  149.3 8.9 copy-start.7
  272.9 12.6 copy-start.33
  275.8 14.5 copy-start.26
  283.8 40.2 %copy-start.37 = (f32[16,2048]{1,0:T(8,128)}, f32[16,2048]{1,0:T(8,128)S(1)}, u32[]{:S(2)}) copy-start(f32[16,2048]{1,0:T(8,128)S(1)} %slice.293) | copy-start | bytes 393220
  290.3 32.9 %copy-start.30 = (f32[64,2048]{1,0:T(8,128)S(1)}, f32[64,2048]{1,0:T(8,128)}, u32[]{:S(2)}) copy-start(f32[64,2048]{1,0:T(8,128)} %get-tuple-element.101) | copy-start | bytes 1572868
  332.7 10.1 copy-start.74
  332.7 10.1 copy-start.79
  332.7 10.1 copy-start.90
  332.7 10.1 copy-start.78
  332.7 10.8 copy-start.77
  332.7 11.7 copy-start.72
  332.7 11.7 copy-start.82
  332.7 12.3 copy-start.95
  335.7 9.4 copy-start.57
  335.7 11.8 copy-start.44
  335.7 11.8 copy-start.63
  698.8 10.9 copy-start.17
  698.8 10.9 copy-start.86
  698.8 10.8 copy-start.97
  709.7 11.9 copy-start.102
  709.7 11.9 copy-start.31
  773.6 23.2 copy-start.64
  775.5 34.0 %copy-start.53 = (f32[8,2048]{1,0:T(8,128)S(1)}, f32[8,2048]{1,0:T(8,128)}, u32[]{:S(2)}) copy-start(f32[8,2048]{1,0:T(8,128)} %slice.299) | copy-start | bytes 196612
  775.5 34.0 %copy-start.59 = (f32[8,2048]{1,0:T(8,128)S(1)}, f32[8,2048]{1,0:T(8,128)}, u32[]{:S(2)}) copy-start(f32[8,2048]{1,0:T(8,128)} %slice.300) | copy-start | bytes 196612
  775.5 34.0 %copy-start.60 = (f32[8,2048]{1,0:T(8,128)S(1)}, f32[8,2048]{1,0:T(8,128)}, u32[]{:S(2)}) copy-start(f32[8,2048]{1,0:T(8,128)} %slice.303) | copy-start | bytes 196612
  779.4 41.5 %copy-start.73 = (f32[7,2048]{1,0:T(8,128)S(1)}, f32[7,2048]{1,0:T(8,128)}, u32[]{:S(2)}) copy-start(f32[7,2048]{1,0:T(8,128)} %get-tuple-element.121) | copy-start | bytes 172036
  780.9 41.4 %copy-start.38 = (f32[16,2048]{1,0:T(8,128)S(1)}, f32[16,2048]{1,0:T(8,128)}, u32[]{:S(2)}) copy-start(f32[16,2048]{1,0:T(8,128)} %copy-done.37) | copy-start | bytes 393220
  780.9 41.4 %copy-start.46 = (f32[16,2048]{1,0:T(8,128)S(1)}, f32[16,2048]{1,0:T(8,128)}, u32[]{:S(2)}) copy-start(f32[16,2048]{1,0:T(8,128)} %slice.294) | copy-start | bytes 393220
  822.3 14.3 copy-start.27
  822.3 14.3 slice-start.5
  841.4 13.2 copy-start.14
  841.4 13.2 slice-start.4
  869.1 13.9 copy-start.36
  873.8 12.0 slice-start.3
  937.5 8.8 copy-start.76
  937.5 8.8 copy-start.81
  946.2 10.7 copy-start.1
  946.2 10.7 copy-start.3
  983.1 271.0 %reduce-scatter.20.cloned.1.call-start = ((), (), s32[]{:S(2)}) async-start(), calls=%async_computation.21 | async-start | bytes 13369344 | tf_op jit(solution)/shard_map/reduce_scatter | solution.py:224
  992.3 399.8 %reduce-scatter.12.cloned.1.call-start = ((), (), s32[]{:S(2)}) async-start(), calls=%async_computation.17 | async-start | bytes 13369344 | tf_op jit(solution)/shard_map/reduce_scatter | solution.py:215
  1001.7 572.1 %reduce-scatter.18.cloned.1.call-start = ((), (), s32[]{:S(2)}) async-start(), calls=%async_computation.20 | async-start | bytes 17825792 | tf_op jit(solution)/shard_map/reduce_scatter | solution.py:221
  1012.6 742.8 %reduce-scatter.16.cloned.1.call-start = ((), (), s32[]{:S(2)}) async-start(), calls=%async_computation.19 | async-start | bytes 17825792 | tf_op jit(solution)/shard_map/reduce_scatter | solution.py:219
  1022.1 1005.7 %reduce-scatter.22.cloned.1.call-start = ((), (), s32[]{:S(2)}) async-start(), calls=%async_computation.22 | async-start | bytes 30081024 | tf_op jit(solution)/shard_map/reduce_scatter | solution.py:161
  1036.4 1263.8 %reduce-scatter.24.cloned.1.call-start = ((), (), s32[]{:S(2)}) async-start(), calls=%async_computation.23 | async-start | bytes 30081024 | tf_op jit(solution)/shard_map/reduce_scatter | solution.py:162
  1049.5 1523.1 %reduce-scatter.26.cloned.1.call-start = ((), (), s32[]{:S(2)}) async-start(), calls=%async_computation.24 | async-start | bytes 30081024 | tf_op jit(solution)/shard_map/reduce_scatter | solution.py:163
  1064.1 1592.4 %reduce-scatter.28.cloned.1.call-start = ((), (), s32[]{:S(2)}) async-start(), calls=%async_computation.25 | async-start | bytes 1114112
  1065.6 1801.5 %all-reduce.99.cloned.1.call-start = ((), (), s32[]{:S(2)}) async-start(), calls=%async_computation.26 | async-start | bytes 19529728 | tf_op jit(solution)/shard_map/psum | solution.py:226
  2578.7 66.5 %copy-start.99 = (f32[256]{0:T(256)S(1)}, f32[256]{0:T(256)}, u32[]{:S(2)}) copy-start(f32[256]{0:T(256)} %copy-done.98) | copy-start | bytes 3076
  (71 other events, 266.3 us)
Sparse Core Ops, SparseCore 0:
  10.3 64.7 all-gather.12
  77.3 73.7 all-gather.14
  153.3 73.2 all-gather.16
  228.6 60.0 all-gather.18
  290.9 60.4 all-gather.20
  353.5 109.2 all-gather.22
  465.1 108.7 all-gather.24
  576.2 108.7 all-gather.26
  983.2 132.9 reduce-scatter.13
  1120.1 133.9 reduce-scatter.19
  1258.1 133.9 reduce-scatter.11
  1396.0 177.6 reduce-scatter.17
  1577.9 177.5 reduce-scatter.15
  1759.5 268.2 reduce-scatter.21
  2031.8 268.3 reduce-scatter.23
  2304.2 268.3 reduce-scatter.25
  2576.6 56.5 reduce-scatter.27
  2636.4 230.5 all-reduce.98
where the time goes:
time: 2900 us; the launch traced here: 2890 us
  waiting for transfers between devices  2040 us (70%)
  local copies, waits for them, and re-layouts  323 us (11%)
  matrix products  213 us (7%)
  blocking collectives  192 us (7%)
  other arithmetic  101 us (3%)
    reduce_scatter x1, waiting for transfers between devices, body(): lax.psum_scatter(grad_down, 'shard', scatter_dimension=0, tiled=True)  272 us
    reduce_scatter x1, waiting for transfers between devices, body(): lax.psum_scatter(grad_up, 'shard', scatter_dimension=0, tiled=True)  272 us
    reduce_scatter x1, waiting for transfers between devices, body(): lax.psum_scatter(grad_gate, 'shard', scatter_dimension=0, tiled=True)  272 us
    psum x1, waiting for transfers between devices, body(): lax.psum((mixer_shares[0], mixer_shares[1], mixer_shares[2], mixer_shares...  204 us
    reduce_scatter x1, waiting for transfers between devices, body(): lax.psum_scatter(grad_recur, 'shard', scatter_dimension=0, tiled=True)  182 us
    reduce_scatter x1, waiting for transfers between devices, body(): lax.psum_scatter(grad_admit, 'shard', scatter_dimension=0, tiled=True)  182 us
    pad x61, local copies, waits for them, and re-layouts, recurrence(): factors, states = lax.associative_scan(combine, (decay, inflow), axis=0)  171 us
    reduce_scatter x1, waiting for transfers between devices, body(): lax.psum_scatter(grad_branch, 'shard', scatter_dimension=0, tiled=True)  138 us
  transfers between devices with their start and end apart: 18, of which 14 were waited for; matrix products, arithmetic and copies ran while one was open for 11% of the time, Pallas kernels for 0%

commit v1 on v0

v1 whole, which is shorter than its diff:
```python
import functools
import math

import jax
import jax.numpy as jnp
from jax import lax
from jax.experimental import pallas as pl
from jax.experimental.pallas import tpu as pltpu
from jax.sharding import PartitionSpec as P

EPS = 1e-06
DECAY_SCALE = 8.0
ROOT_FLOOR = 0.001
GELU_K = math.sqrt(2.0 / math.pi)
GELU_C = 0.044715
ROWS = 16
BF16 = jnp.bfloat16
F32 = jnp.float32


def matmul(left, right):
    return jnp.dot(left, right, preferred_element_type=F32)


def rows_product(left, right):
    return lax.dot_general(left, right, (((0,), (0,)), ((), ())), preferred_element_type=F32)


def cols_product(left, right):
    return lax.dot_general(left, right, (((1,), (1,)), ((), ())), preferred_element_type=F32)


def widen(value):
    return value.astype(F32)


def gelu(v):
    return 0.5 * v * (1.0 + jnp.tanh(GELU_K * (v + GELU_C * v * v * v)))


def gelu_slope(v):
    t = jnp.tanh(GELU_K * (v + GELU_C * v * v * v))
    return 0.5 * (1.0 + t) + 0.5 * v * (1.0 - t * t) * GELU_K * (1.0 + 3.0 * GELU_C * v * v)


def forward_kernel(pre_ref, gates_r_ref, gates_i_ref, admitted_ref, params_ref, mixed_ref, before_ref):
    width = pre_ref.shape[1]
    rbias, abias, rate = params_ref[0:1, :], params_ref[1:2, :], params_ref[2:3, :]
    row = lax.broadcasted_iota(jnp.int32, (ROWS, width), 0)

    def step(i, carry):
        at = pl.ds(pl.multiple_of(i * ROWS, ROWS), ROWS)
        gate_r = jax.nn.sigmoid(gates_r_ref[at, :] + rbias)
        gate_i = jax.nn.sigmoid(gates_i_ref[at, :] + abias)
        a = jnp.exp(-(gate_r * rate))
        b = jnp.sqrt(jnp.maximum(1.0 - a * a, ROOT_FLOOR)) * gate_i * widen(admitted_ref[at, :])
        for d in (1, 2, 4, 8):
            keep = row >= d
            b = b + a * jnp.where(keep, pltpu.roll(b, d, 0), 0.0)
            a = a * jnp.where(keep, pltpu.roll(a, d, 0), 1.0)
        state = b + a * carry
        before_ref[at, :] = jnp.where(row >= 1, pltpu.roll(state, 1, 0), carry)
        mixed_ref[at, :] = (state * gelu(pre_ref[at, :])).astype(BF16)
        return jnp.broadcast_to(state[ROWS - 1 : ROWS, :], (ROWS, width))

    lax.fori_loop(0, pre_ref.shape[0] // ROWS, step, jnp.zeros((ROWS, width), F32))


def backward_kernel(
    cot_ref, pre_ref, gates_r_ref, gates_i_ref, admitted_ref, before_ref, params_ref,
    branch_ref, recur_ref, admit_ref, direct_ref, sums_ref,
):
    width = pre_ref.shape[1]
    rbias, abias, rate = params_ref[0:1, :], params_ref[1:2, :], params_ref[2:3, :]
    row = lax.broadcasted_iota(jnp.int32, (ROWS, width), 0)
    blocks = pre_ref.shape[0] // ROWS

    def step(i, state):
        carry, sum_r, sum_i, sum_d = state
        at = pl.ds(pl.multiple_of((blocks - 1 - i) * ROWS, ROWS), ROWS)
        gate_r = jax.nn.sigmoid(gates_r_ref[at, :] + rbias)
        gate_i = jax.nn.sigmoid(gates_i_ref[at, :] + abias)
        admitted = widen(admitted_ref[at, :])
        a = jnp.exp(-(gate_r * rate))
        rest = 1.0 - a * a
        root = jnp.sqrt(jnp.maximum(rest, ROOT_FLOOR))
        before = before_ref[at, :]
        state_now = a * before + root * gate_i * admitted
        pre = pre_ref[at, :]
        cot = cot_ref[at, :]
        branch_ref[at, :] = (cot * state_now * gelu_slope(pre)).astype(BF16)
        own = cot * gelu(pre)
        f = a
        e = a * own
        for d in (1, 2, 4, 8):
            keep = row < ROWS - d
            e = e + f * jnp.where(keep, pltpu.roll(e, ROWS - d, 0), 0.0)
            f = f * jnp.where(keep, pltpu.roll(f, ROWS - d, 0), 1.0)
        e = e + f * carry
        g = own + jnp.where(row < ROWS - 1, pltpu.roll(e, ROWS - 1, 0), carry)
        direct_ref[at, :] = g * root * gate_i
        share = jnp.where(rest > ROOT_FLOOR, 1.0, jnp.where(rest == ROOT_FLOOR, 0.5, 0.0))
        d_log = a * (g * before - g * gate_i * admitted * (share * a / root))
        d_gate_r = -(d_log * rate)
        d_gate_i = g * root * admitted
        recur = d_gate_r * gate_r * (1.0 - gate_r)
        admit = d_gate_i * gate_i * (1.0 - gate_i)
        recur_ref[at, :] = recur.astype(BF16)
        admit_ref[at, :] = admit.astype(BF16)
        carry = jnp.broadcast_to(e[0:1, :], (ROWS, width))
        return carry, sum_r + recur, sum_i + admit, sum_d + d_log * gate_r

    zero = jnp.zeros((ROWS, width), F32)
    _, sum_r, sum_i, sum_d = lax.fori_loop(0, blocks, step, (zero, zero, zero, zero))
    sums_ref[0:ROWS, :] = sum_r
    sums_ref[ROWS : 2 * ROWS, :] = sum_i
    sums_ref[2 * ROWS : 3 * ROWS, :] = sum_d


def recurrence_forward(pre, gates, admitted, params, length):
    tokens, width = admitted.shape
    tile = math.gcd(width, 512)
    n = width // tile
    near = pl.BlockSpec((length, tile), lambda s, j: (s, j))
    far = pl.BlockSpec((length, tile), lambda s, j: (s, j + n))
    vector = pl.BlockSpec((8, tile), lambda s, j: (0, j))
    return pl.pallas_call(
        forward_kernel,
        grid=(tokens // length, n),
        in_specs=[near, near, far, near, vector],
        out_specs=[near, near],
        out_shape=[
            jax.ShapeDtypeStruct((tokens, width), BF16),
            jax.ShapeDtypeStruct((tokens, width), F32),
        ],
        cost_estimate=pl.CostEstimate(flops=60 * tokens * width, bytes_accessed=20 * tokens * width, transcendentals=6 * tokens * width),
        name="recurrence_forward",
    )(pre, gates, gates, admitted, params)


def recurrence_backward(cot, pre, gates, admitted, before, params, length):
    tokens, width = admitted.shape
    tile = math.gcd(width, 512)
    n = width // tile
    near = pl.BlockSpec((length, tile), lambda s, j: (s, j))
    far = pl.BlockSpec((length, tile), lambda s, j: (s, j + n))
    vector = pl.BlockSpec((8, tile), lambda s, j: (0, j))
    low = jax.ShapeDtypeStruct((tokens, width), BF16)
    return pl.pallas_call(
        backward_kernel,
        grid=(tokens // length, n),
        in_specs=[near, near, near, far, near, near, vector],
        out_specs=[near, near, near, near, pl.BlockSpec((3 * ROWS, tile), lambda s, j: (s, j))],
        out_shape=[
            low, low, low,
            jax.ShapeDtypeStruct((tokens, width), F32),
            jax.ShapeDtypeStruct((3 * ROWS * (tokens // length), width), F32),
        ],
        cost_estimate=pl.CostEstimate(flops=120 * tokens * width, bytes_accessed=34 * tokens * width, transcendentals=8 * tokens * width),
        name="recurrence_backward",
    )(cot, pre, gates, gates, admitted, before, params)


def shifted(values, offset):
    if offset == 0:
        return values
    if offset > 0:
        return jnp.pad(values, ((0, 0), (offset, 0), (0, 0)))[:, : values.shape[1]]
    return jnp.pad(values, ((0, 0), (0, -offset), (0, 0)))[:, -offset:]


def body(
    groups, shards,
    tokens, cotangent, mix_gain, branch_proj, lruin_proj, conv_kernel, conv_bias, recur_proj, recur_bias,
    admit_proj, admit_bias, decay_param, out_proj, ffn_gain, ffn_gate, ffn_up, ffn_down,
):
    cores = 2
    f2 = 2 ** int(math.log2(math.isqrt(shards // cores)))
    f1 = shards // cores // f2
    side = lax.axis_index("rep") % 2
    here = lax.axis_index("shard")
    core, i2, i1 = here % cores, here // cores % f2, here // (cores * f2)
    taps = conv_kernel.shape[0]
    length, width = tokens.shape
    low_r = branch_proj.shape[1]
    half_r = low_r // 2
    half_f = ffn_gate.shape[1] // 2
    piece_f = half_f // shards

    def swap(v):
        return lax.ppermute(v, "rep", [(i, i ^ 1) for i in range(groups)])

    def swap_rows(v):
        v = swap(v)
        return jnp.concatenate([v[length:], v[:length]], axis=0)

    def mine(v, size, axis):
        return lax.dynamic_slice_in_dim(v, side * size, size, axis)

    def theirs(v, size, axis):
        return lax.dynamic_slice_in_dim(v, (1 - side) * size, size, axis)

    def natural(own, other):
        first = jnp.where(side == 0, own, other)
        second = jnp.where(side == 0, other, own)
        return jnp.concatenate([first, second], axis=-1)

    def with_pair(own):
        return jnp.concatenate([own, swap(own)], axis=0)

    clock = []

    def tick(*xs):
        return lax.optimization_barrier(tuple(xs) + tuple(clock))[: len(xs)]

    def tock(*ys):
        clock[:] = ys

    class Scatter:
        def __init__(self, v, kind=BF16):
            self.kind = kind
            rows, n = v.shape[0] // shards, v.shape[1]
            self.v = v.reshape(f1, f2, cores, rows, n)
            send = lax.dynamic_index_in_dim(self.v, 1 - core, 2, False)
            self.got = [lax.ppermute(send, "shard", [(s, s ^ 1) for s in range(shards)])]

        def step(self, v, at, count, axis, stride):
            keep = lax.dynamic_index_in_dim(v, at, axis, False)
            sends = [lax.dynamic_index_in_dim(v, (at + k) % count, axis, False).astype(self.kind) for k in range(1, count)]
            tock(keep, *sends)
            self.v, self.got = keep, []
            for k in range(1, count):
                perm = [(s, s + ((s // stride + k) % count - s // stride % count) * stride) for s in range(shards)]
                self.got.append(lax.ppermute(sends[k - 1], "shard", perm))

        def sum_core(self):
            v, got = tick(self.v, self.got[0])
            v = widen(lax.dynamic_index_in_dim(v, core, 2, False)) + widen(got)
            self.step(v, i2, f2, 1, cores)

        def sum_two(self):
            v, *got = tick(self.v, *self.got)
            for g in got:
                v = v + widen(g)
            self.step(v, i1, f1, 0, cores * f2)

        def sum_one(self):
            v, *got = tick(self.v, *self.got)
            for g in got:
                v = v + widen(g)
            for k in range(1, groups // 2):
                v = v + lax.ppermute(v, "rep", [(i, (i + 2 * k) % groups) for i in range(groups)])
            send = v.astype(self.kind)
            tock(v, send)
            self.v, self.got = v, swap(send)

        def both(self):
            v, got = tick(self.v, self.got)
            return v, widen(got)

    block = 512
    per_d, per_r = mix_gain.shape[0], conv_bias.shape[0]
    vectors = jnp.concatenate(
        [mix_gain, ffn_gain, conv_kernel.reshape(-1), conv_bias, recur_bias, admit_bias, decay_param]
    )
    count = vectors.shape[0]
    vectors = jnp.pad(vectors, (0, -count % 128)).reshape(-1, 128)
    vectors = lax.all_gather(vectors, "shard", axis=0).reshape(shards, -1)[:, :count]
    gain_one = widen(vectors[:, :per_d].reshape(width))
    gain_two = widen(vectors[:, per_d : 2 * per_d].reshape(width))
    channel = vectors[:, 2 * per_d :].reshape(shards, taps + 4, per_r).transpose(1, 0, 2).reshape(taps + 4, low_r)
    channel = widen(mine(channel, half_r, 1))
    taps_half, cbias = channel[:taps], channel[taps]
    rbias, abias, lam = channel[taps + 1], channel[taps + 2], channel[taps + 3]
    rate = DECAY_SCALE * jax.nn.softplus(-lam)
    params = jnp.concatenate([jnp.stack([rbias, abias, rate]), jnp.zeros((5, half_r), F32)])

    def ffn_half(v):
        return lax.dynamic_index_in_dim(v.reshape(v.shape[0], shards, 2, piece_f), side, 2, False).reshape(v.shape[0], half_f)

    def gather_blocks(parts):
        rows = [p[:, at : at + block] for p in parts for at in range(0, p.shape[1], block)]
        whole = lax.all_gather(jnp.concatenate(rows, axis=0), "shard", axis=0)
        out, at = [], 0
        for p in parts:
            cols = []
            for _ in range(0, p.shape[1], block):
                cols.append(whole[:, at : at + p.shape[0]].reshape(shards * p.shape[0], block))
                at += p.shape[0]
            out.append(jnp.concatenate(cols, axis=1))
        return out

    w1, w2, w3 = gather_blocks([
        jnp.concatenate([mine(branch_proj, half_r, 1), mine(lruin_proj, half_r, 1)], axis=1),
        jnp.concatenate([mine(recur_proj, half_r, 1), mine(admit_proj, half_r, 1)], axis=1),
        out_proj,
    ])
    w4, w5 = gather_blocks([
        jnp.concatenate([ffn_half(ffn_gate), ffn_half(ffn_up)], axis=1),
        mine(ffn_down, piece_f, 0),
    ])

    def norm_back(cot, v, scale, gain):
        g = cot * gain
        return scale * (g - v * (scale * scale * jnp.mean(g * v, axis=-1, keepdims=True)))

    values = widen(with_pair(tokens))
    cot_pair = with_pair(cotangent)
    scale_one = lax.rsqrt(jnp.mean(values * values, axis=-1, keepdims=True) + EPS)
    normed = (values * scale_one * gain_one).astype(BF16)
    pre = matmul(normed, w1)
    lru_pre = pre[:, half_r:].reshape(2, length, half_r)
    conv = cbias
    for k in range(taps):
        conv = conv + taps_half[k] * shifted(lru_pre, k)
    admitted = conv.reshape(2 * length, half_r).astype(BF16)
    admitted_all = natural(admitted, swap_rows(admitted))
    gates = matmul(admitted_all, w2)
    mixed, before = recurrence_forward(pre, gates, admitted, params, length)
    mixed_other = jnp.concatenate([swap(mixed[length:]), swap(mixed[:length])], axis=0)
    mixed_all = natural(mixed, mixed_other)
    middle = widen(tokens) + matmul(mixed_all[:length], w3)
    scale_two = lax.rsqrt(jnp.mean(middle * middle, axis=-1, keepdims=True) + EPS)
    normed_two = with_pair((middle * scale_two * gain_two).astype(BF16))
    wide = matmul(normed_two, w4)
    gate_pre, up_pre = wide[:, :half_f], wide[:, half_f:]
    hidden = (gelu(gate_pre) * up_pre).astype(BF16)

    hidden_cot = cols_product(cot_pair, w5)
    gate_cot = (hidden_cot * up_pre * gelu_slope(gate_pre)).astype(BF16)
    up_cot = (hidden_cot * gelu(gate_pre)).astype(BF16)
    wide_cot = jnp.concatenate([gate_cot, up_cot], axis=1)
    part = cols_product(wide_cot, w4)
    tock(part)
    near, far = part[:length], swap(part[length:].astype(BF16))

    def grad(left, right):
        left, right = tick(left, right)
        out = rows_product(left, right).astype(BF16)
        tock(out)
        return Scatter(out)

    down_s = grad(hidden, cot_pair)
    gate_s = grad(normed_two, gate_cot)
    down_s.sum_core()
    near, far = tick(near, far)
    middle_cot = widen(cotangent) + norm_back(near + widen(far), middle, scale_two, gain_two)
    middle_low = middle_cot.astype(BF16)
    tock(middle_low)
    out_cot = with_pair(middle_low)
    up_s = grad(normed_two, up_cot)
    gate_s.sum_core()
    out_cot, = tick(out_cot)
    mixed_cot = cols_product(out_cot, mine(w3, half_r, 0))
    branch_low, recur_low, admit_low, direct, sums = recurrence_backward(
        mixed_cot, pre, gates, admitted, before, params, length
    )
    gates_cot = jnp.concatenate([recur_low, admit_low], axis=1)
    part = cols_product(gates_cot, w2)
    tock(part)
    near, far = mine(part, half_r, 1), swap_rows(theirs(part, half_r, 1).astype(BF16))
    out_s = grad(mixed_all, mine(out_cot, width // 2, 1))
    down_s.sum_two()
    up_s.sum_core()
    branch_s = grad(normed, branch_low)
    recur_s = grad(admitted_all, recur_low)
    admit_s = grad(admitted_all, admit_low)
    direct, near, far = tick(direct, near, far)
    admitted_cot = (direct + near + widen(far)).reshape(2, length, half_r)
    lru_cot = jnp.zeros_like(admitted_cot)
    kernel_grad = []
    for k in range(taps):
        lru_cot = lru_cot + taps_half[k] * shifted(admitted_cot, -k)
        kernel_grad.append(jnp.sum(admitted_cot * shifted(lru_pre, k), axis=(0, 1)))
    lru_cot = lru_cot.reshape(2 * length, half_r).astype(BF16)
    part = cols_product(jnp.concatenate([branch_low, lru_cot], axis=1), w1)
    tock(part)
    near, far = part[:length], swap(part[length:].astype(BF16))
    lruin_s = grad(normed, lru_cot)
    sums = jnp.sum(sums.reshape(2, 3, ROWS, half_r), axis=(0, 2))
    small = jnp.stack(
        kernel_grad
        + [jnp.sum(admitted_cot, axis=(0, 1)), sums[0], sums[1], sums[2] * (DECAY_SCALE * jax.nn.sigmoid(-lam))]
    )
    small = natural(small, jnp.zeros_like(small))
    small_s = Scatter(small.reshape(taps + 4, shards, per_r).transpose(1, 0, 2).reshape(shards * (taps + 4), per_r), F32)
    gate_s.sum_two()
    out_s.sum_core()
    small_s.sum_core()
    near, far = tick(near, far)
    tokens_grad = middle_cot + norm_back(near + widen(far), values[:length], scale_one[:length], gain_one)
    tock(tokens_grad)
    small_s.sum_two()
    hidden_late, = tick(hidden)
    down = matmul(hidden_late, w5)
    tock(down)
    down_far = swap(down[length:].astype(BF16))
    down_s.sum_one()
    up_s.sum_two()
    branch_s.sum_core()
    small_s.sum_one()
    near, far = tick(down[:length], down_far)
    block_out = (middle + near + widen(far)).astype(BF16)
    tock(block_out)
    gate_s.sum_one()
    a, b = down_s.both()
    ffndown_grad = jnp.concatenate([jnp.where(side == 0, a, b), jnp.where(side == 0, b, a)], axis=0)
    tock(ffndown_grad)
    a, b = small_s.both()
    small = a + b

    def weave(own, other):
        first = jnp.where(side == 0, own, other).reshape(-1, shards, 1, piece_f)
        second = jnp.where(side == 0, other, own).reshape(-1, shards, 1, piece_f)
        return jnp.concatenate([first, second], axis=2).reshape(own.shape[0], 2 * half_f)

    out_s.sum_two()
    recur_s.sum_core()
    up_s.sum_one()
    ffngate_grad = weave(*gate_s.both())
    tock(ffngate_grad)
    branch_s.sum_two()
    admit_s.sum_core()
    out_s.sum_one()
    ffnup_grad = weave(*up_s.both())
    tock(ffnup_grad)
    recur_s.sum_two()
    lruin_s.sum_core()
    branch_s.sum_one()
    outproj_grad = natural(*out_s.both())
    tock(outproj_grad)
    admit_s.sum_two()
    recur_s.sum_one()
    branch_grad = natural(*branch_s.both())
    tock(branch_grad)
    lruin_s.sum_two()
    ffngain_grad = jnp.sum(ffngate_grad * widen(ffn_gate) + ffnup_grad * widen(ffn_up), axis=1) / widen(ffn_gain)
    admit_s.sum_one()
    recur_grad = natural(*recur_s.both())
    tock(recur_grad)
    lruin_s.sum_one()
    admit_grad = natural(*admit_s.both())
    tock(admit_grad)
    lruin_grad = natural(*lruin_s.both())
    mixgain_grad = jnp.sum(branch_grad * widen(branch_proj) + lruin_grad * widen(lruin_proj), axis=1) / widen(mix_gain)
    return (
        block_out, tokens_grad, mixgain_grad, branch_grad, lruin_grad, small[:taps], small[taps], recur_grad,
        small[taps + 1], admit_grad, small[taps + 2], small[taps + 3], outproj_grad, ffngain_grad, ffngate_grad,
        ffnup_grad, ffndown_grad,
    )


def solution(mesh):
    groups, shards = mesh.shape["rep"], mesh.shape["shard"]
    whole = P(("rep", "shard"), None)
    row, vec, col = P("shard", None), P("shard"), P(None, "shard")
    in_specs = (whole, whole, vec, row, row, col, vec, row, vec, row, vec, vec, row, vec, row, row, row)
    out_specs = (whole, whole, vec, row, row, col, vec, row, vec, row, vec, vec, row, vec, row, row, row)
    return jax.shard_map(
        functools.partial(body, groups, shards), mesh=mesh, in_specs=in_specs, out_specs=out_specs, check_vma=False
    )
```

time: 2900 us -> 872 us (0.30)
  waiting for transfers between devices: 2040 us -> 322 us
  blocking collectives: 192 us -> 22.7 us
  local copies, waits for them, and re-layouts: 323 us -> 172 us
  starting transfers between devices: 1.1 us -> 127 us
  matrix products: 213 us -> 108 us
    reduce_scatter x8 -> x0, waiting for transfers between devices: 1510 us -> none  [the longest x1 272 us: body(): lax.psum_scatter(grad_down, 'shard', scatter_dimension=0, tiled=True)]
    psum x1 -> x0, waiting for transfers between devices: 204 us -> none  [body(): lax.psum((mixer_shares[0], mixer_shares[1], mixer_shares[2], mixer_shares...]
    ppermute x0 -> x65, waiting for transfers between devices: none -> 174 us  [the longest x20 89.7 us: swap(): return lax.ppermute(v, 'rep', [(i, i ^ 1) for i in range(groups)])]
    all_gather x8 -> x2, waiting for transfers between devices: 322 us -> 148 us  [gather_blocks(): whole = lax.all_gather(jnp.concatenate(rows, axis=0), 'shard', axis=0)]
    pad x61 -> x0, local copies, waits for them, and re-layouts: 171 us -> none  [recurrence(): factors, states = lax.associative_scan(combine, (decay, inflow), axis=0)]
    ppermute x0 -> x65, starting transfers between devices: none -> 127 us  [the longest x36 103 us: step(): self.got.append(lax.ppermute(sends[k - 1], 'shard', perm))]
    unnamed x2 -> x0, blocking collectives: 96 us -> none
    slice x61 -> x26, local copies, waits for them, and re-layouts: 121 us -> 29.7 us  [the longest x4 21.9 us: gather_blocks(): whole[:, at:at + p.shape[0]].reshape(shards * p.shape[0], block)]
  transfers between devices with their start and end apart: 18 -> 67, of which waited for: 14 -> 26; matrix products, arithmetic and copies ran while one was open for 11% -> 30% of each run, Pallas kernels for 0% -> 1%
where the time goes in v1:
time: 872 us; the launch traced here: 867 us
  waiting for transfers between devices  322 us (37%)
  local copies, waits for them, and re-layouts  172 us (20%)
  starting transfers between devices  127 us (15%)
  matrix products  108 us (12%)
  other arithmetic  78.7 us (9%)
  blocking collectives  22.7 us (3%)
  Pallas kernels  20.4 us (2%)
  between operations  16.4 us (2%)
    all_gather x2, waiting for transfers between devices, gather_blocks(): whole = lax.all_gather(jnp.concatenate(rows, axis=0), 'shard', axis=0)  148 us
    ppermute x36, starting transfers between devices, step(): self.got.append(lax.ppermute(sends[k - 1], 'shard', perm))  103 us
    ppermute x20, waiting for transfers between devices, swap(): return lax.ppermute(v, 'rep', [(i, i ^ 1) for i in range(groups)])  89.7 us
    ppermute x36, waiting for transfers between devices, step(): self.got.append(lax.ppermute(sends[k - 1], 'shard', perm))  84.7 us
    unnamed x332, local copies, waits for them, and re-layouts  64.9 us
    dot_general x5, matrix products, cols_product(): lax.dot_general(left, right, (((1,), (1,)), ((), ())), preferred_element_...  38.3 us
    dot_general x8, matrix products, rows_product(): lax.dot_general(left, right, (((0,), (0,)), ((), ())), preferred_element_...  35.4 us
    dot_general x5, matrix products, matmul(): return jnp.dot(left, right, preferred_element_type=F32)  34.1 us
  transfers between devices with their start and end apart: 67, of which 26 were waited for; matrix products, arithmetic and copies ran while one was open for 30% of the time, Pallas kernels for 1%

profile of v1, /device:TPU:0, one launch (start us, length us, event | category | flops | bytes accessed | tf_op | source)
XLA Modules:
  0.0 867.0 jit_solution(12118025931689228142)
XLA Ops:
  30.1 3.0 collective-permute-start
  35.3 22.7 %all_gather.15 = bf16[16,10,128]{2,1,0:T(8,128)(2,1)S(1)} all-gather(bf16[1,10,128]{2,1,0:T(8,128)(2,1)S(1)} %pad_bitcast_fusion), channel_id=1, replica_groups=mesh['rep'=2,'shard'=16] {'shard'}, dimensions={0}, use_global_device_ids=true | all-gather | bytes 43520 | tf_op jit(solution)/shard_map/all_gather | solution.py:268
  60.6 6.9 collective-permute-done.5
  70.1 60.6 %all-gather.5.cloned.1.call-done = bf16[20480,512]{1,0:T(8,128)(2,1)} async-done(((bf16[1280,512]{1,0:T(8,128)(2,1)}), bf16[20480,512]{1,0:T(8,128)(2,1)}) %all-gather.5.cloned.1.call-update) | async-done | bytes 20971536 | tf_op jit(solution)/shard_map/all_gather | solution.py:283
  130.6 5.1 fusion.98
  135.8 8.5 fusion.34.pre_ref
  150.3 5.3 fusion.97
  155.7 87.5 %all-gather.7.cloned.1.call-done = bf16[20736,512]{1,0:T(8,128)(2,1)} async-done(((bf16[1296,512]{1,0:T(8,128)(2,1)}), bf16[20736,512]{1,0:T(8,128)(2,1)}) %all-gather.7.cloned.1.call-update) | async-done | bytes 21233680 | tf_op jit(solution)/shard_map/all_gather | solution.py:283
  243.1 7.8 fusion.96
  262.3 6.5 fusion.33.gates_r_ref.gates_i_ref
  268.8 8.4 recurrence_forward.1
  283.3 10.0 %collective-permute-done.2 = bf16[256,1024]{1,0:T(8,128)(2,1)S(1)} collective-permute-done((bf16[256,1024]{1,0:T(8,128)(2,1)S(1)}, bf16[256,1024]{1,0:T(8,128)(2,1)S(1)}, u32[]{:S(2)}, u32[]{:S(2)}) %collective-permute-start.2) | collective-permute-done | bytes 524320 | tf_op jit(solution)/shard_map/ppermute | solution.py:191
  293.4 10.5 %collective-permute-done.3 = bf16[256,1024]{1,0:T(8,128)(2,1)S(1)} collective-permute-done((bf16[256,1024]{1,0:T(8,128)(2,1)S(1)}, bf16[256,1024]{1,0:T(8,128)(2,1)S(1)}, u32[]{:S(2)}, u32[]{:S(2)}) %collective-permute-start.3) | collective-permute-done | bytes 524320 | tf_op jit(solution)/shard_map/ppermute | solution.py:191
  313.3 3.6 fusion.95
  316.9 11.1 %collective-permute-done.4 = bf16[256,1536]{1,0:T(8,128)(2,1)S(1)} collective-permute-done((bf16[256,1536]{1,0:T(8,128)(2,1)S(1)}, bf16[256,1536]{1,0:T(8,128)(2,1)S(1)}, u32[]{:S(2)}, u32[]{:S(2)}) %collective-permute-start.4) | collective-permute-done | bytes 786464 | tf_op jit(solution)/shard_map/ppermute | solution.py:191
  328.1 13.5 %fusion.84 = f32[512,4608]{1,0:T(8,128)} fusion(bf16[1536,4608]{1,0:T(8,128)(2,1)} %constant_dynamic-update-slice_fusion.11, bf16[256,1536]{1,0:T(8,128)(2,1)S(1)} %collective-permute-done.4, bf16[256,1536]{1,0:T(8,128)(2,1)S(1)} %multiply_convert_fusion.3), kind=kOutput, calls=%fused_computation.326 | convolution fusion | flops 7250903040 | bytes 25165824 | tf_op jit(solution)/shard_map/dot_general | solution.py:22
  341.6 10.6 %fusion.6 = (bf16[512,2304]{1,0:T(8,128)(2,1)}, bf16[512,2304]{1,0:T(8,128)(2,1)S(1)}, bf16[512,2304]{1,0:T(8,128)(2,1)}) fusion(f32[512,4608]{1,0:T(8,128)} %fusion.84, bf16[512,1536]{1,0:T(8,128)(2,1)} %constant_dynamic-update-slice_fusion.20, bf16[2304,512]{1,0:T(8,128)(2,1)S(1)} %bitcast.331, bf16[2304,512]{1,0:T(8,128)(2,1)S(1)} %bitcast.333, ...), kind=kOutput, calls=%fused_computation.18 | convolution fusion | flops 3674603520 | bytes 25165824 | tf_op jit(solution)/shard_map/dot_general | solution.py:30
  352.1 13.5 %fusion.7 = f32[512,1536]{1,0:T(8,128)} fusion(bf16[1536,4608]{1,0:T(8,128)(2,1)} %constant_dynamic-update-slice_fusion.11, bf16[512,2304]{1,0:T(8,128)(2,1)S(1)} %get-tuple-element.151, bf16[512,2304]{1,0:T(8,128)(2,1)} %get-tuple-element.145), kind=kOutput, calls=%fused_computation.19 | convolution fusion | flops 7257194496 | bytes 22020096 | tf_op jit(solution)/shard_map/dot_general | solution.py:30
  365.6 5.5 convolution_convert_fusion.2
  378.5 4.5 pad_maximum_fusion.3
  386.7 4.3 convolution_convert_fusion.1
  397.7 3.0 convert_add_fusion.2
  404.4 11.4 %collective-permute-done.6 = bf16[256,1536]{1,0:T(8,128)(2,1)S(1)} collective-permute-done((bf16[256,1536]{1,0:T(8,128)(2,1)S(1)}, bf16[256,1536]{1,0:T(8,128)(2,1)S(1)}, u32[]{:S(2)}, u32[]{:S(2)}) %collective-permute-start.6) | collective-permute-done | bytes 786464 | tf_op jit(solution)/shard_map/ppermute | solution.py:191
  419.6 4.1 convolution_convert_fusion
  436.4 3.2 fusion.11.cot_ref
  439.6 12.0 %recurrence_backward.1 = (bf16[512,1024]{1,0:T(8,128)(2,1)}, bf16[512,1024]{1,0:T(8,128)(2,1)}, bf16[512,1024]{1,0:T(8,128)(2,1)}, f32[512,1024]{1,0:T(8,128)}, f32[96,1024]{1,0:T(8,128)}) custom-call(f32[512,1024]{1,0:T(8,128)} %fusion.11.cot_ref, f32[512,2048]{1,0:T(8,128)} %copy-done, f32[512,2048]{1,0:T(8,128)} %fusion.33.gates_r_ref.gates_i_ref, ...), custom_call_target="tpu_custom_call" | custom-call | flops 62914560 | bytes 17825792 | tf_op jit(solution)/shard_map/recurrence_backward/pallas_call | solution.py:149
  451.7 7.6 fusion.22
  462.9 3.7 convolution_convert_fusion.7
  476.3 8.8 %collective-permute-done.10 = bf16[512,1024]{1,0:T(8,128)(2,1)} collective-permute-done((bf16[512,1024]{1,0:T(8,128)(2,1)}, bf16[512,1024]{1,0:T(8,128)(2,1)}, u32[]{:S(2)}, u32[]{:S(2)}) %collective-permute-start.10) | collective-permute-done | bytes 1048608 | tf_op jit(solution)/shard_map/ppermute | solution.py:191
  497.7 3.5 convolution_convert_fusion.6
  501.2 4.4 convolution_convert_fusion.5
  505.6 4.4 convolution_convert_fusion.4
  513.2 3.5 fusion.26
  519.2 5.4 convolution_convert_fusion.3
  531.7 2.8 fusion.47
  549.6 8.6 collective-permute-done.17
  561.5 27.9 %collective-permute-done.16 = f32[4,8,128]{2,1,0:T(8,128)S(1)} collective-permute-done((f32[4,8,128]{2,1,0:T(8,128)S(1)}, f32[4,8,128]{2,1,0:T(8,128)S(1)}, u32[]{:S(2)}, u32[]{:S(2)}) %collective-permute-start.16) | collective-permute-done | bytes 16416 | tf_op jit(solution)/shard_map/ppermute | solution.py:234
  590.7 3.8 fusion.13
  607.3 2.8 fusion.50
  617.9 3.0 collective-permute-start.30
  621.6 7.9 collective-permute-done.18
  631.3 17.2 %collective-permute-done.29 = bf16[96,2304]{1,0:T(8,128)(2,1)} collective-permute-done((bf16[96,2304]{1,0:T(8,128)(2,1)S(1)}, bf16[96,2304]{1,0:T(8,128)(2,1)}, u32[]{:S(2)}, u32[]{:S(2)}) %collective-permute-start.29) | collective-permute-done | bytes 442400 | tf_op jit(solution)/shard_map/ppermute | solution.py:234
  656.0 2.8 fusion.92
  668.9 8.1 collective-permute-start.32
  681.8 3.2 convert_add_fusion.4
  687.6 2.9 collective-permute-done.32
  690.5 14.5 %collective-permute-start.44 = (bf16[128,768]{1,0:T(8,128)(2,1)}, bf16[128,768]{1,0:T(8,128)(2,1)}, u32[]{:S(2)}, u32[]{:S(2)}) collective-permute-start(bf16[128,768]{1,0:T(8,128)(2,1)} %get-tuple-element.399), channel_id=1, source_target_pairs={{0,4},{1,5},{2,6},{3,7},{4,8},{5,9},{6,10},{7,11},{8,12},{9,13},{1... | collective-permute-start | bytes 589832 | tf_op jit(solution)/shard_map/ppermute | solution.py:234
  704.9 4.5 collective-permute-done.33
  715.8 5.8 collective-permute-done.31
  726.2 14.0 %collective-permute-done.27 = bf16[4,96,1024]{2,1,0:T(8,128)(2,1)S(1)} collective-permute-done((bf16[4,96,1024]{2,1,0:T(8,128)(2,1)}, bf16[4,96,1024]{2,1,0:T(8,128)(2,1)S(1)}, u32[]{:S(2)}, u32[]{:S(2)}) %collective-permute-start.27) | collective-permute-done | bytes 786464 | tf_op jit(solution)/shard_map/ppermute | solution.py:234
  740.2 4.1 collective-permute-start.46
  754.2 11.3 %collective-permute-start.38 = (bf16[96,1024]{1,0:T(8,128)(2,1)}, bf16[96,1024]{1,0:T(8,128)(2,1)}, u32[]{:S(2)}, u32[]{:S(2)}) collective-permute-start(bf16[96,1024]{1,0:T(8,128)(2,1)} %get-tuple-element.396), channel_id=1, source_target_pairs={{0,4},{1,5},{2,6},{3,7},{4,8},{5,9},{6,10},{7,11},{8,12},{9,13},{1... | collective-permute-start | bytes 589832 | tf_op jit(solution)/shard_map/ppermute | solution.py:234
  769.7 3.0 collective-permute-start.40
  777.9 3.0 copy.166
  780.9 2.8 add_reduce_fusion
  791.8 3.6 collective-permute-start.49
  801.2 9.1 %collective-permute-done.52 = bf16[4,128,1024]{2,1,0:T(8,128)(2,1)S(1)} collective-permute-done((bf16[4,128,1024]{2,1,0:T(8,128)(2,1)S(1)}, bf16[4,128,1024]{2,1,0:T(8,128)(2,1)S(1)}, u32[]{:S(2)}, u32[]{:S(2)}) %collective-permute-start.52) | collective-permute-done | bytes 1048608 | tf_op jit(solution)/shard_map/ppermute | solution.py:234
  810.3 4.5 collective-permute-start.51
  815.5 3.0 collective-permute-start.60
  818.5 4.6 collective-permute-done.51
  823.2 2.8 collective-permute-start.61
  827.8 9.0 %collective-permute-start.55 = (bf16[96,1024]{1,0:T(8,128)(2,1)S(1)}, bf16[96,1024]{1,0:T(8,128)(2,1)S(1)}, u32[]{:S(2)}, u32[]{:S(2)}) collective-permute-start(bf16[96,1024]{1,0:T(8,128)(2,1)S(1)} %get-tuple-element.393), channel_id=1, source_target_pairs={{0,4},{1,5},{2,6},{3,7},{4,8},{5,9},{6,10},{7,11},{8,12},{9,13},{1... | collective-permute-start | bytes 589832 | tf_op jit(solution)/shard_map/ppermute | solution.py:234
  841.1 8.0 collective-permute-start.57
  852.9 2.8 collective-permute-done.63
  (611 shorter events, 264.5 us)
Async XLA Ops:
  7.2 123.4 %all-gather.5.cloned.1.call-start = ((), (), s32[]{:S(2)}) async-start(), calls=%async_computation | async-start | bytes 22282240 | tf_op jit(solution)/shard_map/all_gather | solution.py:283
  18.5 224.6 %all-gather.7.cloned.1.call-start = ((), (), s32[]{:S(2)}) async-start(), calls=%async_computation.1 | async-start | bytes 22560768 | tf_op jit(solution)/shard_map/all_gather | solution.py:283
  30.1 30.1 %collective-permute-start = (bf16[256,1536]{1,0:T(8,128)(2,1)S(1)}, bf16[256,1536]{1,0:T(8,128)(2,1)S(1)}, u32[]{:S(2)}, u32[]{:S(2)}) collective-permute-start(bf16[256,1536]{1,0:T(8,128)(2,1)S(1)} %copy-done.23), channel_id=1, source_target_pairs={{0,16},{16,0},{1,17},{17,1},{2,18},{18,2},{3,19},{19,3},{4,20},{20... | collective-permute-start | bytes 2359304 | tf_op jit(solution)/shard_map/ppermute | solution.py:191
  33.1 34.4 %collective-permute-start.5 = (bf16[256,1536]{1,0:T(8,128)(2,1)S(1)}, bf16[256,1536]{1,0:T(8,128)(2,1)S(1)}, u32[]{:S(2)}, u32[]{:S(2)}) collective-permute-start(bf16[256,1536]{1,0:T(8,128)(2,1)S(1)} %copy-done.51), channel_id=1, source_target_pairs={{0,16},{16,0},{1,17},{17,1},{2,18},{18,2},{3,19},{19,3},{4,20},{20... | collective-permute-start | bytes 2359304 | tf_op jit(solution)/shard_map/ppermute | solution.py:191
  148.8 109.0 %collective-permute-start.1 = (bf16[512,1024]{1,0:T(8,128)(2,1)S(1)}, bf16[512,1024]{1,0:T(8,128)(2,1)}, u32[]{:S(2)}, u32[]{:S(2)}) collective-permute-start(bf16[512,1024]{1,0:T(8,128)(2,1)S(1)} %bitcast.279), channel_id=1, source_target_pairs={{0,16},{16,0},{1,17},{17,1},{2,18},{18,2},{3,19},{19,3},{4,20},{20... | collective-permute-start | bytes 3145736 | tf_op jit(solution)/shard_map/ppermute | solution.py:191
  278.5 14.8 %collective-permute-start.2 = (bf16[256,1024]{1,0:T(8,128)(2,1)S(1)}, bf16[256,1024]{1,0:T(8,128)(2,1)S(1)}, u32[]{:S(2)}, u32[]{:S(2)}) collective-permute-start(bf16[256,1024]{1,0:T(8,128)(2,1)S(1)} %get-tuple-element.405), channel_id=1, source_target_pairs={{0,16},{16,0},{1,17},{17,1},{2,18},{18,2},{3,19},{19,3},{4,20},{20... | collective-permute-start | bytes 1572872 | tf_op jit(solution)/shard_map/ppermute | solution.py:191
  280.1 23.9 %collective-permute-start.3 = (bf16[256,1024]{1,0:T(8,128)(2,1)S(1)}, bf16[256,1024]{1,0:T(8,128)(2,1)S(1)}, u32[]{:S(2)}, u32[]{:S(2)}) collective-permute-start(bf16[256,1024]{1,0:T(8,128)(2,1)S(1)} %get-tuple-element.404), channel_id=1, source_target_pairs={{0,16},{16,0},{1,17},{17,1},{2,18},{18,2},{3,19},{19,3},{4,20},{20... | collective-permute-start | bytes 1572872 | tf_op jit(solution)/shard_map/ppermute | solution.py:191
  309.1 19.0 %collective-permute-start.4 = (bf16[256,1536]{1,0:T(8,128)(2,1)S(1)}, bf16[256,1536]{1,0:T(8,128)(2,1)S(1)}, u32[]{:S(2)}, u32[]{:S(2)}) collective-permute-start(bf16[256,1536]{1,0:T(8,128)(2,1)S(1)} %multiply_convert_fusion.3), channel_id=1, source_target_pairs={{0,16},{16,0},{1,17},{17,1},{2,18},{18,2},{3,19},{19,3},{4,20},{20... | collective-permute-start | bytes 2359304 | tf_op jit(solution)/shard_map/ppermute | solution.py:191
  375.1 21.9 %collective-permute-start.7 = (bf16[4,2,144,1536]{3,2,0,1:T(8,128)(2,1)}, bf16[4,2,144,1536]{3,2,0,1:T(8,128)(2,1)}, u32[]{:S(2)}, u32[]{:S(2)}) collective-permute-start(bf16[4,2,144,1536]{3,2,0,1:T(8,128)(2,1)} %copy_bitcast_fusion), channel_id=1, source_target_pairs={{0,1},{1,0},{2,3},{3,2},{4,5},{5,4},{6,7},{7,6},{8,9},{9,8},{10,11... | collective-permute-start | bytes 10616840 | tf_op jit(solution)/shard_map/ppermute | solution.py:225
  393.2 30.6 %collective-permute-start.9 = (bf16[4,2,96,2304]{3,2,1,0:T(8,128)(2,1)}, bf16[4,2,96,2304]{3,2,1,0:T(8,128)(2,1)}, u32[]{:S(2)}, u32[]{:S(2)}) collective-permute-start(bf16[4,2,96,2304]{3,2,1,0:T(8,128)(2,1)} %dynamic-slice_bitcast_fusion.3), channel_id=1, source_target_pairs={{0,1},{1,0},{2,3},{3,2},{4,5},{5,4},{6,7},{7,6},{8,9},{9,8},{10,11... | collective-permute-start | bytes 10616840 | tf_op jit(solution)/shard_map/ppermute | solution.py:225
  395.5 20.4 %collective-permute-start.6 = (bf16[256,1536]{1,0:T(8,128)(2,1)S(1)}, bf16[256,1536]{1,0:T(8,128)(2,1)S(1)}, u32[]{:S(2)}, u32[]{:S(2)}) collective-permute-start(bf16[256,1536]{1,0:T(8,128)(2,1)S(1)} %slice.513), channel_id=1, source_target_pairs={{0,16},{16,0},{1,17},{17,1},{2,18},{18,2},{3,19},{19,3},{4,20},{20... | collective-permute-start | bytes 2359304 | tf_op jit(solution)/shard_map/ppermute | solution.py:191
  416.8 19.5 %collective-permute-start.8 = (bf16[256,1536]{1,0:T(8,128)(2,1)S(1)}, bf16[256,1536]{1,0:T(8,128)(2,1)S(1)}, u32[]{:S(2)}, u32[]{:S(2)}) collective-permute-start(bf16[256,1536]{1,0:T(8,128)(2,1)S(1)} %get-tuple-element.340), channel_id=1, source_target_pairs={{0,16},{16,0},{1,17},{17,1},{2,18},{18,2},{3,19},{19,3},{4,20},{20... | collective-permute-start | bytes 2359304 | tf_op jit(solution)/shard_map/ppermute | solution.py:191
  418.3 51.9 %collective-permute-start.12 = (bf16[4,144,1536]{2,1,0:T(8,128)(2,1)}, bf16[4,144,1536]{2,1,0:T(8,128)(2,1)}, u32[]{:S(2)}, u32[]{:S(2)}) collective-permute-start(bf16[4,144,1536]{2,1,0:T(8,128)(2,1)} %fusion.30), channel_id=1, source_target_pairs={{0,2},{1,3},{2,0},{3,1},{4,6},{5,7},{6,4},{7,5},{8,10},{9,11},{10,... | collective-permute-start | bytes 5308424 | tf_op jit(solution)/shard_map/ppermute | solution.py:234
  427.6 61.2 %collective-permute-start.11 = (bf16[4,2,96,2304]{3,2,1,0:T(8,128)(2,1)}, bf16[4,2,96,2304]{3,2,1,0:T(8,128)(2,1)}, u32[]{:S(2)}, u32[]{:S(2)}) collective-permute-start(bf16[4,2,96,2304]{3,2,1,0:T(8,128)(2,1)} %dynamic-slice_bitcast_fusion.1), channel_id=1, source_target_pairs={{0,1},{1,0},{2,3},{3,2},{4,5},{5,4},{6,7},{7,6},{8,9},{9,8},{10,11... | collective-permute-start | bytes 10616840 | tf_op jit(solution)/shard_map/ppermute | solution.py:225
  431.8 92.8 %collective-permute-start.15 = (bf16[4,96,2304]{2,1,0:T(8,128)(2,1)}, bf16[4,96,2304]{2,1,0:T(8,128)(2,1)}, u32[]{:S(2)}, u32[]{:S(2)}) collective-permute-start(bf16[4,96,2304]{2,1,0:T(8,128)(2,1)} %fusion.31), channel_id=1, source_target_pairs={{0,2},{1,3},{2,0},{3,1},{4,6},{5,7},{6,4},{7,5},{8,10},{9,11},{10,... | collective-permute-start | bytes 5308424 | tf_op jit(solution)/shard_map/ppermute | solution.py:234
  460.5 24.6 %collective-permute-start.10 = (bf16[512,1024]{1,0:T(8,128)(2,1)}, bf16[512,1024]{1,0:T(8,128)(2,1)}, u32[]{:S(2)}, u32[]{:S(2)}) collective-permute-start(bf16[512,1024]{1,0:T(8,128)(2,1)} %dynamic-slice_convert_fusion.5), channel_id=1, source_target_pairs={{0,16},{16,0},{1,17},{17,1},{2,18},{18,2},{3,19},{19,3},{4,20},{20... | collective-permute-start | bytes 3145736 | tf_op jit(solution)/shard_map/ppermute | solution.py:191
  468.1 66.5 %collective-permute-start.14 = (bf16[4,2,128,768]{3,2,0,1:T(8,128)(2,1)}, bf16[4,2,128,768]{3,2,0,1:T(8,128)(2,1)}, u32[]{:S(2)}, u32[]{:S(2)}) collective-permute-start(bf16[4,2,128,768]{3,2,0,1:T(8,128)(2,1)} %copy_bitcast_fusion.5), channel_id=1, source_target_pairs={{0,1},{1,0},{2,3},{3,2},{4,5},{5,4},{6,7},{7,6},{8,9},{9,8},{10,11... | collective-permute-start | bytes 4718600 | tf_op jit(solution)/shard_map/ppermute | solution.py:225
  473.8 122.4 %collective-permute-start.24 = (bf16[144,1536]{1,0:T(8,128)(2,1)}, bf16[144,1536]{1,0:T(8,128)(2,1)}, u32[]{:S(2)}, u32[]{:S(2)}) collective-permute-start(bf16[144,1536]{1,0:T(8,128)(2,1)} %get-tuple-element.376), channel_id=1, source_target_pairs={{0,4},{1,5},{2,6},{3,7},{4,8},{5,9},{6,10},{7,11},{8,12},{9,13},{1... | collective-permute-start | bytes 1327112 | tf_op jit(solution)/shard_map/ppermute | solution.py:234
  485.1 111.1 %collective-permute-start.25 = (bf16[144,1536]{1,0:T(8,128)(2,1)}, bf16[144,1536]{1,0:T(8,128)(2,1)}, u32[]{:S(2)}, u32[]{:S(2)}) collective-permute-start(bf16[144,1536]{1,0:T(8,128)(2,1)} %get-tuple-element.375), channel_id=1, source_target_pairs={{0,8},{1,9},{2,10},{3,11},{4,12},{5,13},{6,14},{7,15},{8,0},{9,1},... | collective-permute-start | bytes 1327112 | tf_op jit(solution)/shard_map/ppermute | solution.py:234
  488.8 107.9 %collective-permute-start.26 = (bf16[144,1536]{1,0:T(8,128)(2,1)}, bf16[144,1536]{1,0:T(8,128)(2,1)}, u32[]{:S(2)}, u32[]{:S(2)}) collective-permute-start(bf16[144,1536]{1,0:T(8,128)(2,1)} %get-tuple-element.374), channel_id=1, source_target_pairs={{0,12},{1,13},{2,14},{3,15},{4,0},{5,1},{6,2},{7,3},{8,4},{9,5},{1... | collective-permute-start | bytes 1327112 | tf_op jit(solution)/shard_map/ppermute | solution.py:234
  524.6 23.3 %collective-permute-start.13 = (f32[4,2,8,128]{3,2,1,0:T(8,128)S(1)}, f32[4,2,8,128]{3,2,1,0:T(8,128)S(1)}, u32[]{:S(2)}, u32[]{:S(2)}) collective-permute-start(f32[4,2,8,128]{3,2,1,0:T(8,128)S(1)} %dynamic-slice_bitcast_fusion.16), channel_id=1, source_target_pairs={{0,1},{1,0},{2,3},{3,2},{4,5},{5,4},{6,7},{7,6},{8,9},{9,8},{10,11... | collective-permute-start | bytes 98312 | tf_op jit(solution)/shard_map/ppermute | solution.py:225
  538.3 19.9 %collective-permute-start.17 = (bf16[256,1536]{1,0:T(8,128)(2,1)S(1)}, bf16[256,1536]{1,0:T(8,128)(2,1)S(1)}, u32[]{:S(2)}, u32[]{:S(2)}) collective-permute-start(bf16[256,1536]{1,0:T(8,128)(2,1)S(1)} %copy-done.96), channel_id=1, source_target_pairs={{0,16},{16,0},{1,17},{17,1},{2,18},{18,2},{3,19},{19,3},{4,20},{20... | collective-permute-start | bytes 2359304 | tf_op jit(solution)/shard_map/ppermute | solution.py:191
  548.3 51.5 %collective-permute-start.23 = (bf16[4,96,2304]{2,1,0:T(8,128)(2,1)S(1)}, bf16[4,96,2304]{2,1,0:T(8,128)(2,1)S(1)}, u32[]{:S(2)}, u32[]{:S(2)}) collective-permute-start(bf16[4,96,2304]{2,1,0:T(8,128)(2,1)S(1)} %copy-done.76), channel_id=1, source_target_pairs={{0,2},{1,3},{2,0},{3,1},{4,6},{5,7},{6,4},{7,5},{8,10},{9,11},{10,... | collective-permute-start | bytes 5308424 | tf_op jit(solution)/shard_map/ppermute | solution.py:234
  558.2 31.2 %collective-permute-start.16 = (f32[4,8,128]{2,1,0:T(8,128)S(1)}, f32[4,8,128]{2,1,0:T(8,128)S(1)}, u32[]{:S(2)}, u32[]{:S(2)}) collective-permute-start(f32[4,8,128]{2,1,0:T(8,128)S(1)} %get-tuple-element.429), channel_id=1, source_target_pairs={{0,2},{1,3},{2,0},{3,1},{4,6},{5,7},{6,4},{7,5},{8,10},{9,11},{10,... | collective-permute-start | bytes 49160 | tf_op jit(solution)/shard_map/ppermute | solution.py:234
  589.4 75.9 %collective-permute-start.36 = (bf16[4,128,768]{2,1,0:T(8,128)(2,1)}, bf16[4,128,768]{2,1,0:T(8,128)(2,1)}, u32[]{:S(2)}, u32[]{:S(2)}) collective-permute-start(bf16[4,128,768]{2,1,0:T(8,128)(2,1)} %fusion.39), channel_id=1, source_target_pairs={{0,2},{1,3},{2,0},{3,1},{4,6},{5,7},{6,4},{7,5},{8,10},{9,11},{10,... | collective-permute-start | bytes 2359304 | tf_op jit(solution)/shard_map/ppermute | solution.py:234
  596.2 14.0 %collective-permute-start.22 = (bf16[4,2,96,1024]{3,2,0,1:T(8,128)(2,1)}, bf16[4,2,96,1024]{3,2,0,1:T(8,128)(2,1)}, u32[]{:S(2)}, u32[]{:S(2)}) collective-permute-start(bf16[4,2,96,1024]{3,2,0,1:T(8,128)(2,1)} %copy_bitcast_fusion.4), channel_id=1, source_target_pairs={{0,1},{1,0},{2,3},{3,2},{4,5},{5,4},{6,7},{7,6},{8,9},{9,8},{10,11... | collective-permute-start | bytes 4718600 | tf_op jit(solution)/shard_map/ppermute | solution.py:225
  596.2 19.7 %collective-permute-start.19 = (f32[8,128]{1,0:T(8,128)S(1)}, f32[8,128]{1,0:T(8,128)}, u32[]{:S(2)}, u32[]{:S(2)}) collective-permute-start(f32[8,128]{1,0:T(8,128)S(1)} %get-tuple-element.441), channel_id=1, source_target_pairs={{0,4},{1,5},{2,6},{3,7},{4,8},{5,9},{6,10},{7,11},{8,12},{9,13},{1... | collective-permute-start | bytes 12296 | tf_op jit(solution)/shard_map/ppermute | solution.py:234
  596.8 19.5 %collective-permute-start.20 = (f32[8,128]{1,0:T(8,128)S(1)}, f32[8,128]{1,0:T(8,128)}, u32[]{:S(2)}, u32[]{:S(2)}) collective-permute-start(f32[8,128]{1,0:T(8,128)S(1)} %get-tuple-element.440), channel_id=1, source_target_pairs={{0,8},{1,9},{2,10},{3,11},{4,12},{5,13},{6,14},{7,15},{8,0},{9,1},... | collective-permute-start | bytes 12296 | tf_op jit(solution)/shard_map/ppermute | solution.py:234
  599.9 18.0 %collective-permute-start.21 = (f32[8,128]{1,0:T(8,128)S(1)}, f32[8,128]{1,0:T(8,128)}, u32[]{:S(2)}, u32[]{:S(2)}) collective-permute-start(f32[8,128]{1,0:T(8,128)S(1)} %get-tuple-element.439), channel_id=1, source_target_pairs={{0,12},{1,13},{2,14},{3,15},{4,0},{5,1},{6,2},{7,3},{8,4},{9,5},{1... | collective-permute-start | bytes 12296 | tf_op jit(solution)/shard_map/ppermute | solution.py:234
  610.2 19.3 %collective-permute-start.18 = (bf16[256,1536]{1,0:T(8,128)(2,1)S(1)}, bf16[256,1536]{1,0:T(8,128)(2,1)S(1)}, u32[]{:S(2)}, u32[]{:S(2)}) collective-permute-start(bf16[256,1536]{1,0:T(8,128)(2,1)S(1)} %slice.511), channel_id=1, source_target_pairs={{0,16},{16,0},{1,17},{17,1},{2,18},{18,2},{3,19},{19,3},{4,20},{20... | collective-permute-start | bytes 2359304 | tf_op jit(solution)/shard_map/ppermute | solution.py:191
  615.9 15.1 %collective-permute-start.28 = (bf16[96,2304]{1,0:T(8,128)(2,1)S(1)}, bf16[96,2304]{1,0:T(8,128)(2,1)}, u32[]{:S(2)}, u32[]{:S(2)}) collective-permute-start(bf16[96,2304]{1,0:T(8,128)(2,1)S(1)} %copy-done.104), channel_id=1, source_target_pairs={{0,4},{1,5},{2,6},{3,7},{4,8},{5,9},{6,10},{7,11},{8,12},{9,13},{1... | collective-permute-start | bytes 1327112 | tf_op jit(solution)/shard_map/ppermute | solution.py:234
  616.3 32.2 %collective-permute-start.29 = (bf16[96,2304]{1,0:T(8,128)(2,1)S(1)}, bf16[96,2304]{1,0:T(8,128)(2,1)}, u32[]{:S(2)}, u32[]{:S(2)}) collective-permute-start(bf16[96,2304]{1,0:T(8,128)(2,1)S(1)} %copy-done.103), channel_id=1, source_target_pairs={{0,8},{1,9},{2,10},{3,11},{4,12},{5,13},{6,14},{7,15},{8,0},{9,1},... | collective-permute-start | bytes 1327112 | tf_op jit(solution)/shard_map/ppermute | solution.py:234
  617.9 30.6 %collective-permute-start.30 = (bf16[96,2304]{1,0:T(8,128)(2,1)S(1)}, bf16[96,2304]{1,0:T(8,128)(2,1)}, u32[]{:S(2)}, u32[]{:S(2)}) collective-permute-start(bf16[96,2304]{1,0:T(8,128)(2,1)S(1)} %copy-done.102), channel_id=1, source_target_pairs={{0,12},{1,13},{2,14},{3,15},{4,0},{5,1},{6,2},{7,3},{8,4},{9,5},{1... | collective-permute-start | bytes 1327112 | tf_op jit(solution)/shard_map/ppermute | solution.py:234
  629.5 157.8 %collective-permute-start.41 = (bf16[4,2,96,1024]{3,2,0,1:T(8,128)(2,1)}, bf16[4,2,96,1024]{3,2,0,1:T(8,128)(2,1)}, u32[]{:S(2)}, u32[]{:S(2)}) collective-permute-start(bf16[4,2,96,1024]{3,2,0,1:T(8,128)(2,1)} %copy_bitcast_fusion.3), channel_id=1, source_target_pairs={{0,1},{1,0},{2,3},{3,2},{4,5},{5,4},{6,7},{7,6},{8,9},{9,8},{10,11... | collective-permute-start | bytes 4718600 | tf_op jit(solution)/shard_map/ppermute | solution.py:225
  631.0 50.8 %collective-permute-start.35 = (bf16[4,2,128,1024]{3,2,0,1:T(8,128)(2,1)}, bf16[4,2,128,1024]{3,2,0,1:T(8,128)(2,1)}, u32[]{:S(2)}, u32[]{:S(2)}) collective-permute-start(bf16[4,2,128,1024]{3,2,0,1:T(8,128)(2,1)} %copy_bitcast_fusion.2), channel_id=1, source_target_pairs={{0,1},{1,0},{2,3},{3,2},{4,5},{5,4},{6,7},{7,6},{8,9},{9,8},{10,11... | collective-permute-start | bytes 6291464 | tf_op jit(solution)/shard_map/ppermute | solution.py:225
  648.5 99.0 %collective-permute-start.47 = (bf16[4,2,128,1024]{3,2,0,1:T(8,128)(2,1)}, bf16[4,2,128,1024]{3,2,0,1:T(8,128)(2,1)}, u32[]{:S(2)}, u32[]{:S(2)}) collective-permute-start(bf16[4,2,128,1024]{3,2,0,1:T(8,128)(2,1)} %copy_bitcast_fusion.1), channel_id=1, source_target_pairs={{0,1},{1,0},{2,3},{3,2},{4,5},{5,4},{6,7},{7,6},{8,9},{9,8},{10,11... | collective-permute-start | bytes 6291464 | tf_op jit(solution)/shard_map/ppermute | solution.py:225
  648.5 12.9 %collective-permute-start.37 = (bf16[144,1536]{1,0:T(8,128)(2,1)}, bf16[144,1536]{1,0:T(8,128)(2,1)}, u32[]{:S(2)}, u32[]{:S(2)}) collective-permute-start(bf16[144,1536]{1,0:T(8,128)(2,1)} %get-tuple-element.337), channel_id=1, source_target_pairs={{0,16},{16,0},{1,17},{17,1},{2,18},{18,2},{3,19},{19,3},{4,20},{20... | collective-permute-start | bytes 1327112 | tf_op jit(solution)/shard_map/ppermute | solution.py:191
  661.4 16.6 %collective-permute-start.64 = (f32[8,128]{1,0:T(8,128)S(1)}, f32[8,128]{1,0:T(8,128)S(1)}, u32[]{:S(2)}, u32[]{:S(2)}) collective-permute-start(f32[8,128]{1,0:T(8,128)S(1)} %add_add_fusion), channel_id=1, source_target_pairs={{0,16},{16,0},{1,17},{17,1},{2,18},{18,2},{3,19},{19,3},{4,20},{20... | collective-permute-start | bytes 12296 | tf_op jit(solution)/shard_map/ppermute | solution.py:191
  668.9 21.5 %collective-permute-start.32 = (bf16[96,2304]{1,0:T(8,128)(2,1)}, bf16[96,2304]{1,0:T(8,128)(2,1)S(1)}, u32[]{:S(2)}, u32[]{:S(2)}) collective-permute-start(bf16[96,2304]{1,0:T(8,128)(2,1)} %get-tuple-element.370), channel_id=1, source_target_pairs={{0,4},{1,5},{2,6},{3,7},{4,8},{5,9},{6,10},{7,11},{8,12},{9,13},{1... | collective-permute-start | bytes 1327112 | tf_op jit(solution)/shard_map/ppermute | solution.py:234
  678.0 31.4 %collective-permute-start.33 = (bf16[96,2304]{1,0:T(8,128)(2,1)}, bf16[96,2304]{1,0:T(8,128)(2,1)S(1)}, u32[]{:S(2)}, u32[]{:S(2)}) collective-permute-start(bf16[96,2304]{1,0:T(8,128)(2,1)} %get-tuple-element.369), channel_id=1, source_target_pairs={{0,8},{1,9},{2,10},{3,11},{4,12},{5,13},{6,14},{7,15},{8,0},{9,1},... | collective-permute-start | bytes 1327112 | tf_op jit(solution)/shard_map/ppermute | solution.py:234
  681.7 27.7 %collective-permute-start.34 = (bf16[96,2304]{1,0:T(8,128)(2,1)S(1)}, bf16[96,2304]{1,0:T(8,128)(2,1)S(1)}, u32[]{:S(2)}, u32[]{:S(2)}) collective-permute-start(bf16[96,2304]{1,0:T(8,128)(2,1)S(1)} %copy-done.105), channel_id=1, source_target_pairs={{0,12},{1,13},{2,14},{3,15},{4,0},{5,1},{6,2},{7,3},{8,4},{9,5},{1... | collective-permute-start | bytes 1327112 | tf_op jit(solution)/shard_map/ppermute | solution.py:234
  690.5 63.0 %collective-permute-start.44 = (bf16[128,768]{1,0:T(8,128)(2,1)}, bf16[128,768]{1,0:T(8,128)(2,1)}, u32[]{:S(2)}, u32[]{:S(2)}) collective-permute-start(bf16[128,768]{1,0:T(8,128)(2,1)} %get-tuple-element.399), channel_id=1, source_target_pairs={{0,4},{1,5},{2,6},{3,7},{4,8},{5,9},{6,10},{7,11},{8,12},{9,13},{1... | collective-permute-start | bytes 589832 | tf_op jit(solution)/shard_map/ppermute | solution.py:234
  709.4 44.7 %collective-permute-start.45 = (bf16[128,768]{1,0:T(8,128)(2,1)}, bf16[128,768]{1,0:T(8,128)(2,1)}, u32[]{:S(2)}, u32[]{:S(2)}) collective-permute-start(bf16[128,768]{1,0:T(8,128)(2,1)} %get-tuple-element.398), channel_id=1, source_target_pairs={{0,8},{1,9},{2,10},{3,11},{4,12},{5,13},{6,14},{7,15},{8,0},{9,1},... | collective-permute-start | bytes 589832 | tf_op jit(solution)/shard_map/ppermute | solution.py:234
  709.4 12.2 %collective-permute-start.31 = (bf16[96,2304]{1,0:T(8,128)(2,1)}, bf16[96,2304]{1,0:T(8,128)(2,1)}, u32[]{:S(2)}, u32[]{:S(2)}) collective-permute-start(bf16[96,2304]{1,0:T(8,128)(2,1)} %copy.148), channel_id=1, source_target_pairs={{0,16},{16,0},{1,17},{17,1},{2,18},{18,2},{3,19},{19,3},{4,20},{20... | collective-permute-start | bytes 1327112 | tf_op jit(solution)/shard_map/ppermute | solution.py:191
  721.7 18.5 %collective-permute-start.27 = (bf16[4,96,1024]{2,1,0:T(8,128)(2,1)}, bf16[4,96,1024]{2,1,0:T(8,128)(2,1)S(1)}, u32[]{:S(2)}, u32[]{:S(2)}) collective-permute-start(bf16[4,96,1024]{2,1,0:T(8,128)(2,1)} %fusion.40), channel_id=1, source_target_pairs={{0,2},{1,3},{2,0},{3,1},{4,6},{5,7},{6,4},{7,5},{8,10},{9,11},{10,... | collective-permute-start | bytes 2359304 | tf_op jit(solution)/shard_map/ppermute | solution.py:234
  740.2 25.3 %collective-permute-start.46 = (bf16[128,768]{1,0:T(8,128)(2,1)}, bf16[128,768]{1,0:T(8,128)(2,1)S(1)}, u32[]{:S(2)}, u32[]{:S(2)}) collective-permute-start(bf16[128,768]{1,0:T(8,128)(2,1)} %get-tuple-element.397), channel_id=1, source_target_pairs={{0,12},{1,13},{2,14},{3,15},{4,0},{5,1},{6,2},{7,3},{8,4},{9,5},{1... | collective-permute-start | bytes 589832 | tf_op jit(solution)/shard_map/ppermute | solution.py:234
  747.6 21.4 %collective-permute-start.43 = (bf16[96,2304]{1,0:T(8,128)(2,1)S(1)}, bf16[96,2304]{1,0:T(8,128)(2,1)S(1)}, u32[]{:S(2)}, u32[]{:S(2)}) collective-permute-start(bf16[96,2304]{1,0:T(8,128)(2,1)S(1)} %copy-done.99), channel_id=1, source_target_pairs={{0,16},{16,0},{1,17},{17,1},{2,18},{18,2},{3,19},{19,3},{4,20},{20... | collective-permute-start | bytes 1327112 | tf_op jit(solution)/shard_map/ppermute | solution.py:191
  753.4 30.8 %collective-permute-start.42 = (bf16[4,128,1024]{2,1,0:T(8,128)(2,1)}, bf16[4,128,1024]{2,1,0:T(8,128)(2,1)}, u32[]{:S(2)}, u32[]{:S(2)}) collective-permute-start(bf16[4,128,1024]{2,1,0:T(8,128)(2,1)} %fusion.35), channel_id=1, source_target_pairs={{0,2},{1,3},{2,0},{3,1},{4,6},{5,7},{6,4},{7,5},{8,10},{9,11},{10,... | collective-permute-start | bytes 3145736 | tf_op jit(solution)/shard_map/ppermute | solution.py:234
  754.2 37.6 %collective-permute-start.38 = (bf16[96,1024]{1,0:T(8,128)(2,1)}, bf16[96,1024]{1,0:T(8,128)(2,1)}, u32[]{:S(2)}, u32[]{:S(2)}) collective-permute-start(bf16[96,1024]{1,0:T(8,128)(2,1)} %get-tuple-element.396), channel_id=1, source_target_pairs={{0,4},{1,5},{2,6},{3,7},{4,8},{5,9},{6,10},{7,11},{8,12},{9,13},{1... | collective-permute-start | bytes 589832 | tf_op jit(solution)/shard_map/ppermute | solution.py:234
  765.5 29.9 %collective-permute-start.39 = (bf16[96,1024]{1,0:T(8,128)(2,1)}, bf16[96,1024]{1,0:T(8,128)(2,1)}, u32[]{:S(2)}, u32[]{:S(2)}) collective-permute-start(bf16[96,1024]{1,0:T(8,128)(2,1)} %get-tuple-element.395), channel_id=1, source_target_pairs={{0,8},{1,9},{2,10},{3,11},{4,12},{5,13},{6,14},{7,15},{8,0},{9,1},... | collective-permute-start | bytes 589832 | tf_op jit(solution)/shard_map/ppermute | solution.py:234
  769.7 27.2 %collective-permute-start.40 = (bf16[96,1024]{1,0:T(8,128)(2,1)}, bf16[96,1024]{1,0:T(8,128)(2,1)}, u32[]{:S(2)}, u32[]{:S(2)}) collective-permute-start(bf16[96,1024]{1,0:T(8,128)(2,1)} %get-tuple-element.394), channel_id=1, source_target_pairs={{0,12},{1,13},{2,14},{3,15},{4,0},{5,1},{6,2},{7,3},{8,4},{9,5},{1... | collective-permute-start | bytes 589832 | tf_op jit(solution)/shard_map/ppermute | solution.py:234
  784.2 26.1 %collective-permute-start.52 = (bf16[4,128,1024]{2,1,0:T(8,128)(2,1)S(1)}, bf16[4,128,1024]{2,1,0:T(8,128)(2,1)S(1)}, u32[]{:S(2)}, u32[]{:S(2)}) collective-permute-start(bf16[4,128,1024]{2,1,0:T(8,128)(2,1)S(1)} %copy-done.91), channel_id=1, source_target_pairs={{0,2},{1,3},{2,0},{3,1},{4,6},{5,7},{6,4},{7,5},{8,10},{9,11},{10,... | collective-permute-start | bytes 3145736 | tf_op jit(solution)/shard_map/ppermute | solution.py:234
  788.1 11.3 %collective-permute-start.53 = (bf16[128,768]{1,0:T(8,128)(2,1)S(1)}, bf16[128,768]{1,0:T(8,128)(2,1)S(1)}, u32[]{:S(2)}, u32[]{:S(2)}) collective-permute-start(bf16[128,768]{1,0:T(8,128)(2,1)S(1)} %copy-done.108), channel_id=1, source_target_pairs={{0,16},{16,0},{1,17},{17,1},{2,18},{18,2},{3,19},{19,3},{4,20},{20... | collective-permute-start | bytes 589832 | tf_op jit(solution)/shard_map/ppermute | solution.py:191
  791.8 23.6 %collective-permute-start.49 = (bf16[128,1024]{1,0:T(8,128)(2,1)S(1)}, bf16[128,1024]{1,0:T(8,128)(2,1)S(1)}, u32[]{:S(2)}, u32[]{:S(2)}) collective-permute-start(bf16[128,1024]{1,0:T(8,128)(2,1)S(1)} %get-tuple-element.382), channel_id=1, source_target_pairs={{0,4},{1,5},{2,6},{3,7},{4,8},{5,9},{6,10},{7,11},{8,12},{9,13},{1... | collective-permute-start | bytes 786440 | tf_op jit(solution)/shard_map/ppermute | solution.py:234
  795.4 20.1 %collective-permute-start.50 = (bf16[128,1024]{1,0:T(8,128)(2,1)S(1)}, bf16[128,1024]{1,0:T(8,128)(2,1)S(1)}, u32[]{:S(2)}, u32[]{:S(2)}) collective-permute-start(bf16[128,1024]{1,0:T(8,128)(2,1)S(1)} %get-tuple-element.381), channel_id=1, source_target_pairs={{0,8},{1,9},{2,10},{3,11},{4,12},{5,13},{6,14},{7,15},{8,0},{9,1},... | collective-permute-start | bytes 786440 | tf_op jit(solution)/shard_map/ppermute | solution.py:234
  796.9 30.6 %collective-permute-start.54 = (bf16[4,96,1024]{2,1,0:T(8,128)(2,1)S(1)}, bf16[4,96,1024]{2,1,0:T(8,128)(2,1)S(1)}, u32[]{:S(2)}, u32[]{:S(2)}) collective-permute-start(bf16[4,96,1024]{2,1,0:T(8,128)(2,1)S(1)} %fusion.41), channel_id=1, source_target_pairs={{0,2},{1,3},{2,0},{3,1},{4,6},{5,7},{6,4},{7,5},{8,10},{9,11},{10,... | collective-permute-start | bytes 2359304 | tf_op jit(solution)/shard_map/ppermute | solution.py:234
  799.4 26.7 %collective-permute-start.48 = (bf16[96,1024]{1,0:T(8,128)(2,1)S(1)}, bf16[96,1024]{1,0:T(8,128)(2,1)S(1)}, u32[]{:S(2)}, u32[]{:S(2)}) collective-permute-start(bf16[96,1024]{1,0:T(8,128)(2,1)S(1)} %get-tuple-element.329), channel_id=1, source_target_pairs={{0,16},{16,0},{1,17},{17,1},{2,18},{18,2},{3,19},{19,3},{4,20},{20... | collective-permute-start | bytes 589832 | tf_op jit(solution)/shard_map/ppermute | solution.py:191
  810.3 12.9 %collective-permute-start.51 = (bf16[128,1024]{1,0:T(8,128)(2,1)S(1)}, bf16[128,1024]{1,0:T(8,128)(2,1)S(1)}, u32[]{:S(2)}, u32[]{:S(2)}) collective-permute-start(bf16[128,1024]{1,0:T(8,128)(2,1)S(1)} %get-tuple-element.380), channel_id=1, source_target_pairs={{0,12},{1,13},{2,14},{3,15},{4,0},{5,1},{6,2},{7,3},{8,4},{9,5},{1... | collective-permute-start | bytes 786440 | tf_op jit(solution)/shard_map/ppermute | solution.py:234
  815.4 21.5 %collective-permute-start.59 = (bf16[128,1024]{1,0:T(8,128)(2,1)S(1)}, bf16[128,1024]{1,0:T(8,128)(2,1)S(1)}, u32[]{:S(2)}, u32[]{:S(2)}) collective-permute-start(bf16[128,1024]{1,0:T(8,128)(2,1)S(1)} %get-tuple-element.379), channel_id=1, source_target_pairs={{0,4},{1,5},{2,6},{3,7},{4,8},{5,9},{6,10},{7,11},{8,12},{9,13},{1... | collective-permute-start | bytes 786440 | tf_op jit(solution)/shard_map/ppermute | solution.py:234
  815.5 25.6 %collective-permute-start.60 = (bf16[128,1024]{1,0:T(8,128)(2,1)S(1)}, bf16[128,1024]{1,0:T(8,128)(2,1)S(1)}, u32[]{:S(2)}, u32[]{:S(2)}) collective-permute-start(bf16[128,1024]{1,0:T(8,128)(2,1)S(1)} %get-tuple-element.378), channel_id=1, source_target_pairs={{0,8},{1,9},{2,10},{3,11},{4,12},{5,13},{6,14},{7,15},{8,0},{9,1},... | collective-permute-start | bytes 786440 | tf_op jit(solution)/shard_map/ppermute | solution.py:234
  823.2 25.9 %collective-permute-start.61 = (bf16[128,1024]{1,0:T(8,128)(2,1)S(1)}, bf16[128,1024]{1,0:T(8,128)(2,1)S(1)}, u32[]{:S(2)}, u32[]{:S(2)}) collective-permute-start(bf16[128,1024]{1,0:T(8,128)(2,1)S(1)} %get-tuple-element.377), channel_id=1, source_target_pairs={{0,12},{1,13},{2,14},{3,15},{4,0},{5,1},{6,2},{7,3},{8,4},{9,5},{1... | collective-permute-start | bytes 786440 | tf_op jit(solution)/shard_map/ppermute | solution.py:234
  826.1 23.5 %collective-permute-start.58 = (bf16[128,1024]{1,0:T(8,128)(2,1)S(1)}, bf16[128,1024]{1,0:T(8,128)(2,1)S(1)}, u32[]{:S(2)}, u32[]{:S(2)}) collective-permute-start(bf16[128,1024]{1,0:T(8,128)(2,1)S(1)} %get-tuple-element.327), channel_id=1, source_target_pairs={{0,16},{16,0},{1,17},{17,1},{2,18},{18,2},{3,19},{19,3},{4,20},{20... | collective-permute-start | bytes 786440 | tf_op jit(solution)/shard_map/ppermute | solution.py:191
  827.8 23.0 %collective-permute-start.55 = (bf16[96,1024]{1,0:T(8,128)(2,1)S(1)}, bf16[96,1024]{1,0:T(8,128)(2,1)S(1)}, u32[]{:S(2)}, u32[]{:S(2)}) collective-permute-start(bf16[96,1024]{1,0:T(8,128)(2,1)S(1)} %get-tuple-element.393), channel_id=1, source_target_pairs={{0,4},{1,5},{2,6},{3,7},{4,8},{5,9},{6,10},{7,11},{8,12},{9,13},{1... | collective-permute-start | bytes 589832 | tf_op jit(solution)/shard_map/ppermute | solution.py:234
  836.9 15.1 %collective-permute-start.56 = (bf16[96,1024]{1,0:T(8,128)(2,1)S(1)}, bf16[96,1024]{1,0:T(8,128)(2,1)S(1)}, u32[]{:S(2)}, u32[]{:S(2)}) collective-permute-start(bf16[96,1024]{1,0:T(8,128)(2,1)S(1)} %get-tuple-element.392), channel_id=1, source_target_pairs={{0,8},{1,9},{2,10},{3,11},{4,12},{5,13},{6,14},{7,15},{8,0},{9,1},... | collective-permute-start | bytes 589832 | tf_op jit(solution)/shard_map/ppermute | solution.py:234
  (151 other events, 1590.1 us)
Sparse Core Ops, SparseCore 0:
  18.7 111.9 all-gather.4
  132.8 110.2 all-gather.6

commit v2 on v1

--- a/solution.py
+++ b/solution.py
@@ -14,6 +14,8 @@
 GELU_K = math.sqrt(2.0 / math.pi)
 GELU_C = 0.044715
 ROWS = 16
+VMEM = 48 << 20
+SMALL = pl.CostEstimate(flops=1024, bytes_accessed=1024, transcendentals=0)
 BF16 = jnp.bfloat16
 F32 = jnp.float32
 
@@ -156,9 +158,203 @@
             jax.ShapeDtypeStruct((tokens, width), F32),
             jax.ShapeDtypeStruct((3 * ROWS * (tokens // length), width), F32),
         ],
-        cost_estimate=pl.CostEstimate(flops=120 * tokens * width, bytes_accessed=34 * tokens * width, transcendentals=8 * tokens * width),
+        cost_estimate=SMALL,
         name="recurrence_backward",
     )(cot, pre, gates, gates, admitted, before, params)
+
+
+def ffn_kernel(x_ref, cot_ref, gate_ref, up_ref, down_ref, hidden_ref, gate_cot_ref, up_cot_ref, near_ref, far_ref, sum_ref):
+    depth, tile = x_ref.shape[1], gate_ref.shape[2]
+    gate_w = gate_ref[...].reshape(depth, tile)
+    up_w = up_ref[...].reshape(depth, tile)
+    gate = matmul(x_ref[...], gate_w)
+    up = matmul(x_ref[...], up_w)
+    cot = cols_product(cot_ref[...], down_ref[...])
+    t = jnp.tanh(GELU_K * (gate + GELU_C * gate * gate * gate))
+    act = 0.5 * gate * (1.0 + t)
+    slope = 0.5 * (1.0 + t) + 0.5 * gate * (1.0 - t * t) * GELU_K * (1.0 + 3.0 * GELU_C * gate * gate)
+    hidden_ref[...] = (act * up).astype(BF16)
+    gate_cot = (cot * up * slope).astype(BF16)
+    up_cot = (cot * act).astype(BF16)
+    gate_cot_ref[...] = gate_cot
+    up_cot_ref[...] = up_cot
+    part = cols_product(gate_cot, gate_w) + cols_product(up_cot, up_w)
+
+    @pl.when(pl.program_id(0) == 0)
+    def _():
+        sum_ref[...] = part
+
+    @pl.when(pl.program_id(0) > 0)
+    def _():
+        sum_ref[...] += part
+
+    @pl.when(pl.program_id(0) == pl.num_programs(0) - 1)
+    def _():
+        half = near_ref.shape[0]
+        near_ref[...] = sum_ref[:half, :]
+        far_ref[...] = sum_ref[half:, :].astype(BF16)
+
+
+def ffn_pass(x, cot, blocks, down, rows, tiles):
+    tokens, depth = x.shape
+    shards, _, tile = blocks.shape
+    hidden = jax.ShapeDtypeStruct((tokens, tiles * tile), BF16)
+    fixed = pl.BlockSpec((tokens, depth), lambda j: (0, 0))
+    wide = pl.BlockSpec((tokens, tile), lambda j: (0, j))
+    half = pl.BlockSpec((tokens // 2, depth), lambda j: (0, 0))
+    return pl.pallas_call(
+        ffn_kernel,
+        grid=(tiles,),
+        in_specs=[
+            fixed, fixed,
+            pl.BlockSpec((shards, rows, tile), lambda j: (0, j, 0)),
+            pl.BlockSpec((shards, rows, tile), lambda j: (0, j + tiles, 0)),
+            pl.BlockSpec((tile, depth), lambda j: (j, 0)),
+        ],
+        out_specs=[wide, wide, wide, half, half],
+        out_shape=[
+            hidden, hidden, hidden,
+            jax.ShapeDtypeStruct((tokens // 2, depth), F32),
+            jax.ShapeDtypeStruct((tokens // 2, depth), BF16),
+        ],
+        scratch_shapes=[pltpu.VMEM((tokens, depth), F32)],
+        compiler_params=pltpu.CompilerParams(vmem_limit_bytes=VMEM),
+        cost_estimate=SMALL,
+        name="ffn_pass",
+    )(x, cot, blocks, blocks, down)
+
+
+def joined(ref):
+    v = ref[...]
+    if v.shape[1] % 16:
+        return widen(v).reshape(-1, v.shape[2]).astype(BF16)
+    return v.reshape(-1, v.shape[2])
+
+
+def away_kernel(at_ref, left_ref, right_ref, out_ref):
+    out_ref[...] = matmul(joined(left_ref), right_ref[...]).reshape(out_ref.shape).astype(out_ref.dtype)
+
+
+def home_kernel(at_ref, left_ref, right_ref, got_ref, keep_ref, send_ref, sum_ref):
+    shape = got_ref.shape
+    v = matmul(joined(left_ref), right_ref[...]).reshape(shape) + widen(got_ref[...])
+    sum_ref[...] = v.reshape(sum_ref.shape)
+    n = sum_ref.shape[1]
+    keep_ref[...] = sum_ref[:, at_ref[1]]
+    for k in range(1, n):
+        send_ref[k - 1] = sum_ref[:, lax.rem(at_ref[1] + k, n)].astype(send_ref.dtype)
+
+
+def column_tile(n):
+    return max(t for t in (1024, 768, 512, 256, 128) if n % t == 0)
+
+
+def grad_away(left, right, at):
+    owners, _, rows, tokens = left.shape
+    n = right.shape[1]
+    tile = column_tile(n)
+    return pl.pallas_call(
+        away_kernel,
+        grid_spec=pltpu.PrefetchScalarGridSpec(
+            num_scalar_prefetch=1,
+            grid=(n // tile,),
+            in_specs=[
+                pl.BlockSpec((owners, None, rows, tokens), lambda j, at: (0, at[0], 0, 0)),
+                pl.BlockSpec((tokens, tile), lambda j, at: (0, j)),
+            ],
+            out_specs=pl.BlockSpec((owners, rows, tile), lambda j, at: (0, 0, j)),
+        ),
+        out_shape=jax.ShapeDtypeStruct((owners, rows, n), BF16),
+        compiler_params=pltpu.CompilerParams(vmem_limit_bytes=VMEM),
+        cost_estimate=SMALL,
+        name="grad_away",
+    )(at, left, right)
+
+
+def grad_home(left, right, got, at, f1, f2):
+    owners, _, rows, tokens = left.shape
+    n = right.shape[1]
+    tile = column_tile(n)
+    return pl.pallas_call(
+        home_kernel,
+        grid_spec=pltpu.PrefetchScalarGridSpec(
+            num_scalar_prefetch=1,
+            grid=(n // tile,),
+            in_specs=[
+                pl.BlockSpec((owners, None, rows, tokens), lambda j, at: (0, at[0], 0, 0)),
+                pl.BlockSpec((tokens, tile), lambda j, at: (0, j)),
+                pl.BlockSpec((owners, rows, tile), lambda j, at: (0, 0, j)),
+            ],
+            out_specs=[
+                pl.BlockSpec((f1, rows, tile), lambda j, at: (0, 0, j)),
+                pl.BlockSpec((f2 - 1, f1, rows, tile), lambda j, at: (0, 0, 0, j)),
+            ],
+            scratch_shapes=[pltpu.VMEM((f1, f2, rows, tile), F32)],
+        ),
+        out_shape=[
+            jax.ShapeDtypeStruct((f1, rows, n), F32),
+            jax.ShapeDtypeStruct((f2 - 1, f1, rows, n), BF16),
+        ],
+        compiler_params=pltpu.CompilerParams(vmem_limit_bytes=VMEM),
+        cost_estimate=SMALL,
+        name="grad_home",
+    )(at, left, right, got)
+
+
+def spread_kernel(count, gots, at_ref, own_ref, *refs):
+    got_refs, keep_ref, send_refs = refs[:gots], refs[gots], refs[gots + 1 :]
+
+    def total(i):
+        v = own_ref[i]
+        for ref in got_refs:
+            v = v + widen(ref[i])
+        return v
+
+    keep_ref[...] = total(at_ref[2])
+    for k in range(1, count):
+        send_refs[k - 1][...] = total(lax.rem(at_ref[2] + k, count)).astype(BF16)
+
+
+def spread(own, gots, at):
+    count, rows, n = own.shape
+    tile = column_tile(n)
+    many = pl.BlockSpec((count, rows, tile), lambda j, at: (0, 0, j))
+    one = pl.BlockSpec((rows, tile), lambda j, at: (0, j))
+    out = pl.pallas_call(
+        functools.partial(spread_kernel, count, len(gots)),
+        grid_spec=pltpu.PrefetchScalarGridSpec(
+            num_scalar_prefetch=1, grid=(n // tile,), in_specs=[many] * (1 + len(gots)), out_specs=[one] * count
+        ),
+        out_shape=[jax.ShapeDtypeStruct((rows, n), F32)] + [jax.ShapeDtypeStruct((rows, n), BF16)] * (count - 1),
+        compiler_params=pltpu.CompilerParams(vmem_limit_bytes=VMEM),
+        cost_estimate=SMALL,
+        name="spread",
+    )(at, own, *gots)
+    return out[0], out[1:]
+
+
+def settle_kernel(gots, own_ref, *refs):
+    v = own_ref[...]
+    for ref in refs[:gots]:
+        v = v + widen(ref[...])
+    refs[gots][...] = v
+    refs[gots + 1][...] = v.astype(BF16)
+
+
+def settle(own, gots):
+    rows, n = own.shape
+    tile = column_tile(n)
+    one = pl.BlockSpec((rows, tile), lambda j: (0, j))
+    return pl.pallas_call(
+        functools.partial(settle_kernel, len(gots)),
+        grid=(n // tile,),
+        in_specs=[one] * (1 + len(gots)),
+        out_specs=[one, one],
+        out_shape=[jax.ShapeDtypeStruct((rows, n), F32), jax.ShapeDtypeStruct((rows, n), BF16)],
+        compiler_params=pltpu.CompilerParams(vmem_limit_bytes=VMEM),
+        cost_estimate=SMALL,
+        name="settle",
+    )(own, *gots)
 
 
 def shifted(values, offset):
@@ -216,49 +412,70 @@
     def tock(*ys):
         clock[:] = ys
 
+    def along(k, count, stride):
+        return [(s, s + ((s // stride + k) % count - s // stride % count) * stride) for s in range(shards)]
+
+    home = jnp.stack([core, i2, i1]).astype(jnp.int32)
+    away = jnp.stack([1 - core, i2, i1]).astype(jnp.int32)
+
     class Scatter:
-        def __init__(self, v, kind=BF16):
-            self.kind = kind
-            rows, n = v.shape[0] // shards, v.shape[1]
-            self.v = v.reshape(f1, f2, cores, rows, n)
-            send = lax.dynamic_index_in_dim(self.v, 1 - core, 2, False)
-            self.got = [lax.ppermute(send, "shard", [(s, s ^ 1) for s in range(shards)])]
-
-        def step(self, v, at, count, axis, stride):
-            keep = lax.dynamic_index_in_dim(v, at, axis, False)
-            sends = [lax.dynamic_index_in_dim(v, (at + k) % count, axis, False).astype(self.kind) for k in range(1, count)]
-            tock(keep, *sends)
-            self.v, self.got = keep, []
-            for k in range(1, count):
-                perm = [(s, s + ((s // stride + k) % count - s // stride % count) * stride) for s in range(shards)]
-                self.got.append(lax.ppermute(sends[k - 1], "shard", perm))
+        def __init__(self, left, right):
+            left, self.right = tick(left, right)
+            self.left = left.reshape(shards // cores, cores, left.shape[0] // shards, left.shape[1])
+            send = grad_away(self.left, self.right, away)
+            tock(send)
+            self.got = [lax.ppermute(send, "shard", along(1, cores, 1))]
 
         def sum_core(self):
-            v, got = tick(self.v, self.got[0])
-            v = widen(lax.dynamic_index_in_dim(v, core, 2, False)) + widen(got)
-            self.step(v, i2, f2, 1, cores)
+            left, right, got = tick(self.left, self.right, self.got[0])
+            self.v, sends = grad_home(left, right, got, home, f1, f2)
+            tock(self.v, sends)
+            self.got = [lax.ppermute(sends[k - 1], "shard", along(k, f2, cores)) for k in range(1, f2)]
 
         def sum_two(self):
             v, *got = tick(self.v, *self.got)
-            for g in got:
-                v = v + widen(g)
-            self.step(v, i1, f1, 0, cores * f2)
+            self.v, sends = spread(v, got, home)
+            tock(self.v, *sends)
+            self.got = [lax.ppermute(sends[k - 1], "shard", along(k, f1, cores * f2)) for k in range(1, f1)]
 
         def sum_one(self):
             v, *got = tick(self.v, *self.got)
-            for g in got:
-                v = v + widen(g)
-            for k in range(1, groups // 2):
-                v = v + lax.ppermute(v, "rep", [(i, (i + 2 * k) % groups) for i in range(groups)])
-            send = v.astype(self.kind)
+            v, send = settle(v, got)
             tock(v, send)
+            if groups > 2:
+                total = v
+                for k in range(1, groups // 2):
+                    total = total + lax.ppermute(v, "rep", [(i, (i + 2 * k) % groups) for i in range(groups)])
+                v, send = total, total.astype(BF16)
             self.v, self.got = v, swap(send)
 
         def both(self):
             v, got = tick(self.v, self.got)
             return v, widen(got)
 
-    block = 512
+    class SmallScatter:
+        def __init__(self, v):
+            self.v = v.reshape(f1, f2, cores, -1, v.shape[-1])
+
+        def start(self, at, count, axis, stride):
+            v = self.v
+            sends = [lax.dynamic_index_in_dim(v, (at + k) % count, axis, False) for k in range(1, count)]
+            self.v = lax.dynamic_index_in_dim(v, at, axis, False)
+            self.got = [lax.ppermute(sends[k - 1], "shard", along(k, count, stride)) for k in range(1, count)]
+
+        def start_pair(self):
+            v = self.v
+            for k in range(1, groups // 2):
+                self.v = self.v + lax.ppermute(v, "rep", [(i, (i + 2 * k) % groups) for i in range(groups)])
+            self.got = [swap(self.v)]
+
+        def take(self):
+            v, *got = tick(self.v, *self.got)
+            for g in got:
+                v = v + g
+            tock(v)
+            self.v = v
+
     per_d, per_r = mix_gain.shape[0], conv_bias.shape[0]
     vectors = jnp.concatenate(
         [mix_gain, ffn_gain, conv_kernel.reshape(-1), conv_bias, recur_bias, admit_bias, decay_param]
@@ -278,27 +495,28 @@
     def ffn_half(v):
         return lax.dynamic_index_in_dim(v.reshape(v.shape[0], shards, 2, piece_f), side, 2, False).reshape(v.shape[0], half_f)
 
-    def gather_blocks(parts):
+    def gather_blocks(parts, block):
         rows = [p[:, at : at + block] for p in parts for at in range(0, p.shape[1], block)]
-        whole = lax.all_gather(jnp.concatenate(rows, axis=0), "shard", axis=0)
-        out, at = [], 0
-        for p in parts:
-            cols = []
-            for _ in range(0, p.shape[1], block):
-                cols.append(whole[:, at : at + p.shape[0]].reshape(shards * p.shape[0], block))
-                at += p.shape[0]
-            out.append(jnp.concatenate(cols, axis=1))
-        return out
-
-    w1, w2, w3 = gather_blocks([
+        return lax.all_gather(jnp.concatenate(rows, axis=0), "shard", axis=0)
+
+    def unpack(whole, at, rows, columns):
+        block = whole.shape[2]
+        cols = [whole[:, at + i * rows : at + (i + 1) * rows].reshape(shards * rows, block) for i in range(columns // block)]
+        return jnp.concatenate(cols, axis=1)
+
+    per_f, tiles = 2 * piece_f, 3
+    whole = gather_blocks([
         jnp.concatenate([mine(branch_proj, half_r, 1), mine(lruin_proj, half_r, 1)], axis=1),
         jnp.concatenate([mine(recur_proj, half_r, 1), mine(admit_proj, half_r, 1)], axis=1),
         out_proj,
-    ])
-    w4, w5 = gather_blocks([
-        jnp.concatenate([ffn_half(ffn_gate), ffn_half(ffn_up)], axis=1),
-        mine(ffn_down, piece_f, 0),
-    ])
+    ], 512)
+    ffn_blocks = gather_blocks(
+        [ffn_half(ffn_gate), ffn_half(ffn_up), mine(ffn_down, piece_f, 0)], half_f // tiles
+    )
+    at = low_r // 512 * per_d
+    w1 = unpack(whole, 0, per_d, low_r)
+    w2 = unpack(whole, at, per_r, low_r)
+    w3 = unpack(whole, at + low_r // 512 * per_r, per_r, width)
 
     def norm_back(cot, v, scale, gain):
         g = cot * gain
@@ -315,56 +533,48 @@
         conv = conv + taps_half[k] * shifted(lru_pre, k)
     admitted = conv.reshape(2 * length, half_r).astype(BF16)
     admitted_all = natural(admitted, swap_rows(admitted))
+    normed_t, admitted_t = normed.T, admitted_all.T
     gates = matmul(admitted_all, w2)
     mixed, before = recurrence_forward(pre, gates, admitted, params, length)
     mixed_other = jnp.concatenate([swap(mixed[length:]), swap(mixed[:length])], axis=0)
     mixed_all = natural(mixed, mixed_other)
+    mixed_all_t = mixed_all.T
     middle = widen(tokens) + matmul(mixed_all[:length], w3)
     scale_two = lax.rsqrt(jnp.mean(middle * middle, axis=-1, keepdims=True) + EPS)
-    normed_two = with_pair((middle * scale_two * gain_two).astype(BF16))
-    wide = matmul(normed_two, w4)
-    gate_pre, up_pre = wide[:, :half_f], wide[:, half_f:]
-    hidden = (gelu(gate_pre) * up_pre).astype(BF16)
-
-    hidden_cot = cols_product(cot_pair, w5)
-    gate_cot = (hidden_cot * up_pre * gelu_slope(gate_pre)).astype(BF16)
-    up_cot = (hidden_cot * gelu(gate_pre)).astype(BF16)
-    wide_cot = jnp.concatenate([gate_cot, up_cot], axis=1)
-    part = cols_product(wide_cot, w4)
-    tock(part)
-    near, far = part[:length], swap(part[length:].astype(BF16))
-
-    def grad(left, right):
-        left, right = tick(left, right)
-        out = rows_product(left, right).astype(BF16)
-        tock(out)
-        return Scatter(out)
-
-    down_s = grad(hidden, cot_pair)
-    gate_s = grad(normed_two, gate_cot)
+    normed_two = (middle * scale_two * gain_two).astype(BF16)
+    tock(normed_two)
+    normed_two = with_pair(normed_two)
+    ffn_blocks, = tick(ffn_blocks)
+    w5 = unpack(ffn_blocks, 2 * tiles * per_d, piece_f, width)
+
+    hidden, gate_cot, up_cot, near, far = ffn_pass(normed_two, cot_pair, ffn_blocks, w5, per_d, tiles)
+    tock(near, far)
+    far = swap(far)
+    down_s = Scatter(hidden.T, cot_pair)
+    normed_two_t = normed_two.T
+    gate_s = Scatter(normed_two_t, gate_cot)
     down_s.sum_core()
+    up_s = Scatter(normed_two_t, up_cot)
     near, far = tick(near, far)
     middle_cot = widen(cotangent) + norm_back(near + widen(far), middle, scale_two, gain_two)
     middle_low = middle_cot.astype(BF16)
     tock(middle_low)
     out_cot = with_pair(middle_low)
-    up_s = grad(normed_two, up_cot)
     gate_s.sum_core()
     out_cot, = tick(out_cot)
     mixed_cot = cols_product(out_cot, mine(w3, half_r, 0))
     branch_low, recur_low, admit_low, direct, sums = recurrence_backward(
         mixed_cot, pre, gates, admitted, before, params, length
     )
-    gates_cot = jnp.concatenate([recur_low, admit_low], axis=1)
-    part = cols_product(gates_cot, w2)
-    tock(part)
-    near, far = mine(part, half_r, 1), swap_rows(theirs(part, half_r, 1).astype(BF16))
-    out_s = grad(mixed_all, mine(out_cot, width // 2, 1))
+    part = cols_product(jnp.concatenate([recur_low, admit_low], axis=1), w2)
+    far = theirs(part, half_r, 1).astype(BF16)
+    tock(part, far)
+    near, far = mine(part, half_r, 1), swap_rows(far)
     down_s.sum_two()
     up_s.sum_core()
-    branch_s = grad(normed, branch_low)
-    recur_s = grad(admitted_all, recur_low)
-    admit_s = grad(admitted_all, admit_low)
+    out_s = Scatter(mixed_all_t, mine(out_cot, width // 2, 1))
+    branch_s = Scatter(normed_t, branch_low)
+    recur_s = Scatter(admitted_t, recur_low)
     direct, near, far = tick(direct, near, far)
     admitted_cot = (direct + near + widen(far)).reshape(2, length, half_r)
     lru_cot = jnp.zeros_like(admitted_cot)
@@ -374,67 +584,74 @@
         kernel_grad.append(jnp.sum(admitted_cot * shifted(lru_pre, k), axis=(0, 1)))
     lru_cot = lru_cot.reshape(2 * length, half_r).astype(BF16)
     part = cols_product(jnp.concatenate([branch_low, lru_cot], axis=1), w1)
-    tock(part)
-    near, far = part[:length], swap(part[length:].astype(BF16))
-    lruin_s = grad(normed, lru_cot)
+    far = part[length:].astype(BF16)
+    tock(part, far)
+    near, far = part[:length], swap(far)
+    admit_s = Scatter(admitted_t, admit_low)
+    lruin_s = Scatter(normed_t, lru_cot)
     sums = jnp.sum(sums.reshape(2, 3, ROWS, half_r), axis=(0, 2))
     small = jnp.stack(
         kernel_grad
         + [jnp.sum(admitted_cot, axis=(0, 1)), sums[0], sums[1], sums[2] * (DECAY_SCALE * jax.nn.sigmoid(-lam))]
     )
     small = natural(small, jnp.zeros_like(small))
-    small_s = Scatter(small.reshape(taps + 4, shards, per_r).transpose(1, 0, 2).reshape(shards * (taps + 4), per_r), F32)
+    small_s = SmallScatter(small.reshape(taps + 4, shards, per_r).transpose(1, 0, 2))
+    small_s.start(core, cores, 2, 1)
     gate_s.sum_two()
     out_s.sum_core()
-    small_s.sum_core()
     near, far = tick(near, far)
     tokens_grad = middle_cot + norm_back(near + widen(far), values[:length], scale_one[:length], gain_one)
     tock(tokens_grad)
-    small_s.sum_two()
+    small_s.take()
+    small_s.start(i2, f2, 1, cores)
     hidden_late, = tick(hidden)
     down = matmul(hidden_late, w5)
-    tock(down)
-    down_far = swap(down[length:].astype(BF16))
+    down_far = down[length:].astype(BF16)
+    tock(down, down_far)
+    down_far = swap(down_far)
     down_s.sum_one()
     up_s.sum_two()
     branch_s.sum_core()
-    small_s.sum_one()
+    small_s.take()
+    small_s.start(i1, f1, 0, cores * f2)
     near, far = tick(down[:length], down_far)
     block_out = (middle + near + widen(far)).astype(BF16)
     tock(block_out)
     gate_s.sum_one()
+    out_s.sum_two()
+    recur_s.sum_core()
+    small_s.take()
+    small_s.start_pair()
     a, b = down_s.both()
     ffndown_grad = jnp.concatenate([jnp.where(side == 0, a, b), jnp.where(side == 0, b, a)], axis=0)
     tock(ffndown_grad)
-    a, b = small_s.both()
-    small = a + b
 
     def weave(own, other):
         first = jnp.where(side == 0, own, other).reshape(-1, shards, 1, piece_f)
         second = jnp.where(side == 0, other, own).reshape(-1, shards, 1, piece_f)
         return jnp.concatenate([first, second], axis=2).reshape(own.shape[0], 2 * half_f)
 
-    out_s.sum_two()
-    recur_s.sum_core()
+    branch_s.sum_two()
+    admit_s.sum_core()
     up_s.sum_one()
     ffngate_grad = weave(*gate_s.both())
     tock(ffngate_grad)
-    branch_s.sum_two()
-    admit_s.sum_core()
+    recur_s.sum_two()
+    lruin_s.sum_core()
     out_s.sum_one()
     ffnup_grad = weave(*up_s.both())
     tock(ffnup_grad)
-    recur_s.sum_two()
-    lruin_s.sum_core()
+    small_s.take()
+    small = small_s.v.reshape(taps + 4, per_r)
+    admit_s.sum_two()
     branch_s.sum_one()
     outproj_grad = natural(*out_s.both())
     tock(outproj_grad)
-    admit_s.sum_two()
+    lruin_s.sum_two()
+    ffngain_grad = jnp.sum(ffngate_grad * widen(ffn_gate) + ffnup_grad * widen(ffn_up), axis=1) / widen(ffn_gain)
     recur_s.sum_one()
     branch_grad = natural(*branch_s.both())
     tock(branch_grad)
-    lruin_s.sum_two()
-    ffngain_grad = jnp.sum(ffngate_grad * widen(ffn_gate) + ffnup_grad * widen(ffn_up), axis=1) / widen(ffn_gain)
     admit_s.sum_one()
     recur_grad = natural(*recur_s.both())
     tock(recur_grad)

time: 872 us -> 766 us (0.88)
  Pallas kernels: 20.4 us -> 150 us
  waiting for transfers between devices: 322 us -> 237 us
  matrix products: 108 us -> 31.1 us
  local copies, waits for them, and re-layouts: 172 us -> 137 us
  starting transfers between devices: 127 us -> 101 us
  other arithmetic: 78.7 us -> 64.2 us
    pallas_call x0 -> x33, Pallas kernels: none -> 129 us  [the longest x8 44.4 us: grad_home(): pl.pallas_call(home_kernel, grid_spec=pltpu.PrefetchScalarGridSpec(num_sc...]
    all_gather x2, waiting for transfers between devices: 148 us -> 103 us  [gather_blocks(): return lax.all_gather(jnp.concatenate(rows, axis=0), 'shard', axis=0)]
    ppermute x20, waiting for transfers between devices: 89.7 us -> 48.4 us  [swap(): return lax.ppermute(v, 'rep', [(i, i ^ 1) for i in range(groups)])]
    dot_general x8 -> x0, matrix products: 35.4 us -> none  [rows_product(): lax.dot_general(left, right, (((0,), (0,)), ((), ())), preferred_element_...]
    add x20 -> x4, other arithmetic: 31.6 us -> 0.02 us  [take(): v = v + g]
    ppermute x45, starting transfers between devices: 104 us -> 76 us  [the longest x24 59.8 us: sum_two(): lax.ppermute(sends[k - 1], 'shard', along(k, f1, cores * f2))]
    squeeze x25 -> x3, local copies, waits for them, and re-layouts: 28.1 us -> 0.04 us  [start(): lax.dynamic_index_in_dim(v, (at + k) % count, axis, False)]
    dot_general x5 -> x3, matrix products: 38.3 us -> 14.3 us  [cols_product(): lax.dot_general(left, right, (((1,), (1,)), ((), ())), preferred_element_...]
  transfers between devices with their start and end apart: 67 -> 67, of which waited for: 26 -> 25; matrix products, arithmetic and copies ran while one was open for 30% -> 22% of each run, Pallas kernels for 1% -> 15%
where the time goes in v2:
time: 766 us; the launch traced here: 758 us
  waiting for transfers between devices  237 us (31%)
  Pallas kernels  150 us (20%)
  local copies, waits for them, and re-layouts  137 us (18%)
  starting transfers between devices  101 us (13%)
  other arithmetic  64.2 us (8%)
  matrix products  31.1 us (4%)
  blocking collectives  22.2 us (3%)
  between operations  16.1 us (2%)
    all_gather x2, waiting for transfers between devices, gather_blocks(): return lax.all_gather(jnp.concatenate(rows, axis=0), 'shard', axis=0)  103 us
    ppermute x24, waiting for transfers between devices, sum_two(): lax.ppermute(sends[k - 1], 'shard', along(k, f1, cores * f2))  68.1 us
    unnamed x328, local copies, waits for them, and re-layouts  67.8 us
    ppermute x24, starting transfers between devices, sum_two(): lax.ppermute(sends[k - 1], 'shard', along(k, f1, cores * f2))  59.8 us
    ppermute x20, waiting for transfers between devices, swap(): return lax.ppermute(v, 'rep', [(i, i ^ 1) for i in range(groups)])  48.4 us
    pallas_call x8, Pallas kernels, grad_home(): pl.pallas_call(home_kernel, grid_spec=pltpu.PrefetchScalarGridSpec(num_sc...  44.4 us
    pallas_call x1, Pallas kernels, ffn_pass(): pl.pallas_call(ffn_kernel, grid=(tiles,), in_specs=[fixed, fixed, pl.Bloc...  29.3 us
    pallas_call x8, Pallas kernels, grad_away(): pl.pallas_call(away_kernel, grid_spec=pltpu.PrefetchScalarGridSpec(num_sc...  25.1 us
  transfers between devices with their start and end apart: 67, of which 25 were waited for; matrix products, arithmetic and copies ran while one was open for 22% of the time, Pallas kernels for 15%

profile of v2, /device:TPU:0, one launch (start us, length us, event | category | flops | bytes accessed | tf_op | source)
XLA Modules:
  0.0 757.8 jit_solution(3910826540335623022)
XLA Ops:
  23.3 3.0 collective-permute-start
  26.4 22.2 %all_gather.15 = bf16[16,10,128]{2,1,0:T(8,128)(2,1)S(1)} all-gather(bf16[1,10,128]{2,1,0:T(8,128)(2,1)S(1)} %pad_bitcast_fusion), channel_id=1, replica_groups=mesh['rep'=2,'shard'=16] {'shard'}, dimensions={0}, use_global_device_ids=true | all-gather | bytes 43520 | tf_op jit(solution)/shard_map/all_gather | solution.py:485
  49.4 79.5 %all-gather.5.cloned.1.call-done = bf16[20480,512]{1,0:T(8,128)(2,1)} async-done(((bf16[1280,512]{1,0:T(8,128)(2,1)}), bf16[20480,512]{1,0:T(8,128)(2,1)}) %all-gather.5.cloned.1.call-update) | async-done | bytes 20971536 | tf_op jit(solution)/shard_map/all_gather | solution.py:500
  128.9 3.3 fusion.42
  132.2 3.5 fusion.20.pre_ref
  142.8 8.7 %fusion.41 = (bf16[16,128,512]{2,1,0:T(8,128)(2,1)}, bf16[16,128,512]{2,1,0:T(8,128)(2,1)}, bf16[16,128,512]{2,1,0:T(8,128)(2,1)}, bf16[16,128,512]{2,1,0:T(8,12...) fusion(bf16[16,1280,512]{2,1,0:T(8,128)(2,1)} %bitcast.151), kind=kLoop, calls=%fused_computation.171 | loop fusion | bytes 29360128 | tf_op jit(solution)/shard_map/slice | solution.py:504
  151.6 14.4 %collective-permute-done.1 = bf16[512,1024]{1,0:T(8,128)(2,1)S(1)} collective-permute-done((bf16[512,1024]{1,0:T(8,128)(2,1)S(1)}, bf16[512,1024]{1,0:T(8,128)(2,1)S(1)}, u32[]{:S(2)}, u32[]{:S(2)}) %collective-permute-start.1) | collective-permute-done | bytes 1048608 | tf_op jit(solution)/shard_map/ppermute | solution.py:387
  168.1 6.5 fusion.18.gates_r_ref.gates_i_ref
  174.6 8.5 %recurrence_forward.1 = (bf16[512,1024]{1,0:T(8,128)(2,1)}, f32[512,1024]{1,0:T(8,128)}) custom-call(f32[512,2048]{1,0:T(8,128)} %copy-done.75, f32[512,2048]{1,0:T(8,128)} %fusion.18.gates_r_ref.gates_i_ref, f32[512,2048]{1,0:T(8,128)} %fusion.18.gates_r_ref.gates_i_ref, bf16[512,1024]{1,0:T(8,128)(2,1)} %bitcast.156, f32[8,1024]{1,0:T(8,128)} %maximum_maximum_fusion.params_ref), custom_call_target="tpu_custom_call" | custom-call | flops 31457280 | bytes 10485760 | tf_op jit(solution)/shard_map/recurrence_forward/pallas_call | solution.py:129
  190.2 10.5 %collective-permute-done.2 = bf16[256,1024]{1,0:T(8,128)(2,1)} collective-permute-done((bf16[256,1024]{1,0:T(8,128)(2,1)}, bf16[256,1024]{1,0:T(8,128)(2,1)}, u32[]{:S(2)}, u32[]{:S(2)}) %collective-permute-start.2) | collective-permute-done | bytes 524320 | tf_op jit(solution)/shard_map/ppermute | solution.py:387
  201.9 7.5 collective-permute-done.3
  212.5 3.0 multiply_reduce_fusion.7
  218.2 23.1 %all-gather.7.cloned.1.call-done = bf16[13824,768]{1,0:T(8,128)(2,1)} async-done(((bf16[864,768]{1,0:T(8,128)(2,1)}), bf16[13824,768]{1,0:T(8,128)(2,1)}) %all-gather.7.cloned.1.call-update) | async-done | bytes 21233680 | tf_op jit(solution)/shard_map/all_gather | solution.py:500
  241.4 6.4 fusion.40
  247.8 6.5 pad_maximum_fusion.1.down_ref
  257.0 29.3 %ffn_pass.1 = (bf16[512,2304]{1,0:T(8,128)(2,1)}, bf16[512,2304]{1,0:T(8,128)(2,1)}, bf16[512,2304]{1,0:T(8,128)(2,1)}, f32[256,1536]{1,0:T(8,128)S(1)}, bf16[256,1536]{1,0:T(8,128)(2,1)S(1)}) custom-call(bf16[512,1536]{1,0:T(8,128)(2,1)S(1)} %get-tuple-element.500.x_ref, bf16[512,1536]{1,0:T(8,128)(2,1)S(1)} %constant_dynamic-update-slice_fusion.2.cot_ref.right_ref, ...), custom_call_target="tpu_custom_call" | custom-call | flops 1024 | bytes 1024 | tf_op jit(solution)/shard_map/ffn_pass/pallas_call | solution.py:205
  291.7 4.2 grad_away.8
  301.9 4.5 grad_away.9
  308.1 3.1 fusion.35
  311.2 6.4 grad_home.8
  321.0 4.6 grad_away.10
  328.0 3.2 fusion.39
  334.9 3.3 pad_maximum_fusion.3
  339.5 7.4 grad_home.9
  346.8 3.3 collective-permute-done.8
  351.4 3.2 fusion.cot_ref
  354.7 12.0 %recurrence_backward.1 = (bf16[512,1024]{1,0:T(8,128)(2,1)}, bf16[512,1024]{1,0:T(8,128)(2,1)}, bf16[512,1024]{1,0:T(8,128)(2,1)}, f32[512,1024]{1,0:T(8,128)}, f32[96,1024]{1,0:T(8,128)}) custom-call(f32[512,1024]{1,0:T(8,128)} %fusion.cot_ref, f32[512,2048]{1,0:T(8,128)} %copy-done.75, f32[512,2048]{1,0:T(8,128)} %fusion.18.gates_r_ref.gates_i_ref, ...), custom_call_target="tpu_custom_call" | custom-call | flops 1024 | bytes 1024 | tf_op jit(solution)/shard_map/recurrence_backward/pallas_call | solution.py:151
  366.7 7.6 %fusion.10 = f32[512,2048]{1,0:T(8,128)S(1)} fusion(bf16[512,1024]{1,0:T(8,128)(2,1)} %get-tuple-element.342.right_ref, bf16[512,1024]{1,0:T(8,128)(2,1)} %get-tuple-element.325.right_ref, bf16[2048,512]{1,0:T(8,128)(2,1)} %bitcast.178, bf16[2048,512]{1,0:T(8,128)(2,1)} %bitcast.180, bf16[2048,512]{1,0:T(8,128)(2,1)} %bitcast.182, ...), kind=kOutput, calls=%fused_computation.30 | convolution fusion | flops 4332716032 | bytes 14680064 | tf_op jit(solution)/shard_map/dot_general | solution.py:32
  383.0 3.4 constant_dynamic-slice_fusion.5
  386.5 4.0 spread.8
  391.5 7.9 %collective-permute-done.10 = bf16[512,1024]{1,0:T(8,128)(2,1)} collective-permute-done((bf16[512,1024]{1,0:T(8,128)(2,1)}, bf16[512,1024]{1,0:T(8,128)(2,1)}, u32[]{:S(2)}, u32[]{:S(2)}) %collective-permute-start.10) | collective-permute-done | bytes 1048608 | tf_op jit(solution)/shard_map/ppermute | solution.py:387
  401.7 6.8 grad_home.10
  421.0 3.2 copy.115
  424.2 3.1 grad_away.13
  433.5 3.4 fusion.14
  459.6 4.8 spread.9
  468.4 4.8 grad_home.11
  480.5 4.3 multiply_add_fusion
  484.8 6.7 collective-permute-done.31.refs_0_
  492.3 18.4 %collective-permute-done.32.refs_1_ = bf16[96,2304]{1,0:T(8,128)(2,1)S(1)} collective-permute-done((bf16[96,2304]{1,0:T(8,128)(2,1)S(1)}, bf16[96,2304]{1,0:T(8,128)(2,1)S(1)}, u32[]{:S(2)}, u32[]{:S(2)}) %collective-permute-start.32) | collective-permute-done | bytes 442400 | tf_op jit(solution)/shard_map/ppermute | solution.py:439
  512.6 3.8 fusion.37
  518.0 3.3 collective-permute-done.18
  523.0 6.1 collective-permute-start.33
  533.6 4.4 spread.10
  538.0 4.3 grad_home.12
  542.3 14.0 %collective-permute-done.33.refs_2_ = bf16[96,2304]{1,0:T(8,128)(2,1)} collective-permute-done((bf16[96,2304]{1,0:T(8,128)(2,1)}, bf16[96,2304]{1,0:T(8,128)(2,1)}, u32[]{:S(2)}, u32[]{:S(2)}) %collective-permute-start.33) | collective-permute-done | bytes 442400 | tf_op jit(solution)/shard_map/ppermute | solution.py:439
  556.3 3.2 collective-permute-start.26
  577.7 5.3 grad_home.13
  591.7 5.3 grad_home.14
  597.0 10.0 %collective-permute-done.41.refs_1_ = bf16[96,2304]{1,0:T(8,128)(2,1)S(1)} collective-permute-done((bf16[96,2304]{1,0:T(8,128)(2,1)}, bf16[96,2304]{1,0:T(8,128)(2,1)S(1)}, u32[]{:S(2)}, u32[]{:S(2)}) %collective-permute-start.41) | collective-permute-done | bytes 442400 | tf_op jit(solution)/shard_map/ppermute | solution.py:439
  607.0 7.1 collective-permute-start.44
  614.1 3.3 collective-permute-start.45
  634.5 2.9 copy.128
  645.4 4.3 grad_home.15
  651.4 3.3 collective-permute-start.36
  670.6 2.9 copy.129
  674.1 8.2 %collective-permute-done.38.refs_0_ = bf16[4,128,1024]{2,1,0:T(8,128)(2,1)S(1)} collective-permute-done((bf16[4,128,1024]{2,1,0:T(8,128)(2,1)}, bf16[4,128,1024]{2,1,0:T(8,128)(2,1)S(1)}, u32[]{:S(2)}, u32[]{:S(2)}) %collective-permute-start.38) | collective-permute-done | bytes 1048608 | tf_op jit(solution)/shard_map/ppermute | solution.py:433
  692.9 3.7 collective-permute-done.54.refs_0_
  699.1 3.8 collective-permute-start.61
  702.9 7.4 collective-permute-done.52.refs_1_
  710.3 7.5 collective-permute-start.62
  722.8 8.7 %collective-permute-done.61.refs_1_ = bf16[128,1024]{1,0:T(8,128)(2,1)S(1)} collective-permute-done((bf16[128,1024]{1,0:T(8,128)(2,1)S(1)}, bf16[128,1024]{1,0:T(8,128)(2,1)S(1)}, u32[]{:S(2)}, u32[]{:S(2)}) %collective-permute-start.61) | collective-permute-done | bytes 262176 | tf_op jit(solution)/shard_map/ppermute | solution.py:439
  731.5 6.6 collective-permute-start.58
  743.8 3.0 collective-permute-done.64
  (558 shorter events, 239.2 us)
Async XLA Ops:
  7.2 121.7 %all-gather.5.cloned.1.call-start = ((), (), s32[]{:S(2)}) async-start(), calls=%async_computation | async-start | bytes 22282240 | tf_op jit(solution)/shard_map/all_gather | solution.py:500
  16.8 224.6 %all-gather.7.cloned.1.call-start = ((), (), s32[]{:S(2)}) async-start(), calls=%async_computation.1 | async-start | bytes 22560768 | tf_op jit(solution)/shard_map/all_gather | solution.py:500
  23.3 25.7 %collective-permute-start = (bf16[256,1536]{1,0:T(8,128)(2,1)S(1)}, bf16[256,1536]{1,0:T(8,128)(2,1)S(1)}, u32[]{:S(2)}, u32[]{:S(2)}) collective-permute-start(bf16[256,1536]{1,0:T(8,128)(2,1)S(1)} %copy-done.101), channel_id=1, source_target_pairs={{0,16},{16,0},{1,17},{17,1},{2,18},{18,2},{3,19},{19,3},{4,20},{20... | collective-permute-start | bytes 2359304 | tf_op jit(solution)/shard_map/ppermute | solution.py:387
  140.0 26.1 %collective-permute-start.1 = (bf16[512,1024]{1,0:T(8,128)(2,1)S(1)}, bf16[512,1024]{1,0:T(8,128)(2,1)S(1)}, u32[]{:S(2)}, u32[]{:S(2)}) collective-permute-start(bf16[512,1024]{1,0:T(8,128)(2,1)S(1)} %bitcast.155), channel_id=1, source_target_pairs={{0,16},{16,0},{1,17},{17,1},{2,18},{18,2},{3,19},{19,3},{4,20},{20... | collective-permute-start | bytes 3145736 | tf_op jit(solution)/shard_map/ppermute | solution.py:387
  141.5 47.4 %collective-permute-start.5 = (bf16[256,1536]{1,0:T(8,128)(2,1)}, bf16[256,1536]{1,0:T(8,128)(2,1)}, u32[]{:S(2)}, u32[]{:S(2)}) collective-permute-start(bf16[256,1536]{1,0:T(8,128)(2,1)} %param.18), channel_id=1, source_target_pairs={{0,16},{16,0},{1,17},{17,1},{2,18},{18,2},{3,19},{19,3},{4,20},{20... | collective-permute-start | bytes 2359304 | tf_op jit(solution)/shard_map/ppermute | solution.py:387
  185.5 15.2 %collective-permute-start.2 = (bf16[256,1024]{1,0:T(8,128)(2,1)}, bf16[256,1024]{1,0:T(8,128)(2,1)}, u32[]{:S(2)}, u32[]{:S(2)}) collective-permute-start(bf16[256,1024]{1,0:T(8,128)(2,1)} %get-tuple-element.510), channel_id=1, source_target_pairs={{0,16},{16,0},{1,17},{17,1},{2,18},{18,2},{3,19},{19,3},{4,20},{20... | collective-permute-start | bytes 1572872 | tf_op jit(solution)/shard_map/ppermute | solution.py:387
  187.0 22.5 %collective-permute-start.3 = (bf16[256,1024]{1,0:T(8,128)(2,1)}, bf16[256,1024]{1,0:T(8,128)(2,1)S(1)}, u32[]{:S(2)}, u32[]{:S(2)}) collective-permute-start(bf16[256,1024]{1,0:T(8,128)(2,1)} %get-tuple-element.509), channel_id=1, source_target_pairs={{0,16},{16,0},{1,17},{17,1},{2,18},{18,2},{3,19},{19,3},{4,20},{20... | collective-permute-start | bytes 1572872 | tf_op jit(solution)/shard_map/ppermute | solution.py:387
  216.8 37.5 %collective-permute-start.4 = (bf16[256,1536]{1,0:T(8,128)(2,1)}, bf16[256,1536]{1,0:T(8,128)(2,1)}, u32[]{:S(2)}, u32[]{:S(2)}) collective-permute-start(bf16[256,1536]{1,0:T(8,128)(2,1)} %multiply_convert_fusion.1), channel_id=1, source_target_pairs={{0,16},{16,0},{1,17},{17,1},{2,18},{18,2},{3,19},{19,3},{4,20},{20... | collective-permute-start | bytes 2359304 | tf_op jit(solution)/shard_map/ppermute | solution.py:387
  295.9 15.3 %collective-permute-start.7 = (bf16[8,144,1536]{2,1,0:T(8,128)(2,1)}, bf16[8,144,1536]{2,1,0:T(8,128)(2,1)}, u32[]{:S(2)}, u32[]{:S(2)}) collective-permute-start(bf16[8,144,1536]{2,1,0:T(8,128)(2,1)} %grad_away.8), channel_id=1, source_target_pairs={{0,1},{1,0},{2,3},{3,2},{4,5},{5,4},{6,7},{7,6},{8,9},{9,8},{10,11... | collective-permute-start | bytes 10616840 | tf_op jit(solution)/shard_map/ppermute | solution.py:427
  306.4 31.9 %collective-permute-start.9 = (bf16[8,96,2304]{2,1,0:T(8,128)(2,1)}, bf16[8,96,2304]{2,1,0:T(8,128)(2,1)}, u32[]{:S(2)}, u32[]{:S(2)}) collective-permute-start(bf16[8,96,2304]{2,1,0:T(8,128)(2,1)} %grad_away.9), channel_id=1, source_target_pairs={{0,1},{1,0},{2,3},{3,2},{4,5},{5,4},{6,7},{7,6},{8,9},{9,8},{10,11... | collective-permute-start | bytes 10616840 | tf_op jit(solution)/shard_map/ppermute | solution.py:427
  306.6 19.8 %collective-permute-start.6 = (bf16[256,1536]{1,0:T(8,128)(2,1)S(1)}, bf16[256,1536]{1,0:T(8,128)(2,1)}, u32[]{:S(2)}, u32[]{:S(2)}) collective-permute-start(bf16[256,1536]{1,0:T(8,128)(2,1)S(1)} %get-tuple-element.223), channel_id=1, source_target_pairs={{0,16},{16,0},{1,17},{17,1},{2,18},{18,2},{3,19},{19,3},{4,20},{20... | collective-permute-start | bytes 2359304 | tf_op jit(solution)/shard_map/ppermute | solution.py:387
  331.2 19.0 %collective-permute-start.8 = (bf16[256,1536]{1,0:T(8,128)(2,1)S(1)}, bf16[256,1536]{1,0:T(8,128)(2,1)}, u32[]{:S(2)}, u32[]{:S(2)}) collective-permute-start(bf16[256,1536]{1,0:T(8,128)(2,1)S(1)} %get-tuple-element.480), channel_id=1, source_target_pairs={{0,16},{16,0},{1,17},{17,1},{2,18},{18,2},{3,19},{19,3},{4,20},{20... | collective-permute-start | bytes 2359304 | tf_op jit(solution)/shard_map/ppermute | solution.py:387
  334.9 66.9 %collective-permute-start.11 = (bf16[8,96,2304]{2,1,0:T(8,128)(2,1)}, bf16[8,96,2304]{2,1,0:T(8,128)(2,1)}, u32[]{:S(2)}, u32[]{:S(2)}) collective-permute-start(bf16[8,96,2304]{2,1,0:T(8,128)(2,1)} %grad_away.10), channel_id=1, source_target_pairs={{0,1},{1,0},{2,3},{3,2},{4,5},{5,4},{6,7},{7,6},{8,9},{9,8},{10,11... | collective-permute-start | bytes 10616840 | tf_op jit(solution)/shard_map/ppermute | solution.py:427
  338.2 48.2 %collective-permute-start.12 = (bf16[4,144,1536]{2,1,0:T(8,128)(2,1)}, bf16[4,144,1536]{2,1,0:T(8,128)(2,1)}, u32[]{:S(2)}, u32[]{:S(2)}) collective-permute-start(bf16[4,144,1536]{2,1,0:T(8,128)(2,1)} %bitcast.42), channel_id=1, source_target_pairs={{0,2},{1,3},{2,0},{3,1},{4,6},{5,7},{6,4},{7,5},{8,10},{9,11},{10,... | collective-permute-start | bytes 5308424 | tf_op jit(solution)/shard_map/ppermute | solution.py:433
  375.5 23.9 %collective-permute-start.10 = (bf16[512,1024]{1,0:T(8,128)(2,1)}, bf16[512,1024]{1,0:T(8,128)(2,1)}, u32[]{:S(2)}, u32[]{:S(2)}) collective-permute-start(bf16[512,1024]{1,0:T(8,128)(2,1)} %dynamic-slice_convert_fusion), channel_id=1, source_target_pairs={{0,16},{16,0},{1,17},{17,1},{2,18},{18,2},{3,19},{19,3},{4,20},{20... | collective-permute-start | bytes 3145736 | tf_op jit(solution)/shard_map/ppermute | solution.py:387
  380.5 77.7 %collective-permute-start.16 = (bf16[4,96,2304]{2,1,0:T(8,128)(2,1)}, bf16[4,96,2304]{2,1,0:T(8,128)(2,1)}, u32[]{:S(2)}, u32[]{:S(2)}) collective-permute-start(bf16[4,96,2304]{2,1,0:T(8,128)(2,1)} %bitcast.62), channel_id=1, source_target_pairs={{0,2},{1,3},{2,0},{3,1},{4,6},{5,7},{6,4},{7,5},{8,10},{9,11},{10,... | collective-permute-start | bytes 5308424 | tf_op jit(solution)/shard_map/ppermute | solution.py:433
  415.3 52.8 %collective-permute-start.15 = (bf16[8,128,768]{2,1,0:T(8,128)(2,1)}, bf16[8,128,768]{2,1,0:T(8,128)(2,1)}, u32[]{:S(2)}, u32[]{:S(2)}) collective-permute-start(bf16[8,128,768]{2,1,0:T(8,128)(2,1)} %grad_away.11), channel_id=1, source_target_pairs={{0,1},{1,0},{2,3},{3,2},{4,5},{5,4},{6,7},{7,6},{8,9},{9,8},{10,11... | collective-permute-start | bytes 4718600 | tf_op jit(solution)/shard_map/ppermute | solution.py:427
  438.0 35.2 %collective-permute-start.14 = (bf16[256,1536]{1,0:T(8,128)(2,1)}, bf16[256,1536]{1,0:T(8,128)(2,1)}, u32[]{:S(2)}, u32[]{:S(2)}) collective-permute-start(bf16[256,1536]{1,0:T(8,128)(2,1)} %slice.407), channel_id=1, source_target_pairs={{0,16},{16,0},{1,17},{17,1},{2,18},{18,2},{3,19},{19,3},{4,20},{20... | collective-permute-start | bytes 2359304 | tf_op jit(solution)/shard_map/ppermute | solution.py:387
  439.5 36.7 %collective-permute-start.21 = (bf16[144,1536]{1,0:T(8,128)(2,1)}, bf16[144,1536]{1,0:T(8,128)(2,1)}, u32[]{:S(2)}, u32[]{:S(2)}) collective-permute-start(bf16[144,1536]{1,0:T(8,128)(2,1)} %get-tuple-element.253), channel_id=1, source_target_pairs={{0,4},{1,5},{2,6},{3,7},{4,8},{5,9},{6,10},{7,11},{8,12},{9,13},{1... | collective-permute-start | bytes 1327112 | tf_op jit(solution)/shard_map/ppermute | solution.py:439
  441.0 36.2 %collective-permute-start.22 = (bf16[144,1536]{1,0:T(8,128)(2,1)}, bf16[144,1536]{1,0:T(8,128)(2,1)}, u32[]{:S(2)}, u32[]{:S(2)}) collective-permute-start(bf16[144,1536]{1,0:T(8,128)(2,1)} %get-tuple-element.254), channel_id=1, source_target_pairs={{0,8},{1,9},{2,10},{3,11},{4,12},{5,13},{6,14},{7,15},{8,0},{9,1},... | collective-permute-start | bytes 1327112 | tf_op jit(solution)/shard_map/ppermute | solution.py:439
  458.2 21.1 %collective-permute-start.23 = (bf16[144,1536]{1,0:T(8,128)(2,1)S(1)}, bf16[144,1536]{1,0:T(8,128)(2,1)S(1)}, u32[]{:S(2)}, u32[]{:S(2)}) collective-permute-start(bf16[144,1536]{1,0:T(8,128)(2,1)S(1)} %copy-done.63), channel_id=1, source_target_pairs={{0,12},{1,13},{2,14},{3,15},{4,0},{5,1},{6,2},{7,3},{8,4},{9,5},{1... | collective-permute-start | bytes 1327112 | tf_op jit(solution)/shard_map/ppermute | solution.py:439
  468.0 49.4 %collective-permute-start.19 = (bf16[8,96,1024]{2,1,0:T(8,128)(2,1)}, bf16[8,96,1024]{2,1,0:T(8,128)(2,1)}, u32[]{:S(2)}, u32[]{:S(2)}) collective-permute-start(bf16[8,96,1024]{2,1,0:T(8,128)(2,1)} %copy-done.35), channel_id=1, source_target_pairs={{0,1},{1,0},{2,3},{3,2},{4,5},{5,4},{6,7},{7,6},{8,9},{9,8},{10,11... | collective-permute-start | bytes 4718600 | tf_op jit(solution)/shard_map/ppermute | solution.py:427
  473.3 6.7 collective-permute-start.13
  476.2 15.3 %collective-permute-start.31 = (bf16[96,2304]{1,0:T(8,128)(2,1)S(1)}, bf16[96,2304]{1,0:T(8,128)(2,1)S(1)}, u32[]{:S(2)}, u32[]{:S(2)}) collective-permute-start(bf16[96,2304]{1,0:T(8,128)(2,1)S(1)} %copy-done.67), channel_id=1, source_target_pairs={{0,4},{1,5},{2,6},{3,7},{4,8},{5,9},{6,10},{7,11},{8,12},{9,13},{1... | collective-permute-start | bytes 1327112 | tf_op jit(solution)/shard_map/ppermute | solution.py:439
  477.2 33.4 %collective-permute-start.32 = (bf16[96,2304]{1,0:T(8,128)(2,1)S(1)}, bf16[96,2304]{1,0:T(8,128)(2,1)S(1)}, u32[]{:S(2)}, u32[]{:S(2)}) collective-permute-start(bf16[96,2304]{1,0:T(8,128)(2,1)S(1)} %copy-done.65), channel_id=1, source_target_pairs={{0,8},{1,9},{2,10},{3,11},{4,12},{5,13},{6,14},{7,15},{8,0},{9,1},... | collective-permute-start | bytes 1327112 | tf_op jit(solution)/shard_map/ppermute | solution.py:439
  480.0 86.1 %collective-permute-start.29 = (bf16[8,128,1024]{2,1,0:T(8,128)(2,1)}, bf16[8,128,1024]{2,1,0:T(8,128)(2,1)}, u32[]{:S(2)}, u32[]{:S(2)}) collective-permute-start(bf16[8,128,1024]{2,1,0:T(8,128)(2,1)} %grad_away.13), channel_id=1, source_target_pairs={{0,1},{1,0},{2,3},{3,2},{4,5},{5,4},{6,7},{7,6},{8,9},{9,8},{10,11... | collective-permute-start | bytes 6291464 | tf_op jit(solution)/shard_map/ppermute | solution.py:427
  480.0 41.8 %collective-permute-start.20 = (bf16[4,96,2304]{2,1,0:T(8,128)(2,1)S(1)}, bf16[4,96,2304]{2,1,0:T(8,128)(2,1)S(1)}, u32[]{:S(2)}, u32[]{:S(2)}) collective-permute-start(bf16[4,96,2304]{2,1,0:T(8,128)(2,1)S(1)} %bitcast.144), channel_id=1, source_target_pairs={{0,2},{1,3},{2,0},{3,1},{4,6},{5,7},{6,4},{7,5},{8,10},{9,11},{10,... | collective-permute-start | bytes 5308424 | tf_op jit(solution)/shard_map/ppermute | solution.py:433
  492.3 91.8 %collective-permute-start.37 = (bf16[8,128,1024]{2,1,0:T(8,128)(2,1)S(1)}, bf16[8,128,1024]{2,1,0:T(8,128)(2,1)}, u32[]{:S(2)}, u32[]{:S(2)}) collective-permute-start(bf16[8,128,1024]{2,1,0:T(8,128)(2,1)S(1)} %copy-done.28), channel_id=1, source_target_pairs={{0,1},{1,0},{2,3},{3,2},{4,5},{5,4},{6,7},{7,6},{8,9},{9,8},{10,11... | collective-permute-start | bytes 6291464 | tf_op jit(solution)/shard_map/ppermute | solution.py:427
  511.4 9.9 %collective-permute-start.18 = (f32[4,8,128]{2,1,0:T(8,128)S(1)}, f32[4,8,128]{2,1,0:T(8,128)S(1)}, u32[]{:S(2)}, u32[]{:S(2)}) collective-permute-start(f32[4,8,128]{2,1,0:T(8,128)S(1)} %get-tuple-element.533), channel_id=1, source_target_pairs={{0,2},{1,3},{2,0},{3,1},{4,6},{5,7},{6,4},{7,5},{8,10},{9,11},{10,... | collective-permute-start | bytes 49160 | tf_op jit(solution)/shard_map/ppermute | solution.py:464
  517.5 42.1 %collective-permute-start.17 = (bf16[256,1536]{1,0:T(8,128)(2,1)}, bf16[256,1536]{1,0:T(8,128)(2,1)}, u32[]{:S(2)}, u32[]{:S(2)}) collective-permute-start(bf16[256,1536]{1,0:T(8,128)(2,1)} %slice.406), channel_id=1, source_target_pairs={{0,16},{16,0},{1,17},{17,1},{2,18},{18,2},{3,19},{19,3},{4,20},{20... | collective-permute-start | bytes 2359304 | tf_op jit(solution)/shard_map/ppermute | solution.py:387
  521.4 46.5 %collective-permute-start.30 = (bf16[4,128,768]{2,1,0:T(8,128)(2,1)}, bf16[4,128,768]{2,1,0:T(8,128)(2,1)}, u32[]{:S(2)}, u32[]{:S(2)}) collective-permute-start(bf16[4,128,768]{2,1,0:T(8,128)(2,1)} %bitcast.73), channel_id=1, source_target_pairs={{0,2},{1,3},{2,0},{3,1},{4,6},{5,7},{6,4},{7,5},{8,10},{9,11},{10,... | collective-permute-start | bytes 2359304 | tf_op jit(solution)/shard_map/ppermute | solution.py:433
  523.0 33.3 %collective-permute-start.33 = (bf16[96,2304]{1,0:T(8,128)(2,1)}, bf16[96,2304]{1,0:T(8,128)(2,1)}, u32[]{:S(2)}, u32[]{:S(2)}) collective-permute-start(bf16[96,2304]{1,0:T(8,128)(2,1)} %get-tuple-element.280), channel_id=1, source_target_pairs={{0,12},{1,13},{2,14},{3,15},{4,0},{5,1},{6,2},{7,3},{8,4},{9,5},{1... | collective-permute-start | bytes 1327112 | tf_op jit(solution)/shard_map/ppermute | solution.py:439
  561.8 22.3 %collective-permute-start.25 = (bf16[144,1536]{1,0:T(8,128)(2,1)}, bf16[144,1536]{1,0:T(8,128)(2,1)}, u32[]{:S(2)}, u32[]{:S(2)}) collective-permute-start(bf16[144,1536]{1,0:T(8,128)(2,1)} %get-tuple-element.296), channel_id=1, source_target_pairs={{0,16},{16,0},{1,17},{17,1},{2,18},{18,2},{3,19},{19,3},{4,20},{20... | collective-permute-start | bytes 1327112 | tf_op jit(solution)/shard_map/ppermute | solution.py:387
  564.1 20.2 %collective-permute-start.40 = (bf16[96,2304]{1,0:T(8,128)(2,1)S(1)}, bf16[96,2304]{1,0:T(8,128)(2,1)S(1)}, u32[]{:S(2)}, u32[]{:S(2)}) collective-permute-start(bf16[96,2304]{1,0:T(8,128)(2,1)S(1)} %get-tuple-element.300), channel_id=1, source_target_pairs={{0,4},{1,5},{2,6},{3,7},{4,8},{5,9},{6,10},{7,11},{8,12},{9,13},{1... | collective-permute-start | bytes 1327112 | tf_op jit(solution)/shard_map/ppermute | solution.py:439
  566.1 16.8 %collective-permute-start.28 = (f32[8,128]{1,0:T(8,128)S(1)}, f32[8,128]{1,0:T(8,128)S(1)}, u32[]{:S(2)}, u32[]{:S(2)}) collective-permute-start(f32[8,128]{1,0:T(8,128)S(1)} %get-tuple-element.543), channel_id=1, source_target_pairs={{0,12},{1,13},{2,14},{3,15},{4,0},{5,1},{6,2},{7,3},{8,4},{9,5},{1... | collective-permute-start | bytes 12296 | tf_op jit(solution)/shard_map/ppermute | solution.py:464
  567.9 19.2 %collective-permute-start.24 = (bf16[4,96,1024]{2,1,0:T(8,128)(2,1)}, bf16[4,96,1024]{2,1,0:T(8,128)(2,1)S(1)}, u32[]{:S(2)}, u32[]{:S(2)}) collective-permute-start(bf16[4,96,1024]{2,1,0:T(8,128)(2,1)} %bitcast.68), channel_id=1, source_target_pairs={{0,2},{1,3},{2,0},{3,1},{4,6},{5,7},{6,4},{7,5},{8,10},{9,11},{10,... | collective-permute-start | bytes 2359304 | tf_op jit(solution)/shard_map/ppermute | solution.py:433
  582.9 39.2 %collective-permute-start.48 = (bf16[4,128,1024]{2,1,0:T(8,128)(2,1)}, bf16[4,128,1024]{2,1,0:T(8,128)(2,1)S(1)}, u32[]{:S(2)}, u32[]{:S(2)}) collective-permute-start(bf16[4,128,1024]{2,1,0:T(8,128)(2,1)} %bitcast.75), channel_id=1, source_target_pairs={{0,2},{1,3},{2,0},{3,1},{4,6},{5,7},{6,4},{7,5},{8,10},{9,11},{10,... | collective-permute-start | bytes 3145736 | tf_op jit(solution)/shard_map/ppermute | solution.py:433
  584.1 59.9 %collective-permute-start.47 = (bf16[8,96,1024]{2,1,0:T(8,128)(2,1)}, bf16[8,96,1024]{2,1,0:T(8,128)(2,1)}, u32[]{:S(2)}, u32[]{:S(2)}) collective-permute-start(bf16[8,96,1024]{2,1,0:T(8,128)(2,1)} %grad_away.15), channel_id=1, source_target_pairs={{0,1},{1,0},{2,3},{3,2},{4,5},{5,4},{6,7},{7,6},{8,9},{9,8},{10,11... | collective-permute-start | bytes 4718600 | tf_op jit(solution)/shard_map/ppermute | solution.py:427
  584.1 22.9 %collective-permute-start.41 = (bf16[96,2304]{1,0:T(8,128)(2,1)}, bf16[96,2304]{1,0:T(8,128)(2,1)S(1)}, u32[]{:S(2)}, u32[]{:S(2)}) collective-permute-start(bf16[96,2304]{1,0:T(8,128)(2,1)} %get-tuple-element.301), channel_id=1, source_target_pairs={{0,8},{1,9},{2,10},{3,11},{4,12},{5,13},{6,14},{7,15},{8,0},{9,1},... | collective-permute-start | bytes 1327112 | tf_op jit(solution)/shard_map/ppermute | solution.py:439
  584.2 29.9 %collective-permute-start.42 = (bf16[96,2304]{1,0:T(8,128)(2,1)S(1)}, bf16[96,2304]{1,0:T(8,128)(2,1)S(1)}, u32[]{:S(2)}, u32[]{:S(2)}) collective-permute-start(bf16[96,2304]{1,0:T(8,128)(2,1)S(1)} %copy-done.61), channel_id=1, source_target_pairs={{0,12},{1,13},{2,14},{3,15},{4,0},{5,1},{6,2},{7,3},{8,4},{9,5},{1... | collective-permute-start | bytes 1327112 | tf_op jit(solution)/shard_map/ppermute | solution.py:439
  587.1 32.9 %collective-permute-start.49 = (bf16[96,2304]{1,0:T(8,128)(2,1)}, bf16[96,2304]{1,0:T(8,128)(2,1)}, u32[]{:S(2)}, u32[]{:S(2)}) collective-permute-start(bf16[96,2304]{1,0:T(8,128)(2,1)} %get-tuple-element.317), channel_id=1, source_target_pairs={{0,16},{16,0},{1,17},{17,1},{2,18},{18,2},{3,19},{19,3},{4,20},{20... | collective-permute-start | bytes 1327112 | tf_op jit(solution)/shard_map/ppermute | solution.py:387
  607.0 43.8 %collective-permute-start.44 = (bf16[128,768]{1,0:T(8,128)(2,1)}, bf16[128,768]{1,0:T(8,128)(2,1)}, u32[]{:S(2)}, u32[]{:S(2)}) collective-permute-start(bf16[128,768]{1,0:T(8,128)(2,1)} %get-tuple-element.321), channel_id=1, source_target_pairs={{0,4},{1,5},{2,6},{3,7},{4,8},{5,9},{6,10},{7,11},{8,12},{9,13},{1... | collective-permute-start | bytes 589832 | tf_op jit(solution)/shard_map/ppermute | solution.py:439
  614.1 36.8 %collective-permute-start.45 = (bf16[128,768]{1,0:T(8,128)(2,1)}, bf16[128,768]{1,0:T(8,128)(2,1)}, u32[]{:S(2)}, u32[]{:S(2)}) collective-permute-start(bf16[128,768]{1,0:T(8,128)(2,1)} %get-tuple-element.322), channel_id=1, source_target_pairs={{0,8},{1,9},{2,10},{3,11},{4,12},{5,13},{6,14},{7,15},{8,0},{9,1},... | collective-permute-start | bytes 589832 | tf_op jit(solution)/shard_map/ppermute | solution.py:439
  620.0 31.5 %collective-permute-start.46 = (bf16[128,768]{1,0:T(8,128)(2,1)}, bf16[128,768]{1,0:T(8,128)(2,1)}, u32[]{:S(2)}, u32[]{:S(2)}) collective-permute-start(bf16[128,768]{1,0:T(8,128)(2,1)} %get-tuple-element.323), channel_id=1, source_target_pairs={{0,12},{1,13},{2,14},{3,15},{4,0},{5,1},{6,2},{7,3},{8,4},{9,5},{1... | collective-permute-start | bytes 589832 | tf_op jit(solution)/shard_map/ppermute | solution.py:439
  623.1 32.9 %collective-permute-start.43 = (bf16[96,2304]{1,0:T(8,128)(2,1)}, bf16[96,2304]{1,0:T(8,128)(2,1)}, u32[]{:S(2)}, u32[]{:S(2)}) collective-permute-start(bf16[96,2304]{1,0:T(8,128)(2,1)} %get-tuple-element.351), channel_id=1, source_target_pairs={{0,16},{16,0},{1,17},{17,1},{2,18},{18,2},{3,19},{19,3},{4,20},{20... | collective-permute-start | bytes 1327112 | tf_op jit(solution)/shard_map/ppermute | solution.py:387
  643.9 22.6 %collective-permute-start.39 = (f32[8,128]{1,0:T(8,128)S(1)}, f32[8,128]{1,0:T(8,128)S(1)}, u32[]{:S(2)}, u32[]{:S(2)}) collective-permute-start(f32[8,128]{1,0:T(8,128)S(1)} %add_add_fusion), channel_id=1, source_target_pairs={{0,16},{16,0},{1,17},{17,1},{2,18},{18,2},{3,19},{19,3},{4,20},{20... | collective-permute-start | bytes 12296 | tf_op jit(solution)/shard_map/ppermute | solution.py:387
  650.9 33.3 %collective-permute-start.34 = (bf16[96,1024]{1,0:T(8,128)(2,1)}, bf16[96,1024]{1,0:T(8,128)(2,1)}, u32[]{:S(2)}, u32[]{:S(2)}) collective-permute-start(bf16[96,1024]{1,0:T(8,128)(2,1)} %get-tuple-element.338), channel_id=1, source_target_pairs={{0,4},{1,5},{2,6},{3,7},{4,8},{5,9},{6,10},{7,11},{8,12},{9,13},{1... | collective-permute-start | bytes 589832 | tf_op jit(solution)/shard_map/ppermute | solution.py:439
  650.9 33.9 %collective-permute-start.35 = (bf16[96,1024]{1,0:T(8,128)(2,1)}, bf16[96,1024]{1,0:T(8,128)(2,1)}, u32[]{:S(2)}, u32[]{:S(2)}) collective-permute-start(bf16[96,1024]{1,0:T(8,128)(2,1)} %get-tuple-element.339), channel_id=1, source_target_pairs={{0,8},{1,9},{2,10},{3,11},{4,12},{5,13},{6,14},{7,15},{8,0},{9,1},... | collective-permute-start | bytes 589832 | tf_op jit(solution)/shard_map/ppermute | solution.py:439
  651.4 34.9 %collective-permute-start.36 = (bf16[96,1024]{1,0:T(8,128)(2,1)}, bf16[96,1024]{1,0:T(8,128)(2,1)}, u32[]{:S(2)}, u32[]{:S(2)}) collective-permute-start(bf16[96,1024]{1,0:T(8,128)(2,1)} %get-tuple-element.340), channel_id=1, source_target_pairs={{0,12},{1,13},{2,14},{3,15},{4,0},{5,1},{6,2},{7,3},{8,4},{9,5},{1... | collective-permute-start | bytes 589832 | tf_op jit(solution)/shard_map/ppermute | solution.py:439
  656.0 26.4 %collective-permute-start.38 = (bf16[4,128,1024]{2,1,0:T(8,128)(2,1)}, bf16[4,128,1024]{2,1,0:T(8,128)(2,1)S(1)}, u32[]{:S(2)}, u32[]{:S(2)}) collective-permute-start(bf16[4,128,1024]{2,1,0:T(8,128)(2,1)} %bitcast.74), channel_id=1, source_target_pairs={{0,2},{1,3},{2,0},{3,1},{4,6},{5,7},{6,4},{7,5},{8,10},{9,11},{10,... | collective-permute-start | bytes 3145736 | tf_op jit(solution)/shard_map/ppermute | solution.py:433
  666.5 30.1 %collective-permute-start.54 = (bf16[4,96,1024]{2,1,0:T(8,128)(2,1)}, bf16[4,96,1024]{2,1,0:T(8,128)(2,1)}, u32[]{:S(2)}, u32[]{:S(2)}) collective-permute-start(bf16[4,96,1024]{2,1,0:T(8,128)(2,1)} %bitcast.82), channel_id=1, source_target_pairs={{0,2},{1,3},{2,0},{3,1},{4,6},{5,7},{6,4},{7,5},{8,10},{9,11},{10,... | collective-permute-start | bytes 2359304 | tf_op jit(solution)/shard_map/ppermute | solution.py:433
  682.4 8.0 %collective-permute-start.55 = (bf16[128,768]{1,0:T(8,128)(2,1)}, bf16[128,768]{1,0:T(8,128)(2,1)S(1)}, u32[]{:S(2)}, u32[]{:S(2)}) collective-permute-start(bf16[128,768]{1,0:T(8,128)(2,1)} %copy-done.74), channel_id=1, source_target_pairs={{0,16},{16,0},{1,17},{17,1},{2,18},{18,2},{3,19},{19,3},{4,20},{20... | collective-permute-start | bytes 589832 | tf_op jit(solution)/shard_map/ppermute | solution.py:387
  684.2 14.8 %collective-permute-start.51 = (bf16[128,1024]{1,0:T(8,128)(2,1)S(1)}, bf16[128,1024]{1,0:T(8,128)(2,1)S(1)}, u32[]{:S(2)}, u32[]{:S(2)}) collective-permute-start(bf16[128,1024]{1,0:T(8,128)(2,1)S(1)} %copy-done.73), channel_id=1, source_target_pairs={{0,4},{1,5},{2,6},{3,7},{4,8},{5,9},{6,10},{7,11},{8,12},{9,13},{1... | collective-permute-start | bytes 786440 | tf_op jit(solution)/shard_map/ppermute | solution.py:439
  684.8 25.5 %collective-permute-start.52 = (bf16[128,1024]{1,0:T(8,128)(2,1)S(1)}, bf16[128,1024]{1,0:T(8,128)(2,1)S(1)}, u32[]{:S(2)}, u32[]{:S(2)}) collective-permute-start(bf16[128,1024]{1,0:T(8,128)(2,1)S(1)} %copy-done.71), channel_id=1, source_target_pairs={{0,8},{1,9},{2,10},{3,11},{4,12},{5,13},{6,14},{7,15},{8,0},{9,1},... | collective-permute-start | bytes 786440 | tf_op jit(solution)/shard_map/ppermute | solution.py:439
  686.3 31.5 %collective-permute-start.53 = (bf16[128,1024]{1,0:T(8,128)(2,1)S(1)}, bf16[128,1024]{1,0:T(8,128)(2,1)S(1)}, u32[]{:S(2)}, u32[]{:S(2)}) collective-permute-start(bf16[128,1024]{1,0:T(8,128)(2,1)S(1)} %copy-done.69), channel_id=1, source_target_pairs={{0,12},{1,13},{2,14},{3,15},{4,0},{5,1},{6,2},{7,3},{8,4},{9,5},{1... | collective-permute-start | bytes 786440 | tf_op jit(solution)/shard_map/ppermute | solution.py:439
  690.4 29.9 %collective-permute-start.50 = (bf16[96,1024]{1,0:T(8,128)(2,1)S(1)}, bf16[96,1024]{1,0:T(8,128)(2,1)S(1)}, u32[]{:S(2)}, u32[]{:S(2)}) collective-permute-start(bf16[96,1024]{1,0:T(8,128)(2,1)S(1)} %get-tuple-element.386), channel_id=1, source_target_pairs={{0,16},{16,0},{1,17},{17,1},{2,18},{18,2},{3,19},{19,3},{4,20},{20... | collective-permute-start | bytes 589832 | tf_op jit(solution)/shard_map/ppermute | solution.py:387
  696.7 26.1 %collective-permute-start.60 = (bf16[128,1024]{1,0:T(8,128)(2,1)S(1)}, bf16[128,1024]{1,0:T(8,128)(2,1)S(1)}, u32[]{:S(2)}, u32[]{:S(2)}) collective-permute-start(bf16[128,1024]{1,0:T(8,128)(2,1)S(1)} %get-tuple-element.378), channel_id=1, source_target_pairs={{0,4},{1,5},{2,6},{3,7},{4,8},{5,9},{6,10},{7,11},{8,12},{9,13},{1... | collective-permute-start | bytes 786440 | tf_op jit(solution)/shard_map/ppermute | solution.py:439
  699.1 32.5 %collective-permute-start.61 = (bf16[128,1024]{1,0:T(8,128)(2,1)S(1)}, bf16[128,1024]{1,0:T(8,128)(2,1)S(1)}, u32[]{:S(2)}, u32[]{:S(2)}) collective-permute-start(bf16[128,1024]{1,0:T(8,128)(2,1)S(1)} %get-tuple-element.379), channel_id=1, source_target_pairs={{0,8},{1,9},{2,10},{3,11},{4,12},{5,13},{6,14},{7,15},{8,0},{9,1},... | collective-permute-start | bytes 786440 | tf_op jit(solution)/shard_map/ppermute | solution.py:439
  710.3 27.9 %collective-permute-start.62 = (bf16[128,1024]{1,0:T(8,128)(2,1)S(1)}, bf16[128,1024]{1,0:T(8,128)(2,1)S(1)}, u32[]{:S(2)}, u32[]{:S(2)}) collective-permute-start(bf16[128,1024]{1,0:T(8,128)(2,1)S(1)} %get-tuple-element.380), channel_id=1, source_target_pairs={{0,12},{1,13},{2,14},{3,15},{4,0},{5,1},{6,2},{7,3},{8,4},{9,5},{1... | collective-permute-start | bytes 786440 | tf_op jit(solution)/shard_map/ppermute | solution.py:439
  717.8 23.2 %collective-permute-start.56 = (bf16[96,1024]{1,0:T(8,128)(2,1)S(1)}, bf16[96,1024]{1,0:T(8,128)(2,1)S(1)}, u32[]{:S(2)}, u32[]{:S(2)}) collective-permute-start(bf16[96,1024]{1,0:T(8,128)(2,1)S(1)} %get-tuple-element.392), channel_id=1, source_target_pairs={{0,4},{1,5},{2,6},{3,7},{4,8},{5,9},{6,10},{7,11},{8,12},{9,13},{1... | collective-permute-start | bytes 589832 | tf_op jit(solution)/shard_map/ppermute | solution.py:439
  720.3 19.5 %collective-permute-start.59 = (bf16[128,1024]{1,0:T(8,128)(2,1)S(1)}, bf16[128,1024]{1,0:T(8,128)(2,1)S(1)}, u32[]{:S(2)}, u32[]{:S(2)}) collective-permute-start(bf16[128,1024]{1,0:T(8,128)(2,1)S(1)} %get-tuple-element.400), channel_id=1, source_target_pairs={{0,16},{16,0},{1,17},{17,1},{2,18},{18,2},{3,19},{19,3},{4,20},{20... | collective-permute-start | bytes 786440 | tf_op jit(solution)/shard_map/ppermute | solution.py:387
  722.8 18.6 %collective-permute-start.57 = (bf16[96,1024]{1,0:T(8,128)(2,1)S(1)}, bf16[96,1024]{1,0:T(8,128)(2,1)S(1)}, u32[]{:S(2)}, u32[]{:S(2)}) collective-permute-start(bf16[96,1024]{1,0:T(8,128)(2,1)S(1)} %get-tuple-element.393), channel_id=1, source_target_pairs={{0,8},{1,9},{2,10},{3,11},{4,12},{5,13},{6,14},{7,15},{8,0},{9,1},... | collective-permute-start | bytes 589832 | tf_op jit(solution)/shard_map/ppermute | solution.py:439
  731.5 10.7 %collective-permute-start.58 = (bf16[96,1024]{1,0:T(8,128)(2,1)S(1)}, bf16[96,1024]{1,0:T(8,128)(2,1)S(1)}, u32[]{:S(2)}, u32[]{:S(2)}) collective-permute-start(bf16[96,1024]{1,0:T(8,128)(2,1)S(1)} %get-tuple-element.394), channel_id=1, source_target_pairs={{0,12},{1,13},{2,14},{3,15},{4,0},{5,1},{6,2},{7,3},{8,4},{9,5},{1... | collective-permute-start | bytes 589832 | tf_op jit(solution)/shard_map/ppermute | solution.py:439
  738.3 8.5 %collective-permute-start.64 = (bf16[128,1024]{1,0:T(8,128)(2,1)S(1)}, bf16[128,1024]{1,0:T(8,128)(2,1)S(1)}, u32[]{:S(2)}, u32[]{:S(2)}) collective-permute-start(bf16[128,1024]{1,0:T(8,128)(2,1)S(1)} %get-tuple-element.408), channel_id=1, source_target_pairs={{0,16},{16,0},{1,17},{17,1},{2,18},{18,2},{3,19},{19,3},{4,20},{20... | collective-permute-start | bytes 786440 | tf_op jit(solution)/shard_map/ppermute | solution.py:387
  (155 other events, 1099.8 us)
Sparse Core Ops, SparseCore 0:
  16.9 111.9 all-gather.4
  131.0 110.2 all-gather.6

commit v3 on v2

v3 whole, which is shorter than its diff:
```python
import functools
import math

import jax
import jax.numpy as jnp
from jax import lax
from jax.experimental import pallas as pl
from jax.experimental.pallas import tpu as pltpu
from jax.sharding import PartitionSpec as P

EPS = 1e-06
DECAY_SCALE = 8.0
ROOT_FLOOR = 0.001
GELU_K = math.sqrt(2.0 / math.pi)
GELU_C = 0.044715
ROWS = 16
VMEM = 44 << 20
LESS = 24 << 20
SMALL = pl.CostEstimate(flops=1024, bytes_accessed=1024, transcendentals=0)
BF16 = jnp.bfloat16
F32 = jnp.float32


def sent(shape):
    return pltpu.HBM(shape, BF16)


def matmul(left, right):
    return jnp.dot(left, right, preferred_element_type=F32)


def rows_product(left, right):
    return lax.dot_general(left, right, (((0,), (0,)), ((), ())), preferred_element_type=F32)


def cols_product(left, right):
    return lax.dot_general(left, right, (((1,), (1,)), ((), ())), preferred_element_type=F32)


def widen(value):
    return value.astype(F32)


def gelu(v):
    return 0.5 * v * (1.0 + jnp.tanh(GELU_K * (v + GELU_C * v * v * v)))


def gelu_slope(v):
    t = jnp.tanh(GELU_K * (v + GELU_C * v * v * v))
    return 0.5 * (1.0 + t) + 0.5 * v * (1.0 - t * t) * GELU_K * (1.0 + 3.0 * GELU_C * v * v)


def forward_kernel(pre_ref, gates_r_ref, gates_i_ref, admitted_ref, params_ref, mixed_ref, before_ref):
    width = pre_ref.shape[1]
    rbias, abias, rate = params_ref[0:1, :], params_ref[1:2, :], params_ref[2:3, :]
    row = lax.broadcasted_iota(jnp.int32, (ROWS, width), 0)

    def step(i, carry):
        at = pl.ds(pl.multiple_of(i * ROWS, ROWS), ROWS)
        gate_r = jax.nn.sigmoid(gates_r_ref[at, :] + rbias)
        gate_i = jax.nn.sigmoid(gates_i_ref[at, :] + abias)
        a = jnp.exp(-(gate_r * rate))
        b = jnp.sqrt(jnp.maximum(1.0 - a * a, ROOT_FLOOR)) * gate_i * widen(admitted_ref[at, :])
        for d in (1, 2, 4, 8):
            keep = row >= d
            b = b + a * jnp.where(keep, pltpu.roll(b, d, 0), 0.0)
            a = a * jnp.where(keep, pltpu.roll(a, d, 0), 1.0)
        state = b + a * carry
        before_ref[at, :] = jnp.where(row >= 1, pltpu.roll(state, 1, 0), carry)
        mixed_ref[at, :] = (state * gelu(pre_ref[at, :])).astype(BF16)
        return jnp.broadcast_to(state[ROWS - 1 : ROWS, :], (ROWS, width))

    lax.fori_loop(0, pre_ref.shape[0] // ROWS, step, jnp.zeros((ROWS, width), F32))


def chain_kernel(
    side_ref, own_ref, other_ref, out_a_ref, out_b_ref, out_c_ref, recur_w_ref, admit_w_ref, pre_ref, gates_r_ref, gates_i_ref, admitted_ref,
    before_ref, params_ref, branch_ref, gates_cot_ref, direct_ref, sums_ref, near_ref, far_ref, cot_ref, sum_ref,
):
    length = own_ref.shape[0]
    width = pre_ref.shape[1]
    out_w = jnp.concatenate([joined(out_a_ref), joined(out_b_ref), joined(out_c_ref)], axis=1)
    cot_ref[:length, :] = cols_product(own_ref[...], out_w)
    cot_ref[length:, :] = cols_product(other_ref[...], out_w)
    rbias, abias, rate = params_ref[0:1, :], params_ref[1:2, :], params_ref[2:3, :]
    row = lax.broadcasted_iota(jnp.int32, (ROWS, width), 0)
    blocks = length // ROWS
    zero = jnp.zeros((ROWS, width), F32)

    def step(first, i, state):
        carry, sum_r, sum_i, sum_d = state
        at = pl.ds(pl.multiple_of(first + (blocks - 1 - i) * ROWS, ROWS), ROWS)
        gate_r = jax.nn.sigmoid(gates_r_ref[at, :] + rbias)
        gate_i = jax.nn.sigmoid(gates_i_ref[at, :] + abias)
        admitted = widen(admitted_ref[at, :])
        a = jnp.exp(-(gate_r * rate))
        rest = 1.0 - a * a
        root = jnp.sqrt(jnp.maximum(rest, ROOT_FLOOR))
        before = before_ref[at, :]
        state_now = a * before + root * gate_i * admitted
        pre = pre_ref[at, :]
        cot = cot_ref[at, :]
        branch_ref[at, :] = (cot * state_now * gelu_slope(pre)).astype(BF16)
        own = cot * gelu(pre)
        f = a
        e = a * own
        for d in (1, 2, 4, 8):
            keep = row < ROWS - d
            e = e + f * jnp.where(keep, pltpu.roll(e, ROWS - d, 0), 0.0)
            f = f * jnp.where(keep, pltpu.roll(f, ROWS - d, 0), 1.0)
        e = e + f * carry
        g = own + jnp.where(row < ROWS - 1, pltpu.roll(e, ROWS - 1, 0), carry)
        direct_ref[at, :] = g * root * gate_i
        share = jnp.where(rest > ROOT_FLOOR, 1.0, jnp.where(rest == ROOT_FLOOR, 0.5, 0.0))
        d_log = a * (g * before - g * gate_i * admitted * (share * a / root))
        recur = -(d_log * rate) * gate_r * (1.0 - gate_r)
        admit = g * root * admitted * gate_i * (1.0 - gate_i)
        gates_cot_ref[0, at, :] = recur.astype(BF16)
        gates_cot_ref[1, at, :] = admit.astype(BF16)
        carry = jnp.broadcast_to(e[0:1, :], (ROWS, width))
        return carry, sum_r + recur, sum_i + admit, sum_d + d_log * gate_r

    sums = (zero, zero, zero)
    for first in (0, length):
        _, *sums = lax.fori_loop(0, blocks, functools.partial(step, first), (zero, *sums))
    for i in range(3):
        sums_ref[i * ROWS : (i + 1) * ROWS, :] = sums[i]
    depth = sum_ref.shape[1]
    part = cols_product(gates_cot_ref[0], joined(recur_w_ref)) + cols_product(gates_cot_ref[1], joined(admit_w_ref))

    @pl.when(pl.program_id(0) == 0)
    def _():
        sum_ref[...] = part

    @pl.when(pl.program_id(0) > 0)
    def _():
        sum_ref[...] += part

    half = depth // 2
    for side in range(2):
        @pl.when((pl.program_id(0) == pl.num_programs(0) - 1) & (side_ref[0] == side))
        def _(side=side):
            near_ref[...] = sum_ref[:, side * half : (side + 1) * half]
            away = slice((1 - side) * half, (2 - side) * half)
            far_ref[:length, :] = sum_ref[length:, away].astype(BF16)
            far_ref[length:, :] = sum_ref[:length, away].astype(BF16)


def chain_back(side, own, other, whole, at, rows, pre, gates, admitted, before, params):
    length, depth = own.shape
    tokens, width = admitted.shape
    shards, _, tile = whole.shape
    n = width // tile
    at = at // rows
    low = jax.ShapeDtypeStruct((tokens, width), BF16)
    full = pl.BlockSpec((length, depth), lambda j, s: (0, 0))
    near = pl.BlockSpec((tokens, tile), lambda j, s: (0, j))
    fixed = pl.BlockSpec((tokens, width), lambda j, s: (0, 0))
    return pl.pallas_call(
        chain_kernel,
        grid_spec=pltpu.PrefetchScalarGridSpec(
            num_scalar_prefetch=1,
            grid=(n,),
            in_specs=[
                full, full,
                *[
                    pl.BlockSpec((tile // rows, rows, tile), lambda j, s, k=k: (s[0] * n + j, at + 2 * n + k, 0))
                    for k in range(3)
                ],
                pl.BlockSpec((shards, rows, tile), lambda j, s: (0, at + j, 0)),
                pl.BlockSpec((shards, rows, tile), lambda j, s: (0, at + n + j, 0)),
                near, near,
                pl.BlockSpec((tokens, tile), lambda j, s: (0, j + n)),
                near, near,
                pl.BlockSpec((8, tile), lambda j, s: (0, j)),
            ],
            out_specs=[
                near, pl.BlockSpec((2, tokens, tile), lambda j, s: (0, 0, j)), near,
                pl.BlockSpec((3 * ROWS, tile), lambda j, s: (0, j)), fixed, fixed,
            ],
            scratch_shapes=[pltpu.VMEM((tokens, tile), F32), pltpu.VMEM((tokens, 2 * width), F32)],
        ),
        out_shape=[
            low, jax.ShapeDtypeStruct((2, tokens, width), BF16), jax.ShapeDtypeStruct((tokens, width), F32),
            jax.ShapeDtypeStruct((3 * ROWS, width), F32), jax.ShapeDtypeStruct((tokens, width), F32), sent((tokens, width)),
        ],
        compiler_params=pltpu.CompilerParams(vmem_limit_bytes=VMEM),
        cost_estimate=pl.CostEstimate(flops=660000000000, bytes_accessed=1024, transcendentals=0),
        name="chain_back",
    )(side, own, other, *[whole] * 5, pre, gates, gates, admitted, before, params)


def conv_kernel(
    direct_ref, near_in_ref, far_in_ref, lru_ref, branch_ref, taps_ref, branch_w_ref, lruin_w_ref,
    pre_cot_ref, sums_ref, near_ref, far_ref, sum_ref,
):
    tokens, width = direct_ref.shape
    length = tokens // 2
    cot = direct_ref[...] + near_in_ref[...] + widen(far_in_ref[...])
    lru = lru_ref[...]
    token = lax.broadcasted_iota(jnp.int32, (tokens, width), 0)
    token = jnp.where(token >= length, token - length, token)
    total = jnp.zeros_like(cot)
    count = 4
    for k in range(count):
        later = cot if k == 0 else jnp.where(token < length - k, pltpu.roll(cot, tokens - k, 0), 0.0)
        total = total + taps_ref[k : k + 1, :] * later
        sums_ref[k : k + 1, :] = jnp.sum(later * lru, axis=0, keepdims=True)
    sums_ref[count : count + 1, :] = jnp.sum(cot, axis=0, keepdims=True)
    low = total.astype(BF16)
    pre_cot_ref[0] = branch_ref[...]
    pre_cot_ref[1] = low
    part = cols_product(branch_ref[...], joined(branch_w_ref)) + cols_product(low, joined(lruin_w_ref))

    @pl.when(pl.program_id(0) == 0)
    def _():
        sum_ref[...] = part

    @pl.when(pl.program_id(0) > 0)
    def _():
        sum_ref[...] += part

    @pl.when(pl.program_id(0) == pl.num_programs(0) - 1)
    def _():
        near_ref[...] = sum_ref[:length, :]
        far_ref[...] = sum_ref[length:, :].astype(BF16)


def conv_back(direct, near, far, pre, branch, taps, whole, rows, depth):
    tokens, width = direct.shape
    shards, _, tile = whole.shape
    n = width // tile
    one = pl.BlockSpec((tokens, tile), lambda j: (0, j))
    half = pl.BlockSpec((tokens // 2, depth), lambda j: (0, 0))
    return pl.pallas_call(
        conv_kernel,
        grid=(n,),
        in_specs=[
            one, one, one, pl.BlockSpec((tokens, tile), lambda j: (0, j + n)), one,
            pl.BlockSpec((8, tile), lambda j: (0, j)),
            pl.BlockSpec((shards, rows, tile), lambda j: (0, j, 0)),
            pl.BlockSpec((shards, rows, tile), lambda j: (0, n + j, 0)),
        ],
        out_specs=[
            pl.BlockSpec((2, tokens, tile), lambda j: (0, 0, j)), pl.BlockSpec((8, tile), lambda j: (0, j)), half, half,
        ],
        out_shape=[
            jax.ShapeDtypeStruct((2, tokens, width), BF16), jax.ShapeDtypeStruct((8, width), F32),
            jax.ShapeDtypeStruct((tokens // 2, depth), F32), sent((tokens // 2, depth)),
        ],
        scratch_shapes=[pltpu.VMEM((tokens, depth), F32)],
        compiler_params=pltpu.CompilerParams(vmem_limit_bytes=VMEM),
        cost_estimate=pl.CostEstimate(flops=300000000000, bytes_accessed=1024, transcendentals=0),
        name="conv_back",
    )(direct, near, far, pre, branch, taps, whole, whole)


def norm_kernel(near_ref, far_ref, base_ref, v_ref, gain_ref, out_ref, low_ref):
    v = widen(v_ref[...])
    scale = lax.rsqrt(jnp.mean(v * v, axis=-1, keepdims=True) + EPS)
    g = (near_ref[...] + widen(far_ref[...])) * gain_ref[0:1, :]
    out = widen(base_ref[...]) + scale * (g - v * (scale * scale * jnp.mean(g * v, axis=-1, keepdims=True)))
    out_ref[...] = out
    low_ref[...] = out.astype(BF16)


def norm_back(near, far, base, v, gain):
    rows, width = near.shape
    tile = rows // 4
    one = pl.BlockSpec((tile, width), lambda j: (j, 0))
    return pl.pallas_call(
        norm_kernel,
        grid=(rows // tile,),
        in_specs=[one, one, one, one, pl.BlockSpec((8, width), lambda j: (0, 0))],
        out_specs=[one, one],
        out_shape=[jax.ShapeDtypeStruct((rows, width), F32), sent((rows, width))],
        compiler_params=pltpu.CompilerParams(vmem_limit_bytes=LESS),
        cost_estimate=pl.CostEstimate(flops=150000000000, bytes_accessed=1024, transcendentals=0),
        name="norm_back",
    )(near, far, base, v, jnp.broadcast_to(gain, (8, width)))


def flip_kernel(x_ref, out_ref):
    out_ref[...] = widen(x_ref[...]).T.astype(BF16)


def flip(x):
    tokens, n = x.shape
    tile = 256
    return pl.pallas_call(
        flip_kernel,
        grid=(n // tile,),
        in_specs=[pl.BlockSpec((tokens, tile), lambda j: (0, j))],
        out_specs=pl.BlockSpec((tile, tokens), lambda j: (j, 0)),
        out_shape=jax.ShapeDtypeStruct((n, tokens), BF16),
        compiler_params=pltpu.CompilerParams(vmem_limit_bytes=LESS),
        cost_estimate=pl.CostEstimate(flops=150000000000, bytes_accessed=1024, transcendentals=0),
        name="flip",
    )(x)


def pack_kernel(block, side_ref, *refs):
    out_ref, at = refs[-1], 0
    for ref in refs[:-1]:
        rows, n = ref.shape
        for first in range(0, n, block):
            out_ref[at : at + rows, :] = ref[:, first : first + block]
            at += rows


def pack(side, halves, full, block):
    specs = [pl.BlockSpec((p.shape[0], p.shape[1] // 2), lambda j, s: (0, s[0])) for p in halves]
    specs.append(pl.BlockSpec(full.shape, lambda j, s: (0, 0)))
    size = sum(p.shape[0] * p.shape[1] // 2 for p in halves) + full.size
    return pl.pallas_call(
        functools.partial(pack_kernel, block),
        grid_spec=pltpu.PrefetchScalarGridSpec(
            num_scalar_prefetch=1, grid=(1,), in_specs=specs,
            out_specs=pl.BlockSpec((size // block, block), lambda j, s: (0, 0)),
        ),
        out_shape=jax.ShapeDtypeStruct((size // block, block), BF16),
        compiler_params=pltpu.CompilerParams(vmem_limit_bytes=LESS),
        cost_estimate=pl.CostEstimate(flops=30000000000, bytes_accessed=1024, transcendentals=0),
        name="pack",
    )(side, *halves, full)


def columns_kernel(parts, side_ref, own_ref, got_ref, *out_refs):
    n = out_refs[0].shape[1]
    mine = pl.program_id(0) == side_ref[0]

    @pl.when(mine)
    def _():
        for i in range(parts):
            out_refs[i][...] = own_ref[:, i * n : (i + 1) * n]

    @pl.when(jnp.logical_not(mine))
    def _():
        for i in range(parts):
            out_refs[i][...] = widen(got_ref[:, i * n : (i + 1) * n])


def join_columns(side, own, got, parts):
    rows, n = own.shape[0], own.shape[1] // parts
    full = pl.BlockSpec(own.shape, lambda h, s: (0, 0))
    return pl.pallas_call(
        functools.partial(columns_kernel, parts),
        grid_spec=pltpu.PrefetchScalarGridSpec(
            num_scalar_prefetch=1, grid=(2,), in_specs=[full, full],
            out_specs=[pl.BlockSpec((rows, n), lambda h, s: (0, h))] * parts,
        ),
        out_shape=[jax.ShapeDtypeStruct((rows, 2 * n), F32)] * parts,
        compiler_params=pltpu.CompilerParams(vmem_limit_bytes=LESS),
        cost_estimate=pl.CostEstimate(flops=36000000000, bytes_accessed=1024, transcendentals=0),
        name="join_columns",
    )(side, own, got)


def rows_kernel(side_ref, own_a_ref, own_b_ref, got_a_ref, got_b_ref, out_ref):
    n = own_a_ref.shape[1]
    mine = pl.program_id(0) == side_ref[0]

    @pl.when(mine)
    def _():
        out_ref[:, :n] = own_a_ref[...]
        out_ref[:, n:] = own_b_ref[...]

    @pl.when(jnp.logical_not(mine))
    def _():
        out_ref[:, :n] = widen(got_a_ref[...])
        out_ref[:, n:] = widen(got_b_ref[...])


def join_rows(side, a, b):
    rows, n = a[0].shape
    full = pl.BlockSpec((rows, n), lambda h, s: (0, 0))
    return pl.pallas_call(
        rows_kernel,
        grid_spec=pltpu.PrefetchScalarGridSpec(
            num_scalar_prefetch=1, grid=(2,), in_specs=[full] * 4,
            out_specs=pl.BlockSpec((rows, 2 * n), lambda h, s: (h, 0)),
        ),
        out_shape=jax.ShapeDtypeStruct((2 * rows, 2 * n), F32),
        compiler_params=pltpu.CompilerParams(vmem_limit_bytes=LESS),
        cost_estimate=pl.CostEstimate(flops=36000000000, bytes_accessed=1024, transcendentals=0),
        name="join_rows",
    )(side, a[0], b[0], a[1], b[1])


def weave_kernel(piece, side_ref, own_ref, got_ref, out_ref):
    for side in range(2):
        @pl.when(side_ref[0] == side)
        def _(side=side):
            parts = []
            for at in range(0, own_ref.shape[1], piece):
                own = own_ref[:, at : at + piece]
                got = widen(got_ref[:, at : at + piece])
                parts += [got, own] if side else [own, got]
            out_ref[...] = jnp.concatenate(parts, axis=1)


def weave(side, own, got, piece):
    rows, n = own.shape
    return pl.pallas_call(
        functools.partial(weave_kernel, piece),
        grid_spec=pltpu.PrefetchScalarGridSpec(
            num_scalar_prefetch=1, grid=(1,),
            in_specs=[pl.BlockSpec((rows, n), lambda h, s: (0, 0))] * 2,
            out_specs=pl.BlockSpec((rows, 2 * n), lambda h, s: (0, 0)),
        ),
        out_shape=jax.ShapeDtypeStruct((rows, 2 * n), F32),
        compiler_params=pltpu.CompilerParams(vmem_limit_bytes=LESS),
        cost_estimate=pl.CostEstimate(flops=90000000000, bytes_accessed=1024, transcendentals=0),
        name="weave",
    )(side, own, got)


def recurrence_forward(pre, gates, admitted, params, length):
    tokens, width = admitted.shape
    tile = math.gcd(width, 512)
    n = width // tile
    near = pl.BlockSpec((length, tile), lambda s, j: (s, j))
    far = pl.BlockSpec((length, tile), lambda s, j: (s, j + n))
    vector = pl.BlockSpec((8, tile), lambda s, j: (0, j))
    return pl.pallas_call(
        forward_kernel,
        grid=(tokens // length, n),
        in_specs=[near, near, far, near, vector],
        out_specs=[near, near],
        out_shape=[
            jax.ShapeDtypeStruct((tokens, width), BF16),
            jax.ShapeDtypeStruct((tokens, width), F32),
        ],
        cost_estimate=pl.CostEstimate(flops=60 * tokens * width, bytes_accessed=20 * tokens * width, transcendentals=6 * tokens * width),
        name="recurrence_forward",
    )(pre, gates, gates, admitted, params)


def hidden_kernel(x_ref, gate_ref, up_ref, hidden_ref, flipped_ref, act_ref, slope_ref):
    x = x_ref[...]
    gate = matmul(x, joined(gate_ref))
    up = matmul(x, joined(up_ref))
    t = jnp.tanh(GELU_K * (gate + GELU_C * gate * gate * gate))
    act = 0.5 * gate * (1.0 + t)
    slope = 0.5 * (1.0 + t) + 0.5 * gate * (1.0 - t * t) * GELU_K * (1.0 + 3.0 * GELU_C * gate * gate)
    hidden = act * up
    hidden_ref[...] = hidden.astype(BF16)
    flipped_ref[...] = hidden.T.astype(BF16)
    act_ref[...] = act
    slope_ref[...] = up * slope


def hidden_pass(x, blocks, rows, tiles):
    tokens, depth = x.shape
    shards, _, tile = blocks.shape
    n = tiles * tile
    wide = pl.BlockSpec((tokens, tile), lambda j: (0, j))
    return pl.pallas_call(
        hidden_kernel,
        grid=(tiles,),
        in_specs=[
            pl.BlockSpec((tokens, depth), lambda j: (0, 0)),
            pl.BlockSpec((shards, rows, tile), lambda j: (0, j, 0)),
            pl.BlockSpec((shards, rows, tile), lambda j: (0, j + tiles, 0)),
        ],
        out_specs=[wide, pl.BlockSpec((tile, tokens), lambda j: (j, 0)), wide, wide],
        out_shape=[
            jax.ShapeDtypeStruct((tokens, n), BF16), jax.ShapeDtypeStruct((n, tokens), BF16),
            jax.ShapeDtypeStruct((tokens, n), F32), jax.ShapeDtypeStruct((tokens, n), F32),
        ],
        compiler_params=pltpu.CompilerParams(vmem_limit_bytes=VMEM),
        cost_estimate=pl.CostEstimate(flops=420000000000, bytes_accessed=1024, transcendentals=0),
        name="hidden_pass",
    )(x, blocks, blocks)


def halves(sum_ref, part, near_ref, far_ref):
    @pl.when(pl.program_id(0) == 0)
    def _():
        sum_ref[...] = part

    @pl.when(pl.program_id(0) > 0)
    def _():
        sum_ref[...] += part

    @pl.when(pl.program_id(0) == pl.num_programs(0) - 1)
    def _():
        half = near_ref.shape[0]
        near_ref[...] = sum_ref[:half, :]
        far_ref[...] = sum_ref[half:, :].astype(BF16)


def take_tile(down_a_ref, down_b_ref, down_ref):
    rows, n = down_ref.shape[0], down_a_ref.shape[2]
    for j in range(shape_rows(down_a_ref) // rows):
        @pl.when(pl.program_id(0) == j)
        def _(j=j):
            down_ref[:, :n] = joined(down_a_ref)[j * rows : (j + 1) * rows]
            down_ref[:, n:] = joined(down_b_ref)[j * rows : (j + 1) * rows]


def shape_rows(ref):
    return ref.shape[0] * ref.shape[1]


def ffn_back_kernel(
    cot_ref, gate_ref, up_ref, down_a_ref, down_b_ref, act_ref, slope_ref,
    gate_cot_ref, up_cot_ref, near_ref, far_ref, sum_ref, down_ref,
):
    take_tile(down_a_ref, down_b_ref, down_ref)
    cot = cols_product(cot_ref[...], down_ref[...])
    gate_cot = (cot * slope_ref[...]).astype(BF16)
    up_cot = (cot * act_ref[...]).astype(BF16)
    gate_cot_ref[...] = gate_cot
    up_cot_ref[...] = up_cot
    halves(sum_ref, cols_product(gate_cot, joined(gate_ref)) + cols_product(up_cot, joined(up_ref)), near_ref, far_ref)


def down_specs(blocks, rows, tiles, piece):
    shards, _, tile = blocks.shape
    at = 2 * tiles * rows // piece
    return [pl.BlockSpec((shards, piece, tile), lambda j, k=k: (0, at + k, 0), pipeline_mode=pl.Buffered(1)) for k in range(2)]


def ffn_back(cot, blocks, act, slope, rows, tiles, piece):
    tokens, depth = cot.shape
    shards, _, tile = blocks.shape
    low = jax.ShapeDtypeStruct((tokens, tiles * tile), BF16)
    wide = pl.BlockSpec((tokens, tile), lambda j: (0, j))
    half = pl.BlockSpec((tokens // 2, depth), lambda j: (0, 0))
    return pl.pallas_call(
        ffn_back_kernel,
        grid=(tiles,),
        in_specs=[
            pl.BlockSpec((tokens, depth), lambda j: (0, 0)),
            pl.BlockSpec((shards, rows, tile), lambda j: (0, j, 0)),
            pl.BlockSpec((shards, rows, tile), lambda j: (0, j + tiles, 0)),
            *down_specs(blocks, rows, tiles, piece),
            wide, wide,
        ],
        out_specs=[wide, wide, half, half],
        out_shape=[
            low, low,
            jax.ShapeDtypeStruct((tokens // 2, depth), F32), sent((tokens // 2, depth)),
        ],
        scratch_shapes=[pltpu.VMEM((tokens, depth), F32), pltpu.VMEM((tile, depth), BF16)],
        compiler_params=pltpu.CompilerParams(vmem_limit_bytes=VMEM),
        cost_estimate=pl.CostEstimate(flops=690000000000, bytes_accessed=1024, transcendentals=0),
        name="ffn_back",
    )(cot, blocks, blocks, blocks, blocks, act, slope)


def down_kernel(hidden_ref, down_a_ref, down_b_ref, near_ref, far_ref, sum_ref, down_ref):
    take_tile(down_a_ref, down_b_ref, down_ref)
    halves(sum_ref, matmul(hidden_ref[...], down_ref[...]), near_ref, far_ref)


def down_pass(hidden, blocks, depth, rows, tiles, piece):
    tokens, n = hidden.shape
    half = pl.BlockSpec((tokens // 2, depth), lambda j: (0, 0))
    return pl.pallas_call(
        down_kernel,
        grid=(tiles,),
        in_specs=[pl.BlockSpec((tokens, n // tiles), lambda j: (0, j)), *down_specs(blocks, rows, tiles, piece)],
        out_specs=[half, half],
        out_shape=[
            jax.ShapeDtypeStruct((tokens // 2, depth), F32), sent((tokens // 2, depth)),
        ],
        scratch_shapes=[pltpu.VMEM((tokens, depth), F32), pltpu.VMEM((n // tiles, depth), BF16)],
        compiler_params=pltpu.CompilerParams(vmem_limit_bytes=VMEM),
        cost_estimate=pl.CostEstimate(flops=270000000000, bytes_accessed=1024, transcendentals=0),
        name="down_pass",
    )(hidden, blocks, blocks)


def joined(ref):
    v = ref[...]
    if v.shape[1] % 16:
        return widen(v).reshape(-1, v.shape[2]).astype(BF16)
    return v.reshape(-1, v.shape[2])


def away_kernel(at_ref, left_ref, right_ref, out_ref):
    out_ref[...] = matmul(joined(left_ref), right_ref[...]).reshape(out_ref.shape).astype(out_ref.dtype)


def home_kernel(bit, at_ref, left_ref, right_ref, got_ref, keep_ref, send_ref, sum_ref):
    v = matmul(joined(left_ref), right_ref[...]).reshape(got_ref.shape) + widen(got_ref[...])
    sum_ref[...] = v.reshape(sum_ref.shape)
    keep_ref[...] = sum_ref[:, at_ref[bit]]
    send_ref[...] = sum_ref[:, 1 - at_ref[bit]].astype(send_ref.dtype)


def column_tile(n, choices=(1024, 768, 512, 256, 128)):
    return max(t for t in choices if n % t == 0)


def tiling(right, columns, skip):
    parts, _, n = right.shape
    tile = column_tile(columns or n)
    each = n // tile

    def index(j, at):
        at_tile = j + (at[0] if skip < 0 else skip)
        return at_tile // each, 0, at_tile % each

    return tile, columns or parts * n, index


def grad_away(left, right, at, columns=0, skip=0):
    owners, _, rows, tokens = left.shape
    tile, n, index = tiling(right, columns, skip)
    return pl.pallas_call(
        away_kernel,
        grid_spec=pltpu.PrefetchScalarGridSpec(
            num_scalar_prefetch=1,
            grid=(n // tile,),
            in_specs=[
                pl.BlockSpec((owners, None, rows, tokens), lambda j, at: (0, 1 - at[1], 0, 0)),
                pl.BlockSpec((None, tokens, tile), index),
            ],
            out_specs=pl.BlockSpec((owners, rows, tile), lambda j, at: (0, 0, j)),
        ),
        out_shape=sent((owners, rows, n)),
        compiler_params=pltpu.CompilerParams(vmem_limit_bytes=LESS),
        cost_estimate=pl.CostEstimate(flops=105000000000, bytes_accessed=1024, transcendentals=0),
        name="grad_away",
    )(at, left, right)


def grad_home(left, right, got, at, bit, low, columns=0, skip=0):
    owners, _, rows, tokens = left.shape
    tile, n, index = tiling(right, columns, skip)
    high = owners // (2 * low)
    half = pl.BlockSpec((high, low, rows, tile), lambda j, at: (0, 0, 0, j))
    return pl.pallas_call(
        functools.partial(home_kernel, bit),
        grid_spec=pltpu.PrefetchScalarGridSpec(
            num_scalar_prefetch=1,
            grid=(n // tile,),
            in_specs=[
                pl.BlockSpec((owners, None, rows, tokens), lambda j, at: (0, at[1], 0, 0)),
                pl.BlockSpec((None, tokens, tile), index),
                pl.BlockSpec((owners, rows, tile), lambda j, at: (0, 0, j)),
            ],
            out_specs=[half, half],
            scratch_shapes=[pltpu.VMEM((high, 2, low, rows, tile), F32)],
        ),
        out_shape=[
            jax.ShapeDtypeStruct((high, low, rows, n), F32), sent((high, low, rows, n)),
        ],
        compiler_params=pltpu.CompilerParams(vmem_limit_bytes=LESS),
        cost_estimate=pl.CostEstimate(flops=165000000000, bytes_accessed=1024, transcendentals=0),
        name="grad_home",
    )(at, left, right, got)


def fold_kernel(bit, at_ref, own_ref, got_ref, keep_ref, send_ref):
    mine, other = at_ref[bit], 1 - at_ref[bit]
    keep_ref[...] = own_ref[:, mine] + widen(got_ref[:, mine])
    send_ref[...] = (own_ref[:, other] + widen(got_ref[:, other])).astype(BF16)


def fold(own, got, at, bit, low):
    rows, n = own.shape[2:]
    high = own.shape[0] * own.shape[1] // (2 * low)
    tile = column_tile(n, (1024, 768, 512, 256, 128))
    both = pl.BlockSpec((high, 2, low, rows, tile), lambda j, at: (0, 0, 0, 0, j))
    half = pl.BlockSpec((high, low, rows, tile), lambda j, at: (0, 0, 0, j))
    shape = (high, 2, low, rows, n)
    return pl.pallas_call(
        functools.partial(fold_kernel, bit),
        grid_spec=pltpu.PrefetchScalarGridSpec(
            num_scalar_prefetch=1, grid=(n // tile,), in_specs=[both, both], out_specs=[half, half]
        ),
        out_shape=[
            jax.ShapeDtypeStruct((high, low, rows, n), F32), sent((high, low, rows, n)),
        ],
        compiler_params=pltpu.CompilerParams(vmem_limit_bytes=LESS),
        cost_estimate=pl.CostEstimate(flops=75000000000, bytes_accessed=1024, transcendentals=0),
        name="fold",
    )(at, own.reshape(shape), got.reshape(shape))


def settle_kernel(own_ref, got_ref, out_ref, low_ref):
    v = own_ref[...] + widen(got_ref[...])
    out_ref[...] = v
    low_ref[...] = v.astype(BF16)


def settle(own, got):
    rows, n = own.shape
    tile = column_tile(n, (1024, 768, 512, 256, 128))
    one = pl.BlockSpec((rows, tile), lambda j: (0, j))
    return pl.pallas_call(
        settle_kernel,
        grid=(n // tile,),
        in_specs=[one, one],
        out_specs=[one, one],
        out_shape=[jax.ShapeDtypeStruct((rows, n), F32), sent((rows, n))],
        compiler_params=pltpu.CompilerParams(vmem_limit_bytes=LESS),
        cost_estimate=pl.CostEstimate(flops=45000000000, bytes_accessed=1024, transcendentals=0),
        name="settle",
    )(own, got)


def shifted(values, offset):
    if offset == 0:
        return values
    if offset > 0:
        return jnp.pad(values, ((0, 0), (offset, 0), (0, 0)))[:, : values.shape[1]]
    return jnp.pad(values, ((0, 0), (0, -offset), (0, 0)))[:, -offset:]


def body(
    groups, shards,
    tokens, cotangent, mix_gain, branch_proj, lruin_proj, conv_kernel, conv_bias, recur_proj, recur_bias,
    admit_proj, admit_bias, decay_param, out_proj, ffn_gain, ffn_gate, ffn_up, ffn_down,
):
    cores, bits = 2, shards.bit_length() - 1
    side = lax.axis_index("rep") % 2
    here = lax.axis_index("shard")
    taps = conv_kernel.shape[0]
    length, width = tokens.shape
    low_r = branch_proj.shape[1]
    half_r = low_r // 2
    half_f = ffn_gate.shape[1] // 2
    piece_f = half_f // shards

    def swap(v):
        return lax.ppermute(v, "rep", [(i, i ^ 1) for i in range(groups)])

    def swap_rows(v):
        v = swap(v)
        return jnp.concatenate([v[length:], v[:length]], axis=0)

    def mine(v, size, axis):
        return lax.dynamic_slice_in_dim(v, side * size, size, axis)

    def theirs(v, size, axis):
        return lax.dynamic_slice_in_dim(v, (1 - side) * size, size, axis)

    def natural(own, other):
        first = jnp.where(side == 0, own, other)
        second = jnp.where(side == 0, other, own)
        return jnp.concatenate([first, second], axis=-1)

    def with_pair(own):
        return jnp.concatenate([own, swap(own)], axis=0)

    clock = []

    def tick(*xs):
        return lax.optimization_barrier(tuple(xs) + tuple(clock))[: len(xs)]

    def tock(*ys):
        clock[:] = ys

    place = jnp.stack([side] + [(here >> i) & 1 for i in range(bits)]).astype(jnp.int32)
    here_side = place[:1]

    def cross(v, bit):
        return lax.ppermute(v, "shard", [(i, i ^ (1 << bit)) for i in range(shards)])

    class Scatter:
        def __init__(self, left, right, order=None, columns=0, skip=0):
            self.right, = tick(right if right.ndim == 3 else right[None])
            self.left = left.reshape(shards // cores, cores, left.shape[0] // shards, left.shape[1])
            self.order = list(order or range(1, bits))
            self.span = dict(columns=columns, skip=skip)
            send = grad_away(self.left, self.right, place, **self.span)
            tock(send)
            self.got = cross(send, 0)

        def next(self):
            bit, rest = self.order[0], self.order[1:]
            self.order = rest
            return bit, 2 ** sum(other < bit for other in rest)

        def home(self):
            right, got = tick(self.right, self.got)
            bit, low = self.next()
            self.v, send = grad_home(self.left, right, got, place, bit + 1, low, **self.span)
            tock(self.v, send)
            self.got = cross(send, bit)

        def fold(self):
            v, got = tick(self.v, self.got)
            bit, low = self.next()
            self.v, send = fold(v, got, place, bit + 1, low)
            tock(self.v, send)
            self.got = cross(send, bit)

        def two(self):
            while len(self.order) > 1:
                self.fold()

        def settle(self):
            v, got = tick(self.v, self.got)
            v, send = settle(v.reshape(v.shape[2:]), got.reshape(got.shape[2:]))
            tock(v, send)
            if groups > 2:
                total = v
                for k in range(1, groups // 2):
                    total = total + lax.ppermute(v, "rep", [(i, (i + 2 * k) % groups) for i in range(groups)])
                v, send = total, total.astype(BF16)
            self.v, self.got = v, swap(send)

        def both(self):
            return tick(self.v, self.got)

    class SmallScatter:
        def __init__(self, v):
            self.v = v

        def start(self, bit):
            v = self.v.reshape((-1, 2) + self.v.shape[1:]) if bit < bits else self.v
            if bit == bits:
                for k in range(1, groups // 2):
                    self.v = self.v + lax.ppermute(v, "rep", [(i, (i + 2 * k) % groups) for i in range(groups)])
                self.got = swap(self.v)
                return
            self.v = lax.dynamic_index_in_dim(v, (here >> bit) & 1, 1, False)
            self.got = cross(lax.dynamic_index_in_dim(v, 1 - ((here >> bit) & 1), 1, False), bit)

        def take(self):
            v, got = tick(self.v, self.got)
            self.v = v + got
            tock(self.v)

    per_d, per_r = mix_gain.shape[0], conv_bias.shape[0]
    vectors = jnp.concatenate(
        [mix_gain, ffn_gain, conv_kernel.reshape(-1), conv_bias, recur_bias, admit_bias, decay_param]
    )
    count = vectors.shape[0]
    vectors = jnp.pad(vectors, (0, -count % 128)).reshape(-1, 128)
    vectors = lax.all_gather(vectors, "shard", axis=0).reshape(shards, -1)[:, :count]
    gain_one = widen(vectors[:, :per_d].reshape(width))
    gain_two = widen(vectors[:, per_d : 2 * per_d].reshape(width))
    channel = vectors[:, 2 * per_d :].reshape(shards, taps + 4, per_r).transpose(1, 0, 2).reshape(taps + 4, low_r)
    channel = widen(mine(channel, half_r, 1))
    taps_half, cbias = channel[:taps], channel[taps]
    rbias, abias, lam = channel[taps + 1], channel[taps + 2], channel[taps + 3]
    rate = DECAY_SCALE * jax.nn.softplus(-lam)
    params = jnp.concatenate([jnp.stack([rbias, abias, rate]), jnp.zeros((5, half_r), F32)])

    def ffn_half(v):
        return lax.dynamic_index_in_dim(v.reshape(v.shape[0], shards, 2, piece_f), side, 2, False).reshape(v.shape[0], half_f)

    def gather_blocks(parts, block):
        rows = [p[:, at : at + block] for p in parts for at in range(0, p.shape[1], block)]
        return lax.all_gather(jnp.concatenate(rows, axis=0), "shard", axis=0)

    def unpack(whole, at, rows, columns):
        block = whole.shape[2]
        cols = [whole[:, at + i * rows : at + (i + 1) * rows].reshape(shards * rows, block) for i in range(columns // block)]
        return jnp.concatenate(cols, axis=1)

    per_f, tiles = 2 * piece_f, 3
    whole = lax.all_gather(
        pack(here_side, [branch_proj, lruin_proj, recur_proj, admit_proj], out_proj, 512), "shard", axis=0
    )
    ffn_blocks = gather_blocks(
        [ffn_half(ffn_gate), ffn_half(ffn_up), mine(ffn_down, piece_f, 0)], half_f // tiles
    )
    cot_pair = with_pair(cotangent)
    values = widen(with_pair(tokens))
    scale_one = lax.rsqrt(jnp.mean(values * values, axis=-1, keepdims=True) + EPS)
    normed = (values * scale_one * gain_one).astype(BF16)
    normed_t = flip(normed)
    tock(normed_t, cot_pair)
    whole, = tick(whole)
    at = low_r // 512 * per_d
    w1 = unpack(whole, 0, per_d, low_r)
    w2 = unpack(whole, at, per_r, low_r)
    w3 = unpack(whole, at + low_r // 512 * per_r, per_r, width)
    pre = matmul(normed, w1)
    lru_pre = pre[:, half_r:].reshape(2, length, half_r)
    conv = cbias
    for k in range(taps):
        conv = conv + taps_half[k] * shifted(lru_pre, k)
    admitted = conv.reshape(2 * length, half_r).astype(BF16)
    admitted_all = natural(admitted, swap_rows(admitted))
    gates = matmul(admitted_all, w2)
    mixed, before = recurrence_forward(pre, gates, admitted, params, length)
    tock(mixed)
    admitted_all, = tick(admitted_all)
    admitted_t = flip(admitted_all)
    tock(admitted_t)
    mixed_other, = tick(swap(mixed[length:]))
    mixed_own = natural(mixed[:length], mixed_other)
    middle = widen(tokens) + matmul(mixed_own, w3)
    scale_two = lax.rsqrt(jnp.mean(middle * middle, axis=-1, keepdims=True) + EPS)
    normed_two = (middle * scale_two * gain_two).astype(BF16)
    tock(normed_two)
    mixed_late, mixed_far = tick(mixed[length:], swap(mixed[:length]))
    mixed_t = flip(jnp.concatenate([mixed_own, natural(mixed_late, mixed_far)], axis=0))
    tock(mixed_t)
    normed_two = jnp.concatenate([normed_two, *tick(swap(normed_two))], axis=0)
    tock(normed_two)
    ffn_blocks, = tick(ffn_blocks)

    ffn = dict(rows=per_d, tiles=tiles)
    hidden, hidden_t, act, slope = hidden_pass(normed_two, ffn_blocks, **ffn)
    tock(hidden, hidden_t)
    down_a = Scatter(hidden_t, cot_pair, columns=width // 2)
    down_b = Scatter(hidden_t, cot_pair, columns=width // 2, skip=1)
    act, = tick(act)
    gate_cot, up_cot, near, far = ffn_back(cot_pair, ffn_blocks, act, slope, piece=piece_f, **ffn)
    tock(near, far)
    far = swap(far)
    down_a.home()
    down_b.home()
    normed_two, = tick(normed_two)
    normed_two_t = flip(normed_two)
    tock(normed_two_t)
    gate_s = Scatter(normed_two_t, gate_cot)
    near, far = tick(near, far)
    middle_cot, middle_low = norm_back(near, far, cotangent, middle, gain_two)
    tock(middle_cot, middle_low)
    middle_other = swap(middle_low)
    gate_s.home()
    down_a.two()
    up_s = Scatter(normed_two_t, up_cot)
    middle_low, middle_other = tick(middle_low, middle_other)
    branch_low, gates_cot, direct, sums, near, far = chain_back(
        here_side, middle_low, middle_other, whole, at, per_r, pre, gates, admitted, before, params
    )
    tock(near, far)
    far = swap(far)
    down_b.two()
    down_a.fold()
    up_s.home()
    down_b.fold()
    near, far = tick(near, far)
    pre_cot, conv_sums, near, far = conv_back(direct, near, far, pre, branch_low, channel, whole, per_d, width)
    tock(near, far, pre_cot)
    far = swap(far)
    down_a.settle()
    down_b.settle()
    gate_s.two()
    near, far = tick(near, far)
    tokens_grad, _ = norm_back(near, far, middle_cot, tokens, gain_one)
    tock(tokens_grad)
    gates_s = Scatter(admitted_t, gates_cot, [2, 1] + list(range(3, bits)))
    ffndown_grad = join_rows(here_side, down_a.both(), down_b.both())
    tock(ffndown_grad)
    sums = jnp.sum(sums.reshape(3, ROWS, half_r), axis=1)
    small = jnp.concatenate(
        [conv_sums[: taps + 1], sums[:2], sums[2:] * (DECAY_SCALE * jax.nn.sigmoid(-lam))]
    )
    small = natural(small, jnp.zeros_like(small))
    small_s = SmallScatter(small.reshape(taps + 4, shards, per_r).transpose(1, 0, 2))
    small_s.start(0)
    hidden_late, = tick(hidden)
    near, far = down_pass(hidden_late, ffn_blocks, width, piece=piece_f, **ffn)
    tock(near, far)
    far = swap(far)
    small_s.take()
    gates_s.home()
    pre_s = Scatter(normed_t, pre_cot)
    gate_s.fold()
    near, far = tick(near, far)
    block_out = (middle + near + widen(far)).astype(BF16)
    tock(block_out)
    small_s.start(1)
    up_s.two()
    pre_s.home()
    out_s = Scatter(mixed_t, jnp.concatenate([middle_low, middle_other], axis=0), columns=width // 2, skip=-1)
    gate_s.settle()
    up_s.fold()
    ffngate_grad = weave(here_side, *gate_s.both(), piece_f)
    tock(ffngate_grad)
    small_s.take()
    for bit in range(2, bits - 1):
        small_s.start(bit)
        small_s.take()
    out_s.home()
    gates_s.two()
    small_s.start(bits - 1)
    up_s.settle()
    pre_s.two()
    ffnup_grad = weave(here_side, *up_s.both(), piece_f)
    tock(ffnup_grad)
    small_s.take()
    out_s.two()
    small_s.start(bits)
    ffngain_grad = jnp.sum(ffngate_grad * widen(ffn_gate) + ffnup_grad * widen(ffn_up), axis=1) / widen(ffn_gain)
    pre_s.fold()
    gates_s.fold()
    out_s.fold()
    pre_s.settle()
    small_s.take()
    small = small_s.v.reshape(taps + 4, per_r)
    gates_s.settle()
    branch_grad, lruin_grad = join_columns(here_side, *pre_s.both(), 2)
    tock(branch_grad)
    out_s.settle()
    recur_grad, admit_grad = join_columns(here_side, *gates_s.both(), 2)
    tock(recur_grad)
    outproj_grad, = join_columns(here_side, *out_s.both(), 1)
    mixgain_grad = jnp.sum(branch_grad * widen(branch_proj) + lruin_grad * widen(lruin_proj), axis=1) / widen(mix_gain)
    return (
        block_out, tokens_grad, mixgain_grad, branch_grad, lruin_grad, small[:taps], small[taps], recur_grad,
        small[taps + 1], admit_grad, small[taps + 2], small[taps + 3], outproj_grad, ffngain_grad, ffngate_grad,
        ffnup_grad, ffndown_grad,
    )


def solution(mesh):
    groups, shards = mesh.shape["rep"], mesh.shape["shard"]
    whole = P(("rep", "shard"), None)
    row, vec, col = P("shard", None), P("shard"), P(None, "shard")
    in_specs = (whole, whole, vec, row, row, col, vec, row, vec, row, vec, vec, row, vec, row, row, row)
    out_specs = (whole, whole, vec, row, row, col, vec, row, vec, row, vec, vec, row, vec, row, row, row)
    return jax.shard_map(
        functools.partial(body, groups, shards), mesh=mesh, in_specs=in_specs, out_specs=out_specs, check_vma=False
    )
```

time: 766 us -> 661 us (0.86)
  local copies, waits for them, and re-layouts: 137 us -> 50.8 us
  Pallas kernels: 150 us -> 230 us
  starting transfers between devices: 101 us -> 53.4 us
  other arithmetic: 64.2 us -> 20.8 us
  matrix products: 31.1 us -> 14.2 us
    all_gather x2 -> x1, waiting for transfers between devices: 103 us -> 13.8 us  [gather_blocks(): return lax.all_gather(jnp.concatenate(rows, axis=0), 'shard', axis=0)]
    pallas_call x26 -> x46, Pallas kernels: 116 us -> 196 us  [the longest x14 42 us: fold(): pl.pallas_call(functools.partial(fold_kernel, bit), grid_spec=pltpu.Prefe...]
    all_gather x0 -> x1, waiting for transfers between devices: none -> 64.8 us  [body(): lax.all_gather(pack(here_side, [branch_proj, lruin_proj, recur_proj, admi...]
    ppermute x45 -> x32, starting transfers between devices: 76 us -> 29.9 us  [cross(): return lax.ppermute(v, 'shard', [(i, i ^ 1 << bit) for i in range(shards)])]
    unnamed x328 -> x217, local copies, waits for them, and re-layouts: 67.8 us -> 26.9 us
    ppermute x20 -> x19, waiting for transfers between devices: 48.4 us -> 70.1 us  [swap(): return lax.ppermute(v, 'rep', [(i, i ^ 1) for i in range(groups)])]
    optimization_barrier x8 -> x0, local copies, waits for them, and re-layouts: 20.4 us -> none  [tick(): return lax.optimization_barrier(tuple(xs) + tuple(clock))[:len(xs)]]
    concatenate x7 -> x2, other arithmetic: 17 us -> 1.71 us  [the longest x1 1.57 us: body(): normed_two = jnp.concatenate([normed_two, *tick(swap(normed_two))], axis=0)]
  transfers between devices with their start and end apart: 67 -> 53, of which waited for: 25 -> 21; matrix products, arithmetic and copies ran while one was open for 22% -> 11% of each run, Pallas kernels for 15% -> 33%
where the time goes in v3:
time: 661 us; the launch traced here: 650 us
  waiting for transfers between devices  242 us (37%)
  Pallas kernels  230 us (35%)
  starting transfers between devices  53.4 us (8%)
  local copies, waits for them, and re-layouts  50.8 us (8%)
  blocking collectives  22.7 us (3%)
  other arithmetic  20.8 us (3%)
  between operations  15.5 us (2%)
  matrix products  14.2 us (2%)
    ppermute x32, waiting for transfers between devices, cross(): return lax.ppermute(v, 'shard', [(i, i ^ 1 << bit) for i in range(shards)])  93.5 us
    ppermute x19, waiting for transfers between devices, swap(): return lax.ppermute(v, 'rep', [(i, i ^ 1) for i in range(groups)])  70.1 us
    all_gather x1, waiting for transfers between devices, body(): lax.all_gather(pack(here_side, [branch_proj, lruin_proj, recur_proj, admi...  64.8 us
    pallas_call x14, Pallas kernels, fold(): pl.pallas_call(functools.partial(fold_kernel, bit), grid_spec=pltpu.Prefe...  42 us
    pallas_call x7, Pallas kernels, grad_home(): pl.pallas_call(functools.partial(home_kernel, bit), grid_spec=pltpu.Prefe...  37.9 us
    ppermute x32, starting transfers between devices, cross(): return lax.ppermute(v, 'shard', [(i, i ^ 1 << bit) for i in range(shards)])  29.9 us
    unnamed x217, local copies, waits for them, and re-layouts  26.9 us
    pallas_call x7, Pallas kernels, grad_away(): pl.pallas_call(away_kernel, grid_spec=pltpu.PrefetchScalarGridSpec(num_sc...  25.8 us
  transfers between devices with their start and end apart: 53, of which 21 were waited for; matrix products, arithmetic and copies ran while one was open for 11% of the time, Pallas kernels for 33%

profile of v3, /device:TPU:0, one launch (start us, length us, event | category | flops | bytes accessed | tf_op | source)
XLA Modules:
  0.0 649.9 jit_solution(997798222045999715)
XLA Ops:
  13.8 2.9 collective-permute-start
  28.4 22.7 %all_gather.15 = bf16[16,10,128]{2,1,0:T(8,128)(2,1)S(1)} all-gather(bf16[1,10,128]{2,1,0:T(8,128)(2,1)S(1)} %pad_bitcast_fusion), channel_id=1, replica_groups=mesh['rep'=2,'shard'=16] {'shard'}, dimensions={0}, use_global_device_ids=true | all-gather | bytes 43520 | tf_op jit(solution)/shard_map/all_gather | solution.py:837
  60.8 64.8 %all-gather.5.cloned.1.call-done = bf16[20480,512]{1,0:T(8,128)(2,1)} async-done(((bf16[1280,512]{1,0:T(8,128)(2,1)}), bf16[20480,512]{1,0:T(8,128)(2,1)}) %all-gather.5.cloned.1.call-update) | async-done | bytes 20971536 | tf_op jit(solution)/shard_map/all_gather | solution.py:860
  125.6 3.2 fusion.45
  128.8 3.4 fusion.8.pre_ref.lru_ref
  139.1 8.6 %fusion.44 = (bf16[16,128,512]{2,1,0:T(8,128)(2,1)S(1)}, bf16[16,128,512]{2,1,0:T(8,128)(2,1)}, bf16[16,128,512]{2,1,0:T(8,128)(2,1)}, bf16[16,128,512]{2,1,0:T(...) fusion(bf16[16,1280,512]{2,1,0:T(8,128)(2,1)} %bitcast.197), kind=kLoop, calls=%fused_computation.110 | loop fusion | bytes 29360128 | tf_op jit(solution)/shard_map/slice | solution.py:856
  147.8 12.9 %collective-permute-done.2 = bf16[512,1024]{1,0:T(8,128)(2,1)S(1)} collective-permute-done((bf16[512,1024]{1,0:T(8,128)(2,1)S(1)}, bf16[512,1024]{1,0:T(8,128)(2,1)S(1)}, u32[]{:S(2)}, u32[]{:S(2)}) %collective-permute-start.2) | collective-permute-done | bytes 1048608 | tf_op jit(solution)/shard_map/ppermute | solution.py:731
  161.3 6.4 fusion.gates_r_ref.gates_i_ref
  167.8 8.6 %recurrence_forward.1 = (bf16[512,1024]{1,0:T(8,128)(2,1)}, f32[512,1024]{1,0:T(8,128)}) custom-call(f32[512,2048]{1,0:T(8,128)} %copy-done.63, f32[512,2048]{1,0:T(8,128)} %fusion.gates_r_ref.gates_i_ref, f32[512,2048]{1,0:T(8,128)} %fusion.gates_r_ref.gates_i_ref, bf16[512,1024]{1,0:T(8,128)(2,1)} %bitcast.147, f32[8,1024]{1,0:T(8,128)} %maximum_maximum_fusion.1.params_ref), custom_call_target="tpu_custom_call" | custom-call | flops 31457280 | bytes 10485760 | tf_op jit(solution)/shard_map/recurrence_forward/pallas_call | solution.py:425
  181.5 10.5 %collective-permute-done.3 = bf16[256,1024]{1,0:T(8,128)(2,1)} collective-permute-done((bf16[256,1024]{1,0:T(8,128)(2,1)}, bf16[256,1024]{1,0:T(8,128)(2,1)}, u32[]{:S(2)}, u32[]{:S(2)}) %collective-permute-start.3) | collective-permute-done | bytes 524320 | tf_op jit(solution)/shard_map/ppermute | solution.py:731
  194.7 4.3 multiply_reduce_fusion
  201.0 7.1 %collective-permute-done.5 = bf16[256,1024]{1,0:T(8,128)(2,1)S(1)} collective-permute-done((bf16[256,1024]{1,0:T(8,128)(2,1)S(1)}, bf16[256,1024]{1,0:T(8,128)(2,1)S(1)}, u32[]{:S(2)}, u32[]{:S(2)}) %collective-permute-start.5) | collective-permute-done | bytes 524320 | tf_op jit(solution)/shard_map/ppermute | solution.py:731
  212.2 10.5 %collective-permute-done.4 = bf16[256,1536]{1,0:T(8,128)(2,1)} collective-permute-done((bf16[256,1536]{1,0:T(8,128)(2,1)}, bf16[256,1536]{1,0:T(8,128)(2,1)}, u32[]{:S(2)}, u32[]{:S(2)}) %collective-permute-start.4) | collective-permute-done | bytes 786464 | tf_op jit(solution)/shard_map/ppermute | solution.py:731
  224.2 13.8 %all-gather.7.cloned.1.call-done = bf16[13824,768]{1,0:T(8,128)(2,1)} async-done(((bf16[864,768]{1,0:T(8,128)(2,1)}), bf16[13824,768]{1,0:T(8,128)(2,1)}) %all-gather.7.cloned.1.call-update) | async-done | bytes 21233680 | tf_op jit(solution)/shard_map/all_gather | solution.py:852
  238.1 13.7 %hidden_pass.1 = (bf16[512,2304]{1,0:T(8,128)(2,1)S(1)}, bf16[2304,512]{1,0:T(8,128)(2,1)S(1)}, f32[512,2304]{1,0:T(8,128)}, f32[512,2304]{1,0:T(8,128)}) custom-call(bf16[512,1536]{1,0:T(8,128)(2,1)S(1)} %pad_maximum_fusion.2.x_ref, bf16[16,864,768]{2,1,0:T(8,128)(2,1)} %bitcast.238, bf16[16,864,768]{2,1,0:T(8,128)(2,1)} %bitcast.239), custom_call_target="tpu_custom_call" | custom-call | flops 420000006144 | bytes 1024 | tf_op jit(solution)/shard_map/hidden_pass/pallas_call | solution.py:458
  251.8 2.8 grad_away.7
  254.9 2.8 grad_away.8
  258.0 23.9 %ffn_back.1 = (bf16[512,2304]{1,0:T(8,128)(2,1)S(1)}, bf16[512,2304]{1,0:T(8,128)(2,1)S(1)}, f32[256,1536]{1,0:T(8,128)S(1)}, bf16[256,1536]{1,0:T(8,128)(2,1)}) custom-call(bf16[512,1536]{1,0:T(8,128)(2,1)S(1)} %copy-done.17, bf16[16,864,768]{2,1,0:T(8,128)(2,1)} %bitcast.240, bf16[16,864,768]{2,1,0:T(8,128)(2,1)} %bitcast.241, ...), custom_call_target="tpu_custom_call" | custom-call | flops 689999970304 | bytes 1024 | tf_op jit(solution)/shard_map/ffn_back/pallas_call | solution.py:531
  283.4 4.3 grad_home.7
  289.0 4.3 grad_home.8
  295.1 4.6 grad_away.9
  299.7 2.2 collective-permute-done.10.far_ref
  302.0 3.9 norm_back.2
  308.5 6.2 grad_home.9
  315.9 2.6 fold.14
  320.0 4.5 grad_away.10
  326.2 22.1 %chain_back.1 = (bf16[512,1024]{1,0:T(8,128)(2,1)S(1)}, bf16[2,512,1024]{2,1,0:T(8,128)(2,1)S(1)}, f32[512,1024]{1,0:T(8,128)S(1)}, f32[48,1024]{1,0:T(8,128)S(1...) custom-call(s32[1]{0:T(128)} %bitcast.2.side_ref, bf16[256,1536]{1,0:T(8,128)(2,1)S(1)} %copy-done.10, ...), custom_call_target="tpu_custom_call" | custom-call | flops 660000014336 | bytes 1024 | tf_op jit(solution)/shard_map/chain_back/pallas_call | solution.py:159
  349.9 2.9 fold.15
  356.9 3.2 fold.16
  360.1 2.4 collective-permute-start.14
  362.5 6.2 grad_home.10
  369.2 2.6 fold.17
  373.0 9.6 %conv_back.1 = (bf16[2,512,1024]{2,1,0:T(8,128)(2,1)S(1)}, f32[8,1024]{1,0:T(8,128)S(1)}, f32[256,1536]{1,0:T(8,128)S(1)}, bf16[256,1536]{1,0:T(8,128)(2,1)}) custom-call(f32[512,1024]{1,0:T(8,128)S(1)} %copy-done.58, f32[512,1024]{1,0:T(8,128)S(1)} %copy-done.60, bf16[512,1024]{1,0:T(8,128)(2,1)} %collective-permute-done.15.far_in_ref, ...), custom_call_target="tpu_custom_call" | custom-call | flops 299999985664 | bytes 1024 | tf_op jit(solution)/shard_map/conv_back/pallas_call | solution.py:235
  390.8 4.4 fold.18
  395.3 8.1 %collective-permute-done.19.far_ref = bf16[256,1536]{1,0:T(8,128)(2,1)} collective-permute-done((bf16[256,1536]{1,0:T(8,128)(2,1)}, bf16[256,1536]{1,0:T(8,128)(2,1)}, u32[]{:S(2)}, u32[]{:S(2)}) %collective-permute-start.19) | collective-permute-done | bytes 786464 | tf_op jit(solution)/shard_map/ppermute | solution.py:731
  404.2 4.1 norm_back.3
  408.3 4.5 grad_away.11
  412.9 2.5 join_rows.1
  415.3 9.8 %down_pass.1 = (f32[256,1536]{1,0:T(8,128)S(1)}, bf16[256,1536]{1,0:T(8,128)(2,1)}) custom-call(bf16[512,2304]{1,0:T(8,128)(2,1)S(1)} %copy-done.56, bf16[16,864,768]{2,1,0:T(8,128)(2,1)} %bitcast.244, bf16[16,864,768]{2,1,0:T(8,128)(2,1)} %bitcast.245), custom_call_target="tpu_custom_call" | custom-call | flops 269999996928 | bytes 1024 | tf_op jit(solution)/shard_map/down_pass/pallas_call | solution.py:561
  430.9 6.7 %grad_home.11 = (f32[2,2,128,2048]{3,2,1,0:T(8,128)S(1)}, bf16[2,2,128,2048]{3,2,1,0:T(8,128)(2,1)}) custom-call(s32[5]{0:T(128)S(1)} %stack.24.at_ref, bf16[8,2,128,512]{3,2,1,0:T(8,128)(2,1)S(1)} %bitcast.172, bf16[2,512,1024]{2,1,0:T(8,128)(2,1)S(1)} %copy-done.47, bf16[8,128,2048]{2,1,0:T(8,128)(2,1)} %collective-permute-done.25.got_ref), custom_call_target="tpu_custom_call" | custom-call | flops 165000003584 | bytes 1024 | tf_op jit(solution)/shard_map/grad_home/pallas_call | solution.py:636
  437.6 3.8 grad_away.12
  441.5 3.4 fold.19
  446.6 2.4 add_convert_fusion
  449.0 4.3 fold.20
  454.6 5.7 grad_home.12
  460.3 2.7 grad_away.13
  463.0 5.2 collective-permute-done.31
  468.2 2.7 settle.9
  471.6 13.2 %collective-permute-done.30 = bf16[2,1,96,2304]{3,2,0,1:T(8,128)(2,1)} collective-permute-done((bf16[2,1,96,2304]{3,2,0,1:T(8,128)(2,1)}, bf16[2,1,96,2304]{3,2,0,1:T(8,128)(2,1)}, u32[]{:S(2)}, u32[]{:S(2)}) %collective-permute-start.30) | collective-permute-done | bytes 884768 | tf_op jit(solution)/shard_map/ppermute | solution.py:763
  484.7 3.4 fold.21
  495.1 2.6 collective-permute-start.40
  499.3 4.4 grad_home.13
  504.3 43.4 %collective-permute-done.33 = bf16[2,2,128,2048]{3,2,1,0:T(8,128)(2,1)} collective-permute-done((bf16[2,2,128,2048]{3,2,1,0:T(8,128)(2,1)}, bf16[2,2,128,2048]{3,2,1,0:T(8,128)(2,1)}, u32[]{:S(2)}, u32[]{:S(2)}) %collective-permute-start.33) | collective-permute-done | bytes 2097184 | tf_op jit(solution)/shard_map/ppermute | solution.py:763
  547.7 3.3 fold.22
  551.0 2.9 settle.10
  554.2 3.0 fold.23
  558.3 6.5 collective-permute-done.41.got_ref
  570.7 2.5 fold.24
  575.3 2.5 fold.25
  580.9 2.7 fold.26
  584.8 11.2 %collective-permute-done.43 = bf16[2,1,128,768]{3,2,0,1:T(8,128)(2,1)S(1)} collective-permute-done((bf16[2,1,128,768]{3,2,0,1:T(8,128)(2,1)S(1)}, bf16[2,1,128,768]{3,2,0,1:T(8,128)(2,1)S(1)}, u32[]{:S(2)}, u32[]{:S(2)}) %collective-permute-start.43) | collective-permute-done | bytes 393248 | tf_op jit(solution)/shard_map/ppermute | solution.py:763
  597.3 3.7 collective-permute-start.49
  606.2 16.2 %collective-permute-done.46 = bf16[1,1,128,2048]{3,2,1,0:T(8,128)(2,1)S(1)} collective-permute-done((bf16[1,1,128,2048]{3,2,1,0:T(8,128)(2,1)}, bf16[1,1,128,2048]{3,2,1,0:T(8,128)(2,1)S(1)}, u32[]{:S(2)}, u32[]{:S(2)}) %collective-permute-start.46) | collective-permute-done | bytes 524320 | tf_op jit(solution)/shard_map/ppermute | solution.py:763
  629.8 8.7 %collective-permute-done.48.got_ref = bf16[128,2048]{1,0:T(8,128)(2,1)S(1)} collective-permute-done((bf16[128,2048]{1,0:T(8,128)(2,1)}, bf16[128,2048]{1,0:T(8,128)(2,1)S(1)}, u32[]{:S(2)}, u32[]{:S(2)}) %collective-permute-start.48) | collective-permute-done | bytes 524320 | tf_op jit(solution)/shard_map/ppermute | solution.py:731
  (382 shorter events, 128.8 us)
Async XLA Ops:
  7.2 118.4 %all-gather.5.cloned.1.call-start = ((), (), s32[]{:S(2)}) async-start(), calls=%async_computation | async-start | bytes 22282240 | tf_op jit(solution)/shard_map/all_gather | solution.py:860
  13.5 224.6 %all-gather.7.cloned.1.call-start = ((), (), s32[]{:S(2)}) async-start(), calls=%async_computation.1 | async-start | bytes 22560768 | tf_op jit(solution)/shard_map/all_gather | solution.py:852
  13.8 41.5 %collective-permute-start = (bf16[256,1536]{1,0:T(8,128)(2,1)S(1)}, bf16[256,1536]{1,0:T(8,128)(2,1)S(1)}, u32[]{:S(2)}, u32[]{:S(2)}) collective-permute-start(bf16[256,1536]{1,0:T(8,128)(2,1)S(1)} %copy-done.5), channel_id=1, source_target_pairs={{0,16},{16,0},{1,17},{17,1},{2,18},{18,2},{3,19},{19,3},{4,20},{20... | collective-permute-start | bytes 2359304 | tf_op jit(solution)/shard_map/ppermute | solution.py:731
  16.7 41.7 %collective-permute-start.1 = (bf16[256,1536]{1,0:T(8,128)(2,1)}, bf16[256,1536]{1,0:T(8,128)(2,1)}, u32[]{:S(2)}, u32[]{:S(2)}) collective-permute-start(bf16[256,1536]{1,0:T(8,128)(2,1)} %base_ref.1), channel_id=1, source_target_pairs={{0,16},{16,0},{1,17},{17,1},{2,18},{18,2},{3,19},{19,3},{4,20},{20... | collective-permute-start | bytes 2359304 | tf_op jit(solution)/shard_map/ppermute | solution.py:731
  135.3 25.5 %copy-start = (bf16[2,256,1024]{2,1,0:T(8,128)(2,1)}, bf16[2,256,1024]{2,1,0:T(8,128)(2,1)S(1)}, u32[]{:S(2)}) copy-start(bf16[2,256,1024]{2,1,0:T(8,128)(2,1)S(1)} %fusion.32) | copy-start | bytes 3145732
  135.3 25.4 %collective-permute-start.2 = (bf16[512,1024]{1,0:T(8,128)(2,1)S(1)}, bf16[512,1024]{1,0:T(8,128)(2,1)S(1)}, u32[]{:S(2)}, u32[]{:S(2)}) collective-permute-start(bf16[512,1024]{1,0:T(8,128)(2,1)S(1)} %bitcast.146), channel_id=1, source_target_pairs={{0,16},{16,0},{1,17},{17,1},{2,18},{18,2},{3,19},{19,3},{4,20},{20... | collective-permute-start | bytes 3145736 | tf_op jit(solution)/shard_map/ppermute | solution.py:731
  178.3 13.7 %collective-permute-start.3 = (bf16[256,1024]{1,0:T(8,128)(2,1)}, bf16[256,1024]{1,0:T(8,128)(2,1)}, u32[]{:S(2)}, u32[]{:S(2)}) collective-permute-start(bf16[256,1024]{1,0:T(8,128)(2,1)} %slice.179), channel_id=1, source_target_pairs={{0,16},{16,0},{1,17},{17,1},{2,18},{18,2},{3,19},{19,3},{4,20},{20... | collective-permute-start | bytes 1572872 | tf_op jit(solution)/shard_map/ppermute | solution.py:731
  193.2 14.9 %collective-permute-start.5 = (bf16[256,1024]{1,0:T(8,128)(2,1)S(1)}, bf16[256,1024]{1,0:T(8,128)(2,1)S(1)}, u32[]{:S(2)}, u32[]{:S(2)}) collective-permute-start(bf16[256,1024]{1,0:T(8,128)(2,1)S(1)} %get-tuple-element.418), channel_id=1, source_target_pairs={{0,16},{16,0},{1,17},{17,1},{2,18},{18,2},{3,19},{19,3},{4,20},{20... | collective-permute-start | bytes 1572872 | tf_op jit(solution)/shard_map/ppermute | solution.py:731
  200.3 22.3 %collective-permute-start.4 = (bf16[256,1536]{1,0:T(8,128)(2,1)}, bf16[256,1536]{1,0:T(8,128)(2,1)}, u32[]{:S(2)}, u32[]{:S(2)}) collective-permute-start(bf16[256,1536]{1,0:T(8,128)(2,1)} %multiply_convert_fusion), channel_id=1, source_target_pairs={{0,16},{16,0},{1,17},{17,1},{2,18},{18,2},{3,19},{19,3},{4,20},{20... | collective-permute-start | bytes 2359304 | tf_op jit(solution)/shard_map/ppermute | solution.py:731
  238.1 13.7 %copy-start.17 = (bf16[512,1536]{1,0:T(8,128)(2,1)S(1)}, bf16[512,1536]{1,0:T(8,128)(2,1)}, u32[]{:S(2)}) copy-start(bf16[512,1536]{1,0:T(8,128)(2,1)} %copy-done.16) | copy-start | bytes 4718596
  254.6 28.8 %collective-permute-start.6 = (bf16[8,144,768]{2,1,0:T(8,128)(2,1)}, bf16[8,144,768]{2,1,0:T(8,128)(2,1)}, u32[]{:S(2)}, u32[]{:S(2)}) collective-permute-start(bf16[8,144,768]{2,1,0:T(8,128)(2,1)} %grad_away.7), channel_id=1, source_target_pairs={{0,1},{1,0},{2,3},{3,2},{4,5},{5,4},{6,7},{7,6},{8,9},{9,8},{10,11... | collective-permute-start | bytes 5308424 | tf_op jit(solution)/shard_map/ppermute | solution.py:763
  257.7 31.3 %collective-permute-start.8 = (bf16[8,144,768]{2,1,0:T(8,128)(2,1)}, bf16[8,144,768]{2,1,0:T(8,128)(2,1)}, u32[]{:S(2)}, u32[]{:S(2)}) collective-permute-start(bf16[8,144,768]{2,1,0:T(8,128)(2,1)} %grad_away.8), channel_id=1, source_target_pairs={{0,1},{1,0},{2,3},{3,2},{4,5},{5,4},{6,7},{7,6},{8,9},{9,8},{10,11... | collective-permute-start | bytes 5308424 | tf_op jit(solution)/shard_map/ppermute | solution.py:763
  258.0 25.4 %copy-start.33 = (bf16[2304,512]{1,0:T(8,128)(2,1)S(1)}, bf16[2304,512]{1,0:T(8,128)(2,1)}, u32[]{:S(2)}) copy-start(bf16[2304,512]{1,0:T(8,128)(2,1)} %copy-done.32) | copy-start | bytes 7077892
  281.9 38.1 %copy-start.30 = (bf16[512,2304]{1,0:T(8,128)(2,1)}, bf16[512,2304]{1,0:T(8,128)(2,1)S(1)}, u32[]{:S(2)}) copy-start(bf16[512,2304]{1,0:T(8,128)(2,1)S(1)} %get-tuple-element.249) | copy-start | bytes 7077892
  281.9 20.0 %collective-permute-start.10 = (bf16[256,1536]{1,0:T(8,128)(2,1)}, bf16[256,1536]{1,0:T(8,128)(2,1)}, u32[]{:S(2)}, u32[]{:S(2)}) collective-permute-start(bf16[256,1536]{1,0:T(8,128)(2,1)} %get-tuple-element.225), channel_id=1, source_target_pairs={{0,16},{16,0},{1,17},{17,1},{2,18},{18,2},{3,19},{19,3},{4,20},{20... | collective-permute-start | bytes 2359304 | tf_op jit(solution)/shard_map/ppermute | solution.py:731
  287.7 28.2 %collective-permute-start.7 = (bf16[4,1,144,768]{3,2,1,0:T(8,128)(2,1)}, bf16[4,1,144,768]{3,2,1,0:T(8,128)(2,1)}, u32[]{:S(2)}, u32[]{:S(2)}) collective-permute-start(bf16[4,1,144,768]{3,2,1,0:T(8,128)(2,1)} %get-tuple-element.229), channel_id=1, source_target_pairs={{0,2},{1,3},{2,0},{3,1},{4,6},{5,7},{6,4},{7,5},{8,10},{9,11},{10,... | collective-permute-start | bytes 2654216 | tf_op jit(solution)/shard_map/ppermute | solution.py:763
  293.3 56.6 %collective-permute-start.12 = (bf16[4,1,144,768]{3,2,1,0:T(8,128)(2,1)}, bf16[4,1,144,768]{3,2,1,0:T(8,128)(2,1)}, u32[]{:S(2)}, u32[]{:S(2)}) collective-permute-start(bf16[4,1,144,768]{3,2,1,0:T(8,128)(2,1)} %get-tuple-element.233), channel_id=1, source_target_pairs={{0,2},{1,3},{2,0},{3,1},{4,6},{5,7},{6,4},{7,5},{8,10},{9,11},{10,... | collective-permute-start | bytes 2654216 | tf_op jit(solution)/shard_map/ppermute | solution.py:763
  295.1 24.9 %copy-start.43 = (bf16[1536,512]{1,0:T(8,128)(2,1)}, bf16[1536,512]{1,0:T(8,128)(2,1)S(1)}, u32[]{:S(2)}) copy-start(bf16[1536,512]{1,0:T(8,128)(2,1)S(1)} %flip.7) | copy-start | bytes 4718596
  299.7 8.7 %collective-permute-start.9 = (bf16[8,96,2304]{2,1,0:T(8,128)(2,1)}, bf16[8,96,2304]{2,1,0:T(8,128)(2,1)}, u32[]{:S(2)}, u32[]{:S(2)}) collective-permute-start(bf16[8,96,2304]{2,1,0:T(8,128)(2,1)} %grad_away.9), channel_id=1, source_target_pairs={{0,1},{1,0},{2,3},{3,2},{4,5},{5,4},{6,7},{7,6},{8,9},{9,8},{10,11... | collective-permute-start | bytes 10616840 | tf_op jit(solution)/shard_map/ppermute | solution.py:763
  307.0 19.2 %collective-permute-start.13 = (bf16[256,1536]{1,0:T(8,128)(2,1)}, bf16[256,1536]{1,0:T(8,128)(2,1)}, u32[]{:S(2)}, u32[]{:S(2)}) collective-permute-start(bf16[256,1536]{1,0:T(8,128)(2,1)} %get-tuple-element.251.own_ref), channel_id=1, source_target_pairs={{0,16},{16,0},{1,17},{17,1},{2,18},{18,2},{3,19},{19,3},{4,20},{20... | collective-permute-start | bytes 2359304 | tf_op jit(solution)/shard_map/ppermute | solution.py:731
  314.6 75.0 %collective-permute-start.20 = (bf16[4,1,96,2304]{3,2,1,0:T(8,128)(2,1)}, bf16[4,1,96,2304]{3,2,1,0:T(8,128)(2,1)}, u32[]{:S(2)}, u32[]{:S(2)}) collective-permute-start(bf16[4,1,96,2304]{3,2,1,0:T(8,128)(2,1)} %get-tuple-element.244), channel_id=1, source_target_pairs={{0,2},{1,3},{2,0},{3,1},{4,6},{5,7},{6,4},{7,5},{8,10},{9,11},{10,... | collective-permute-start | bytes 5308424 | tf_op jit(solution)/shard_map/ppermute | solution.py:763
  318.5 38.4 %collective-permute-start.11 = (bf16[2,1,144,768]{3,2,0,1:T(8,128)(2,1)}, bf16[2,1,144,768]{3,2,0,1:T(8,128)(2,1)}, u32[]{:S(2)}, u32[]{:S(2)}) collective-permute-start(bf16[2,1,144,768]{3,2,0,1:T(8,128)(2,1)} %bitcast.249), channel_id=1, source_target_pairs={{0,4},{1,5},{2,6},{3,7},{4,0},{5,1},{6,2},{7,3},{8,12},{9,13},{10,... | collective-permute-start | bytes 1327112 | tf_op jit(solution)/shard_map/ppermute | solution.py:763
  324.5 37.9 %collective-permute-start.17 = (bf16[8,96,2304]{2,1,0:T(8,128)(2,1)}, bf16[8,96,2304]{2,1,0:T(8,128)(2,1)}, u32[]{:S(2)}, u32[]{:S(2)}) collective-permute-start(bf16[8,96,2304]{2,1,0:T(8,128)(2,1)} %grad_away.10), channel_id=1, source_target_pairs={{0,1},{1,0},{2,3},{3,2},{4,5},{5,4},{6,7},{7,6},{8,9},{9,8},{10,11... | collective-permute-start | bytes 10616840 | tf_op jit(solution)/shard_map/ppermute | solution.py:763
  348.3 24.7 %collective-permute-start.15 = (bf16[512,1024]{1,0:T(8,128)(2,1)}, bf16[512,1024]{1,0:T(8,128)(2,1)}, u32[]{:S(2)}, u32[]{:S(2)}) collective-permute-start(bf16[512,1024]{1,0:T(8,128)(2,1)} %get-tuple-element.255), channel_id=1, source_target_pairs={{0,16},{16,0},{1,17},{17,1},{2,18},{18,2},{3,19},{19,3},{4,20},{20... | collective-permute-start | bytes 3145736 | tf_op jit(solution)/shard_map/ppermute | solution.py:731
  352.8 16.4 %collective-permute-start.16 = (bf16[2,1,144,768]{3,2,0,1:T(8,128)(2,1)}, bf16[2,1,144,768]{3,2,0,1:T(8,128)(2,1)}, u32[]{:S(2)}, u32[]{:S(2)}) collective-permute-start(bf16[2,1,144,768]{3,2,0,1:T(8,128)(2,1)} %bitcast.250), channel_id=1, source_target_pairs={{0,4},{1,5},{2,6},{3,7},{4,0},{5,1},{6,2},{7,3},{8,12},{9,13},{10,... | collective-permute-start | bytes 1327112 | tf_op jit(solution)/shard_map/ppermute | solution.py:763
  356.9 103.4 %copy-start.8 = (bf16[1,512,1536]{2,1,0:T(8,128)(2,1)}, bf16[1,512,1536]{2,1,0:T(8,128)(2,1)S(1)}, u32[]{:S(2)}) copy-start(bf16[1,512,1536]{2,1,0:T(8,128)(2,1)S(1)} %maximum_bitcast_fusion.right_ref) | copy-start | bytes 4718596
  360.1 23.5 %collective-permute-start.14 = (bf16[1,1,144,768]{3,2,1,0:T(8,128)(2,1)}, bf16[1,1,144,768]{3,2,1,0:T(8,128)(2,1)}, u32[]{:S(2)}, u32[]{:S(2)}) collective-permute-start(bf16[1,1,144,768]{3,2,1,0:T(8,128)(2,1)} %get-tuple-element.263), channel_id=1, source_target_pairs={{0,8},{1,9},{2,10},{3,11},{4,12},{5,13},{6,14},{7,15},{8,0},{9,1},... | collective-permute-start | bytes 663560 | tf_op jit(solution)/shard_map/ppermute | solution.py:763
  368.6 80.4 %collective-permute-start.28 = (bf16[4,1,96,2304]{3,2,1,0:T(8,128)(2,1)}, bf16[4,1,96,2304]{3,2,1,0:T(8,128)(2,1)}, u32[]{:S(2)}, u32[]{:S(2)}) collective-permute-start(bf16[4,1,96,2304]{3,2,1,0:T(8,128)(2,1)} %get-tuple-element.268), channel_id=1, source_target_pairs={{0,2},{1,3},{2,0},{3,1},{4,6},{5,7},{6,4},{7,5},{8,10},{9,11},{10,... | collective-permute-start | bytes 5308424 | tf_op jit(solution)/shard_map/ppermute | solution.py:763
  371.8 16.0 %collective-permute-start.21 = (bf16[1,1,144,768]{3,2,1,0:T(8,128)(2,1)}, bf16[1,1,144,768]{3,2,1,0:T(8,128)(2,1)}, u32[]{:S(2)}, u32[]{:S(2)}) collective-permute-start(bf16[1,1,144,768]{3,2,1,0:T(8,128)(2,1)} %get-tuple-element.272), channel_id=1, source_target_pairs={{0,8},{1,9},{2,10},{3,11},{4,12},{5,13},{6,14},{7,15},{8,0},{9,1},... | collective-permute-start | bytes 663560 | tf_op jit(solution)/shard_map/ppermute | solution.py:763
  382.6 20.8 %collective-permute-start.19 = (bf16[256,1536]{1,0:T(8,128)(2,1)}, bf16[256,1536]{1,0:T(8,128)(2,1)}, u32[]{:S(2)}, u32[]{:S(2)}) collective-permute-start(bf16[256,1536]{1,0:T(8,128)(2,1)} %get-tuple-element.277), channel_id=1, source_target_pairs={{0,16},{16,0},{1,17},{17,1},{2,18},{18,2},{3,19},{19,3},{4,20},{20... | collective-permute-start | bytes 2359304 | tf_op jit(solution)/shard_map/ppermute | solution.py:731
  385.5 27.3 %collective-permute-start.18 = (bf16[144,768]{1,0:T(8,128)(2,1)}, bf16[144,768]{1,0:T(8,128)(2,1)}, u32[]{:S(2)}, u32[]{:S(2)}) collective-permute-start(bf16[144,768]{1,0:T(8,128)(2,1)} %get-tuple-element.282), channel_id=1, source_target_pairs={{0,16},{16,0},{1,17},{17,1},{2,18},{18,2},{3,19},{19,3},{4,20},{20... | collective-permute-start | bytes 663560 | tf_op jit(solution)/shard_map/ppermute | solution.py:731
  387.8 38.9 %collective-permute-start.26 = (f32[8,8,128]{2,1,0:T(8,128)}, f32[8,8,128]{2,1,0:T(8,128)}, u32[]{:S(2)}, u32[]{:S(2)}) collective-permute-start(f32[8,8,128]{2,1,0:T(8,128)} %bitcast.142), channel_id=1, source_target_pairs={{0,1},{1,0},{2,3},{3,2},{4,5},{5,4},{6,7},{7,6},{8,9},{9,8},{10,11... | collective-permute-start | bytes 98312 | tf_op jit(solution)/shard_map/ppermute | solution.py:763
  389.7 23.2 %collective-permute-start.22 = (bf16[144,768]{1,0:T(8,128)(2,1)}, bf16[144,768]{1,0:T(8,128)(2,1)}, u32[]{:S(2)}, u32[]{:S(2)}) collective-permute-start(bf16[144,768]{1,0:T(8,128)(2,1)} %get-tuple-element.287), channel_id=1, source_target_pairs={{0,16},{16,0},{1,17},{17,1},{2,18},{18,2},{3,19},{19,3},{4,20},{20... | collective-permute-start | bytes 663560 | tf_op jit(solution)/shard_map/ppermute | solution.py:731
  390.8 13.4 %copy-start.7 = (bf16[256,1536]{1,0:T(8,128)(2,1)S(1)}, bf16[256,1536]{1,0:T(8,128)(2,1)}, u32[]{:S(2)}) copy-start(bf16[256,1536]{1,0:T(8,128)(2,1)} %v_ref.1) | copy-start | bytes 2359300
  390.8 13.4 %copy-start.52 = (f32[256,1536]{1,0:T(8,128)S(1)}, f32[256,1536]{1,0:T(8,128)}, u32[]{:S(2)}) copy-start(f32[256,1536]{1,0:T(8,128)} %copy-done.51) | copy-start | bytes 4718596
  390.8 13.4 %copy-start.54 = (f32[256,1536]{1,0:T(8,128)S(1)}, f32[256,1536]{1,0:T(8,128)}, u32[]{:S(2)}) copy-start(f32[256,1536]{1,0:T(8,128)} %copy-done.53) | copy-start | bytes 4718596
  403.4 38.1 %collective-permute-start.24 = (bf16[2,1,96,2304]{3,2,0,1:T(8,128)(2,1)}, bf16[2,1,96,2304]{3,2,0,1:T(8,128)(2,1)}, u32[]{:S(2)}, u32[]{:S(2)}) collective-permute-start(bf16[2,1,96,2304]{3,2,0,1:T(8,128)(2,1)} %bitcast.246), channel_id=1, source_target_pairs={{0,4},{1,5},{2,6},{3,7},{4,0},{5,1},{6,2},{7,3},{8,12},{9,13},{10,... | collective-permute-start | bytes 2654216 | tf_op jit(solution)/shard_map/ppermute | solution.py:763
  412.8 16.5 %collective-permute-start.25 = (bf16[8,128,2048]{2,1,0:T(8,128)(2,1)}, bf16[8,128,2048]{2,1,0:T(8,128)(2,1)}, u32[]{:S(2)}, u32[]{:S(2)}) collective-permute-start(bf16[8,128,2048]{2,1,0:T(8,128)(2,1)} %grad_away.11), channel_id=1, source_target_pairs={{0,1},{1,0},{2,3},{3,2},{4,5},{5,4},{6,7},{7,6},{8,9},{9,8},{10,11... | collective-permute-start | bytes 12582920 | tf_op jit(solution)/shard_map/ppermute | solution.py:763
  415.3 14.0 %copy-start.39 = (bf16[2048,512]{1,0:T(8,128)(2,1)S(1)}, bf16[2048,512]{1,0:T(8,128)(2,1)}, u32[]{:S(2)}) copy-start(bf16[2048,512]{1,0:T(8,128)(2,1)} %copy-done.37) | copy-start | bytes 6291460
  425.2 21.4 %collective-permute-start.23 = (bf16[256,1536]{1,0:T(8,128)(2,1)}, bf16[256,1536]{1,0:T(8,128)(2,1)}, u32[]{:S(2)}, u32[]{:S(2)}) collective-permute-start(bf16[256,1536]{1,0:T(8,128)(2,1)} %get-tuple-element.302), channel_id=1, source_target_pairs={{0,16},{16,0},{1,17},{17,1},{2,18},{18,2},{3,19},{19,3},{4,20},{20... | collective-permute-start | bytes 2359304 | tf_op jit(solution)/shard_map/ppermute | solution.py:731
  428.1 61.9 %collective-permute-start.35 = (f32[4,8,128]{2,1,0:T(8,128)}, f32[4,8,128]{2,1,0:T(8,128)}, u32[]{:S(2)}, u32[]{:S(2)}) collective-permute-start(f32[4,8,128]{2,1,0:T(8,128)} %get-tuple-element.431), channel_id=1, source_target_pairs={{0,2},{1,3},{2,0},{3,1},{4,6},{5,7},{6,4},{7,5},{8,10},{9,11},{10,... | collective-permute-start | bytes 49160 | tf_op jit(solution)/shard_map/ppermute | solution.py:763
  441.5 13.1 %collective-permute-start.27 = (bf16[8,96,2048]{2,1,0:T(8,128)(2,1)}, bf16[8,96,2048]{2,1,0:T(8,128)(2,1)}, u32[]{:S(2)}, u32[]{:S(2)}) collective-permute-start(bf16[8,96,2048]{2,1,0:T(8,128)(2,1)} %grad_away.12), channel_id=1, source_target_pairs={{0,1},{1,0},{2,3},{3,2},{4,5},{5,4},{6,7},{7,6},{8,9},{9,8},{10,11... | collective-permute-start | bytes 9437192 | tf_op jit(solution)/shard_map/ppermute | solution.py:763
  444.9 23.3 %collective-permute-start.31 = (bf16[1,1,96,2304]{3,2,1,0:T(8,128)(2,1)}, bf16[1,1,96,2304]{3,2,1,0:T(8,128)(2,1)}, u32[]{:S(2)}, u32[]{:S(2)}) collective-permute-start(bf16[1,1,96,2304]{3,2,1,0:T(8,128)(2,1)} %get-tuple-element.315), channel_id=1, source_target_pairs={{0,8},{1,9},{2,10},{3,11},{4,12},{5,13},{6,14},{7,15},{8,0},{9,1},... | collective-permute-start | bytes 1327112 | tf_op jit(solution)/shard_map/ppermute | solution.py:763
  453.3 31.5 %collective-permute-start.30 = (bf16[2,1,96,2304]{3,2,0,1:T(8,128)(2,1)}, bf16[2,1,96,2304]{3,2,0,1:T(8,128)(2,1)}, u32[]{:S(2)}, u32[]{:S(2)}) collective-permute-start(bf16[2,1,96,2304]{3,2,0,1:T(8,128)(2,1)} %bitcast.247), channel_id=1, source_target_pairs={{0,4},{1,5},{2,6},{3,7},{4,0},{5,1},{6,2},{7,3},{8,12},{9,13},{10,... | collective-permute-start | bytes 2654216 | tf_op jit(solution)/shard_map/ppermute | solution.py:763
  463.0 34.7 %collective-permute-start.34 = (bf16[8,128,768]{2,1,0:T(8,128)(2,1)}, bf16[8,128,768]{2,1,0:T(8,128)(2,1)}, u32[]{:S(2)}, u32[]{:S(2)}) collective-permute-start(bf16[8,128,768]{2,1,0:T(8,128)(2,1)} %grad_away.13), channel_id=1, source_target_pairs={{0,1},{1,0},{2,3},{3,2},{4,5},{5,4},{6,7},{7,6},{8,9},{9,8},{10,11... | collective-permute-start | bytes 4718600 | tf_op jit(solution)/shard_map/ppermute | solution.py:763
  471.0 17.2 %collective-permute-start.36 = (bf16[96,2304]{1,0:T(8,128)(2,1)}, bf16[96,2304]{1,0:T(8,128)(2,1)S(1)}, u32[]{:S(2)}, u32[]{:S(2)}) collective-permute-start(bf16[96,2304]{1,0:T(8,128)(2,1)} %get-tuple-element.330), channel_id=1, source_target_pairs={{0,16},{16,0},{1,17},{17,1},{2,18},{18,2},{3,19},{19,3},{4,20},{20... | collective-permute-start | bytes 1327112 | tf_op jit(solution)/shard_map/ppermute | solution.py:731
  490.7 3.8 collective-permute-start.37
  490.7 57.0 %collective-permute-start.33 = (bf16[2,2,128,2048]{3,2,1,0:T(8,128)(2,1)}, bf16[2,2,128,2048]{3,2,1,0:T(8,128)(2,1)}, u32[]{:S(2)}, u32[]{:S(2)}) collective-permute-start(bf16[2,2,128,2048]{3,2,1,0:T(8,128)(2,1)} %get-tuple-element.310), channel_id=1, source_target_pairs={{0,4},{1,5},{2,6},{3,7},{4,0},{5,1},{6,2},{7,3},{8,12},{9,13},{10,... | collective-permute-start | bytes 6291464 | tf_op jit(solution)/shard_map/ppermute | solution.py:763
  492.7 61.5 %collective-permute-start.29 = (bf16[4,1,96,2048]{3,2,1,0:T(8,128)(2,1)}, bf16[4,1,96,2048]{3,2,1,0:T(8,128)(2,1)}, u32[]{:S(2)}, u32[]{:S(2)}) collective-permute-start(bf16[4,1,96,2048]{3,2,1,0:T(8,128)(2,1)} %get-tuple-element.325), channel_id=1, source_target_pairs={{0,2},{1,3},{2,0},{3,1},{4,6},{5,7},{6,4},{7,5},{8,10},{9,11},{10,... | collective-permute-start | bytes 4718600 | tf_op jit(solution)/shard_map/ppermute | solution.py:763
  494.1 56.9 %collective-permute-start.32 = (bf16[1,1,96,2304]{3,2,1,0:T(8,128)(2,1)}, bf16[1,1,96,2304]{3,2,1,0:T(8,128)(2,1)}, u32[]{:S(2)}, u32[]{:S(2)}) collective-permute-start(bf16[1,1,96,2304]{3,2,1,0:T(8,128)(2,1)} %get-tuple-element.334), channel_id=1, source_target_pairs={{0,8},{1,9},{2,10},{3,11},{4,12},{5,13},{6,14},{7,15},{8,0},{9,1},... | collective-permute-start | bytes 1327112 | tf_op jit(solution)/shard_map/ppermute | solution.py:763
  495.1 71.5 %collective-permute-start.40 = (f32[1,8,128]{2,1,0:T(8,128)}, f32[1,8,128]{2,1,0:T(8,128)}, u32[]{:S(2)}, u32[]{:S(2)}) collective-permute-start(f32[1,8,128]{2,1,0:T(8,128)} %get-tuple-element.443), channel_id=1, source_target_pairs={{0,8},{1,9},{2,10},{3,11},{4,12},{5,13},{6,14},{7,15},{8,0},{9,1},... | collective-permute-start | bytes 12296 | tf_op jit(solution)/shard_map/ppermute | solution.py:763
  499.3 48.4 %copy-start.25 = (f32[2,2,128,2048]{3,2,1,0:T(8,128)S(1)}, f32[2,2,128,2048]{3,2,1,0:T(8,128)}, u32[]{:S(2)}) copy-start(f32[2,2,128,2048]{3,2,1,0:T(8,128)} %copy-done.24) | copy-start | bytes 12582916
  503.7 67.0 %collective-permute-start.39 = (bf16[4,1,128,768]{3,2,1,0:T(8,128)(2,1)}, bf16[4,1,128,768]{3,2,1,0:T(8,128)(2,1)}, u32[]{:S(2)}, u32[]{:S(2)}) collective-permute-start(bf16[4,1,128,768]{3,2,1,0:T(8,128)(2,1)} %get-tuple-element.344), channel_id=1, source_target_pairs={{0,2},{1,3},{2,0},{3,1},{4,6},{5,7},{6,4},{7,5},{8,10},{9,11},{10,... | collective-permute-start | bytes 2359304 | tf_op jit(solution)/shard_map/ppermute | solution.py:763
  553.9 10.8 %collective-permute-start.41 = (bf16[96,2304]{1,0:T(8,128)(2,1)}, bf16[96,2304]{1,0:T(8,128)(2,1)S(1)}, u32[]{:S(2)}, u32[]{:S(2)}) collective-permute-start(bf16[96,2304]{1,0:T(8,128)(2,1)} %get-tuple-element.352), channel_id=1, source_target_pairs={{0,16},{16,0},{1,17},{17,1},{2,18},{18,2},{3,19},{19,3},{4,20},{20... | collective-permute-start | bytes 1327112 | tf_op jit(solution)/shard_map/ppermute | solution.py:731
  557.2 18.0 %collective-permute-start.38 = (bf16[2,1,96,2048]{3,2,0,1:T(8,128)(2,1)}, bf16[2,1,96,2048]{3,2,0,1:T(8,128)(2,1)}, u32[]{:S(2)}, u32[]{:S(2)}) collective-permute-start(bf16[2,1,96,2048]{3,2,0,1:T(8,128)(2,1)} %bitcast.248), channel_id=1, source_target_pairs={{0,4},{1,5},{2,6},{3,7},{4,0},{5,1},{6,2},{7,3},{8,12},{9,13},{10,... | collective-permute-start | bytes 2359304 | tf_op jit(solution)/shard_map/ppermute | solution.py:763
  557.2 23.7 %collective-permute-start.44 = (bf16[2,1,128,2048]{3,2,0,1:T(8,128)(2,1)}, bf16[2,1,128,2048]{3,2,0,1:T(8,128)(2,1)}, u32[]{:S(2)}, u32[]{:S(2)}) collective-permute-start(bf16[2,1,128,2048]{3,2,0,1:T(8,128)(2,1)} %bitcast.93), channel_id=1, source_target_pairs={{0,2},{1,3},{2,0},{3,1},{4,6},{5,7},{6,4},{7,5},{8,10},{9,11},{10,... | collective-permute-start | bytes 3145736 | tf_op jit(solution)/shard_map/ppermute | solution.py:763
  567.8 36.6 %collective-permute-start.47 = (f32[1,8,128]{2,1,0:T(8,128)}, f32[1,8,128]{2,1,0:T(8,128)}, u32[]{:S(2)}, u32[]{:S(2)}) collective-permute-start(f32[1,8,128]{2,1,0:T(8,128)} %add.165), channel_id=1, source_target_pairs={{0,16},{16,0},{1,17},{17,1},{2,18},{18,2},{3,19},{19,3},{4,20},{20... | collective-permute-start | bytes 12296 | tf_op jit(solution)/shard_map/ppermute | solution.py:731
  577.8 23.1 %collective-permute-start.42 = (bf16[1,1,96,2048]{3,2,1,0:T(8,128)(2,1)}, bf16[1,1,96,2048]{3,2,1,0:T(8,128)(2,1)}, u32[]{:S(2)}, u32[]{:S(2)}) collective-permute-start(bf16[1,1,96,2048]{3,2,1,0:T(8,128)(2,1)} %get-tuple-element.368), channel_id=1, source_target_pairs={{0,8},{1,9},{2,10},{3,11},{4,12},{5,13},{6,14},{7,15},{8,0},{9,1},... | collective-permute-start | bytes 1179656 | tf_op jit(solution)/shard_map/ppermute | solution.py:763
  577.8 18.2 %collective-permute-start.43 = (bf16[2,1,128,768]{3,2,0,1:T(8,128)(2,1)S(1)}, bf16[2,1,128,768]{3,2,0,1:T(8,128)(2,1)S(1)}, u32[]{:S(2)}, u32[]{:S(2)}) collective-permute-start(bf16[2,1,128,768]{3,2,0,1:T(8,128)(2,1)S(1)} %bitcast.251), channel_id=1, source_target_pairs={{0,4},{1,5},{2,6},{3,7},{4,0},{5,1},{6,2},{7,3},{8,12},{9,13},{10,... | collective-permute-start | bytes 1179656 | tf_op jit(solution)/shard_map/ppermute | solution.py:763
  583.5 38.9 %collective-permute-start.46 = (bf16[1,1,128,2048]{3,2,1,0:T(8,128)(2,1)}, bf16[1,1,128,2048]{3,2,1,0:T(8,128)(2,1)S(1)}, u32[]{:S(2)}, u32[]{:S(2)}) collective-permute-start(bf16[1,1,128,2048]{3,2,1,0:T(8,128)(2,1)} %get-tuple-element.372), channel_id=1, source_target_pairs={{0,8},{1,9},{2,10},{3,11},{4,12},{5,13},{6,14},{7,15},{8,0},{9,1},... | collective-permute-start | bytes 1572872 | tf_op jit(solution)/shard_map/ppermute | solution.py:763
  597.3 29.3 %collective-permute-start.49 = (bf16[1,1,128,768]{3,2,1,0:T(8,128)(2,1)}, bf16[1,1,128,768]{3,2,1,0:T(8,128)(2,1)S(1)}, u32[]{:S(2)}, u32[]{:S(2)}) collective-permute-start(bf16[1,1,128,768]{3,2,1,0:T(8,128)(2,1)} %get-tuple-element.376), channel_id=1, source_target_pairs={{0,8},{1,9},{2,10},{3,11},{4,12},{5,13},{6,14},{7,15},{8,0},{9,1},... | collective-permute-start | bytes 589832 | tf_op jit(solution)/shard_map/ppermute | solution.py:763
  602.7 22.5 %collective-permute-start.45 = (bf16[96,2048]{1,0:T(8,128)(2,1)}, bf16[96,2048]{1,0:T(8,128)(2,1)S(1)}, u32[]{:S(2)}, u32[]{:S(2)}) collective-permute-start(bf16[96,2048]{1,0:T(8,128)(2,1)} %get-tuple-element.380), channel_id=1, source_target_pairs={{0,16},{16,0},{1,17},{17,1},{2,18},{18,2},{3,19},{19,3},{4,20},{20... | collective-permute-start | bytes 1179656 | tf_op jit(solution)/shard_map/ppermute | solution.py:731
  623.5 15.0 %collective-permute-start.48 = (bf16[128,2048]{1,0:T(8,128)(2,1)}, bf16[128,2048]{1,0:T(8,128)(2,1)S(1)}, u32[]{:S(2)}, u32[]{:S(2)}) collective-permute-start(bf16[128,2048]{1,0:T(8,128)(2,1)} %get-tuple-element.386), channel_id=1, source_target_pairs={{0,16},{16,0},{1,17},{17,1},{2,18},{18,2},{3,19},{19,3},{4,20},{20... | collective-permute-start | bytes 1572872 | tf_op jit(solution)/shard_map/ppermute | solution.py:731
  627.3 14.4 %collective-permute-start.50 = (bf16[128,768]{1,0:T(8,128)(2,1)}, bf16[128,768]{1,0:T(8,128)(2,1)S(1)}, u32[]{:S(2)}, u32[]{:S(2)}) collective-permute-start(bf16[128,768]{1,0:T(8,128)(2,1)} %get-tuple-element.394), channel_id=1, source_target_pairs={{0,16},{16,0},{1,17},{17,1},{2,18},{18,2},{3,19},{19,3},{4,20},{20... | collective-permute-start | bytes 589832 | tf_op jit(solution)/shard_map/ppermute | solution.py:731
  (88 other events, 368.6 us)
Sparse Core Ops, SparseCore 0:
  13.6 111.9 all-gather.4
  127.7 110.2 all-gather.6

commit v4 on v3

--- a/solution.py
+++ b/solution.py
@@ -16,7 +16,14 @@
 ROWS = 16
 VMEM = 44 << 20
 LESS = 24 << 20
-SMALL = pl.CostEstimate(flops=1024, bytes_accessed=1024, transcendentals=0)
+STEPS = (
+    "hidden", "ffn_in", "turn", "away_u", "away_d", "norm_two", "home_u", "home_d", "mixer", "away_r", "two_u",
+    "two_d", "home_r", "away_g", "conv_in", "fold_u", "fold_d", "home_g", "away_b", "away_o", "two_r", "home_b",
+    "home_o", "small", "settle_u", "two_g", "fold_r", "join_u", "settle_d", "two_o", "fold_g", "join_d", "down",
+    "two_b", "settle_r", "settle_g", "fold_o", "result", "fold_b", "join_r", "settle_o", "norm_one", "small_end",
+    "settle_b", "join_g", "join_o", "join_b",
+)
+HINT = pl.CostEstimate(flops=100000000000, bytes_accessed=1024, transcendentals=0)
 BF16 = jnp.bfloat16
 F32 = jnp.float32
 
@@ -185,7 +192,7 @@
             jax.ShapeDtypeStruct((3 * ROWS, width), F32), jax.ShapeDtypeStruct((tokens, width), F32), sent((tokens, width)),
         ],
         compiler_params=pltpu.CompilerParams(vmem_limit_bytes=VMEM),
-        cost_estimate=pl.CostEstimate(flops=660000000000, bytes_accessed=1024, transcendentals=0),
+        cost_estimate=HINT,
         name="chain_back",
     )(side, own, other, *[whole] * 5, pre, gates, gates, admitted, before, params)
 
@@ -250,7 +257,7 @@
         ],
         scratch_shapes=[pltpu.VMEM((tokens, depth), F32)],
         compiler_params=pltpu.CompilerParams(vmem_limit_bytes=VMEM),
-        cost_estimate=pl.CostEstimate(flops=300000000000, bytes_accessed=1024, transcendentals=0),
+        cost_estimate=HINT,
         name="conv_back",
     )(direct, near, far, pre, branch, taps, whole, whole)
 
@@ -275,7 +282,7 @@
         out_specs=[one, one],
         out_shape=[jax.ShapeDtypeStruct((rows, width), F32), sent((rows, width))],
         compiler_params=pltpu.CompilerParams(vmem_limit_bytes=LESS),
-        cost_estimate=pl.CostEstimate(flops=150000000000, bytes_accessed=1024, transcendentals=0),
+        cost_estimate=HINT,
         name="norm_back",
     )(near, far, base, v, jnp.broadcast_to(gain, (8, width)))
 
@@ -294,7 +301,7 @@
         out_specs=pl.BlockSpec((tile, tokens), lambda j: (j, 0)),
         out_shape=jax.ShapeDtypeStruct((n, tokens), BF16),
         compiler_params=pltpu.CompilerParams(vmem_limit_bytes=LESS),
-        cost_estimate=pl.CostEstimate(flops=150000000000, bytes_accessed=1024, transcendentals=0),
+        cost_estimate=HINT,
         name="flip",
     )(x)
 
@@ -320,7 +327,7 @@
         ),
         out_shape=jax.ShapeDtypeStruct((size // block, block), BF16),
         compiler_params=pltpu.CompilerParams(vmem_limit_bytes=LESS),
-        cost_estimate=pl.CostEstimate(flops=30000000000, bytes_accessed=1024, transcendentals=0),
+        cost_estimate=HINT,
         name="pack",
     )(side, *halves, full)
 
@@ -351,40 +358,37 @@
         ),
         out_shape=[jax.ShapeDtypeStruct((rows, 2 * n), F32)] * parts,
         compiler_params=pltpu.CompilerParams(vmem_limit_bytes=LESS),
-        cost_estimate=pl.CostEstimate(flops=36000000000, bytes_accessed=1024, transcendentals=0),
+        cost_estimate=HINT,
         name="join_columns",
     )(side, own, got)
 
 
-def rows_kernel(side_ref, own_a_ref, own_b_ref, got_a_ref, got_b_ref, out_ref):
-    n = own_a_ref.shape[1]
+def rows_kernel(side_ref, own_ref, got_ref, out_ref):
     mine = pl.program_id(0) == side_ref[0]
 
     @pl.when(mine)
     def _():
-        out_ref[:, :n] = own_a_ref[...]
-        out_ref[:, n:] = own_b_ref[...]
+        out_ref[...] = own_ref[...]
 
     @pl.when(jnp.logical_not(mine))
     def _():
-        out_ref[:, :n] = widen(got_a_ref[...])
-        out_ref[:, n:] = widen(got_b_ref[...])
-
-
-def join_rows(side, a, b):
-    rows, n = a[0].shape
+        out_ref[...] = widen(got_ref[...])
+
+
+def join_rows(side, own, got):
+    rows, n = own.shape
     full = pl.BlockSpec((rows, n), lambda h, s: (0, 0))
     return pl.pallas_call(
         rows_kernel,
         grid_spec=pltpu.PrefetchScalarGridSpec(
-            num_scalar_prefetch=1, grid=(2,), in_specs=[full] * 4,
-            out_specs=pl.BlockSpec((rows, 2 * n), lambda h, s: (h, 0)),
+            num_scalar_prefetch=1, grid=(2,), in_specs=[full] * 2,
+            out_specs=pl.BlockSpec((rows, n), lambda h, s: (h, 0)),
         ),
-        out_shape=jax.ShapeDtypeStruct((2 * rows, 2 * n), F32),
+        out_shape=jax.ShapeDtypeStruct((2 * rows, n), F32),
         compiler_params=pltpu.CompilerParams(vmem_limit_bytes=LESS),
-        cost_estimate=pl.CostEstimate(flops=36000000000, bytes_accessed=1024, transcendentals=0),
+        cost_estimate=HINT,
         name="join_rows",
-    )(side, a[0], b[0], a[1], b[1])
+    )(side, own, got)
 
 
 def weave_kernel(piece, side_ref, own_ref, got_ref, out_ref):
@@ -410,7 +414,7 @@
         ),
         out_shape=jax.ShapeDtypeStruct((rows, 2 * n), F32),
         compiler_params=pltpu.CompilerParams(vmem_limit_bytes=LESS),
-        cost_estimate=pl.CostEstimate(flops=90000000000, bytes_accessed=1024, transcendentals=0),
+        cost_estimate=HINT,
         name="weave",
     )(side, own, got)
 
@@ -469,7 +473,7 @@
             jax.ShapeDtypeStruct((tokens, n), F32), jax.ShapeDtypeStruct((tokens, n), F32),
         ],
         compiler_params=pltpu.CompilerParams(vmem_limit_bytes=VMEM),
-        cost_estimate=pl.CostEstimate(flops=420000000000, bytes_accessed=1024, transcendentals=0),
+        cost_estimate=HINT,
         name="hidden_pass",
     )(x, blocks, blocks)
 
@@ -545,7 +549,7 @@
         ],
         scratch_shapes=[pltpu.VMEM((tokens, depth), F32), pltpu.VMEM((tile, depth), BF16)],
         compiler_params=pltpu.CompilerParams(vmem_limit_bytes=VMEM),
-        cost_estimate=pl.CostEstimate(flops=690000000000, bytes_accessed=1024, transcendentals=0),
+        cost_estimate=HINT,
         name="ffn_back",
     )(cot, blocks, blocks, blocks, blocks, act, slope)
 
@@ -568,7 +572,7 @@
         ],
         scratch_shapes=[pltpu.VMEM((tokens, depth), F32), pltpu.VMEM((n // tiles, depth), BF16)],
         compiler_params=pltpu.CompilerParams(vmem_limit_bytes=VMEM),
-        cost_estimate=pl.CostEstimate(flops=270000000000, bytes_accessed=1024, transcendentals=0),
+        cost_estimate=HINT,
         name="down_pass",
     )(hidden, blocks, blocks)
 
@@ -623,7 +627,7 @@
         ),
         out_shape=sent((owners, rows, n)),
         compiler_params=pltpu.CompilerParams(vmem_limit_bytes=LESS),
-        cost_estimate=pl.CostEstimate(flops=105000000000, bytes_accessed=1024, transcendentals=0),
+        cost_estimate=HINT,
         name="grad_away",
     )(at, left, right)
 
@@ -650,7 +654,7 @@
             jax.ShapeDtypeStruct((high, low, rows, n), F32), sent((high, low, rows, n)),
         ],
         compiler_params=pltpu.CompilerParams(vmem_limit_bytes=LESS),
-        cost_estimate=pl.CostEstimate(flops=165000000000, bytes_accessed=1024, transcendentals=0),
+        cost_estimate=HINT,
         name="grad_home",
     )(at, left, right, got)
 
@@ -677,7 +681,7 @@
             jax.ShapeDtypeStruct((high, low, rows, n), F32), sent((high, low, rows, n)),
         ],
         compiler_params=pltpu.CompilerParams(vmem_limit_bytes=LESS),
-        cost_estimate=pl.CostEstimate(flops=75000000000, bytes_accessed=1024, transcendentals=0),
+        cost_estimate=HINT,
         name="fold",
     )(at, own.reshape(shape), got.reshape(shape))
 
@@ -699,7 +703,7 @@
         out_specs=[one, one],
         out_shape=[jax.ShapeDtypeStruct((rows, n), F32), sent((rows, n))],
         compiler_params=pltpu.CompilerParams(vmem_limit_bytes=LESS),
-        cost_estimate=pl.CostEstimate(flops=45000000000, bytes_accessed=1024, transcendentals=0),
+        cost_estimate=HINT,
         name="settle",
     )(own, got)
 
@@ -808,25 +812,6 @@
 
         def both(self):
             return tick(self.v, self.got)
-
-    class SmallScatter:
-        def __init__(self, v):
-            self.v = v
-
-        def start(self, bit):
-            v = self.v.reshape((-1, 2) + self.v.shape[1:]) if bit < bits else self.v
-            if bit == bits:
-                for k in range(1, groups // 2):
-                    self.v = self.v + lax.ppermute(v, "rep", [(i, (i + 2 * k) % groups) for i in range(groups)])
-                self.got = swap(self.v)
-                return
-            self.v = lax.dynamic_index_in_dim(v, (here >> bit) & 1, 1, False)
-            self.got = cross(lax.dynamic_index_in_dim(v, 1 - ((here >> bit) & 1), 1, False), bit)
-
-        def take(self):
-            v, got = tick(self.v, self.got)
-            self.v = v + got
-            tock(self.v)
 
     per_d, per_r = mix_gain.shape[0], conv_bias.shape[0]
     vectors = jnp.concatenate(
@@ -901,109 +886,149 @@
     ffn_blocks, = tick(ffn_blocks)
 
     ffn = dict(rows=per_d, tiles=tiles)
-    hidden, hidden_t, act, slope = hidden_pass(normed_two, ffn_blocks, **ffn)
-    tock(hidden, hidden_t)
-    down_a = Scatter(hidden_t, cot_pair, columns=width // 2)
-    down_b = Scatter(hidden_t, cot_pair, columns=width // 2, skip=1)
-    act, = tick(act)
-    gate_cot, up_cot, near, far = ffn_back(cot_pair, ffn_blocks, act, slope, piece=piece_f, **ffn)
-    tock(near, far)
-    far = swap(far)
-    down_a.home()
-    down_b.home()
-    normed_two, = tick(normed_two)
-    normed_two_t = flip(normed_two)
-    tock(normed_two_t)
-    gate_s = Scatter(normed_two_t, gate_cot)
-    near, far = tick(near, far)
-    middle_cot, middle_low = norm_back(near, far, cotangent, middle, gain_two)
-    tock(middle_cot, middle_low)
-    middle_other = swap(middle_low)
-    gate_s.home()
-    down_a.two()
-    up_s = Scatter(normed_two_t, up_cot)
-    middle_low, middle_other = tick(middle_low, middle_other)
-    branch_low, gates_cot, direct, sums, near, far = chain_back(
-        here_side, middle_low, middle_other, whole, at, per_r, pre, gates, admitted, before, params
-    )
-    tock(near, far)
-    far = swap(far)
-    down_b.two()
-    down_a.fold()
-    up_s.home()
-    down_b.fold()
-    near, far = tick(near, far)
-    pre_cot, conv_sums, near, far = conv_back(direct, near, far, pre, branch_low, channel, whole, per_d, width)
-    tock(near, far, pre_cot)
-    far = swap(far)
-    down_a.settle()
-    down_b.settle()
-    gate_s.two()
-    near, far = tick(near, far)
-    tokens_grad, _ = norm_back(near, far, middle_cot, tokens, gain_one)
-    tock(tokens_grad)
-    gates_s = Scatter(admitted_t, gates_cot, [2, 1] + list(range(3, bits)))
-    ffndown_grad = join_rows(here_side, down_a.both(), down_b.both())
-    tock(ffndown_grad)
-    sums = jnp.sum(sums.reshape(3, ROWS, half_r), axis=1)
-    small = jnp.concatenate(
-        [conv_sums[: taps + 1], sums[:2], sums[2:] * (DECAY_SCALE * jax.nn.sigmoid(-lam))]
-    )
-    small = natural(small, jnp.zeros_like(small))
-    small_s = SmallScatter(small.reshape(taps + 4, shards, per_r).transpose(1, 0, 2))
-    small_s.start(0)
-    hidden_late, = tick(hidden)
-    near, far = down_pass(hidden_late, ffn_blocks, width, piece=piece_f, **ffn)
-    tock(near, far)
-    far = swap(far)
-    small_s.take()
-    gates_s.home()
-    pre_s = Scatter(normed_t, pre_cot)
-    gate_s.fold()
-    near, far = tick(near, far)
-    block_out = (middle + near + widen(far)).astype(BF16)
-    tock(block_out)
-    small_s.start(1)
-    up_s.two()
-    pre_s.home()
-    out_s = Scatter(mixed_t, jnp.concatenate([middle_low, middle_other], axis=0), columns=width // 2, skip=-1)
-    gate_s.settle()
-    up_s.fold()
-    ffngate_grad = weave(here_side, *gate_s.both(), piece_f)
-    tock(ffngate_grad)
-    small_s.take()
-    for bit in range(2, bits - 1):
-        small_s.start(bit)
-        small_s.take()
-    out_s.home()
-    gates_s.two()
-    small_s.start(bits - 1)
-    up_s.settle()
-    pre_s.two()
-    ffnup_grad = weave(here_side, *up_s.both(), piece_f)
-    tock(ffnup_grad)
-    small_s.take()
-    out_s.two()
-    small_s.start(bits)
-    ffngain_grad = jnp.sum(ffngate_grad * widen(ffn_gate) + ffnup_grad * widen(ffn_up), axis=1) / widen(ffn_gain)
-    pre_s.fold()
-    gates_s.fold()
-    out_s.fold()
-    pre_s.settle()
-    small_s.take()
-    small = small_s.v.reshape(taps + 4, per_r)
-    gates_s.settle()
-    branch_grad, lruin_grad = join_columns(here_side, *pre_s.both(), 2)
-    tock(branch_grad)
-    out_s.settle()
-    recur_grad, admit_grad = join_columns(here_side, *gates_s.both(), 2)
-    tock(recur_grad)
-    outproj_grad, = join_columns(here_side, *out_s.both(), 1)
+    have, grads, steps = {}, {}, {}
+
+    def step(run):
+        steps[run.__name__] = run
+        return run
+
+    @step
+    def hidden():
+        x, = tick(normed_two)
+        have["hidden"], have["hidden_t"], have["act"], have["slope"] = hidden_pass(x, ffn_blocks, **ffn)
+        tock(have["hidden"], have["hidden_t"])
+
+    @step
+    def ffn_in():
+        act, = tick(have["act"])
+        have["gate_cot"], have["up_cot"], near, far = ffn_back(
+            cot_pair, ffn_blocks, act, have["slope"], piece=piece_f, **ffn
+        )
+        tock(near, far)
+        have["ffn"] = near, swap(far)
+
+    @step
+    def turn():
+        x, = tick(normed_two)
+        have["normed_two_t"] = flip(x)
+        tock(have["normed_two_t"])
+
+    @step
+    def norm_two():
+        near, far = tick(*have["ffn"])
+        have["middle_cot"], low = norm_back(near, far, cotangent, middle, gain_two)
+        tock(have["middle_cot"], low)
+        have["middle_low"] = low, swap(low)
+
+    @step
+    def mixer():
+        low, other = tick(*have["middle_low"])
+        have["branch_low"], have["gates_cot"], have["direct"], have["sums"], near, far = chain_back(
+            here_side, low, other, whole, at, per_r, pre, gates, admitted, before, params
+        )
+        have["out_cot"] = jnp.concatenate([low, other], axis=0)
+        tock(near, far)
+        have["admitted"] = near, swap(far)
+
+    @step
+    def conv_in():
+        direct, near, far = tick(have["direct"], *have["admitted"])
+        have["pre_cot"], have["conv_sums"], near, far = conv_back(
+            direct, near, far, pre, have["branch_low"], channel, whole, per_d, width
+        )
+        tock(near, far, have["pre_cot"])
+        have["normed"] = near, swap(far)
+
+    @step
+    def norm_one():
+        near, far = tick(*have["normed"])
+        have["tokens_grad"], _ = norm_back(near, far, have["middle_cot"], tokens, gain_one)
+        tock(have["tokens_grad"])
+
+    @step
+    def down():
+        x, = tick(have["hidden"])
+        near, far = down_pass(x, ffn_blocks, width, piece=piece_f, **ffn)
+        tock(near, far)
+        have["down"] = near, swap(far)
+
+    @step
+    def result():
+        near, far = tick(*have["down"])
+        have["block_out"] = (middle + near + widen(far)).astype(BF16)
+        tock(have["block_out"])
+
+    @step
+    def small():
+        conv_sums, sums = tick(have["conv_sums"], have["sums"])
+        sums = jnp.sum(sums.reshape(3, ROWS, half_r), axis=1)
+        v = jnp.concatenate([conv_sums[: taps + 1], sums[:2], sums[2:] * (DECAY_SCALE * jax.nn.sigmoid(-lam))])
+        v = natural(v, jnp.zeros_like(v))
+        tock(v)
+        have["small"] = lax.psum(v, ("rep", "shard"))
+
+    @step
+    def small_end():
+        v, = tick(have["small"])
+        have["small"] = lax.dynamic_slice_in_dim(v, here * per_r, per_r, 1)
+        tock(have["small"])
+
+    def late(name, left, right, order=None, **span):
+        def away():
+            grads[name] = Scatter(left(), right(), order, **span)
+
+        steps["away_" + name] = away
+        for stage in ("home", "two", "fold", "settle"):
+            steps[stage + "_" + name] = lambda stage=stage: getattr(grads[name], stage)()
+
+    z_first = [2, 1] + list(range(3, bits))
+    late("d", lambda: have["hidden_t"], lambda: cot_pair)
+    late("g", lambda: have["normed_two_t"], lambda: have["gate_cot"])
+    late("u", lambda: have["normed_two_t"], lambda: have["up_cot"], z_first)
+    late("r", lambda: admitted_t, lambda: have["gates_cot"])
+    late("b", lambda: normed_t, lambda: have["pre_cot"])
+    late("o", lambda: mixed_t, lambda: have["out_cot"], columns=width // 2, skip=-1)
+
+    @step
+    def join_d():
+        v, got = grads["d"].both()
+        have["d"] = join_rows(here_side, v, got)
+        tock(have["d"])
+
+    @step
+    def join_g():
+        have["g"] = weave(here_side, *grads["g"].both(), piece_f)
+        tock(have["g"])
+
+    @step
+    def join_u():
+        have["u"] = weave(here_side, *grads["u"].both(), piece_f)
+        tock(have["u"])
+
+    @step
+    def join_r():
+        have["r"] = join_columns(here_side, *grads["r"].both(), 2)
+        tock(*have["r"])
+
+    @step
+    def join_b():
+        have["b"] = join_columns(here_side, *grads["b"].both(), 2)
+        tock(*have["b"])
+
+    @step
+    def join_o():
+        have["o"], = join_columns(here_side, *grads["o"].both(), 1)
+        tock(have["o"])
+
+    for name in STEPS:
+        steps[name]()
+    small_grad, (branch_grad, lruin_grad) = have["small"], have["b"]
+    ffngain_grad = jnp.sum(have["g"] * widen(ffn_gate) + have["u"] * widen(ffn_up), axis=1) / widen(ffn_gain)
     mixgain_grad = jnp.sum(branch_grad * widen(branch_proj) + lruin_grad * widen(lruin_proj), axis=1) / widen(mix_gain)
     return (
-        block_out, tokens_grad, mixgain_grad, branch_grad, lruin_grad, small[:taps], small[taps], recur_grad,
-        small[taps + 1], admit_grad, small[taps + 2], small[taps + 3], outproj_grad, ffngain_grad, ffngate_grad,
-        ffnup_grad, ffndown_grad,
+        have["block_out"], have["tokens_grad"], mixgain_grad, branch_grad, lruin_grad, small_grad[:taps],
+        small_grad[taps], have["r"][0], small_grad[taps + 1], have["r"][1], small_grad[taps + 2],
+        small_grad[taps + 3], have["o"], ffngain_grad, have["g"], have["u"], have["d"],
     )
 
 

time: 661 us -> 613 us (0.927); the launches traced: 650 us -> 609 us
  starting transfers between devices: 53.4 us -> 39.6 us
  other arithmetic: 20.8 us -> 11.6 us
    ppermute x32 -> x24, waiting for transfers between devices: 93.5 us -> 80.3 us  [cross(): return lax.ppermute(v, 'shard', [(i, i ^ 1 << bit) for i in range(shards)])]
    ppermute x32 -> x24, starting transfers between devices: 29.9 us -> 19.4 us  [cross(): return lax.ppermute(v, 'shard', [(i, i ^ 1 << bit) for i in range(shards)])]
    ppermute x19 -> x17, waiting for transfers between devices: 70.1 us -> 79.3 us  [swap(): return lax.ppermute(v, 'rep', [(i, i ^ 1) for i in range(groups)])]
    pallas_call x14 -> x12, Pallas kernels: 42 us -> 36.9 us  [fold(): pl.pallas_call(functools.partial(fold_kernel, bit), grid_spec=pltpu.Prefe...]
    ppermute x19 -> x17, starting transfers between devices: 23.4 us -> 20.1 us  [swap(): return lax.ppermute(v, 'rep', [(i, i ^ 1) for i in range(groups)])]
    pallas_call x7 -> x6, Pallas kernels: 37.9 us -> 34.7 us  [grad_home(): pl.pallas_call(functools.partial(home_kernel, bit), grid_spec=pltpu.Prefe...]
    pallas_call x7 -> x6, Pallas kernels: 25.8 us -> 24.4 us  [grad_away(): pl.pallas_call(away_kernel, grid_spec=pltpu.PrefetchScalarGridSpec(num_sc...]
    pallas_call x7 -> x6, Pallas kernels: 13.1 us -> 13.4 us  [settle(): pl.pallas_call(settle_kernel, grid=(n // tile,), in_specs=[one, one], out...]
  transfers between devices with their start and end apart: 53 -> 44, of which waited for: 21 -> 19; matrix products, arithmetic and copies ran while one was open for 11% -> 8% of each run, Pallas kernels for 33% -> 30%
where the time goes in v4:
time: 613 us; the launch traced here: 609 us
  waiting for transfers between devices  236 us (38%)
  Pallas kernels  225 us (37%)
  local copies, waits for them, and re-layouts  46.6 us (8%)
  starting transfers between devices  39.6 us (6%)
  blocking collectives  23.2 us (4%)
  between operations  14.8 us (2%)
  matrix products  11.9 us (2%)
  other arithmetic  11.6 us (2%)
    ppermute x24, waiting for transfers between devices, cross(): return lax.ppermute(v, 'shard', [(i, i ^ 1 << bit) for i in range(shards)])  80.3 us
    ppermute x17, waiting for transfers between devices, swap(): return lax.ppermute(v, 'rep', [(i, i ^ 1) for i in range(groups)])  79.3 us
    all_gather x1, waiting for transfers between devices, body(): lax.all_gather(pack(here_side, [branch_proj, lruin_proj, recur_proj, admi...  59.6 us
    pallas_call x12, Pallas kernels, fold(): pl.pallas_call(functools.partial(fold_kernel, bit), grid_spec=pltpu.Prefe...  36.9 us
    pallas_call x6, Pallas kernels, grad_home(): pl.pallas_call(functools.partial(home_kernel, bit), grid_spec=pltpu.Prefe...  34.7 us
    unnamed x185, local copies, waits for them, and re-layouts  27.1 us
    pallas_call x6, Pallas kernels, grad_away(): pl.pallas_call(away_kernel, grid_spec=pltpu.PrefetchScalarGridSpec(num_sc...  24.4 us
    pallas_call x1, Pallas kernels, ffn_back(): pl.pallas_call(ffn_back_kernel, grid=(tiles,), in_specs=[pl.BlockSpec((to...  23.7 us
  transfers between devices with their start and end apart: 44, of which 19 were waited for; matrix products, arithmetic and copies ran while one was open for 8% of the time, Pallas kernels for 30%

profile of v4, /device:TPU:0, one launch (start us, length us, event | category | flops | bytes accessed | tf_op | source)
XLA Modules:
  0.0 608.9 jit_solution(3417344272225973779)
XLA Ops:
  24.7 3.0 collective-permute-start
  27.9 23.2 %all_gather.15 = bf16[16,10,128]{2,1,0:T(8,128)(2,1)S(1)} all-gather(bf16[1,10,128]{2,1,0:T(8,128)(2,1)S(1)} %pad_bitcast_fusion), channel_id=1, replica_groups=mesh['rep'=2,'shard'=16] {'shard'}, dimensions={0}, use_global_device_ids=true | all-gather | bytes 43520 | tf_op jit(solution)/shard_map/all_gather | solution.py:822
  52.0 10.2 %collective-permute-done.1 = bf16[256,1536]{1,0:T(8,128)(2,1)S(1)} collective-permute-done((bf16[256,1536]{1,0:T(8,128)(2,1)S(1)}, bf16[256,1536]{1,0:T(8,128)(2,1)S(1)}, u32[]{:S(2)}, u32[]{:S(2)}) %collective-permute-start.1) | collective-permute-done | bytes 786464 | tf_op jit(solution)/shard_map/ppermute | solution.py:735
  66.0 59.6 %all-gather.5.cloned.1.call-done = bf16[20480,512]{1,0:T(8,128)(2,1)} async-done(((bf16[1280,512]{1,0:T(8,128)(2,1)}), bf16[20480,512]{1,0:T(8,128)(2,1)}) %all-gather.5.cloned.1.call-update) | async-done | bytes 20971536 | tf_op jit(solution)/shard_map/all_gather | solution.py:845
  125.6 3.2 fusion.45
  128.8 3.4 fusion.8.pre_ref.lru_ref
  137.7 8.3 %fusion.44 = (bf16[16,128,512]{2,1,0:T(8,128)(2,1)S(1)}, bf16[16,128,512]{2,1,0:T(8,128)(2,1)}, bf16[16,128,512]{2,1,0:T(8,128)(2,1)}, bf16[16,128,512]{2,1,0:T(...) fusion(bf16[16,1280,512]{2,1,0:T(8,128)(2,1)} %bitcast.151), kind=kLoop, calls=%fused_computation.96 | loop fusion | bytes 29360128 | tf_op jit(solution)/shard_map/slice | solution.py:841
  146.1 14.6 %collective-permute-done.2 = bf16[512,1024]{1,0:T(8,128)(2,1)S(1)} collective-permute-done((bf16[512,1024]{1,0:T(8,128)(2,1)S(1)}, bf16[512,1024]{1,0:T(8,128)(2,1)S(1)}, u32[]{:S(2)}, u32[]{:S(2)}) %collective-permute-start.2) | collective-permute-done | bytes 1048608 | tf_op jit(solution)/shard_map/ppermute | solution.py:735
  161.4 6.6 %fusion.gates_r_ref.gates_i_ref = f32[512,2048]{1,0:T(8,128)} fusion(bf16[2048,512]{1,0:T(8,128)(2,1)S(1)} %bitcast.168, bf16[2048,512]{1,0:T(8,128)(2,1)S(1)} %bitcast.169, bf16[2048,512]{1,0:T(8,128)(2,1)S(1)} %bitcast.170, bf16[2048,512]{1,0:T(8,128)(2,1)S(1)} %bitcast.167, bf16[512,1024]{1,0:T(8,128)(2,1)S(1)} %get-tuple-element.365, ...), kind=kOutput, calls=%fused_computation | convolution fusion | flops 4332716032 | bytes 14680064 | tf_op jit(solution)/shard_map/dot_general | solution.py:36
  168.0 8.6 %recurrence_forward.1 = (bf16[512,1024]{1,0:T(8,128)(2,1)}, f32[512,1024]{1,0:T(8,128)}) custom-call(f32[512,2048]{1,0:T(8,128)} %copy-done.60, f32[512,2048]{1,0:T(8,128)} %fusion.gates_r_ref.gates_i_ref, f32[512,2048]{1,0:T(8,128)} %fusion.gates_r_ref.gates_i_ref, bf16[512,1024]{1,0:T(8,128)(2,1)} %bitcast.109, f32[8,1024]{1,0:T(8,128)} %maximum_maximum_fusion.1.params_ref), custom_call_target="tpu_custom_call" | custom-call | flops 31457280 | bytes 10485760 | tf_op jit(solution)/shard_map/recurrence_forward/pallas_call | solution.py:429
  180.9 10.4 %collective-permute-done.3 = bf16[256,1024]{1,0:T(8,128)(2,1)S(1)} collective-permute-done((bf16[256,1024]{1,0:T(8,128)(2,1)S(1)}, bf16[256,1024]{1,0:T(8,128)(2,1)S(1)}, u32[]{:S(2)}, u32[]{:S(2)}) %collective-permute-start.3) | collective-permute-done | bytes 524320 | tf_op jit(solution)/shard_map/ppermute | solution.py:735
  195.7 10.6 %collective-permute-done.5 = bf16[256,1024]{1,0:T(8,128)(2,1)S(1)} collective-permute-done((bf16[256,1024]{1,0:T(8,128)(2,1)S(1)}, bf16[256,1024]{1,0:T(8,128)(2,1)S(1)}, u32[]{:S(2)}, u32[]{:S(2)}) %collective-permute-start.5) | collective-permute-done | bytes 524320 | tf_op jit(solution)/shard_map/ppermute | solution.py:735
  209.5 11.4 %collective-permute-done.4 = bf16[256,1536]{1,0:T(8,128)(2,1)S(1)} collective-permute-done((bf16[256,1536]{1,0:T(8,128)(2,1)S(1)}, bf16[256,1536]{1,0:T(8,128)(2,1)S(1)}, u32[]{:S(2)}, u32[]{:S(2)}) %collective-permute-start.4) | collective-permute-done | bytes 786464 | tf_op jit(solution)/shard_map/ppermute | solution.py:735
  221.0 17.0 %all-gather.7.cloned.1.call-done = bf16[13824,768]{1,0:T(8,128)(2,1)} async-done(((bf16[864,768]{1,0:T(8,128)(2,1)}), bf16[13824,768]{1,0:T(8,128)(2,1)}) %all-gather.7.cloned.1.call-update) | async-done | bytes 21233680 | tf_op jit(solution)/shard_map/all_gather | solution.py:837
  238.1 13.4 %hidden_pass.1 = (bf16[512,2304]{1,0:T(8,128)(2,1)S(1)}, bf16[2304,512]{1,0:T(8,128)(2,1)S(1)}, f32[512,2304]{1,0:T(8,128)}, f32[512,2304]{1,0:T(8,128)}) custom-call(bf16[512,1536]{1,0:T(8,128)(2,1)S(1)} %pad_maximum_fusion.2.x_ref, bf16[16,864,768]{2,1,0:T(8,128)(2,1)} %bitcast.185, bf16[16,864,768]{2,1,0:T(8,128)(2,1)} %bitcast.186), custom_call_target="tpu_custom_call" | custom-call | flops 99999997952 | bytes 1024 | tf_op jit(solution)/shard_map/hidden_pass/pallas_call | solution.py:462
  253.0 23.7 %ffn_back.1 = (bf16[512,2304]{1,0:T(8,128)(2,1)S(1)}, bf16[512,2304]{1,0:T(8,128)(2,1)S(1)}, f32[256,1536]{1,0:T(8,128)S(1)}, bf16[256,1536]{1,0:T(8,128)(2,1)}) custom-call(bf16[512,1536]{1,0:T(8,128)(2,1)S(1)} %copy-done.16, bf16[16,864,768]{2,1,0:T(8,128)(2,1)} %bitcast.187, bf16[16,864,768]{2,1,0:T(8,128)(2,1)} %bitcast.188, ...), custom_call_target="tpu_custom_call" | custom-call | flops 99999997952 | bytes 1024 | tf_op jit(solution)/shard_map/ffn_back/pallas_call | solution.py:535
  279.2 4.6 grad_away.6
  283.8 4.3 grad_away.7
  288.5 8.2 %collective-permute-done.8.far_ref = bf16[256,1536]{1,0:T(8,128)(2,1)} collective-permute-done((bf16[256,1536]{1,0:T(8,128)(2,1)}, bf16[256,1536]{1,0:T(8,128)(2,1)}, u32[]{:S(2)}, u32[]{:S(2)}) %collective-permute-start.8) | collective-permute-done | bytes 786464 | tf_op jit(solution)/shard_map/ppermute | solution.py:735
  296.7 3.6 norm_back.2
  301.9 6.2 %grad_home.6 = (f32[2,2,96,2304]{3,2,1,0:T(8,128)S(1)}, bf16[2,2,96,2304]{3,2,1,0:T(8,128)(2,1)}) custom-call(s32[5]{0:T(128)S(1)} %stack.24.at_ref, bf16[8,2,96,512]{3,2,1,0:T(8,128)(2,1)S(1)} %bitcast.138, bf16[1,512,2304]{2,1,0:T(8,128)(2,1)S(1)} %bitcast.126, bf16[8,96,2304]{2,1,0:T(8,128)(2,1)} %collective-permute-done.7.got_ref), custom_call_target="tpu_custom_call" | custom-call | flops 99999997952 | bytes 1024 | tf_op jit(solution)/shard_map/grad_home/pallas_call | solution.py:640
  309.6 6.0 grad_home.7
  319.6 22.2 %chain_back.1 = (bf16[512,1024]{1,0:T(8,128)(2,1)S(1)}, bf16[2,512,1024]{2,1,0:T(8,128)(2,1)S(1)}, f32[512,1024]{1,0:T(8,128)S(1)}, f32[48,1024]{1,0:T(8,128)S(1...) custom-call(s32[1]{0:T(128)} %bitcast.2.side_ref, bf16[256,1536]{1,0:T(8,128)(2,1)S(1)} %copy-done.10, ...), custom_call_target="tpu_custom_call" | custom-call | flops 99999997952 | bytes 1024 | tf_op jit(solution)/shard_map/chain_back/pallas_call | solution.py:166
  343.3 4.5 grad_away.8
  349.2 4.3 fold.12
  353.4 3.7 collective-permute-done.9
  358.4 3.2 fold.13
  363.3 6.7 %grad_home.8 = (f32[4,1,128,2048]{3,2,1,0:T(8,128)S(1)}, bf16[4,1,128,2048]{3,2,1,0:T(8,128)(2,1)}) custom-call(s32[5]{0:T(128)S(1)} %stack.24.at_ref, bf16[8,2,128,512]{3,2,1,0:T(8,128)(2,1)S(1)} %bitcast.130, bf16[2,512,1024]{2,1,0:T(8,128)(2,1)S(1)} %get-tuple-element.234.right_ref, bf16[8,128,2048]{2,1,0:T(8,128)(2,1)} %collective-permute-done.15.got_ref), custom_call_target="tpu_custom_call" | custom-call | flops 99999997952 | bytes 1024 | tf_op jit(solution)/shard_map/grad_home/pallas_call | solution.py:640
  370.9 4.5 grad_away.9
  375.4 9.3 %conv_back.1 = (bf16[2,512,1024]{2,1,0:T(8,128)(2,1)S(1)}, f32[8,1024]{1,0:T(8,128)S(1)}, f32[256,1536]{1,0:T(8,128)S(1)}, bf16[256,1536]{1,0:T(8,128)(2,1)}) custom-call(f32[512,1024]{1,0:T(8,128)S(1)} %copy-done.51, f32[512,1024]{1,0:T(8,128)S(1)} %copy-done.53, bf16[512,1024]{1,0:T(8,128)(2,1)} %collective-permute-done.14.far_in_ref, ...), custom_call_target="tpu_custom_call" | custom-call | flops 99999997952 | bytes 1024 | tf_op jit(solution)/shard_map/conv_back/pallas_call | solution.py:242
  386.9 3.4 fold.14
  390.3 2.4 collective-permute-start.17
  392.7 3.3 fold.15
  396.6 6.2 %grad_home.9 = (f32[4,1,96,2304]{3,2,1,0:T(8,128)S(1)}, bf16[4,1,96,2304]{3,2,1,0:T(8,128)(2,1)}) custom-call(s32[5]{0:T(128)S(1)} %stack.24.at_ref, bf16[8,2,96,512]{3,2,1,0:T(8,128)(2,1)S(1)} %bitcast.140, bf16[1,512,2304]{2,1,0:T(8,128)(2,1)S(1)} %bitcast.122, bf16[8,96,2304]{2,1,0:T(8,128)(2,1)} %collective-permute-done.18.got_ref), custom_call_target="tpu_custom_call" | custom-call | flops 99999997952 | bytes 1024 | tf_op jit(solution)/shard_map/grad_home/pallas_call | solution.py:640
  402.8 3.8 grad_away.10
  406.6 2.7 grad_away.11
  409.3 12.6 %collective-permute-done.21 = bf16[4,1,128,2048]{3,2,1,0:T(8,128)(2,1)} collective-permute-done((bf16[4,1,128,2048]{3,2,1,0:T(8,128)(2,1)}, bf16[4,1,128,2048]{3,2,1,0:T(8,128)(2,1)}, u32[]{:S(2)}, u32[]{:S(2)}) %collective-permute-start.21) | collective-permute-done | bytes 2097184 | tf_op jit(solution)/shard_map/ppermute | solution.py:767
  421.9 3.3 fold.16
  427.8 5.5 grad_home.10
  433.8 4.1 grad_home.11
  440.7 2.9 settle.6
  443.6 24.9 %collective-permute-done.24 = bf16[4,1,96,2304]{3,2,1,0:T(8,128)(2,1)} collective-permute-done((bf16[4,1,96,2304]{3,2,1,0:T(8,128)(2,1)}, bf16[4,1,96,2304]{3,2,1,0:T(8,128)(2,1)}, u32[]{:S(2)}, u32[]{:S(2)}) %collective-permute-start.24) | collective-permute-done | bytes 1769504 | tf_op jit(solution)/shard_map/ppermute | solution.py:767
  469.3 4.0 fold.17
  474.5 2.7 fold.18
  477.2 3.2 collective-permute-done.22.got_ref
  480.4 2.4 collective-permute-start.31
  482.8 2.8 weave.2
  489.0 2.6 fold.19
  491.6 25.7 %collective-permute-done.26 = bf16[2,1,96,2304]{3,2,0,1:T(8,128)(2,1)} collective-permute-done((bf16[2,1,96,2304]{3,2,0,1:T(8,128)(2,1)}, bf16[2,1,96,2304]{3,2,0,1:T(8,128)(2,1)}, u32[]{:S(2)}, u32[]{:S(2)}) %collective-permute-start.26) | collective-permute-done | bytes 884768 | tf_op jit(solution)/shard_map/ppermute | solution.py:767
  517.3 3.4 fold.20
  521.1 2.4 join_rows.1
  523.5 9.8 %down_pass.1 = (f32[256,1536]{1,0:T(8,128)S(1)}, bf16[256,1536]{1,0:T(8,128)(2,1)}) custom-call(bf16[512,2304]{1,0:T(8,128)(2,1)S(1)} %copy-done.55, bf16[16,864,768]{2,1,0:T(8,128)(2,1)} %bitcast.191, bf16[16,864,768]{2,1,0:T(8,128)(2,1)} %bitcast.192), custom_call_target="tpu_custom_call" | custom-call | flops 99999997952 | bytes 1024 | tf_op jit(solution)/shard_map/down_pass/pallas_call | solution.py:565
  534.0 3.0 fold.21
  541.2 2.8 settle.9
  545.6 2.3 fold.22
  547.9 6.4 %collective-permute-done.28 = bf16[256,1536]{1,0:T(8,128)(2,1)} collective-permute-done((bf16[256,1536]{1,0:T(8,128)(2,1)}, bf16[256,1536]{1,0:T(8,128)(2,1)}, u32[]{:S(2)}, u32[]{:S(2)}) %collective-permute-start.28) | collective-permute-done | bytes 786464 | tf_op jit(solution)/shard_map/ppermute | solution.py:735
  554.3 2.6 collective-permute-start.34
  556.9 2.4 add_convert_fusion
  559.2 7.2 %collective-permute-done.36 = bf16[2,1,96,2048]{3,2,0,1:T(8,128)(2,1)S(1)} collective-permute-done((bf16[2,1,96,2048]{3,2,0,1:T(8,128)(2,1)S(1)}, bf16[2,1,96,2048]{3,2,0,1:T(8,128)(2,1)S(1)}, u32[]{:S(2)}, u32[]{:S(2)}) %collective-permute-start.36) | collective-permute-done | bytes 786464 | tf_op jit(solution)/shard_map/ppermute | solution.py:767
  568.1 2.4 join_columns.3
  573.6 3.9 norm_back.3
  579.3 5.3 collective-permute-done.37
  587.6 2.8 weave.3
  594.6 3.3 collective-permute-done.38.got_ref
  (321 shorter events, 96.8 us)
Async XLA Ops:
  7.2 118.4 %all-gather.5.cloned.1.call-start = ((), (), s32[]{:S(2)}) async-start(), calls=%async_computation.1 | async-start | bytes 22282240 | tf_op jit(solution)/shard_map/all_gather | solution.py:845
  13.5 224.6 %all-gather.7.cloned.1.call-start = ((), (), s32[]{:S(2)}) async-start(), calls=%async_computation.2 | async-start | bytes 22560768 | tf_op jit(solution)/shard_map/all_gather | solution.py:837
  24.6 552.9 %all-reduce.6.cloned.1.call-start = ((), (), s32[]{:S(2)}) async-start(), calls=%async_computation | async-start | bytes 131072 | tf_op jit(solution)/shard_map/psum | solution.py:968
  24.7 26.9 %collective-permute-start = (bf16[256,1536]{1,0:T(8,128)(2,1)S(1)}, bf16[256,1536]{1,0:T(8,128)(2,1)S(1)}, u32[]{:S(2)}, u32[]{:S(2)}) collective-permute-start(bf16[256,1536]{1,0:T(8,128)(2,1)S(1)} %copy-done.5), channel_id=1, source_target_pairs={{0,16},{16,0},{1,17},{17,1},{2,18},{18,2},{3,19},{19,3},{4,20},{20... | collective-permute-start | bytes 2359304 | tf_op jit(solution)/shard_map/ppermute | solution.py:735
  27.7 34.5 %collective-permute-start.1 = (bf16[256,1536]{1,0:T(8,128)(2,1)S(1)}, bf16[256,1536]{1,0:T(8,128)(2,1)S(1)}, u32[]{:S(2)}, u32[]{:S(2)}) collective-permute-start(bf16[256,1536]{1,0:T(8,128)(2,1)S(1)} %copy-done.8), channel_id=1, source_target_pairs={{0,16},{16,0},{1,17},{17,1},{2,18},{18,2},{3,19},{19,3},{4,20},{20... | collective-permute-start | bytes 2359304 | tf_op jit(solution)/shard_map/ppermute | solution.py:735
  51.3 10.9 %copy-start.72 = (f32[1536]{0:T(1024)}, f32[1536]{0:T(1024)S(1)}, u32[]{:S(2)}) copy-start(f32[1536]{0:T(1024)S(1)} %reshape.324) | copy-start | bytes 18436
  135.3 25.5 %copy-start = (bf16[2,256,1024]{2,1,0:T(8,128)(2,1)}, bf16[2,256,1024]{2,1,0:T(8,128)(2,1)S(1)}, u32[]{:S(2)}) copy-start(bf16[2,256,1024]{2,1,0:T(8,128)(2,1)S(1)} %fusion.32) | copy-start | bytes 3145732
  135.3 25.4 %collective-permute-start.2 = (bf16[512,1024]{1,0:T(8,128)(2,1)S(1)}, bf16[512,1024]{1,0:T(8,128)(2,1)S(1)}, u32[]{:S(2)}, u32[]{:S(2)}) collective-permute-start(bf16[512,1024]{1,0:T(8,128)(2,1)S(1)} %bitcast.108), channel_id=1, source_target_pairs={{0,16},{16,0},{1,17},{17,1},{2,18},{18,2},{3,19},{19,3},{4,20},{20... | collective-permute-start | bytes 3145736 | tf_op jit(solution)/shard_map/ppermute | solution.py:735
  136.9 58.0 %copy-start.74 = (f32[1536]{0:T(1024)}, f32[1536]{0:T(1024)S(1)}, u32[]{:S(2)}) copy-start(f32[1536]{0:T(1024)S(1)} %reshape.325) | copy-start | bytes 18436
  177.9 13.5 %copy-start.71 = (bf16[512,1024]{1,0:T(8,128)(2,1)S(1)}, bf16[512,1024]{1,0:T(8,128)(2,1)}, u32[]{:S(2)}) copy-start(bf16[512,1024]{1,0:T(8,128)(2,1)} %get-tuple-element.186) | copy-start | bytes 3145732
  177.9 13.4 %collective-permute-start.3 = (bf16[256,1024]{1,0:T(8,128)(2,1)S(1)}, bf16[256,1024]{1,0:T(8,128)(2,1)S(1)}, u32[]{:S(2)}, u32[]{:S(2)}) collective-permute-start(bf16[256,1024]{1,0:T(8,128)(2,1)S(1)} %slice.172), channel_id=1, source_target_pairs={{0,16},{16,0},{1,17},{17,1},{2,18},{18,2},{3,19},{19,3},{4,20},{20... | collective-permute-start | bytes 1572872 | tf_op jit(solution)/shard_map/ppermute | solution.py:735
  179.4 13.6 %copy-start.65 = (bf16[16,128,512]{2,1,0:T(8,128)(2,1)S(1)}, bf16[16,128,512]{2,1,0:T(8,128)(2,1)}, u32[]{:S(2)}) copy-start(bf16[16,128,512]{2,1,0:T(8,128)(2,1)} %get-tuple-element.354) | copy-start | bytes 6291460
  179.4 13.6 %copy-start.66 = (bf16[16,128,512]{2,1,0:T(8,128)(2,1)S(1)}, bf16[16,128,512]{2,1,0:T(8,128)(2,1)}, u32[]{:S(2)}) copy-start(bf16[16,128,512]{2,1,0:T(8,128)(2,1)} %get-tuple-element.355) | copy-start | bytes 6291460
  179.4 13.6 %copy-start.67 = (bf16[16,128,512]{2,1,0:T(8,128)(2,1)S(1)}, bf16[16,128,512]{2,1,0:T(8,128)(2,1)}, u32[]{:S(2)}) copy-start(bf16[16,128,512]{2,1,0:T(8,128)(2,1)} %get-tuple-element.356) | copy-start | bytes 6291460
  180.9 12.1 %copy-start.34 = (bf16[2048,512]{1,0:T(8,128)(2,1)}, bf16[2048,512]{1,0:T(8,128)(2,1)S(1)}, u32[]{:S(2)}) copy-start(bf16[2048,512]{1,0:T(8,128)(2,1)S(1)} %flip.5) | copy-start | bytes 6291460
  180.9 12.1 %copy-start.6 = (bf16[256,1536]{1,0:T(8,128)(2,1)S(1)}, bf16[256,1536]{1,0:T(8,128)(2,1)}, u32[]{:S(2)}) copy-start(bf16[256,1536]{1,0:T(8,128)(2,1)} %v_ref.1) | copy-start | bytes 2359300
  191.4 14.9 %collective-permute-start.5 = (bf16[256,1024]{1,0:T(8,128)(2,1)S(1)}, bf16[256,1024]{1,0:T(8,128)(2,1)S(1)}, u32[]{:S(2)}, u32[]{:S(2)}) collective-permute-start(bf16[256,1024]{1,0:T(8,128)(2,1)S(1)} %get-tuple-element.370), channel_id=1, source_target_pairs={{0,16},{16,0},{1,17},{17,1},{2,18},{18,2},{3,19},{19,3},{4,20},{20... | collective-permute-start | bytes 1572872 | tf_op jit(solution)/shard_map/ppermute | solution.py:735
  194.9 11.6 %copy-start.2 = (f32[256,1536]{1,0:T(8,128)}, f32[256,1536]{1,0:T(8,128)S(1)}, u32[]{:S(2)}) copy-start(f32[256,1536]{1,0:T(8,128)S(1)} %get-tuple-element.394.v_ref) | copy-start | bytes 4718596
  195.1 25.8 %collective-permute-start.4 = (bf16[256,1536]{1,0:T(8,128)(2,1)S(1)}, bf16[256,1536]{1,0:T(8,128)(2,1)S(1)}, u32[]{:S(2)}, u32[]{:S(2)}) collective-permute-start(bf16[256,1536]{1,0:T(8,128)(2,1)S(1)} %multiply_convert_fusion), channel_id=1, source_target_pairs={{0,16},{16,0},{1,17},{17,1},{2,18},{18,2},{3,19},{19,3},{4,20},{20... | collective-permute-start | bytes 2359304 | tf_op jit(solution)/shard_map/ppermute | solution.py:735
  238.1 14.9 %copy-start.16 = (bf16[512,1536]{1,0:T(8,128)(2,1)S(1)}, bf16[512,1536]{1,0:T(8,128)(2,1)}, u32[]{:S(2)}) copy-start(bf16[512,1536]{1,0:T(8,128)(2,1)} %copy-done.15) | copy-start | bytes 4718596
  276.7 20.0 %collective-permute-start.8 = (bf16[256,1536]{1,0:T(8,128)(2,1)}, bf16[256,1536]{1,0:T(8,128)(2,1)}, u32[]{:S(2)}, u32[]{:S(2)}) collective-permute-start(bf16[256,1536]{1,0:T(8,128)(2,1)} %get-tuple-element.200), channel_id=1, source_target_pairs={{0,16},{16,0},{1,17},{17,1},{2,18},{18,2},{3,19},{19,3},{4,20},{20... | collective-permute-start | bytes 2359304 | tf_op jit(solution)/shard_map/ppermute | solution.py:735
  279.2 22.7 %copy-start.45 = (bf16[1536,512]{1,0:T(8,128)(2,1)}, bf16[1536,512]{1,0:T(8,128)(2,1)S(1)}, u32[]{:S(2)}) copy-start(bf16[1536,512]{1,0:T(8,128)(2,1)S(1)} %flip.7) | copy-start | bytes 4718596
  283.8 18.1 %collective-permute-start.7 = (bf16[8,96,2304]{2,1,0:T(8,128)(2,1)}, bf16[8,96,2304]{2,1,0:T(8,128)(2,1)}, u32[]{:S(2)}, u32[]{:S(2)}) collective-permute-start(bf16[8,96,2304]{2,1,0:T(8,128)(2,1)} %grad_away.6), channel_id=1, source_target_pairs={{0,1},{1,0},{2,3},{3,2},{4,5},{5,4},{6,7},{7,6},{8,9},{9,8},{10,11... | collective-permute-start | bytes 10616840 | tf_op jit(solution)/shard_map/ppermute | solution.py:767
  283.8 13.0 %copy-start.75 = (f32[1536]{0:T(1024)S(1)}, f32[1536]{0:T(1024)}, u32[]{:S(2)}) copy-start(f32[1536]{0:T(1024)} %copy-done.74) | copy-start | bytes 18436
  283.8 13.0 %copy-start.3 = (f32[256,1536]{1,0:T(8,128)S(1)}, f32[256,1536]{1,0:T(8,128)}, u32[]{:S(2)}) copy-start(f32[256,1536]{1,0:T(8,128)} %copy-done.2) | copy-start | bytes 4718596
  283.8 13.0 %copy-start.9 = (bf16[256,1536]{1,0:T(8,128)(2,1)S(1)}, bf16[256,1536]{1,0:T(8,128)(2,1)}, u32[]{:S(2)}) copy-start(bf16[256,1536]{1,0:T(8,128)(2,1)} %base_ref.1) | copy-start | bytes 2359300
  288.0 21.5 %collective-permute-start.6 = (bf16[8,144,1536]{2,1,0:T(8,128)(2,1)}, bf16[8,144,1536]{2,1,0:T(8,128)(2,1)}, u32[]{:S(2)}, u32[]{:S(2)}) collective-permute-start(bf16[8,144,1536]{2,1,0:T(8,128)(2,1)} %grad_away.7), channel_id=1, source_target_pairs={{0,1},{1,0},{2,3},{3,2},{4,5},{5,4},{6,7},{7,6},{8,9},{9,8},{10,11... | collective-permute-start | bytes 10616840 | tf_op jit(solution)/shard_map/ppermute | solution.py:767
  300.4 19.2 %collective-permute-start.11 = (bf16[256,1536]{1,0:T(8,128)(2,1)}, bf16[256,1536]{1,0:T(8,128)(2,1)}, u32[]{:S(2)}, u32[]{:S(2)}) collective-permute-start(bf16[256,1536]{1,0:T(8,128)(2,1)} %get-tuple-element.217.own_ref), channel_id=1, source_target_pairs={{0,16},{16,0},{1,17},{17,1},{2,18},{18,2},{3,19},{19,3},{4,20},{20... | collective-permute-start | bytes 2359304 | tf_op jit(solution)/shard_map/ppermute | solution.py:735
  308.1 41.1 %collective-permute-start.10 = (bf16[2,2,96,2304]{3,2,1,0:T(8,128)(2,1)}, bf16[2,2,96,2304]{3,2,1,0:T(8,128)(2,1)}, u32[]{:S(2)}, u32[]{:S(2)}) collective-permute-start(bf16[2,2,96,2304]{3,2,1,0:T(8,128)(2,1)} %get-tuple-element.212), channel_id=1, source_target_pairs={{0,4},{1,5},{2,6},{3,7},{4,0},{5,1},{6,2},{7,3},{8,12},{9,13},{10,... | collective-permute-start | bytes 5308424 | tf_op jit(solution)/shard_map/ppermute | solution.py:767
  309.5 10.1 %copy-start.10 = (bf16[256,1536]{1,0:T(8,128)(2,1)S(1)}, bf16[256,1536]{1,0:T(8,128)(2,1)}, u32[]{:S(2)}) copy-start(bf16[256,1536]{1,0:T(8,128)(2,1)} %get-tuple-element.217.own_ref) | copy-start | bytes 2359300
  317.4 39.7 %collective-permute-start.9 = (bf16[4,1,144,1536]{3,2,1,0:T(8,128)(2,1)}, bf16[4,1,144,1536]{3,2,1,0:T(8,128)(2,1)}, u32[]{:S(2)}, u32[]{:S(2)}) collective-permute-start(bf16[4,1,144,1536]{3,2,1,0:T(8,128)(2,1)} %get-tuple-element.216), channel_id=1, source_target_pairs={{0,2},{1,3},{2,0},{3,1},{4,6},{5,7},{6,4},{7,5},{8,10},{9,11},{10,... | collective-permute-start | bytes 5308424 | tf_op jit(solution)/shard_map/ppermute | solution.py:767
  319.6 23.7 %copy-start.35 = (bf16[2048,512]{1,0:T(8,128)(2,1)S(1)}, bf16[2048,512]{1,0:T(8,128)(2,1)}, u32[]{:S(2)}) copy-start(bf16[2048,512]{1,0:T(8,128)(2,1)} %copy-done.34) | copy-start | bytes 6291460
  341.8 33.6 %collective-permute-start.14 = (bf16[512,1024]{1,0:T(8,128)(2,1)}, bf16[512,1024]{1,0:T(8,128)(2,1)}, u32[]{:S(2)}, u32[]{:S(2)}) collective-permute-start(bf16[512,1024]{1,0:T(8,128)(2,1)} %get-tuple-element.222), channel_id=1, source_target_pairs={{0,16},{16,0},{1,17},{17,1},{2,18},{18,2},{3,19},{19,3},{4,20},{20... | collective-permute-start | bytes 3145736 | tf_op jit(solution)/shard_map/ppermute | solution.py:735
  347.9 15.4 %collective-permute-start.15 = (bf16[8,128,2048]{2,1,0:T(8,128)(2,1)}, bf16[8,128,2048]{2,1,0:T(8,128)(2,1)}, u32[]{:S(2)}, u32[]{:S(2)}) collective-permute-start(bf16[8,128,2048]{2,1,0:T(8,128)(2,1)} %grad_away.8), channel_id=1, source_target_pairs={{0,1},{1,0},{2,3},{3,2},{4,5},{5,4},{6,7},{7,6},{8,9},{9,8},{10,11... | collective-permute-start | bytes 12582920 | tf_op jit(solution)/shard_map/ppermute | solution.py:767
  357.1 28.3 %collective-permute-start.13 = (bf16[2,1,96,2304]{3,2,0,1:T(8,128)(2,1)}, bf16[2,1,96,2304]{3,2,0,1:T(8,128)(2,1)}, u32[]{:S(2)}, u32[]{:S(2)}) collective-permute-start(bf16[2,1,96,2304]{3,2,0,1:T(8,128)(2,1)} %bitcast.193), channel_id=1, source_target_pairs={{0,2},{1,3},{2,0},{3,1},{4,6},{5,7},{6,4},{7,5},{8,10},{9,11},{10,... | collective-permute-start | bytes 2654216 | tf_op jit(solution)/shard_map/ppermute | solution.py:767
  362.8 30.0 %collective-permute-start.12 = (bf16[2,1,144,1536]{3,2,0,1:T(8,128)(2,1)}, bf16[2,1,144,1536]{3,2,0,1:T(8,128)(2,1)}, u32[]{:S(2)}, u32[]{:S(2)}) collective-permute-start(bf16[2,1,144,1536]{3,2,0,1:T(8,128)(2,1)} %bitcast.194), channel_id=1, source_target_pairs={{0,4},{1,5},{2,6},{3,7},{4,0},{5,1},{6,2},{7,3},{8,12},{9,13},{10,... | collective-permute-start | bytes 2654216 | tf_op jit(solution)/shard_map/ppermute | solution.py:767
  370.0 51.9 %collective-permute-start.21 = (bf16[4,1,128,2048]{3,2,1,0:T(8,128)(2,1)}, bf16[4,1,128,2048]{3,2,1,0:T(8,128)(2,1)}, u32[]{:S(2)}, u32[]{:S(2)}) collective-permute-start(bf16[4,1,128,2048]{3,2,1,0:T(8,128)(2,1)} %get-tuple-element.237), channel_id=1, source_target_pairs={{0,2},{1,3},{2,0},{3,1},{4,6},{5,7},{6,4},{7,5},{8,10},{9,11},{10,... | collective-permute-start | bytes 6291464 | tf_op jit(solution)/shard_map/ppermute | solution.py:767
  375.4 21.2 %collective-permute-start.18 = (bf16[8,96,2304]{2,1,0:T(8,128)(2,1)}, bf16[8,96,2304]{2,1,0:T(8,128)(2,1)}, u32[]{:S(2)}, u32[]{:S(2)}) collective-permute-start(bf16[8,96,2304]{2,1,0:T(8,128)(2,1)} %grad_away.9), channel_id=1, source_target_pairs={{0,1},{1,0},{2,3},{3,2},{4,5},{5,4},{6,7},{7,6},{8,9},{9,8},{10,11... | collective-permute-start | bytes 10616840 | tf_op jit(solution)/shard_map/ppermute | solution.py:767
  384.7 188.8 %collective-permute-start.33 = (bf16[256,1536]{1,0:T(8,128)(2,1)}, bf16[256,1536]{1,0:T(8,128)(2,1)}, u32[]{:S(2)}, u32[]{:S(2)}) collective-permute-start(bf16[256,1536]{1,0:T(8,128)(2,1)} %get-tuple-element.244), channel_id=1, source_target_pairs={{0,16},{16,0},{1,17},{17,1},{2,18},{18,2},{3,19},{19,3},{4,20},{20... | collective-permute-start | bytes 2359304 | tf_op jit(solution)/shard_map/ppermute | solution.py:735
  390.3 49.5 %collective-permute-start.17 = (bf16[1,1,96,2304]{3,2,1,0:T(8,128)(2,1)}, bf16[1,1,96,2304]{3,2,1,0:T(8,128)(2,1)}, u32[]{:S(2)}, u32[]{:S(2)}) collective-permute-start(bf16[1,1,96,2304]{3,2,1,0:T(8,128)(2,1)} %get-tuple-element.249), channel_id=1, source_target_pairs={{0,8},{1,9},{2,10},{3,11},{4,12},{5,13},{6,14},{7,15},{8,0},{9,1},... | collective-permute-start | bytes 1327112 | tf_op jit(solution)/shard_map/ppermute | solution.py:767
  396.0 89.7 %collective-permute-start.16 = (bf16[1,1,144,1536]{3,2,1,0:T(8,128)(2,1)}, bf16[1,1,144,1536]{3,2,1,0:T(8,128)(2,1)}, u32[]{:S(2)}, u32[]{:S(2)}) collective-permute-start(bf16[1,1,144,1536]{3,2,1,0:T(8,128)(2,1)} %get-tuple-element.253), channel_id=1, source_target_pairs={{0,8},{1,9},{2,10},{3,11},{4,12},{5,13},{6,14},{7,15},{8,0},{9,1},... | collective-permute-start | bytes 1327112 | tf_op jit(solution)/shard_map/ppermute | solution.py:767
  406.6 19.9 %collective-permute-start.20 = (bf16[8,96,2048]{2,1,0:T(8,128)(2,1)}, bf16[8,96,2048]{2,1,0:T(8,128)(2,1)}, u32[]{:S(2)}, u32[]{:S(2)}) collective-permute-start(bf16[8,96,2048]{2,1,0:T(8,128)(2,1)} %grad_away.10), channel_id=1, source_target_pairs={{0,1},{1,0},{2,3},{3,2},{4,5},{5,4},{6,7},{7,6},{8,9},{9,8},{10,11... | collective-permute-start | bytes 9437192 | tf_op jit(solution)/shard_map/ppermute | solution.py:767
  421.9 11.4 %collective-permute-start.19 = (bf16[8,128,768]{2,1,0:T(8,128)(2,1)}, bf16[8,128,768]{2,1,0:T(8,128)(2,1)}, u32[]{:S(2)}, u32[]{:S(2)}) collective-permute-start(bf16[8,128,768]{2,1,0:T(8,128)(2,1)} %grad_away.11), channel_id=1, source_target_pairs={{0,1},{1,0},{2,3},{3,2},{4,5},{5,4},{6,7},{7,6},{8,9},{9,8},{10,11... | collective-permute-start | bytes 4718600 | tf_op jit(solution)/shard_map/ppermute | solution.py:767
  426.6 42.0 %collective-permute-start.24 = (bf16[4,1,96,2304]{3,2,1,0:T(8,128)(2,1)}, bf16[4,1,96,2304]{3,2,1,0:T(8,128)(2,1)}, u32[]{:S(2)}, u32[]{:S(2)}) collective-permute-start(bf16[4,1,96,2304]{3,2,1,0:T(8,128)(2,1)} %get-tuple-element.259), channel_id=1, source_target_pairs={{0,2},{1,3},{2,0},{3,1},{4,6},{5,7},{6,4},{7,5},{8,10},{9,11},{10,... | collective-permute-start | bytes 5308424 | tf_op jit(solution)/shard_map/ppermute | solution.py:767
  433.3 40.1 %collective-permute-start.23 = (bf16[2,1,128,2048]{3,2,0,1:T(8,128)(2,1)}, bf16[2,1,128,2048]{3,2,0,1:T(8,128)(2,1)}, u32[]{:S(2)}, u32[]{:S(2)}) collective-permute-start(bf16[2,1,128,2048]{3,2,0,1:T(8,128)(2,1)} %bitcast.57), channel_id=1, source_target_pairs={{0,4},{1,5},{2,6},{3,7},{4,0},{5,1},{6,2},{7,3},{8,12},{9,13},{10,... | collective-permute-start | bytes 3145736 | tf_op jit(solution)/shard_map/ppermute | solution.py:767
  439.8 48.5 %collective-permute-start.27 = (bf16[4,1,128,768]{3,2,1,0:T(8,128)(2,1)}, bf16[4,1,128,768]{3,2,1,0:T(8,128)(2,1)}, u32[]{:S(2)}, u32[]{:S(2)}) collective-permute-start(bf16[4,1,128,768]{3,2,1,0:T(8,128)(2,1)} %get-tuple-element.273), channel_id=1, source_target_pairs={{0,2},{1,3},{2,0},{3,1},{4,6},{5,7},{6,4},{7,5},{8,10},{9,11},{10,... | collective-permute-start | bytes 2359304 | tf_op jit(solution)/shard_map/ppermute | solution.py:767
  440.7 28.7 %copy-start.23 = (f32[4,1,96,2304]{3,2,1,0:T(8,128)S(1)}, f32[4,1,96,2304]{3,2,1,0:T(8,128)}, u32[]{:S(2)}) copy-start(f32[4,1,96,2304]{3,2,1,0:T(8,128)} %copy-done.22) | copy-start | bytes 10616836
  468.5 11.9 %collective-permute-start.22 = (bf16[96,2304]{1,0:T(8,128)(2,1)}, bf16[96,2304]{1,0:T(8,128)(2,1)}, u32[]{:S(2)}, u32[]{:S(2)}) collective-permute-start(bf16[96,2304]{1,0:T(8,128)(2,1)} %get-tuple-element.279), channel_id=1, source_target_pairs={{0,16},{16,0},{1,17},{17,1},{2,18},{18,2},{3,19},{19,3},{4,20},{20... | collective-permute-start | bytes 1327112 | tf_op jit(solution)/shard_map/ppermute | solution.py:735
  473.3 60.0 %collective-permute-start.32 = (bf16[4,1,96,2048]{3,2,1,0:T(8,128)(2,1)}, bf16[4,1,96,2048]{3,2,1,0:T(8,128)(2,1)}, u32[]{:S(2)}, u32[]{:S(2)}) collective-permute-start(bf16[4,1,96,2048]{3,2,1,0:T(8,128)(2,1)} %get-tuple-element.269), channel_id=1, source_target_pairs={{0,2},{1,3},{2,0},{3,1},{4,6},{5,7},{6,4},{7,5},{8,10},{9,11},{10,... | collective-permute-start | bytes 4718600 | tf_op jit(solution)/shard_map/ppermute | solution.py:767
  480.4 56.6 %collective-permute-start.31 = (bf16[1,1,128,2048]{3,2,1,0:T(8,128)(2,1)}, bf16[1,1,128,2048]{3,2,1,0:T(8,128)(2,1)}, u32[]{:S(2)}, u32[]{:S(2)}) collective-permute-start(bf16[1,1,128,2048]{3,2,1,0:T(8,128)(2,1)} %get-tuple-element.287), channel_id=1, source_target_pairs={{0,8},{1,9},{2,10},{3,11},{4,12},{5,13},{6,14},{7,15},{8,0},{9,1},... | collective-permute-start | bytes 1572872 | tf_op jit(solution)/shard_map/ppermute | solution.py:767
  485.7 31.7 %collective-permute-start.26 = (bf16[2,1,96,2304]{3,2,0,1:T(8,128)(2,1)}, bf16[2,1,96,2304]{3,2,0,1:T(8,128)(2,1)}, u32[]{:S(2)}, u32[]{:S(2)}) collective-permute-start(bf16[2,1,96,2304]{3,2,0,1:T(8,128)(2,1)} %bitcast.64), channel_id=1, source_target_pairs={{0,4},{1,5},{2,6},{3,7},{4,0},{5,1},{6,2},{7,3},{8,12},{9,13},{10,... | collective-permute-start | bytes 2654216 | tf_op jit(solution)/shard_map/ppermute | solution.py:767
  488.3 32.4 %collective-permute-start.25 = (bf16[144,1536]{1,0:T(8,128)(2,1)}, bf16[144,1536]{1,0:T(8,128)(2,1)}, u32[]{:S(2)}, u32[]{:S(2)}) collective-permute-start(bf16[144,1536]{1,0:T(8,128)(2,1)} %get-tuple-element.293), channel_id=1, source_target_pairs={{0,16},{16,0},{1,17},{17,1},{2,18},{18,2},{3,19},{19,3},{4,20},{20... | collective-permute-start | bytes 1327112 | tf_op jit(solution)/shard_map/ppermute | solution.py:735
  517.3 27.3 %collective-permute-start.29 = (bf16[2,1,128,768]{3,2,0,1:T(8,128)(2,1)}, bf16[2,1,128,768]{3,2,0,1:T(8,128)(2,1)}, u32[]{:S(2)}, u32[]{:S(2)}) collective-permute-start(bf16[2,1,128,768]{3,2,0,1:T(8,128)(2,1)} %bitcast.196), channel_id=1, source_target_pairs={{0,4},{1,5},{2,6},{3,7},{4,0},{5,1},{6,2},{7,3},{8,12},{9,13},{10,... | collective-permute-start | bytes 1179656 | tf_op jit(solution)/shard_map/ppermute | solution.py:767
  520.8 20.4 %collective-permute-start.30 = (bf16[1,1,96,2304]{3,2,1,0:T(8,128)(2,1)}, bf16[1,1,96,2304]{3,2,1,0:T(8,128)(2,1)}, u32[]{:S(2)}, u32[]{:S(2)}) collective-permute-start(bf16[1,1,96,2304]{3,2,1,0:T(8,128)(2,1)} %get-tuple-element.301), channel_id=1, source_target_pairs={{0,8},{1,9},{2,10},{3,11},{4,12},{5,13},{6,14},{7,15},{8,0},{9,1},... | collective-permute-start | bytes 1327112 | tf_op jit(solution)/shard_map/ppermute | solution.py:767
  523.5 10.5 %copy-start.27 = (f32[4,1,96,2048]{3,2,1,0:T(8,128)S(1)}, f32[4,1,96,2048]{3,2,1,0:T(8,128)}, u32[]{:S(2)}) copy-start(f32[4,1,96,2048]{3,2,1,0:T(8,128)} %copy-done.26) | copy-start | bytes 9437188
  533.4 20.9 %collective-permute-start.28 = (bf16[256,1536]{1,0:T(8,128)(2,1)}, bf16[256,1536]{1,0:T(8,128)(2,1)}, u32[]{:S(2)}, u32[]{:S(2)}) collective-permute-start(bf16[256,1536]{1,0:T(8,128)(2,1)} %get-tuple-element.306), channel_id=1, source_target_pairs={{0,16},{16,0},{1,17},{17,1},{2,18},{18,2},{3,19},{19,3},{4,20},{20... | collective-permute-start | bytes 2359304 | tf_op jit(solution)/shard_map/ppermute | solution.py:735
  538.9 29.1 %collective-permute-start.35 = (bf16[128,2048]{1,0:T(8,128)(2,1)}, bf16[128,2048]{1,0:T(8,128)(2,1)}, u32[]{:S(2)}, u32[]{:S(2)}) collective-permute-start(bf16[128,2048]{1,0:T(8,128)(2,1)} %get-tuple-element.314), channel_id=1, source_target_pairs={{0,16},{16,0},{1,17},{17,1},{2,18},{18,2},{3,19},{19,3},{4,20},{20... | collective-permute-start | bytes 1572872 | tf_op jit(solution)/shard_map/ppermute | solution.py:735
  544.0 43.6 %collective-permute-start.40 = (bf16[96,2304]{1,0:T(8,128)(2,1)}, bf16[96,2304]{1,0:T(8,128)(2,1)}, u32[]{:S(2)}, u32[]{:S(2)}) collective-permute-start(bf16[96,2304]{1,0:T(8,128)(2,1)} %get-tuple-element.318), channel_id=1, source_target_pairs={{0,16},{16,0},{1,17},{17,1},{2,18},{18,2},{3,19},{19,3},{4,20},{20... | collective-permute-start | bytes 1327112 | tf_op jit(solution)/shard_map/ppermute | solution.py:735
  544.7 21.8 %collective-permute-start.36 = (bf16[2,1,96,2048]{3,2,0,1:T(8,128)(2,1)S(1)}, bf16[2,1,96,2048]{3,2,0,1:T(8,128)(2,1)S(1)}, u32[]{:S(2)}, u32[]{:S(2)}) collective-permute-start(bf16[2,1,96,2048]{3,2,0,1:T(8,128)(2,1)S(1)} %bitcast.195), channel_id=1, source_target_pairs={{0,4},{1,5},{2,6},{3,7},{4,0},{5,1},{6,2},{7,3},{8,12},{9,13},{10,... | collective-permute-start | bytes 2359304 | tf_op jit(solution)/shard_map/ppermute | solution.py:767
  545.6 11.3 %copy-start.4 = (f32[256,1536]{1,0:T(8,128)S(1)}, f32[256,1536]{1,0:T(8,128)}, u32[]{:S(2)}) copy-start(f32[256,1536]{1,0:T(8,128)} %copy-done.2) | copy-start | bytes 4718596
  554.3 16.2 %collective-permute-start.34 = (bf16[1,1,128,768]{3,2,1,0:T(8,128)(2,1)}, bf16[1,1,128,768]{3,2,1,0:T(8,128)(2,1)}, u32[]{:S(2)}, u32[]{:S(2)}) collective-permute-start(bf16[1,1,128,768]{3,2,1,0:T(8,128)(2,1)} %get-tuple-element.322), channel_id=1, source_target_pairs={{0,8},{1,9},{2,10},{3,11},{4,12},{5,13},{6,14},{7,15},{8,0},{9,1},... | collective-permute-start | bytes 589832 | tf_op jit(solution)/shard_map/ppermute | solution.py:767
  568.0 16.6 %collective-permute-start.37 = (bf16[1,1,96,2048]{3,2,1,0:T(8,128)(2,1)}, bf16[1,1,96,2048]{3,2,1,0:T(8,128)(2,1)}, u32[]{:S(2)}, u32[]{:S(2)}) collective-permute-start(bf16[1,1,96,2048]{3,2,1,0:T(8,128)(2,1)} %get-tuple-element.328), channel_id=1, source_target_pairs={{0,8},{1,9},{2,10},{3,11},{4,12},{5,13},{6,14},{7,15},{8,0},{9,1},... | collective-permute-start | bytes 1179656 | tf_op jit(solution)/shard_map/ppermute | solution.py:767
  572.3 18.2 %collective-permute-start.39 = (bf16[128,768]{1,0:T(8,128)(2,1)}, bf16[128,768]{1,0:T(8,128)(2,1)}, u32[]{:S(2)}, u32[]{:S(2)}) collective-permute-start(bf16[128,768]{1,0:T(8,128)(2,1)} %get-tuple-element.336), channel_id=1, source_target_pairs={{0,16},{16,0},{1,17},{17,1},{2,18},{18,2},{3,19},{19,3},{4,20},{20... | collective-permute-start | bytes 589832 | tf_op jit(solution)/shard_map/ppermute | solution.py:735
  586.4 11.4 %collective-permute-start.38 = (bf16[96,2048]{1,0:T(8,128)(2,1)}, bf16[96,2048]{1,0:T(8,128)(2,1)}, u32[]{:S(2)}, u32[]{:S(2)}) collective-permute-start(bf16[96,2048]{1,0:T(8,128)(2,1)} %get-tuple-element.344), channel_id=1, source_target_pairs={{0,16},{16,0},{1,17},{17,1},{2,18},{18,2},{3,19},{19,3},{4,20},{20... | collective-permute-start | bytes 1179656 | tf_op jit(solution)/shard_map/ppermute | solution.py:735
  (66 other events, 290.2 us)
Sparse Core Ops, SparseCore 0:
  13.6 111.9 all-gather.4
  127.7 110.2 all-gather.6
  440.8 131.2 all-reduce.5

commit v5 on v4

--- a/solution.py
+++ b/solution.py
@@ -14,18 +14,20 @@
 GELU_K = math.sqrt(2.0 / math.pi)
 GELU_C = 0.044715
 ROWS = 16
+FACTORS = 7
 VMEM = 44 << 20
 LESS = 24 << 20
 STEPS = (
-    "hidden", "ffn_in", "turn", "away_u", "away_d", "norm_two", "home_u", "home_d", "mixer", "away_r", "two_u",
-    "two_d", "home_r", "away_g", "conv_in", "fold_u", "fold_d", "home_g", "away_b", "away_o", "two_r", "home_b",
-    "home_o", "small", "settle_u", "two_g", "fold_r", "join_u", "settle_d", "two_o", "fold_g", "join_d", "down",
-    "two_b", "settle_r", "settle_g", "fold_o", "result", "fold_b", "join_r", "settle_o", "norm_one", "small_end",
-    "settle_b", "join_g", "join_o", "join_b",
+    "hidden", "ffn_in", "turn", "away_u", "away_d", "norm_two", "home_u", "home_d", "away_g", "mixer", "away_r",
+    "two_u", "two_d", "home_g", "home_r", "conv_in", "fold_u", "fold_d", "away_b", "small", "settle_u", "down",
+    "home_b", "norm_one", "two_g", "two_r", "join_u", "away_o", "two_b", "fold_g", "settle_d", "home_o", "fold_r",
+    "settle_g", "join_d", "two_o", "fold_b", "join_g", "settle_r", "small_end", "fold_o", "settle_b", "result",
+    "join_r", "settle_o", "join_b", "join_o",
 )
 HINT = pl.CostEstimate(flops=100000000000, bytes_accessed=1024, transcendentals=0)
 BF16 = jnp.bfloat16
 F32 = jnp.float32
+KEEP = BF16
 
 
 def sent(shape):
@@ -57,7 +59,7 @@
     return 0.5 * (1.0 + t) + 0.5 * v * (1.0 - t * t) * GELU_K * (1.0 + 3.0 * GELU_C * v * v)
 
 
-def forward_kernel(pre_ref, gates_r_ref, gates_i_ref, admitted_ref, params_ref, mixed_ref, before_ref):
+def forward_kernel(pre_ref, gates_r_ref, gates_i_ref, admitted_ref, params_ref, mixed_ref, *factor_refs):
     width = pre_ref.shape[1]
     rbias, abias, rate = params_ref[0:1, :], params_ref[1:2, :], params_ref[2:3, :]
     row = lax.broadcasted_iota(jnp.int32, (ROWS, width), 0)
@@ -66,30 +68,46 @@
         at = pl.ds(pl.multiple_of(i * ROWS, ROWS), ROWS)
         gate_r = jax.nn.sigmoid(gates_r_ref[at, :] + rbias)
         gate_i = jax.nn.sigmoid(gates_i_ref[at, :] + abias)
-        a = jnp.exp(-(gate_r * rate))
-        b = jnp.sqrt(jnp.maximum(1.0 - a * a, ROOT_FLOOR)) * gate_i * widen(admitted_ref[at, :])
+        admitted = widen(admitted_ref[at, :])
+        decay = jnp.exp(-(gate_r * rate))
+        rest = 1.0 - decay * decay
+        root = jnp.sqrt(jnp.maximum(rest, ROOT_FLOOR))
+        through = root * gate_i
+        a, b = decay, through * admitted
         for d in (1, 2, 4, 8):
             keep = row >= d
             b = b + a * jnp.where(keep, pltpu.roll(b, d, 0), 0.0)
             a = a * jnp.where(keep, pltpu.roll(a, d, 0), 1.0)
         state = b + a * carry
-        before_ref[at, :] = jnp.where(row >= 1, pltpu.roll(state, 1, 0), carry)
-        mixed_ref[at, :] = (state * gelu(pre_ref[at, :])).astype(BF16)
+        before = jnp.where(row >= 1, pltpu.roll(state, 1, 0), carry)
+        pre = pre_ref[at, :]
+        t = jnp.tanh(GELU_K * (pre + GELU_C * pre * pre * pre))
+        act = 0.5 * pre * (1.0 + t)
+        slope = 0.5 * (1.0 + t) + 0.5 * pre * (1.0 - t * t) * GELU_K * (1.0 + 3.0 * GELU_C * pre * pre)
+        mixed_ref[at, :] = (state * act).astype(BF16)
+        share = jnp.where(rest > ROOT_FLOOR, 1.0, jnp.where(rest == ROOT_FLOOR, 0.5, 0.0))
+        log = decay * (before - gate_i * admitted * (share * decay / root))
+        factors = (
+            decay, act, state * slope, through, through * admitted * (1.0 - gate_i),
+            -(log * rate) * gate_r * (1.0 - gate_r), log * gate_r,
+        )
+        for ref, factor in zip(factor_refs, factors, strict=True):
+            ref[at, :] = factor
         return jnp.broadcast_to(state[ROWS - 1 : ROWS, :], (ROWS, width))
 
     lax.fori_loop(0, pre_ref.shape[0] // ROWS, step, jnp.zeros((ROWS, width), F32))
 
 
 def chain_kernel(
-    side_ref, own_ref, other_ref, out_a_ref, out_b_ref, out_c_ref, recur_w_ref, admit_w_ref, pre_ref, gates_r_ref, gates_i_ref, admitted_ref,
-    before_ref, params_ref, branch_ref, gates_cot_ref, direct_ref, sums_ref, near_ref, far_ref, cot_ref, sum_ref,
+    side_ref, own_ref, other_ref, out_a_ref, out_b_ref, out_c_ref, recur_w_ref, admit_w_ref, decay_ref, act_ref,
+    branch_f_ref, direct_f_ref, admit_f_ref, recur_f_ref, rate_f_ref,
+    branch_ref, gates_cot_ref, direct_ref, sums_ref, near_ref, far_ref, cot_ref, sum_ref,
 ):
     length = own_ref.shape[0]
-    width = pre_ref.shape[1]
+    width = act_ref.shape[1]
     out_w = jnp.concatenate([joined(out_a_ref), joined(out_b_ref), joined(out_c_ref)], axis=1)
     cot_ref[:length, :] = cols_product(own_ref[...], out_w)
     cot_ref[length:, :] = cols_product(other_ref[...], out_w)
-    rbias, abias, rate = params_ref[0:1, :], params_ref[1:2, :], params_ref[2:3, :]
     row = lax.broadcasted_iota(jnp.int32, (ROWS, width), 0)
     blocks = length // ROWS
     zero = jnp.zeros((ROWS, width), F32)
@@ -97,35 +115,24 @@
     def step(first, i, state):
         carry, sum_r, sum_i, sum_d = state
         at = pl.ds(pl.multiple_of(first + (blocks - 1 - i) * ROWS, ROWS), ROWS)
-        gate_r = jax.nn.sigmoid(gates_r_ref[at, :] + rbias)
-        gate_i = jax.nn.sigmoid(gates_i_ref[at, :] + abias)
-        admitted = widen(admitted_ref[at, :])
-        a = jnp.exp(-(gate_r * rate))
-        rest = 1.0 - a * a
-        root = jnp.sqrt(jnp.maximum(rest, ROOT_FLOOR))
-        before = before_ref[at, :]
-        state_now = a * before + root * gate_i * admitted
-        pre = pre_ref[at, :]
         cot = cot_ref[at, :]
-        branch_ref[at, :] = (cot * state_now * gelu_slope(pre)).astype(BF16)
-        own = cot * gelu(pre)
-        f = a
-        e = a * own
+        branch_ref[at, :] = (cot * branch_f_ref[at, :]).astype(BF16)
+        own = cot * act_ref[at, :]
+        f = decay_ref[at, :]
+        e = f * own
         for d in (1, 2, 4, 8):
             keep = row < ROWS - d
             e = e + f * jnp.where(keep, pltpu.roll(e, ROWS - d, 0), 0.0)
             f = f * jnp.where(keep, pltpu.roll(f, ROWS - d, 0), 1.0)
         e = e + f * carry
         g = own + jnp.where(row < ROWS - 1, pltpu.roll(e, ROWS - 1, 0), carry)
-        direct_ref[at, :] = g * root * gate_i
-        share = jnp.where(rest > ROOT_FLOOR, 1.0, jnp.where(rest == ROOT_FLOOR, 0.5, 0.0))
-        d_log = a * (g * before - g * gate_i * admitted * (share * a / root))
-        recur = -(d_log * rate) * gate_r * (1.0 - gate_r)
-        admit = g * root * admitted * gate_i * (1.0 - gate_i)
+        direct_ref[at, :] = g * direct_f_ref[at, :]
+        recur = g * recur_f_ref[at, :]
+        admit = g * admit_f_ref[at, :]
         gates_cot_ref[0, at, :] = recur.astype(BF16)
         gates_cot_ref[1, at, :] = admit.astype(BF16)
         carry = jnp.broadcast_to(e[0:1, :], (ROWS, width))
-        return carry, sum_r + recur, sum_i + admit, sum_d + d_log * gate_r
+        return carry, sum_r + recur, sum_i + admit, sum_d + g * rate_f_ref[at, :]
 
     sums = (zero, zero, zero)
     for first in (0, length):
@@ -153,9 +160,9 @@
             far_ref[length:, :] = sum_ref[:length, away].astype(BF16)
 
 
-def chain_back(side, own, other, whole, at, rows, pre, gates, admitted, before, params):
+def chain_back(side, own, other, whole, at, rows, factors):
     length, depth = own.shape
-    tokens, width = admitted.shape
+    tokens, width = factors[0].shape
     shards, _, tile = whole.shape
     n = width // tile
     at = at // rows
@@ -176,10 +183,7 @@
                 ],
                 pl.BlockSpec((shards, rows, tile), lambda j, s: (0, at + j, 0)),
                 pl.BlockSpec((shards, rows, tile), lambda j, s: (0, at + n + j, 0)),
-                near, near,
-                pl.BlockSpec((tokens, tile), lambda j, s: (0, j + n)),
-                near, near,
-                pl.BlockSpec((8, tile), lambda j, s: (0, j)),
+                *[near] * FACTORS,
             ],
             out_specs=[
                 near, pl.BlockSpec((2, tokens, tile), lambda j, s: (0, 0, j)), near,
@@ -194,7 +198,7 @@
         compiler_params=pltpu.CompilerParams(vmem_limit_bytes=VMEM),
         cost_estimate=HINT,
         name="chain_back",
-    )(side, own, other, *[whole] * 5, pre, gates, gates, admitted, before, params)
+    )(side, own, other, *[whole] * 5, *factors)
 
 
 def conv_kernel(
@@ -430,11 +434,8 @@
         forward_kernel,
         grid=(tokens // length, n),
         in_specs=[near, near, far, near, vector],
-        out_specs=[near, near],
-        out_shape=[
-            jax.ShapeDtypeStruct((tokens, width), BF16),
-            jax.ShapeDtypeStruct((tokens, width), F32),
-        ],
+        out_specs=[near] * (1 + FACTORS),
+        out_shape=[jax.ShapeDtypeStruct((tokens, width), BF16)] + [jax.ShapeDtypeStruct((tokens, width), F32)] * FACTORS,
         cost_estimate=pl.CostEstimate(flops=60 * tokens * width, bytes_accessed=20 * tokens * width, transcendentals=6 * tokens * width),
         name="recurrence_forward",
     )(pre, gates, gates, admitted, params)
@@ -591,7 +592,7 @@
 def home_kernel(bit, at_ref, left_ref, right_ref, got_ref, keep_ref, send_ref, sum_ref):
     v = matmul(joined(left_ref), right_ref[...]).reshape(got_ref.shape) + widen(got_ref[...])
     sum_ref[...] = v.reshape(sum_ref.shape)
-    keep_ref[...] = sum_ref[:, at_ref[bit]]
+    keep_ref[...] = sum_ref[:, at_ref[bit]].astype(keep_ref.dtype)
     send_ref[...] = sum_ref[:, 1 - at_ref[bit]].astype(send_ref.dtype)
 
 
@@ -651,7 +652,7 @@
             scratch_shapes=[pltpu.VMEM((high, 2, low, rows, tile), F32)],
         ),
         out_shape=[
-            jax.ShapeDtypeStruct((high, low, rows, n), F32), sent((high, low, rows, n)),
+            jax.ShapeDtypeStruct((high, low, rows, n), KEEP), sent((high, low, rows, n)),
         ],
         compiler_params=pltpu.CompilerParams(vmem_limit_bytes=LESS),
         cost_estimate=HINT,
@@ -661,8 +662,8 @@
 
 def fold_kernel(bit, at_ref, own_ref, got_ref, keep_ref, send_ref):
     mine, other = at_ref[bit], 1 - at_ref[bit]
-    keep_ref[...] = own_ref[:, mine] + widen(got_ref[:, mine])
-    send_ref[...] = (own_ref[:, other] + widen(got_ref[:, other])).astype(BF16)
+    keep_ref[...] = (widen(own_ref[:, mine]) + widen(got_ref[:, mine])).astype(keep_ref.dtype)
+    send_ref[...] = (widen(own_ref[:, other]) + widen(got_ref[:, other])).astype(BF16)
 
 
 def fold(own, got, at, bit, low):
@@ -678,7 +679,7 @@
             num_scalar_prefetch=1, grid=(n // tile,), in_specs=[both, both], out_specs=[half, half]
         ),
         out_shape=[
-            jax.ShapeDtypeStruct((high, low, rows, n), F32), sent((high, low, rows, n)),
+            jax.ShapeDtypeStruct((high, low, rows, n), KEEP), sent((high, low, rows, n)),
         ],
         compiler_params=pltpu.CompilerParams(vmem_limit_bytes=LESS),
         cost_estimate=HINT,
@@ -687,7 +688,7 @@
 
 
 def settle_kernel(own_ref, got_ref, out_ref, low_ref):
-    v = own_ref[...] + widen(got_ref[...])
+    v = widen(own_ref[...]) + widen(got_ref[...])
     out_ref[...] = v
     low_ref[...] = v.astype(BF16)
 
@@ -867,7 +868,7 @@
     admitted = conv.reshape(2 * length, half_r).astype(BF16)
     admitted_all = natural(admitted, swap_rows(admitted))
     gates = matmul(admitted_all, w2)
-    mixed, before = recurrence_forward(pre, gates, admitted, params, length)
+    mixed, *factors = recurrence_forward(pre, gates, admitted, params, length)
     tock(mixed)
     admitted_all, = tick(admitted_all)
     admitted_t = flip(admitted_all)
@@ -924,7 +925,7 @@
     def mixer():
         low, other = tick(*have["middle_low"])
         have["branch_low"], have["gates_cot"], have["direct"], have["sums"], near, far = chain_back(
-            here_side, low, other, whole, at, per_r, pre, gates, admitted, before, params
+            here_side, low, other, whole, at, per_r, factors
         )
         have["out_cot"] = jnp.concatenate([low, other], axis=0)
         tock(near, far)
@@ -985,7 +986,7 @@
     late("d", lambda: have["hidden_t"], lambda: cot_pair)
     late("g", lambda: have["normed_two_t"], lambda: have["gate_cot"])
     late("u", lambda: have["normed_two_t"], lambda: have["up_cot"], z_first)
-    late("r", lambda: admitted_t, lambda: have["gates_cot"])
+    late("r", lambda: admitted_t, lambda: have["gates_cot"], z_first)
     late("b", lambda: normed_t, lambda: have["pre_cot"])
     late("o", lambda: mixed_t, lambda: have["out_cot"], columns=width // 2, skip=-1)
 

time: 613 us -> 596 us (0.972)
  waiting for transfers between devices: 236 us -> 217 us
    ppermute x17, waiting for transfers between devices: 79.3 us -> 67.2 us  [swap(): return lax.ppermute(v, 'rep', [(i, i ^ 1) for i in range(groups)])]
    unnamed x185 -> x173, local copies, waits for them, and re-layouts: 27.1 us -> 23.4 us
  transfers between devices with their start and end apart: 44 -> 44, of which waited for: 19 -> 18; matrix products, arithmetic and copies ran while one was open for 8% -> 8% of each run, Pallas kernels for 30% -> 31%
where the time goes in v5:
time: 596 us; the launch traced here: 591 us
  Pallas kernels  224 us (38%)
  waiting for transfers between devices  217 us (36%)
  starting transfers between devices  45.7 us (8%)
  local copies, waits for them, and re-layouts  43 us (7%)
  blocking collectives  23 us (4%)
  between operations  14.9 us (2%)
  matrix products  11.8 us (2%)
  other arithmetic  11.7 us (2%)
    ppermute x24, waiting for transfers between devices, cross(): return lax.ppermute(v, 'shard', [(i, i ^ 1 << bit) for i in range(shards)])  76.7 us
    ppermute x17, waiting for transfers between devices, swap(): return lax.ppermute(v, 'rep', [(i, i ^ 1) for i in range(groups)])  67.2 us
    all_gather x1, waiting for transfers between devices, body(): lax.all_gather(pack(here_side, [branch_proj, lruin_proj, recur_proj, admi...  59.6 us
    pallas_call x12, Pallas kernels, fold(): pl.pallas_call(functools.partial(fold_kernel, bit), grid_spec=pltpu.Prefe...  37.3 us
    pallas_call x6, Pallas kernels, grad_home(): pl.pallas_call(functools.partial(home_kernel, bit), grid_spec=pltpu.Prefe...  34.2 us
    ppermute x17, starting transfers between devices, swap(): return lax.ppermute(v, 'rep', [(i, i ^ 1) for i in range(groups)])  24.7 us
    pallas_call x6, Pallas kernels, grad_away(): pl.pallas_call(away_kernel, grid_spec=pltpu.PrefetchScalarGridSpec(num_sc...  24.4 us
    pallas_call x1, Pallas kernels, ffn_back(): pl.pallas_call(ffn_back_kernel, grid=(tiles,), in_specs=[pl.BlockSpec((to...  23.7 us
  transfers between devices with their start and end apart: 44, of which 18 were waited for; matrix products, arithmetic and copies ran while one was open for 8% of the time, Pallas kernels for 31%

profile of v5, /device:TPU:0, one launch (start us, length us, event | category | flops | bytes accessed | tf_op | source)
XLA Modules:
  0.0 591.0 jit_solution(8038474026799692588)
XLA Ops:
  24.7 3.0 collective-permute-start
  27.9 23.0 %all_gather.15 = bf16[16,10,128]{2,1,0:T(8,128)(2,1)S(1)} all-gather(bf16[1,10,128]{2,1,0:T(8,128)(2,1)S(1)} %pad_bitcast_fusion), channel_id=1, replica_groups=mesh['rep'=2,'shard'=16] {'shard'}, dimensions={0}, use_global_device_ids=true | all-gather | bytes 43520 | tf_op jit(solution)/shard_map/all_gather | solution.py:823
  51.7 10.4 %collective-permute-done.1 = bf16[256,1536]{1,0:T(8,128)(2,1)S(1)} collective-permute-done((bf16[256,1536]{1,0:T(8,128)(2,1)S(1)}, bf16[256,1536]{1,0:T(8,128)(2,1)S(1)}, u32[]{:S(2)}, u32[]{:S(2)}) %collective-permute-start.1) | collective-permute-done | bytes 786464 | tf_op jit(solution)/shard_map/ppermute | solution.py:736
  66.0 59.6 %all-gather.5.cloned.1.call-done = bf16[20480,512]{1,0:T(8,128)(2,1)} async-done(((bf16[1280,512]{1,0:T(8,128)(2,1)}), bf16[20480,512]{1,0:T(8,128)(2,1)}) %all-gather.5.cloned.1.call-update) | async-done | bytes 20971536 | tf_op jit(solution)/shard_map/all_gather | solution.py:846
  125.6 3.2 fusion.45
  128.8 3.4 fusion.8.pre_ref.lru_ref
  137.7 8.4 %fusion.44 = (bf16[16,128,512]{2,1,0:T(8,128)(2,1)S(1)}, bf16[16,128,512]{2,1,0:T(8,128)(2,1)}, bf16[16,128,512]{2,1,0:T(8,128)(2,1)}, bf16[16,128,512]{2,1,0:T(...) fusion(bf16[16,1280,512]{2,1,0:T(8,128)(2,1)} %bitcast.147), kind=kLoop, calls=%fused_computation.96 | loop fusion | bytes 29360128 | tf_op jit(solution)/shard_map/slice | solution.py:842
  146.1 14.5 %collective-permute-done.2 = bf16[512,1024]{1,0:T(8,128)(2,1)S(1)} collective-permute-done((bf16[512,1024]{1,0:T(8,128)(2,1)S(1)}, bf16[512,1024]{1,0:T(8,128)(2,1)S(1)}, u32[]{:S(2)}, u32[]{:S(2)}) %collective-permute-start.2) | collective-permute-done | bytes 1048608 | tf_op jit(solution)/shard_map/ppermute | solution.py:736
  161.4 6.5 %fusion.gates_r_ref.gates_i_ref = f32[512,2048]{1,0:T(8,128)} fusion(bf16[2048,512]{1,0:T(8,128)(2,1)S(1)} %bitcast.166, bf16[2048,512]{1,0:T(8,128)(2,1)S(1)} %bitcast.167, bf16[2048,512]{1,0:T(8,128)(2,1)S(1)} %bitcast.168, bf16[2048,512]{1,0:T(8,128)(2,1)S(1)} %bitcast.165, bf16[512,1024]{1,0:T(8,128)(2,1)S(1)} %get-tuple-element.377, ...), kind=kOutput, calls=%fused_computation | convolution fusion | flops 4332716032 | bytes 14680064 | tf_op jit(solution)/shard_map/dot_general | solution.py:38
  167.9 12.3 %recurrence_forward.1 = (bf16[512,1024]{1,0:T(8,128)(2,1)}, f32[512,1024]{1,0:T(8,128)}, f32[512,1024]{1,0:T(8,128)}, f32[512,1024]{1,0:T(8,128)}, f32[512,1024]...) custom-call(f32[512,2048]{1,0:T(8,128)} %copy-done.54, ...), custom_call_target="tpu_custom_call" | custom-call | flops 31457280 | bytes 10485760 | tf_op jit(solution)/shard_map/recurrence_forward/pallas_call | solution.py:433
  184.5 10.4 %collective-permute-done.3 = bf16[256,1024]{1,0:T(8,128)(2,1)S(1)} collective-permute-done((bf16[256,1024]{1,0:T(8,128)(2,1)S(1)}, bf16[256,1024]{1,0:T(8,128)(2,1)S(1)}, u32[]{:S(2)}, u32[]{:S(2)}) %collective-permute-start.3) | collective-permute-done | bytes 524320 | tf_op jit(solution)/shard_map/ppermute | solution.py:736
  199.3 10.6 %collective-permute-done.5 = bf16[256,1024]{1,0:T(8,128)(2,1)S(1)} collective-permute-done((bf16[256,1024]{1,0:T(8,128)(2,1)S(1)}, bf16[256,1024]{1,0:T(8,128)(2,1)S(1)}, u32[]{:S(2)}, u32[]{:S(2)}) %collective-permute-start.5) | collective-permute-done | bytes 524320 | tf_op jit(solution)/shard_map/ppermute | solution.py:736
  213.0 11.5 %collective-permute-done.4 = bf16[256,1536]{1,0:T(8,128)(2,1)S(1)} collective-permute-done((bf16[256,1536]{1,0:T(8,128)(2,1)S(1)}, bf16[256,1536]{1,0:T(8,128)(2,1)S(1)}, u32[]{:S(2)}, u32[]{:S(2)}) %collective-permute-start.4) | collective-permute-done | bytes 786464 | tf_op jit(solution)/shard_map/ppermute | solution.py:736
  224.6 13.4 %all-gather.7.cloned.1.call-done = bf16[13824,768]{1,0:T(8,128)(2,1)} async-done(((bf16[864,768]{1,0:T(8,128)(2,1)}), bf16[13824,768]{1,0:T(8,128)(2,1)}) %all-gather.7.cloned.1.call-update) | async-done | bytes 21233680 | tf_op jit(solution)/shard_map/all_gather | solution.py:838
  238.1 13.7 %hidden_pass.1 = (bf16[512,2304]{1,0:T(8,128)(2,1)S(1)}, bf16[2304,512]{1,0:T(8,128)(2,1)S(1)}, f32[512,2304]{1,0:T(8,128)}, f32[512,2304]{1,0:T(8,128)}) custom-call(bf16[512,1536]{1,0:T(8,128)(2,1)S(1)} %pad_maximum_fusion.2.x_ref, bf16[16,864,768]{2,1,0:T(8,128)(2,1)} %bitcast.183, bf16[16,864,768]{2,1,0:T(8,128)(2,1)} %bitcast.184), custom_call_target="tpu_custom_call" | custom-call | flops 99999997952 | bytes 1024 | tf_op jit(solution)/shard_map/hidden_pass/pallas_call | solution.py:463
  253.2 23.7 %ffn_back.1 = (bf16[512,2304]{1,0:T(8,128)(2,1)S(1)}, bf16[512,2304]{1,0:T(8,128)(2,1)S(1)}, f32[256,1536]{1,0:T(8,128)S(1)}, bf16[256,1536]{1,0:T(8,128)(2,1)}) custom-call(bf16[512,1536]{1,0:T(8,128)(2,1)S(1)} %copy-done.14, bf16[16,864,768]{2,1,0:T(8,128)(2,1)} %bitcast.185, bf16[16,864,768]{2,1,0:T(8,128)(2,1)} %bitcast.186, ...), custom_call_target="tpu_custom_call" | custom-call | flops 99999997952 | bytes 1024 | tf_op jit(solution)/shard_map/ffn_back/pallas_call | solution.py:536
  279.4 4.5 grad_away.6
  283.9 4.2 grad_away.7
  288.7 8.3 %collective-permute-done.7.far_ref = bf16[256,1536]{1,0:T(8,128)(2,1)} collective-permute-done((bf16[256,1536]{1,0:T(8,128)(2,1)}, bf16[256,1536]{1,0:T(8,128)(2,1)}, u32[]{:S(2)}, u32[]{:S(2)}) %collective-permute-start.7) | collective-permute-done | bytes 786464 | tf_op jit(solution)/shard_map/ppermute | solution.py:736
  297.0 3.6 norm_back.2
  302.1 6.1 %grad_home.6 = (bf16[2,2,96,2304]{3,2,1,0:T(8,128)(2,1)S(1)}, bf16[2,2,96,2304]{3,2,1,0:T(8,128)(2,1)}) custom-call(s32[5]{0:T(128)S(1)} %stack.24.at_ref, bf16[8,2,96,512]{3,2,1,0:T(8,128)(2,1)S(1)} %bitcast.129, bf16[1,512,2304]{2,1,0:T(8,128)(2,1)S(1)} %bitcast.117, bf16[8,96,2304]{2,1,0:T(8,128)(2,1)} %collective-permute-done.6.got_ref), custom_call_target="tpu_custom_call" | custom-call | flops 99999997952 | bytes 1024 | tf_op jit(solution)/shard_map/grad_home/pallas_call | solution.py:641
  309.6 5.7 grad_home.7
  316.6 4.6 grad_away.8
  321.2 18.2 %chain_back.1 = (bf16[512,1024]{1,0:T(8,128)(2,1)S(1)}, bf16[2,512,1024]{2,1,0:T(8,128)(2,1)S(1)}, f32[512,1024]{1,0:T(8,128)S(1)}, f32[48,1024]{1,0:T(8,128)S(1...) custom-call(s32[1]{0:T(128)} %bitcast.2.side_ref, bf16[256,1536]{1,0:T(8,128)(2,1)S(1)} %copy-done.8, ...), custom_call_target="tpu_custom_call" | custom-call | flops 99999997952 | bytes 1024 | tf_op jit(solution)/shard_map/chain_back/pallas_call | solution.py:173
  340.1 4.6 grad_away.9
  348.2 4.0 fold.12
  352.1 2.9 collective-permute-done.15
  356.3 3.4 fold.13
  360.2 6.1 %grad_home.8 = (bf16[4,1,96,2304]{3,2,1,0:T(8,128)(2,1)S(1)}, bf16[4,1,96,2304]{3,2,1,0:T(8,128)(2,1)}) custom-call(s32[5]{0:T(128)S(1)} %stack.24.at_ref, bf16[8,2,96,512]{3,2,1,0:T(8,128)(2,1)S(1)} %bitcast.131, bf16[1,512,2304]{2,1,0:T(8,128)(2,1)S(1)} %bitcast.113, bf16[8,96,2304]{2,1,0:T(8,128)(2,1)} %collective-permute-done.14.got_ref), custom_call_target="tpu_custom_call" | custom-call | flops 99999997952 | bytes 1024 | tf_op jit(solution)/shard_map/grad_home/pallas_call | solution.py:641
  368.3 6.6 %grad_home.9 = (bf16[2,2,128,2048]{3,2,1,0:T(8,128)(2,1)S(1)}, bf16[2,2,128,2048]{3,2,1,0:T(8,128)(2,1)}) custom-call(s32[5]{0:T(128)S(1)} %stack.24.at_ref, bf16[8,2,128,512]{3,2,1,0:T(8,128)(2,1)S(1)} %bitcast.121, bf16[2,512,1024]{2,1,0:T(8,128)(2,1)S(1)} %copy-done.43, bf16[8,128,2048]{2,1,0:T(8,128)(2,1)} %collective-permute-done.13.got_ref), custom_call_target="tpu_custom_call" | custom-call | flops 99999997952 | bytes 1024 | tf_op jit(solution)/shard_map/grad_home/pallas_call | solution.py:641
  376.3 9.5 %conv_back.1 = (bf16[2,512,1024]{2,1,0:T(8,128)(2,1)S(1)}, f32[8,1024]{1,0:T(8,128)S(1)}, f32[256,1536]{1,0:T(8,128)S(1)}, bf16[256,1536]{1,0:T(8,128)(2,1)}) custom-call(f32[512,1024]{1,0:T(8,128)S(1)} %copy-done.39, f32[512,1024]{1,0:T(8,128)S(1)} %copy-done.41, bf16[512,1024]{1,0:T(8,128)(2,1)} %collective-permute-done.12.far_in_ref, ...), custom_call_target="tpu_custom_call" | custom-call | flops 99999997952 | bytes 1024 | tf_op jit(solution)/shard_map/conv_back/pallas_call | solution.py:246
  385.8 3.6 fold.14
  389.4 2.4 collective-permute-start.16
  391.9 2.5 fold.15
  395.2 3.8 grad_away.10
  401.9 7.6 %collective-permute-done.16 = bf16[1,1,96,2304]{3,2,1,0:T(8,128)(2,1)} collective-permute-done((bf16[1,1,96,2304]{3,2,1,0:T(8,128)(2,1)}, bf16[1,1,96,2304]{3,2,1,0:T(8,128)(2,1)}, u32[]{:S(2)}, u32[]{:S(2)}) %collective-permute-start.16) | collective-permute-done | bytes 442400 | tf_op jit(solution)/shard_map/ppermute | solution.py:768
  409.5 2.9 settle.6
  412.4 9.9 %down_pass.1 = (f32[256,1536]{1,0:T(8,128)S(1)}, bf16[256,1536]{1,0:T(8,128)(2,1)}) custom-call(bf16[512,2304]{1,0:T(8,128)(2,1)S(1)} %copy-done.45, bf16[16,864,768]{2,1,0:T(8,128)(2,1)} %bitcast.189, bf16[16,864,768]{2,1,0:T(8,128)(2,1)} %bitcast.190), custom_call_target="tpu_custom_call" | custom-call | flops 99999997952 | bytes 1024 | tf_op jit(solution)/shard_map/down_pass/pallas_call | solution.py:566
  422.9 5.6 grad_home.10
  430.0 4.1 norm_back.3
  435.3 4.0 fold.16
  439.3 25.5 %collective-permute-done.22 = bf16[2,2,128,2048]{3,2,1,0:T(8,128)(2,1)} collective-permute-done((bf16[2,2,128,2048]{3,2,1,0:T(8,128)(2,1)}, bf16[2,2,128,2048]{3,2,1,0:T(8,128)(2,1)}, u32[]{:S(2)}, u32[]{:S(2)}) %collective-permute-start.22) | collective-permute-done | bytes 2097184 | tf_op jit(solution)/shard_map/ppermute | solution.py:768
  464.8 3.2 fold.17
  468.0 3.0 weave.2
  471.0 2.7 grad_away.11
  475.0 3.2 fold.18
  478.2 15.2 %collective-permute-done.28 = bf16[2,1,96,2304]{3,2,0,1:T(8,128)(2,1)} collective-permute-done((bf16[2,1,96,2304]{3,2,0,1:T(8,128)(2,1)}, bf16[2,1,96,2304]{3,2,0,1:T(8,128)(2,1)}, u32[]{:S(2)}, u32[]{:S(2)}) %collective-permute-start.28) | collective-permute-done | bytes 884768 | tf_op jit(solution)/shard_map/ppermute | solution.py:768
  493.4 3.4 fold.19
  501.5 4.1 grad_home.11
  507.9 2.6 fold.20
  510.5 8.7 %collective-permute-done.31 = bf16[1,1,96,2304]{3,2,1,0:T(8,128)(2,1)} collective-permute-done((bf16[1,1,96,2304]{3,2,1,0:T(8,128)(2,1)}, bf16[1,1,96,2304]{3,2,1,0:T(8,128)(2,1)}, u32[]{:S(2)}, u32[]{:S(2)}) %collective-permute-start.31) | collective-permute-done | bytes 442400 | tf_op jit(solution)/shard_map/ppermute | solution.py:768
  519.2 2.7 settle.8
  522.5 2.3 join_rows.1
  524.8 2.5 fold.21
  527.3 11.9 %collective-permute-done.25 = bf16[2,1,96,2048]{3,2,0,1:T(8,128)(2,1)} collective-permute-done((bf16[2,1,96,2048]{3,2,0,1:T(8,128)(2,1)}, bf16[2,1,96,2048]{3,2,0,1:T(8,128)(2,1)}, u32[]{:S(2)}, u32[]{:S(2)}) %collective-permute-start.25) | collective-permute-done | bytes 786464 | tf_op jit(solution)/shard_map/ppermute | solution.py:768
  539.2 2.5 fold.22
  542.5 2.8 weave.3
  545.4 3.0 collective-permute-done.35
  552.2 6.8 %collective-permute-start.39 = (bf16[128,2048]{1,0:T(8,128)(2,1)}, bf16[128,2048]{1,0:T(8,128)(2,1)}, u32[]{:S(2)}, u32[]{:S(2)}) collective-permute-start(bf16[128,2048]{1,0:T(8,128)(2,1)} %get-tuple-element.339), channel_id=1, source_target_pairs={{0,16},{16,0},{1,17},{17,1},{2,18},{18,2},{3,19},{19,3},{4,20},{20... | collective-permute-start | bytes 1572872 | tf_op jit(solution)/shard_map/ppermute | solution.py:736
  561.3 2.3 fold.23
  563.6 2.9 collective-permute-start.38
  568.4 2.4 collective-permute-start.37
  570.8 2.5 add_convert_fusion
  573.3 2.4 join_columns.3
  (309 shorter events, 91.0 us)
Async XLA Ops:
  7.2 118.4 %all-gather.5.cloned.1.call-start = ((), (), s32[]{:S(2)}) async-start(), calls=%async_computation.1 | async-start | bytes 22282240 | tf_op jit(solution)/shard_map/all_gather | solution.py:846
  13.5 224.6 %all-gather.7.cloned.1.call-start = ((), (), s32[]{:S(2)}) async-start(), calls=%async_computation.2 | async-start | bytes 22560768 | tf_op jit(solution)/shard_map/all_gather | solution.py:838
  24.7 534.3 %all-reduce.6.cloned.1.call-start = ((), (), s32[]{:S(2)}) async-start(), calls=%async_computation | async-start | bytes 131072 | tf_op jit(solution)/shard_map/psum | solution.py:969
  24.7 26.6 %collective-permute-start = (bf16[256,1536]{1,0:T(8,128)(2,1)S(1)}, bf16[256,1536]{1,0:T(8,128)(2,1)S(1)}, u32[]{:S(2)}, u32[]{:S(2)}) collective-permute-start(bf16[256,1536]{1,0:T(8,128)(2,1)S(1)} %copy-done.3), channel_id=1, source_target_pairs={{0,16},{16,0},{1,17},{17,1},{2,18},{18,2},{3,19},{19,3},{4,20},{20... | collective-permute-start | bytes 2359304 | tf_op jit(solution)/shard_map/ppermute | solution.py:736
  27.7 34.5 %collective-permute-start.1 = (bf16[256,1536]{1,0:T(8,128)(2,1)S(1)}, bf16[256,1536]{1,0:T(8,128)(2,1)S(1)}, u32[]{:S(2)}, u32[]{:S(2)}) collective-permute-start(bf16[256,1536]{1,0:T(8,128)(2,1)S(1)} %copy-done.6), channel_id=1, source_target_pairs={{0,16},{16,0},{1,17},{17,1},{2,18},{18,2},{3,19},{19,3},{4,20},{20... | collective-permute-start | bytes 2359304 | tf_op jit(solution)/shard_map/ppermute | solution.py:736
  51.1 11.1 %copy-start.67 = (f32[1536]{0:T(1024)}, f32[1536]{0:T(1024)S(1)}, u32[]{:S(2)}) copy-start(f32[1536]{0:T(1024)S(1)} %reshape.324) | copy-start | bytes 18436
  135.3 25.5 %copy-start.55 = (bf16[2,256,1024]{2,1,0:T(8,128)(2,1)}, bf16[2,256,1024]{2,1,0:T(8,128)(2,1)S(1)}, u32[]{:S(2)}) copy-start(bf16[2,256,1024]{2,1,0:T(8,128)(2,1)S(1)} %fusion.32) | copy-start | bytes 3145732
  135.3 25.4 %collective-permute-start.2 = (bf16[512,1024]{1,0:T(8,128)(2,1)S(1)}, bf16[512,1024]{1,0:T(8,128)(2,1)S(1)}, u32[]{:S(2)}, u32[]{:S(2)}) collective-permute-start(bf16[512,1024]{1,0:T(8,128)(2,1)S(1)} %bitcast.155), channel_id=1, source_target_pairs={{0,16},{16,0},{1,17},{17,1},{2,18},{18,2},{3,19},{19,3},{4,20},{20... | collective-permute-start | bytes 3145736 | tf_op jit(solution)/shard_map/ppermute | solution.py:736
  136.9 61.6 %copy-start.69 = (f32[1536]{0:T(1024)}, f32[1536]{0:T(1024)S(1)}, u32[]{:S(2)}) copy-start(f32[1536]{0:T(1024)S(1)} %reshape.325) | copy-start | bytes 18436
  137.0 258.1 %copy-start.15 = (s32[5]{0:T(128)}, s32[5]{0:T(128)S(1)}, u32[]{:S(2)}) copy-start(s32[5]{0:T(128)S(1)} %stack.24.at_ref) | copy-start | bytes 64
  181.5 13.5 %copy-start.66 = (bf16[512,1024]{1,0:T(8,128)(2,1)S(1)}, bf16[512,1024]{1,0:T(8,128)(2,1)}, u32[]{:S(2)}) copy-start(bf16[512,1024]{1,0:T(8,128)(2,1)} %get-tuple-element.192) | copy-start | bytes 3145732
  181.5 13.4 %collective-permute-start.3 = (bf16[256,1024]{1,0:T(8,128)(2,1)S(1)}, bf16[256,1024]{1,0:T(8,128)(2,1)S(1)}, u32[]{:S(2)}, u32[]{:S(2)}) collective-permute-start(bf16[256,1024]{1,0:T(8,128)(2,1)S(1)} %slice.172), channel_id=1, source_target_pairs={{0,16},{16,0},{1,17},{17,1},{2,18},{18,2},{3,19},{19,3},{4,20},{20... | collective-permute-start | bytes 1572872 | tf_op jit(solution)/shard_map/ppermute | solution.py:736
  183.0 13.6 %copy-start.60 = (bf16[16,128,512]{2,1,0:T(8,128)(2,1)S(1)}, bf16[16,128,512]{2,1,0:T(8,128)(2,1)}, u32[]{:S(2)}) copy-start(bf16[16,128,512]{2,1,0:T(8,128)(2,1)} %get-tuple-element.366) | copy-start | bytes 6291460
  183.0 13.6 %copy-start.61 = (bf16[16,128,512]{2,1,0:T(8,128)(2,1)S(1)}, bf16[16,128,512]{2,1,0:T(8,128)(2,1)}, u32[]{:S(2)}) copy-start(bf16[16,128,512]{2,1,0:T(8,128)(2,1)} %get-tuple-element.367) | copy-start | bytes 6291460
  183.0 13.6 %copy-start.62 = (bf16[16,128,512]{2,1,0:T(8,128)(2,1)S(1)}, bf16[16,128,512]{2,1,0:T(8,128)(2,1)}, u32[]{:S(2)}) copy-start(bf16[16,128,512]{2,1,0:T(8,128)(2,1)} %get-tuple-element.368) | copy-start | bytes 6291460
  184.5 12.1 %copy-start.25 = (bf16[2048,512]{1,0:T(8,128)(2,1)}, bf16[2048,512]{1,0:T(8,128)(2,1)S(1)}, u32[]{:S(2)}) copy-start(bf16[2048,512]{1,0:T(8,128)(2,1)S(1)} %flip.5) | copy-start | bytes 6291460
  184.5 12.1 %copy-start.4 = (bf16[256,1536]{1,0:T(8,128)(2,1)S(1)}, bf16[256,1536]{1,0:T(8,128)(2,1)}, u32[]{:S(2)}) copy-start(bf16[256,1536]{1,0:T(8,128)(2,1)} %v_ref.1) | copy-start | bytes 2359300
  195.0 14.9 %collective-permute-start.5 = (bf16[256,1024]{1,0:T(8,128)(2,1)S(1)}, bf16[256,1024]{1,0:T(8,128)(2,1)S(1)}, u32[]{:S(2)}, u32[]{:S(2)}) collective-permute-start(bf16[256,1024]{1,0:T(8,128)(2,1)S(1)} %get-tuple-element.382), channel_id=1, source_target_pairs={{0,16},{16,0},{1,17},{17,1},{2,18},{18,2},{3,19},{19,3},{4,20},{20... | collective-permute-start | bytes 1572872 | tf_op jit(solution)/shard_map/ppermute | solution.py:736
  198.5 11.6 %copy-start = (f32[256,1536]{1,0:T(8,128)}, f32[256,1536]{1,0:T(8,128)S(1)}, u32[]{:S(2)}) copy-start(f32[256,1536]{1,0:T(8,128)S(1)} %get-tuple-element.406.v_ref) | copy-start | bytes 4718596
  198.7 25.8 %collective-permute-start.4 = (bf16[256,1536]{1,0:T(8,128)(2,1)S(1)}, bf16[256,1536]{1,0:T(8,128)(2,1)S(1)}, u32[]{:S(2)}, u32[]{:S(2)}) collective-permute-start(bf16[256,1536]{1,0:T(8,128)(2,1)S(1)} %multiply_convert_fusion), channel_id=1, source_target_pairs={{0,16},{16,0},{1,17},{17,1},{2,18},{18,2},{3,19},{19,3},{4,20},{20... | collective-permute-start | bytes 2359304 | tf_op jit(solution)/shard_map/ppermute | solution.py:736
  238.1 15.1 %copy-start.14 = (bf16[512,1536]{1,0:T(8,128)(2,1)S(1)}, bf16[512,1536]{1,0:T(8,128)(2,1)}, u32[]{:S(2)}) copy-start(bf16[512,1536]{1,0:T(8,128)(2,1)} %copy-done.13) | copy-start | bytes 4718596
  276.9 39.7 %copy-start.21 = (bf16[512,2304]{1,0:T(8,128)(2,1)}, bf16[512,2304]{1,0:T(8,128)(2,1)S(1)}, u32[]{:S(2)}) copy-start(bf16[512,2304]{1,0:T(8,128)(2,1)S(1)} %get-tuple-element.219) | copy-start | bytes 7077892
  276.9 20.0 %collective-permute-start.7 = (bf16[256,1536]{1,0:T(8,128)(2,1)}, bf16[256,1536]{1,0:T(8,128)(2,1)}, u32[]{:S(2)}, u32[]{:S(2)}) collective-permute-start(bf16[256,1536]{1,0:T(8,128)(2,1)} %get-tuple-element.206), channel_id=1, source_target_pairs={{0,16},{16,0},{1,17},{17,1},{2,18},{18,2},{3,19},{19,3},{4,20},{20... | collective-permute-start | bytes 2359304 | tf_op jit(solution)/shard_map/ppermute | solution.py:736
  279.4 37.2 %copy-start.34 = (bf16[1536,512]{1,0:T(8,128)(2,1)}, bf16[1536,512]{1,0:T(8,128)(2,1)S(1)}, u32[]{:S(2)}) copy-start(bf16[1536,512]{1,0:T(8,128)(2,1)S(1)} %flip.7) | copy-start | bytes 4718596
  283.9 18.2 %collective-permute-start.6 = (bf16[8,96,2304]{2,1,0:T(8,128)(2,1)}, bf16[8,96,2304]{2,1,0:T(8,128)(2,1)}, u32[]{:S(2)}, u32[]{:S(2)}) collective-permute-start(bf16[8,96,2304]{2,1,0:T(8,128)(2,1)} %grad_away.6), channel_id=1, source_target_pairs={{0,1},{1,0},{2,3},{3,2},{4,5},{5,4},{6,7},{7,6},{8,9},{9,8},{10,11... | collective-permute-start | bytes 10616840 | tf_op jit(solution)/shard_map/ppermute | solution.py:768
  283.9 13.0 %copy-start.70 = (f32[1536]{0:T(1024)S(1)}, f32[1536]{0:T(1024)}, u32[]{:S(2)}) copy-start(f32[1536]{0:T(1024)} %copy-done.69) | copy-start | bytes 18436
  283.9 13.0 %copy-start.1 = (f32[256,1536]{1,0:T(8,128)S(1)}, f32[256,1536]{1,0:T(8,128)}, u32[]{:S(2)}) copy-start(f32[256,1536]{1,0:T(8,128)} %copy-done) | copy-start | bytes 4718596
  283.9 13.0 %copy-start.7 = (bf16[256,1536]{1,0:T(8,128)(2,1)S(1)}, bf16[256,1536]{1,0:T(8,128)(2,1)}, u32[]{:S(2)}) copy-start(bf16[256,1536]{1,0:T(8,128)(2,1)} %base_ref.1) | copy-start | bytes 2359300
  288.2 21.5 %collective-permute-start.10 = (bf16[8,144,1536]{2,1,0:T(8,128)(2,1)}, bf16[8,144,1536]{2,1,0:T(8,128)(2,1)}, u32[]{:S(2)}, u32[]{:S(2)}) collective-permute-start(bf16[8,144,1536]{2,1,0:T(8,128)(2,1)} %grad_away.7), channel_id=1, source_target_pairs={{0,1},{1,0},{2,3},{3,2},{4,5},{5,4},{6,7},{7,6},{8,9},{9,8},{10,11... | collective-permute-start | bytes 10616840 | tf_op jit(solution)/shard_map/ppermute | solution.py:768
  300.6 20.6 %collective-permute-start.9 = (bf16[256,1536]{1,0:T(8,128)(2,1)}, bf16[256,1536]{1,0:T(8,128)(2,1)}, u32[]{:S(2)}, u32[]{:S(2)}) collective-permute-start(bf16[256,1536]{1,0:T(8,128)(2,1)} %get-tuple-element.225.own_ref), channel_id=1, source_target_pairs={{0,16},{16,0},{1,17},{17,1},{2,18},{18,2},{3,19},{19,3},{4,20},{20... | collective-permute-start | bytes 2359304 | tf_op jit(solution)/shard_map/ppermute | solution.py:736
  308.2 40.0 %collective-permute-start.8 = (bf16[2,2,96,2304]{3,2,1,0:T(8,128)(2,1)}, bf16[2,2,96,2304]{3,2,1,0:T(8,128)(2,1)}, u32[]{:S(2)}, u32[]{:S(2)}) collective-permute-start(bf16[2,2,96,2304]{3,2,1,0:T(8,128)(2,1)} %get-tuple-element.218), channel_id=1, source_target_pairs={{0,4},{1,5},{2,6},{3,7},{4,0},{5,1},{6,2},{7,3},{8,12},{9,13},{10,... | collective-permute-start | bytes 5308424 | tf_op jit(solution)/shard_map/ppermute | solution.py:768
  315.3 39.7 %collective-permute-start.15 = (bf16[4,1,144,1536]{3,2,1,0:T(8,128)(2,1)}, bf16[4,1,144,1536]{3,2,1,0:T(8,128)(2,1)}, u32[]{:S(2)}, u32[]{:S(2)}) collective-permute-start(bf16[4,1,144,1536]{3,2,1,0:T(8,128)(2,1)} %get-tuple-element.223), channel_id=1, source_target_pairs={{0,2},{1,3},{2,0},{3,1},{4,6},{5,7},{6,4},{7,5},{8,10},{9,11},{10,... | collective-permute-start | bytes 5308424 | tf_op jit(solution)/shard_map/ppermute | solution.py:768
  321.2 39.0 %collective-permute-start.14 = (bf16[8,96,2304]{2,1,0:T(8,128)(2,1)}, bf16[8,96,2304]{2,1,0:T(8,128)(2,1)}, u32[]{:S(2)}, u32[]{:S(2)}) collective-permute-start(bf16[8,96,2304]{2,1,0:T(8,128)(2,1)} %grad_away.8), channel_id=1, source_target_pairs={{0,1},{1,0},{2,3},{3,2},{4,5},{5,4},{6,7},{7,6},{8,9},{9,8},{10,11... | collective-permute-start | bytes 10616840 | tf_op jit(solution)/shard_map/ppermute | solution.py:768
  321.2 18.9 %copy-start.26 = (bf16[2048,512]{1,0:T(8,128)(2,1)S(1)}, bf16[2048,512]{1,0:T(8,128)(2,1)}, u32[]{:S(2)}) copy-start(bf16[2048,512]{1,0:T(8,128)(2,1)} %copy-done.25) | copy-start | bytes 6291460
  339.4 36.8 %collective-permute-start.12 = (bf16[512,1024]{1,0:T(8,128)(2,1)}, bf16[512,1024]{1,0:T(8,128)(2,1)}, u32[]{:S(2)}, u32[]{:S(2)}) collective-permute-start(bf16[512,1024]{1,0:T(8,128)(2,1)} %get-tuple-element.236), channel_id=1, source_target_pairs={{0,16},{16,0},{1,17},{17,1},{2,18},{18,2},{3,19},{19,3},{4,20},{20... | collective-permute-start | bytes 3145736 | tf_op jit(solution)/shard_map/ppermute | solution.py:736
  344.7 23.6 %collective-permute-start.13 = (bf16[8,128,2048]{2,1,0:T(8,128)(2,1)}, bf16[8,128,2048]{2,1,0:T(8,128)(2,1)}, u32[]{:S(2)}, u32[]{:S(2)}) collective-permute-start(bf16[8,128,2048]{2,1,0:T(8,128)(2,1)} %grad_away.9), channel_id=1, source_target_pairs={{0,1},{1,0},{2,3},{3,2},{4,5},{5,4},{6,7},{7,6},{8,9},{9,8},{10,11... | collective-permute-start | bytes 12582920 | tf_op jit(solution)/shard_map/ppermute | solution.py:768
  355.0 30.8 %collective-permute-start.11 = (bf16[2,1,96,2304]{3,2,0,1:T(8,128)(2,1)}, bf16[2,1,96,2304]{3,2,0,1:T(8,128)(2,1)}, u32[]{:S(2)}, u32[]{:S(2)}) collective-permute-start(bf16[2,1,96,2304]{3,2,0,1:T(8,128)(2,1)} %bitcast.191), channel_id=1, source_target_pairs={{0,2},{1,3},{2,0},{3,1},{4,6},{5,7},{6,4},{7,5},{8,10},{9,11},{10,... | collective-permute-start | bytes 2654216 | tf_op jit(solution)/shard_map/ppermute | solution.py:768
  359.7 32.2 %collective-permute-start.17 = (bf16[2,1,144,1536]{3,2,0,1:T(8,128)(2,1)}, bf16[2,1,144,1536]{3,2,0,1:T(8,128)(2,1)}, u32[]{:S(2)}, u32[]{:S(2)}) collective-permute-start(bf16[2,1,144,1536]{3,2,0,1:T(8,128)(2,1)} %bitcast.192), channel_id=1, source_target_pairs={{0,4},{1,5},{2,6},{3,7},{4,0},{5,1},{6,2},{7,3},{8,12},{9,13},{10,... | collective-permute-start | bytes 2654216 | tf_op jit(solution)/shard_map/ppermute | solution.py:768
  367.5 66.6 %collective-permute-start.23 = (bf16[4,1,96,2304]{3,2,1,0:T(8,128)(2,1)}, bf16[4,1,96,2304]{3,2,1,0:T(8,128)(2,1)}, u32[]{:S(2)}, u32[]{:S(2)}) collective-permute-start(bf16[4,1,96,2304]{3,2,1,0:T(8,128)(2,1)} %get-tuple-element.250), channel_id=1, source_target_pairs={{0,2},{1,3},{2,0},{3,1},{4,6},{5,7},{6,4},{7,5},{8,10},{9,11},{10,... | collective-permute-start | bytes 5308424 | tf_op jit(solution)/shard_map/ppermute | solution.py:768
  389.4 20.0 %collective-permute-start.16 = (bf16[1,1,96,2304]{3,2,1,0:T(8,128)(2,1)}, bf16[1,1,96,2304]{3,2,1,0:T(8,128)(2,1)}, u32[]{:S(2)}, u32[]{:S(2)}) collective-permute-start(bf16[1,1,96,2304]{3,2,1,0:T(8,128)(2,1)} %get-tuple-element.265), channel_id=1, source_target_pairs={{0,8},{1,9},{2,10},{3,11},{4,12},{5,13},{6,14},{7,15},{8,0},{9,1},... | collective-permute-start | bytes 1327112 | tf_op jit(solution)/shard_map/ppermute | solution.py:768
  399.1 23.2 %collective-permute-start.19 = (bf16[8,96,2048]{2,1,0:T(8,128)(2,1)}, bf16[8,96,2048]{2,1,0:T(8,128)(2,1)}, u32[]{:S(2)}, u32[]{:S(2)}) collective-permute-start(bf16[8,96,2048]{2,1,0:T(8,128)(2,1)} %grad_away.10), channel_id=1, source_target_pairs={{0,1},{1,0},{2,3},{3,2},{4,5},{5,4},{6,7},{7,6},{8,9},{9,8},{10,11... | collective-permute-start | bytes 9437192 | tf_op jit(solution)/shard_map/ppermute | solution.py:768
  399.1 29.4 %collective-permute-start.24 = (bf16[256,1536]{1,0:T(8,128)(2,1)}, bf16[256,1536]{1,0:T(8,128)(2,1)}, u32[]{:S(2)}, u32[]{:S(2)}) collective-permute-start(bf16[256,1536]{1,0:T(8,128)(2,1)} %get-tuple-element.260), channel_id=1, source_target_pairs={{0,16},{16,0},{1,17},{17,1},{2,18},{18,2},{3,19},{19,3},{4,20},{20... | collective-permute-start | bytes 2359304 | tf_op jit(solution)/shard_map/ppermute | solution.py:736
  399.7 65.0 %collective-permute-start.22 = (bf16[2,2,128,2048]{3,2,1,0:T(8,128)(2,1)}, bf16[2,2,128,2048]{3,2,1,0:T(8,128)(2,1)}, u32[]{:S(2)}, u32[]{:S(2)}) collective-permute-start(bf16[2,2,128,2048]{3,2,1,0:T(8,128)(2,1)} %get-tuple-element.254), channel_id=1, source_target_pairs={{0,4},{1,5},{2,6},{3,7},{4,0},{5,1},{6,2},{7,3},{8,12},{9,13},{10,... | collective-permute-start | bytes 6291464 | tf_op jit(solution)/shard_map/ppermute | solution.py:768
  409.4 89.6 %collective-permute-start.27 = (bf16[1,1,144,1536]{3,2,1,0:T(8,128)(2,1)}, bf16[1,1,144,1536]{3,2,1,0:T(8,128)(2,1)}, u32[]{:S(2)}, u32[]{:S(2)}) collective-permute-start(bf16[1,1,144,1536]{3,2,1,0:T(8,128)(2,1)} %get-tuple-element.271), channel_id=1, source_target_pairs={{0,8},{1,9},{2,10},{3,11},{4,12},{5,13},{6,14},{7,15},{8,0},{9,1},... | collective-permute-start | bytes 1327112 | tf_op jit(solution)/shard_map/ppermute | solution.py:768
  412.4 10.4 %copy-start.33 = (bf16[1536,512]{1,0:T(8,128)(2,1)S(1)}, bf16[1536,512]{1,0:T(8,128)(2,1)}, u32[]{:S(2)}) copy-start(bf16[1536,512]{1,0:T(8,128)(2,1)} %copy-done.31) | copy-start | bytes 4718596
  422.3 45.7 %collective-permute-start.21 = (bf16[96,2304]{1,0:T(8,128)(2,1)}, bf16[96,2304]{1,0:T(8,128)(2,1)}, u32[]{:S(2)}, u32[]{:S(2)}) collective-permute-start(bf16[96,2304]{1,0:T(8,128)(2,1)} %get-tuple-element.278), channel_id=1, source_target_pairs={{0,16},{16,0},{1,17},{17,1},{2,18},{18,2},{3,19},{19,3},{4,20},{20... | collective-permute-start | bytes 1327112 | tf_op jit(solution)/shard_map/ppermute | solution.py:736
  428.5 142.3 %collective-permute-start.18 = (bf16[256,1536]{1,0:T(8,128)(2,1)}, bf16[256,1536]{1,0:T(8,128)(2,1)}, u32[]{:S(2)}, u32[]{:S(2)}) collective-permute-start(bf16[256,1536]{1,0:T(8,128)(2,1)} %get-tuple-element.281), channel_id=1, source_target_pairs={{0,16},{16,0},{1,17},{17,1},{2,18},{18,2},{3,19},{19,3},{4,20},{20... | collective-permute-start | bytes 2359304 | tf_op jit(solution)/shard_map/ppermute | solution.py:736
  434.1 39.7 %collective-permute-start.20 = (bf16[4,1,96,2048]{3,2,1,0:T(8,128)(2,1)}, bf16[4,1,96,2048]{3,2,1,0:T(8,128)(2,1)}, u32[]{:S(2)}, u32[]{:S(2)}) collective-permute-start(bf16[4,1,96,2048]{3,2,1,0:T(8,128)(2,1)} %get-tuple-element.285), channel_id=1, source_target_pairs={{0,2},{1,3},{2,0},{3,1},{4,6},{5,7},{6,4},{7,5},{8,10},{9,11},{10,... | collective-permute-start | bytes 4718600 | tf_op jit(solution)/shard_map/ppermute | solution.py:768
  435.3 29.5 %copy-start.28 = (bf16[2,2,128,2048]{3,2,1,0:T(8,128)(2,1)S(1)}, bf16[2,2,128,2048]{3,2,1,0:T(8,128)(2,1)}, u32[]{:S(2)}) copy-start(bf16[2,2,128,2048]{3,2,1,0:T(8,128)(2,1)} %copy-done.27) | copy-start | bytes 6291460
  471.0 22.4 %collective-permute-start.28 = (bf16[2,1,96,2304]{3,2,0,1:T(8,128)(2,1)}, bf16[2,1,96,2304]{3,2,0,1:T(8,128)(2,1)}, u32[]{:S(2)}, u32[]{:S(2)}) collective-permute-start(bf16[2,1,96,2304]{3,2,0,1:T(8,128)(2,1)} %bitcast.62), channel_id=1, source_target_pairs={{0,4},{1,5},{2,6},{3,7},{4,0},{5,1},{6,2},{7,3},{8,12},{9,13},{10,... | collective-permute-start | bytes 2654216 | tf_op jit(solution)/shard_map/ppermute | solution.py:768
  473.7 27.8 %collective-permute-start.26 = (bf16[8,128,768]{2,1,0:T(8,128)(2,1)}, bf16[8,128,768]{2,1,0:T(8,128)(2,1)}, u32[]{:S(2)}, u32[]{:S(2)}) collective-permute-start(bf16[8,128,768]{2,1,0:T(8,128)(2,1)} %grad_away.11), channel_id=1, source_target_pairs={{0,1},{1,0},{2,3},{3,2},{4,5},{5,4},{6,7},{7,6},{8,9},{9,8},{10,11... | collective-permute-start | bytes 4718600 | tf_op jit(solution)/shard_map/ppermute | solution.py:768
  473.7 32.3 %collective-permute-start.32 = (bf16[2,1,128,2048]{3,2,0,1:T(8,128)(2,1)}, bf16[2,1,128,2048]{3,2,0,1:T(8,128)(2,1)}, u32[]{:S(2)}, u32[]{:S(2)}) collective-permute-start(bf16[2,1,128,2048]{3,2,0,1:T(8,128)(2,1)} %bitcast.67), channel_id=1, source_target_pairs={{0,2},{1,3},{2,0},{3,1},{4,6},{5,7},{6,4},{7,5},{8,10},{9,11},{10,... | collective-permute-start | bytes 3145736 | tf_op jit(solution)/shard_map/ppermute | solution.py:768
  496.8 22.4 %collective-permute-start.31 = (bf16[1,1,96,2304]{3,2,1,0:T(8,128)(2,1)}, bf16[1,1,96,2304]{3,2,1,0:T(8,128)(2,1)}, u32[]{:S(2)}, u32[]{:S(2)}) collective-permute-start(bf16[1,1,96,2304]{3,2,1,0:T(8,128)(2,1)} %get-tuple-element.307), channel_id=1, source_target_pairs={{0,8},{1,9},{2,10},{3,11},{4,12},{5,13},{6,14},{7,15},{8,0},{9,1},... | collective-permute-start | bytes 1327112 | tf_op jit(solution)/shard_map/ppermute | solution.py:768
  500.9 21.1 %collective-permute-start.30 = (bf16[144,1536]{1,0:T(8,128)(2,1)}, bf16[144,1536]{1,0:T(8,128)(2,1)}, u32[]{:S(2)}, u32[]{:S(2)}) collective-permute-start(bf16[144,1536]{1,0:T(8,128)(2,1)} %get-tuple-element.311), channel_id=1, source_target_pairs={{0,16},{16,0},{1,17},{17,1},{2,18},{18,2},{3,19},{19,3},{4,20},{20... | collective-permute-start | bytes 1327112 | tf_op jit(solution)/shard_map/ppermute | solution.py:736
  505.5 19.2 %collective-permute-start.29 = (bf16[4,1,128,768]{3,2,1,0:T(8,128)(2,1)}, bf16[4,1,128,768]{3,2,1,0:T(8,128)(2,1)}, u32[]{:S(2)}, u32[]{:S(2)}) collective-permute-start(bf16[4,1,128,768]{3,2,1,0:T(8,128)(2,1)} %get-tuple-element.315), channel_id=1, source_target_pairs={{0,2},{1,3},{2,0},{3,1},{4,6},{5,7},{6,4},{7,5},{8,10},{9,11},{10,... | collective-permute-start | bytes 2359304 | tf_op jit(solution)/shard_map/ppermute | solution.py:768
  506.1 33.1 %collective-permute-start.25 = (bf16[2,1,96,2048]{3,2,0,1:T(8,128)(2,1)}, bf16[2,1,96,2048]{3,2,0,1:T(8,128)(2,1)}, u32[]{:S(2)}, u32[]{:S(2)}) collective-permute-start(bf16[2,1,96,2048]{3,2,0,1:T(8,128)(2,1)} %bitcast.61), channel_id=1, source_target_pairs={{0,4},{1,5},{2,6},{3,7},{4,0},{5,1},{6,2},{7,3},{8,12},{9,13},{10,... | collective-permute-start | bytes 2359304 | tf_op jit(solution)/shard_map/ppermute | solution.py:768
  519.2 29.1 %collective-permute-start.35 = (bf16[1,1,128,2048]{3,2,1,0:T(8,128)(2,1)}, bf16[1,1,128,2048]{3,2,1,0:T(8,128)(2,1)}, u32[]{:S(2)}, u32[]{:S(2)}) collective-permute-start(bf16[1,1,128,2048]{3,2,1,0:T(8,128)(2,1)} %get-tuple-element.319), channel_id=1, source_target_pairs={{0,8},{1,9},{2,10},{3,11},{4,12},{5,13},{6,14},{7,15},{8,0},{9,1},... | collective-permute-start | bytes 1572872 | tf_op jit(solution)/shard_map/ppermute | solution.py:768
  522.0 20.5 %collective-permute-start.36 = (bf16[96,2304]{1,0:T(8,128)(2,1)}, bf16[96,2304]{1,0:T(8,128)(2,1)}, u32[]{:S(2)}, u32[]{:S(2)}) collective-permute-start(bf16[96,2304]{1,0:T(8,128)(2,1)} %get-tuple-element.323), channel_id=1, source_target_pairs={{0,16},{16,0},{1,17},{17,1},{2,18},{18,2},{3,19},{19,3},{4,20},{20... | collective-permute-start | bytes 1327112 | tf_op jit(solution)/shard_map/ppermute | solution.py:736
  539.2 22.1 %collective-permute-start.34 = (bf16[2,1,128,768]{3,2,0,1:T(8,128)(2,1)}, bf16[2,1,128,768]{3,2,0,1:T(8,128)(2,1)}, u32[]{:S(2)}, u32[]{:S(2)}) collective-permute-start(bf16[2,1,128,768]{3,2,0,1:T(8,128)(2,1)} %bitcast.193), channel_id=1, source_target_pairs={{0,4},{1,5},{2,6},{3,7},{4,0},{5,1},{6,2},{7,3},{8,12},{9,13},{10,... | collective-permute-start | bytes 1179656 | tf_op jit(solution)/shard_map/ppermute | solution.py:768
  541.7 24.8 %collective-permute-start.33 = (bf16[1,1,96,2048]{3,2,1,0:T(8,128)(2,1)}, bf16[1,1,96,2048]{3,2,1,0:T(8,128)(2,1)}, u32[]{:S(2)}, u32[]{:S(2)}) collective-permute-start(bf16[1,1,96,2048]{3,2,1,0:T(8,128)(2,1)} %get-tuple-element.333), channel_id=1, source_target_pairs={{0,8},{1,9},{2,10},{3,11},{4,12},{5,13},{6,14},{7,15},{8,0},{9,1},... | collective-permute-start | bytes 1179656 | tf_op jit(solution)/shard_map/ppermute | solution.py:768
  552.2 21.1 %collective-permute-start.39 = (bf16[128,2048]{1,0:T(8,128)(2,1)}, bf16[128,2048]{1,0:T(8,128)(2,1)}, u32[]{:S(2)}, u32[]{:S(2)}) collective-permute-start(bf16[128,2048]{1,0:T(8,128)(2,1)} %get-tuple-element.339), channel_id=1, source_target_pairs={{0,16},{16,0},{1,17},{17,1},{2,18},{18,2},{3,19},{19,3},{4,20},{20... | collective-permute-start | bytes 1572872 | tf_op jit(solution)/shard_map/ppermute | solution.py:736
  563.6 12.2 %collective-permute-start.38 = (bf16[1,1,128,768]{3,2,1,0:T(8,128)(2,1)}, bf16[1,1,128,768]{3,2,1,0:T(8,128)(2,1)}, u32[]{:S(2)}, u32[]{:S(2)}) collective-permute-start(bf16[1,1,128,768]{3,2,1,0:T(8,128)(2,1)} %get-tuple-element.344), channel_id=1, source_target_pairs={{0,8},{1,9},{2,10},{3,11},{4,12},{5,13},{6,14},{7,15},{8,0},{9,1},... | collective-permute-start | bytes 589832 | tf_op jit(solution)/shard_map/ppermute | solution.py:768
  568.4 9.7 %collective-permute-start.37 = (bf16[96,2048]{1,0:T(8,128)(2,1)}, bf16[96,2048]{1,0:T(8,128)(2,1)}, u32[]{:S(2)}, u32[]{:S(2)}) collective-permute-start(bf16[96,2048]{1,0:T(8,128)(2,1)} %get-tuple-element.348), channel_id=1, source_target_pairs={{0,16},{16,0},{1,17},{17,1},{2,18},{18,2},{3,19},{19,3},{4,20},{20... | collective-permute-start | bytes 1179656 | tf_op jit(solution)/shard_map/ppermute | solution.py:736
  577.4 5.9 collective-permute-start.40
  (60 other events, 282.3 us)
Sparse Core Ops, SparseCore 0:
  13.6 111.9 all-gather.4
  127.7 110.2 all-gather.6
  409.6 137.4 all-reduce.5

commit v6 on v5

--- a/solution.py
+++ b/solution.py
@@ -17,12 +17,14 @@
 FACTORS = 7
 VMEM = 44 << 20
 LESS = 24 << 20
+MORE = 50 << 20
+PARTS = 2
 STEPS = (
-    "hidden", "ffn_in", "turn", "away_u", "away_d", "norm_two", "home_u", "home_d", "away_g", "mixer", "away_r",
-    "two_u", "two_d", "home_g", "home_r", "conv_in", "fold_u", "fold_d", "away_b", "small", "settle_u", "down",
-    "home_b", "norm_one", "two_g", "two_r", "join_u", "away_o", "two_b", "fold_g", "settle_d", "home_o", "fold_r",
-    "settle_g", "join_d", "two_o", "fold_b", "join_g", "settle_r", "small_end", "fold_o", "settle_b", "result",
-    "join_r", "settle_o", "join_b", "join_o",
+    "turn", "ffn_in", "away_u", "away_d", "norm_two", "home_u", "home_d", "away_g", "mixer", "away_r", "two_u",
+    "two_d", "home_g", "home_r", "conv_in", "fold_u", "fold_d", "away_b", "small", "settle_u", "down", "home_b",
+    "norm_one", "two_g", "two_r", "join_u", "two_b", "away_o", "fold_g", "settle_d", "home_o", "fold_r", "settle_g",
+    "join_d", "two_o", "fold_b", "join_g", "settle_r", "fold_o", "result", "small_end", "settle_b", "join_r",
+    "settle_o", "join_b", "join_o",
 )
 HINT = pl.CostEstimate(flops=100000000000, bytes_accessed=1024, transcendentals=0)
 BF16 = jnp.bfloat16
@@ -333,7 +335,7 @@
         compiler_params=pltpu.CompilerParams(vmem_limit_bytes=LESS),
         cost_estimate=HINT,
         name="pack",
-    )(side, *halves, full)
+    )(side, *[pltpu.with_memory_space_constraint(p, pltpu.HBM) for p in (*halves, full)])
 
 
 def columns_kernel(parts, side_ref, own_ref, got_ref, *out_refs):
@@ -441,60 +443,6 @@
     )(pre, gates, gates, admitted, params)
 
 
-def hidden_kernel(x_ref, gate_ref, up_ref, hidden_ref, flipped_ref, act_ref, slope_ref):
-    x = x_ref[...]
-    gate = matmul(x, joined(gate_ref))
-    up = matmul(x, joined(up_ref))
-    t = jnp.tanh(GELU_K * (gate + GELU_C * gate * gate * gate))
-    act = 0.5 * gate * (1.0 + t)
-    slope = 0.5 * (1.0 + t) + 0.5 * gate * (1.0 - t * t) * GELU_K * (1.0 + 3.0 * GELU_C * gate * gate)
-    hidden = act * up
-    hidden_ref[...] = hidden.astype(BF16)
-    flipped_ref[...] = hidden.T.astype(BF16)
-    act_ref[...] = act
-    slope_ref[...] = up * slope
-
-
-def hidden_pass(x, blocks, rows, tiles):
-    tokens, depth = x.shape
-    shards, _, tile = blocks.shape
-    n = tiles * tile
-    wide = pl.BlockSpec((tokens, tile), lambda j: (0, j))
-    return pl.pallas_call(
-        hidden_kernel,
-        grid=(tiles,),
-        in_specs=[
-            pl.BlockSpec((tokens, depth), lambda j: (0, 0)),
-            pl.BlockSpec((shards, rows, tile), lambda j: (0, j, 0)),
-            pl.BlockSpec((shards, rows, tile), lambda j: (0, j + tiles, 0)),
-        ],
-        out_specs=[wide, pl.BlockSpec((tile, tokens), lambda j: (j, 0)), wide, wide],
-        out_shape=[
-            jax.ShapeDtypeStruct((tokens, n), BF16), jax.ShapeDtypeStruct((n, tokens), BF16),
-            jax.ShapeDtypeStruct((tokens, n), F32), jax.ShapeDtypeStruct((tokens, n), F32),
-        ],
-        compiler_params=pltpu.CompilerParams(vmem_limit_bytes=VMEM),
-        cost_estimate=HINT,
-        name="hidden_pass",
-    )(x, blocks, blocks)
-
-
-def halves(sum_ref, part, near_ref, far_ref):
-    @pl.when(pl.program_id(0) == 0)
-    def _():
-        sum_ref[...] = part
-
-    @pl.when(pl.program_id(0) > 0)
-    def _():
-        sum_ref[...] += part
-
-    @pl.when(pl.program_id(0) == pl.num_programs(0) - 1)
-    def _():
-        half = near_ref.shape[0]
-        near_ref[...] = sum_ref[:half, :]
-        far_ref[...] = sum_ref[half:, :].astype(BF16)
-
-
 def take_tile(down_a_ref, down_b_ref, down_ref):
     rows, n = down_ref.shape[0], down_a_ref.shape[2]
     for j in range(shape_rows(down_a_ref) // rows):
@@ -508,17 +456,44 @@
     return ref.shape[0] * ref.shape[1]
 
 
-def ffn_back_kernel(
-    cot_ref, gate_ref, up_ref, down_a_ref, down_b_ref, act_ref, slope_ref,
-    gate_cot_ref, up_cot_ref, near_ref, far_ref, sum_ref, down_ref,
+def ffn_kernel(
+    x_ref, cot_ref, gate_ref, up_ref, down_a_ref, down_b_ref,
+    hidden_ref, flipped_ref, gate_cot_ref, up_cot_ref, near_ref, far_ref, sum_ref, down_ref,
 ):
     take_tile(down_a_ref, down_b_ref, down_ref)
-    cot = cols_product(cot_ref[...], down_ref[...])
-    gate_cot = (cot * slope_ref[...]).astype(BF16)
-    up_cot = (cot * act_ref[...]).astype(BF16)
-    gate_cot_ref[...] = gate_cot
-    up_cot_ref[...] = up_cot
-    halves(sum_ref, cols_product(gate_cot, joined(gate_ref)) + cols_product(up_cot, joined(up_ref)), near_ref, far_ref)
+    gate_w, up_w, down_w = joined(gate_ref), joined(up_ref), down_ref[...]
+    tokens = x_ref.shape[0]
+    for first in range(0, tokens, tokens // PARTS):
+        rows = slice(first, first + tokens // PARTS)
+        x = x_ref[rows, :]
+        gate = matmul(x, gate_w)
+        up = matmul(x, up_w)
+        cot = cols_product(cot_ref[rows, :], down_w)
+        t = jnp.tanh(GELU_K * (gate + GELU_C * gate * gate * gate))
+        act = 0.5 * gate * (1.0 + t)
+        slope = 0.5 * (1.0 + t) + 0.5 * gate * (1.0 - t * t) * GELU_K * (1.0 + 3.0 * GELU_C * gate * gate)
+        hidden = act * up
+        hidden_ref[rows, :] = hidden.astype(BF16)
+        flipped_ref[:, rows] = hidden.T.astype(BF16)
+        gate_cot = (cot * up * slope).astype(BF16)
+        up_cot = (cot * act).astype(BF16)
+        gate_cot_ref[rows, :] = gate_cot
+        up_cot_ref[rows, :] = up_cot
+        part = cols_product(gate_cot, gate_w) + cols_product(up_cot, up_w)
+
+        @pl.when(pl.program_id(0) == 0)
+        def _(part=part, rows=rows):
+            sum_ref[rows, :] = part
+
+        @pl.when(pl.program_id(0) > 0)
+        def _(part=part, rows=rows):
+            sum_ref[rows, :] += part
+
+    @pl.when(pl.program_id(0) == pl.num_programs(0) - 1)
+    def _():
+        half = near_ref.shape[0]
+        near_ref[...] = sum_ref[:half, :]
+        far_ref[...] = sum_ref[half:, :].astype(BF16)
 
 
 def down_specs(blocks, rows, tiles, piece):
@@ -527,51 +502,73 @@
     return [pl.BlockSpec((shards, piece, tile), lambda j, k=k: (0, at + k, 0), pipeline_mode=pl.Buffered(1)) for k in range(2)]
 
 
-def ffn_back(cot, blocks, act, slope, rows, tiles, piece):
-    tokens, depth = cot.shape
+def ffn_pass(x, cot, blocks, rows, tiles, piece):
+    tokens, depth = x.shape
     shards, _, tile = blocks.shape
-    low = jax.ShapeDtypeStruct((tokens, tiles * tile), BF16)
+    n = tiles * tile
+    low = jax.ShapeDtypeStruct((tokens, n), BF16)
+    fixed = pl.BlockSpec((tokens, depth), lambda j: (0, 0))
     wide = pl.BlockSpec((tokens, tile), lambda j: (0, j))
     half = pl.BlockSpec((tokens // 2, depth), lambda j: (0, 0))
     return pl.pallas_call(
-        ffn_back_kernel,
+        ffn_kernel,
         grid=(tiles,),
         in_specs=[
-            pl.BlockSpec((tokens, depth), lambda j: (0, 0)),
+            fixed, fixed,
             pl.BlockSpec((shards, rows, tile), lambda j: (0, j, 0)),
             pl.BlockSpec((shards, rows, tile), lambda j: (0, j + tiles, 0)),
             *down_specs(blocks, rows, tiles, piece),
-            wide, wide,
         ],
-        out_specs=[wide, wide, half, half],
+        out_specs=[wide, pl.BlockSpec((tile, tokens), lambda j: (j, 0)), wide, wide, half, half],
         out_shape=[
-            low, low,
+            low, jax.ShapeDtypeStruct((n, tokens), BF16), low, low,
             jax.ShapeDtypeStruct((tokens // 2, depth), F32), sent((tokens // 2, depth)),
         ],
         scratch_shapes=[pltpu.VMEM((tokens, depth), F32), pltpu.VMEM((tile, depth), BF16)],
-        compiler_params=pltpu.CompilerParams(vmem_limit_bytes=VMEM),
-        cost_estimate=HINT,
-        name="ffn_back",
-    )(cot, blocks, blocks, blocks, blocks, act, slope)
-
-
-def down_kernel(hidden_ref, down_a_ref, down_b_ref, near_ref, far_ref, sum_ref, down_ref):
-    take_tile(down_a_ref, down_b_ref, down_ref)
-    halves(sum_ref, matmul(hidden_ref[...], down_ref[...]), near_ref, far_ref)
+        compiler_params=pltpu.CompilerParams(vmem_limit_bytes=MORE),
+        cost_estimate=HINT,
+        name="ffn_pass",
+    )(x, cot, blocks, blocks, blocks, blocks)
+
+
+def down_kernel(hidden_ref, down_a_ref, down_b_ref, near_ref, far_ref, sum_ref):
+    hidden = hidden_ref[...]
+    n = down_a_ref.shape[2]
+    first = pl.program_id(0) == 0
+    for k, ref in enumerate((down_a_ref, down_b_ref)):
+        at = slice(k * n, (k + 1) * n)
+        part = matmul(hidden, joined(ref))
+
+        @pl.when(first)
+        def _(part=part, at=at):
+            sum_ref[:, at] = part
+
+        @pl.when(jnp.logical_not(first))
+        def _(part=part, at=at):
+            sum_ref[:, at] += part
+
+    @pl.when(pl.program_id(0) == pl.num_programs(0) - 1)
+    def _():
+        half = near_ref.shape[0]
+        near_ref[...] = sum_ref[:half, :]
+        far_ref[...] = sum_ref[half:, :].astype(BF16)
 
 
 def down_pass(hidden, blocks, depth, rows, tiles, piece):
     tokens, n = hidden.shape
+    shards, _, tile = blocks.shape
+    at = 2 * tiles * rows // piece
     half = pl.BlockSpec((tokens // 2, depth), lambda j: (0, 0))
     return pl.pallas_call(
         down_kernel,
-        grid=(tiles,),
-        in_specs=[pl.BlockSpec((tokens, n // tiles), lambda j: (0, j)), *down_specs(blocks, rows, tiles, piece)],
+        grid=(2,),
+        in_specs=[
+            pl.BlockSpec((tokens, n // 2), lambda j: (0, j)),
+            *[pl.BlockSpec((shards // 2, piece, tile), lambda j, k=k: (j, at + k, 0)) for k in range(2)],
+        ],
         out_specs=[half, half],
-        out_shape=[
-            jax.ShapeDtypeStruct((tokens // 2, depth), F32), sent((tokens // 2, depth)),
-        ],
-        scratch_shapes=[pltpu.VMEM((tokens, depth), F32), pltpu.VMEM((n // tiles, depth), BF16)],
+        out_shape=[jax.ShapeDtypeStruct((tokens // 2, depth), F32), sent((tokens // 2, depth))],
+        scratch_shapes=[pltpu.VMEM((tokens, depth), F32)],
         compiler_params=pltpu.CompilerParams(vmem_limit_bytes=VMEM),
         cost_estimate=HINT,
         name="down_pass",
@@ -669,7 +666,7 @@
 def fold(own, got, at, bit, low):
     rows, n = own.shape[2:]
     high = own.shape[0] * own.shape[1] // (2 * low)
-    tile = column_tile(n, (1024, 768, 512, 256, 128))
+    tile = column_tile(n, (2304, 2048, 1536, 1024, 768, 512, 256, 128))
     both = pl.BlockSpec((high, 2, low, rows, tile), lambda j, at: (0, 0, 0, 0, j))
     half = pl.BlockSpec((high, low, rows, tile), lambda j, at: (0, 0, 0, j))
     shape = (high, 2, low, rows, n)
@@ -695,7 +692,7 @@
 
 def settle(own, got):
     rows, n = own.shape
-    tile = column_tile(n, (1024, 768, 512, 256, 128))
+    tile = column_tile(n, (2304, 2048, 1536, 1024, 768, 512, 256, 128))
     one = pl.BlockSpec((rows, tile), lambda j: (0, j))
     return pl.pallas_call(
         settle_kernel,
@@ -894,16 +891,10 @@
         return run
 
     @step
-    def hidden():
+    def ffn_in():
         x, = tick(normed_two)
-        have["hidden"], have["hidden_t"], have["act"], have["slope"] = hidden_pass(x, ffn_blocks, **ffn)
-        tock(have["hidden"], have["hidden_t"])
-
-    @step
-    def ffn_in():
-        act, = tick(have["act"])
-        have["gate_cot"], have["up_cot"], near, far = ffn_back(
-            cot_pair, ffn_blocks, act, have["slope"], piece=piece_f, **ffn
+        have["hidden"], have["hidden_t"], have["gate_cot"], have["up_cot"], near, far = ffn_pass(
+            x, cot_pair, ffn_blocks, piece=piece_f, **ffn
         )
         tock(near, far)
         have["ffn"] = near, swap(far)

time: 596 us -> 589 us (0.988); the launches traced: 591 us -> 577 us
  Pallas kernels: 224 us -> 218 us
    ppermute x17, waiting for transfers between devices: 67.2 us -> 58.1 us  [swap(): return lax.ppermute(v, 'rep', [(i, i ^ 1) for i in range(groups)])]
    all_gather x1, waiting for transfers between devices: 59.6 us -> 66 us  [body(): lax.all_gather(pack(here_side, [branch_proj, lruin_proj, recur_proj, admi...]
    pallas_call x3 -> x2, Pallas kernels: 47.3 us -> 41 us  [the longest x1 31.2 us: ffn_pass(): pl.pallas_call(ffn_kernel, grid=(tiles,), in_specs=[fixed, fixed, pl.Bloc...]
    unnamed x173 -> x155, local copies, waits for them, and re-layouts: 23.4 us -> 18.6 us
  transfers between devices with their start and end apart: 44 -> 44, of which waited for: 18 -> 18; matrix products, arithmetic and copies ran while one was open for 8% -> 9% of each run, Pallas kernels for 31% -> 32%
where the time goes in v6:
time: 589 us; the launch traced here: 577 us
  Pallas kernels  218 us (37%)
  waiting for transfers between devices  216 us (37%)
  starting transfers between devices  40.5 us (7%)
  local copies, waits for them, and re-layouts  40.3 us (7%)
  blocking collectives  22.7 us (4%)
  between operations  15.1 us (3%)
  other arithmetic  13.7 us (2%)
  matrix products  11.7 us (2%)
    ppermute x24, waiting for transfers between devices, cross(): return lax.ppermute(v, 'shard', [(i, i ^ 1 << bit) for i in range(shards)])  80.9 us
    all_gather x1, waiting for transfers between devices, body(): lax.all_gather(pack(here_side, [branch_proj, lruin_proj, recur_proj, admi...  66 us
    ppermute x17, waiting for transfers between devices, swap(): return lax.ppermute(v, 'rep', [(i, i ^ 1) for i in range(groups)])  58.1 us
    pallas_call x12, Pallas kernels, fold(): pl.pallas_call(functools.partial(fold_kernel, bit), grid_spec=pltpu.Prefe...  35.4 us
    pallas_call x6, Pallas kernels, grad_home(): pl.pallas_call(functools.partial(home_kernel, bit), grid_spec=pltpu.Prefe...  34.7 us
    pallas_call x1, Pallas kernels, ffn_pass(): pl.pallas_call(ffn_kernel, grid=(tiles,), in_specs=[fixed, fixed, pl.Bloc...  31.2 us
    pallas_call x6, Pallas kernels, grad_away(): pl.pallas_call(away_kernel, grid_spec=pltpu.PrefetchScalarGridSpec(num_sc...  25.5 us
    all_gather x1, blocking collectives, body(): lax.all_gather(vectors, 'shard', axis=0).reshape(shards, -1)[:, :count]  22.7 us
  transfers between devices with their start and end apart: 44, of which 18 were waited for; matrix products, arithmetic and copies ran while one was open for 9% of the time, Pallas kernels for 32%

profile of v6, /device:TPU:0, one launch (start us, length us, event | category | flops | bytes accessed | tf_op | source)
XLA Modules:
  0.0 577.4 jit_solution(231023382739201760)
XLA Ops:
  7.3 2.6 pack.1
  10.0 3.0 collective-permute-start
  24.7 22.7 %all_gather.15 = bf16[16,10,128]{2,1,0:T(8,128)(2,1)S(1)} all-gather(bf16[1,10,128]{2,1,0:T(8,128)(2,1)S(1)} %pad_bitcast_fusion), channel_id=1, replica_groups=mesh['rep'=2,'shard'=16] {'shard'}, dimensions={0}, use_global_device_ids=true | all-gather | bytes 43520 | tf_op jit(solution)/shard_map/all_gather | solution.py:820
  56.2 66.0 %all-gather.5.cloned.1.call-done = bf16[20480,512]{1,0:T(8,128)(2,1)} async-done(((bf16[1280,512]{1,0:T(8,128)(2,1)}), bf16[20480,512]{1,0:T(8,128)(2,1)}) %all-gather.5.cloned.1.call-update) | async-done | bytes 20971536 | tf_op jit(solution)/shard_map/all_gather | solution.py:843
  122.1 3.2 fusion.45
  125.4 3.4 fusion.8.pre_ref.lru_ref
  134.3 8.3 %fusion.44 = (bf16[16,128,512]{2,1,0:T(8,128)(2,1)S(1)}, bf16[16,128,512]{2,1,0:T(8,128)(2,1)}, bf16[16,128,512]{2,1,0:T(8,128)(2,1)}, bf16[16,128,512]{2,1,0:T(...) fusion(bf16[16,1280,512]{2,1,0:T(8,128)(2,1)} %bitcast.145), kind=kLoop, calls=%fused_computation.96 | loop fusion | bytes 29360128 | tf_op jit(solution)/shard_map/slice | solution.py:839
  142.6 14.6 %collective-permute-done.2 = bf16[512,1024]{1,0:T(8,128)(2,1)S(1)} collective-permute-done((bf16[512,1024]{1,0:T(8,128)(2,1)S(1)}, bf16[512,1024]{1,0:T(8,128)(2,1)S(1)}, u32[]{:S(2)}, u32[]{:S(2)}) %collective-permute-start.2) | collective-permute-done | bytes 1048608 | tf_op jit(solution)/shard_map/ppermute | solution.py:733
  158.7 6.4 %fusion.gates_r_ref.gates_i_ref = f32[512,2048]{1,0:T(8,128)} fusion(bf16[2048,512]{1,0:T(8,128)(2,1)S(1)} %bitcast.164, bf16[2048,512]{1,0:T(8,128)(2,1)S(1)} %bitcast.165, bf16[2048,512]{1,0:T(8,128)(2,1)S(1)} %bitcast.166, bf16[2048,512]{1,0:T(8,128)(2,1)S(1)} %bitcast.163, bf16[512,1024]{1,0:T(8,128)(2,1)S(1)} %get-tuple-element.371, ...), kind=kOutput, calls=%fused_computation | convolution fusion | flops 4332716032 | bytes 14680064 | tf_op jit(solution)/shard_map/dot_general | solution.py:40
  165.1 12.3 %recurrence_forward.1 = (bf16[512,1024]{1,0:T(8,128)(2,1)}, f32[512,1024]{1,0:T(8,128)}, f32[512,1024]{1,0:T(8,128)}, f32[512,1024]{1,0:T(8,128)}, f32[512,1024]...) custom-call(f32[512,2048]{1,0:T(8,128)} %copy-done.41, ...), custom_call_target="tpu_custom_call" | custom-call | flops 31457280 | bytes 10485760 | tf_op jit(solution)/shard_map/recurrence_forward/pallas_call | solution.py:435
  181.8 10.2 %collective-permute-done.3 = bf16[256,1024]{1,0:T(8,128)(2,1)S(1)} collective-permute-done((bf16[256,1024]{1,0:T(8,128)(2,1)S(1)}, bf16[256,1024]{1,0:T(8,128)(2,1)S(1)}, u32[]{:S(2)}, u32[]{:S(2)}) %collective-permute-start.3) | collective-permute-done | bytes 524320 | tf_op jit(solution)/shard_map/ppermute | solution.py:733
  196.4 10.6 %collective-permute-done.5 = bf16[256,1024]{1,0:T(8,128)(2,1)S(1)} collective-permute-done((bf16[256,1024]{1,0:T(8,128)(2,1)S(1)}, bf16[256,1024]{1,0:T(8,128)(2,1)S(1)}, u32[]{:S(2)}, u32[]{:S(2)}) %collective-permute-start.5) | collective-permute-done | bytes 524320 | tf_op jit(solution)/shard_map/ppermute | solution.py:733
  210.0 11.5 %collective-permute-done.4 = bf16[256,1536]{1,0:T(8,128)(2,1)S(1)} collective-permute-done((bf16[256,1536]{1,0:T(8,128)(2,1)S(1)}, bf16[256,1536]{1,0:T(8,128)(2,1)S(1)}, u32[]{:S(2)}, u32[]{:S(2)}) %collective-permute-start.4) | collective-permute-done | bytes 786464 | tf_op jit(solution)/shard_map/ppermute | solution.py:733
  223.8 10.8 %all-gather.7.cloned.1.call-done = bf16[13824,768]{1,0:T(8,128)(2,1)} async-done(((bf16[864,768]{1,0:T(8,128)(2,1)}), bf16[13824,768]{1,0:T(8,128)(2,1)}) %all-gather.7.cloned.1.call-update) | async-done | bytes 21233680 | tf_op jit(solution)/shard_map/all_gather | solution.py:835
  234.6 31.2 %ffn_pass.1 = (bf16[512,2304]{1,0:T(8,128)(2,1)}, bf16[2304,512]{1,0:T(8,128)(2,1)}, bf16[512,2304]{1,0:T(8,128)(2,1)}, bf16[512,2304]{1,0:T(8,128)(2,1)}, f32[2...) custom-call(bf16[512,1536]{1,0:T(8,128)(2,1)S(1)} %pad_maximum_fusion.2.x_ref, ...), custom_call_target="tpu_custom_call" | custom-call | flops 99999997952 | bytes 1024 | tf_op jit(solution)/shard_map/ffn_pass/pallas_call | solution.py:513
  269.1 4.5 grad_away.6
  273.6 5.2 grad_away.7
  279.4 6.6 %collective-permute-done.7.far_ref = bf16[256,1536]{1,0:T(8,128)(2,1)} collective-permute-done((bf16[256,1536]{1,0:T(8,128)(2,1)}, bf16[256,1536]{1,0:T(8,128)(2,1)}, u32[]{:S(2)}, u32[]{:S(2)}) %collective-permute-start.7) | collective-permute-done | bytes 786464 | tf_op jit(solution)/shard_map/ppermute | solution.py:733
  286.0 3.8 norm_back.2
  291.3 6.1 %grad_home.6 = (bf16[2,2,96,2304]{3,2,1,0:T(8,128)(2,1)S(1)}, bf16[2,2,96,2304]{3,2,1,0:T(8,128)(2,1)}) custom-call(s32[5]{0:T(128)S(1)} %stack.24.at_ref, bf16[8,2,96,512]{3,2,1,0:T(8,128)(2,1)S(1)} %bitcast.127, bf16[1,512,2304]{2,1,0:T(8,128)(2,1)S(1)} %bitcast.115, bf16[8,96,2304]{2,1,0:T(8,128)(2,1)} %collective-permute-done.6.got_ref), custom_call_target="tpu_custom_call" | custom-call | flops 99999997952 | bytes 1024 | tf_op jit(solution)/shard_map/grad_home/pallas_call | solution.py:638
  298.9 6.0 %grad_home.7 = (bf16[4,1,144,1536]{3,2,1,0:T(8,128)(2,1)S(1)}, bf16[4,1,144,1536]{3,2,1,0:T(8,128)(2,1)}) custom-call(s32[5]{0:T(128)S(1)} %stack.24.at_ref, bf16[8,2,144,512]{3,2,1,0:T(8,128)(2,1)S(1)} %bitcast.113, bf16[1,512,1536]{2,1,0:T(8,128)(2,1)} %bitcast.36.right_ref, bf16[8,144,1536]{2,1,0:T(8,128)(2,1)} %collective-permute-done.10.got_ref), custom_call_target="tpu_custom_call" | custom-call | flops 99999997952 | bytes 1024 | tf_op jit(solution)/shard_map/grad_home/pallas_call | solution.py:638
  306.2 4.7 grad_away.8
  310.9 18.2 %chain_back.1 = (bf16[512,1024]{1,0:T(8,128)(2,1)S(1)}, bf16[2,512,1024]{2,1,0:T(8,128)(2,1)S(1)}, f32[512,1024]{1,0:T(8,128)S(1)}, f32[48,1024]{1,0:T(8,128)S(1...) custom-call(s32[1]{0:T(128)} %bitcast.2.side_ref, bf16[256,1536]{1,0:T(8,128)(2,1)S(1)} %copy-done.7, ...), custom_call_target="tpu_custom_call" | custom-call | flops 99999997952 | bytes 1024 | tf_op jit(solution)/shard_map/chain_back/pallas_call | solution.py:175
  329.8 4.6 grad_away.9
  337.4 3.3 fold.12
  341.9 4.9 collective-permute-done.15
  346.8 3.6 fold.13
  350.6 6.1 %grad_home.8 = (bf16[4,1,96,2304]{3,2,1,0:T(8,128)(2,1)S(1)}, bf16[4,1,96,2304]{3,2,1,0:T(8,128)(2,1)}) custom-call(s32[5]{0:T(128)S(1)} %stack.24.at_ref, bf16[8,2,96,512]{3,2,1,0:T(8,128)(2,1)S(1)} %bitcast.129, bf16[1,512,2304]{2,1,0:T(8,128)(2,1)S(1)} %bitcast.111, bf16[8,96,2304]{2,1,0:T(8,128)(2,1)} %collective-permute-done.14.got_ref), custom_call_target="tpu_custom_call" | custom-call | flops 99999997952 | bytes 1024 | tf_op jit(solution)/shard_map/grad_home/pallas_call | solution.py:638
  359.1 6.7 %grad_home.9 = (bf16[2,2,128,2048]{3,2,1,0:T(8,128)(2,1)S(1)}, bf16[2,2,128,2048]{3,2,1,0:T(8,128)(2,1)}) custom-call(s32[5]{0:T(128)S(1)} %stack.24.at_ref, bf16[8,2,128,512]{3,2,1,0:T(8,128)(2,1)S(1)} %bitcast.119, bf16[2,512,1024]{2,1,0:T(8,128)(2,1)S(1)} %copy-done.33, bf16[8,128,2048]{2,1,0:T(8,128)(2,1)} %collective-permute-done.13.got_ref), custom_call_target="tpu_custom_call" | custom-call | flops 99999997952 | bytes 1024 | tf_op jit(solution)/shard_map/grad_home/pallas_call | solution.py:638
  367.1 9.6 %conv_back.1 = (bf16[2,512,1024]{2,1,0:T(8,128)(2,1)S(1)}, f32[8,1024]{1,0:T(8,128)S(1)}, f32[256,1536]{1,0:T(8,128)S(1)}, bf16[256,1536]{1,0:T(8,128)(2,1)}) custom-call(f32[512,1024]{1,0:T(8,128)S(1)} %copy-done.29, f32[512,1024]{1,0:T(8,128)S(1)} %copy-done.31, bf16[512,1024]{1,0:T(8,128)(2,1)} %collective-permute-done.12.far_in_ref, ...), custom_call_target="tpu_custom_call" | custom-call | flops 99999997952 | bytes 1024 | tf_op jit(solution)/shard_map/conv_back/pallas_call | solution.py:248
  376.7 3.3 fold.14
  380.0 2.7 collective-permute-start.16
  382.7 2.6 fold.15
  385.3 3.9 grad_away.10
  390.9 7.6 %collective-permute-done.16 = bf16[1,1,96,2304]{3,2,1,0:T(8,128)(2,1)} collective-permute-done((bf16[1,1,96,2304]{3,2,1,0:T(8,128)(2,1)}, bf16[1,1,96,2304]{3,2,1,0:T(8,128)(2,1)}, u32[]{:S(2)}, u32[]{:S(2)}) %collective-permute-start.16) | collective-permute-done | bytes 442400 | tf_op jit(solution)/shard_map/ppermute | solution.py:765
  400.5 9.8 %down_pass.1 = (f32[256,1536]{1,0:T(8,128)S(1)}, bf16[256,1536]{1,0:T(8,128)(2,1)}) custom-call(bf16[512,2304]{1,0:T(8,128)(2,1)S(1)} %copy-done.34, bf16[16,864,768]{2,1,0:T(8,128)(2,1)} %bitcast.185, bf16[16,864,768]{2,1,0:T(8,128)(2,1)} %bitcast.186), custom_call_target="tpu_custom_call" | custom-call | flops 99999997952 | bytes 1024 | tf_op jit(solution)/shard_map/down_pass/pallas_call | solution.py:562
  411.5 5.7 grad_home.10
  418.1 4.1 norm_back.3
  422.9 3.4 fold.16
  426.3 27.5 %collective-permute-done.22 = bf16[2,2,128,2048]{3,2,1,0:T(8,128)(2,1)} collective-permute-done((bf16[2,2,128,2048]{3,2,1,0:T(8,128)(2,1)}, bf16[2,2,128,2048]{3,2,1,0:T(8,128)(2,1)}, u32[]{:S(2)}, u32[]{:S(2)}) %collective-permute-start.22) | collective-permute-done | bytes 2097184 | tf_op jit(solution)/shard_map/ppermute | solution.py:765
  453.8 3.5 fold.17
  458.1 3.1 weave.2
  461.1 3.2 fold.18
  464.4 2.7 grad_away.11
  467.0 12.7 %collective-permute-done.27 = bf16[2,1,96,2304]{3,2,0,1:T(8,128)(2,1)} collective-permute-done((bf16[2,1,96,2304]{3,2,0,1:T(8,128)(2,1)}, bf16[2,1,96,2304]{3,2,0,1:T(8,128)(2,1)}, u32[]{:S(2)}, u32[]{:S(2)}) %collective-permute-start.27) | collective-permute-done | bytes 884768 | tf_op jit(solution)/shard_map/ppermute | solution.py:765
  479.7 2.6 fold.19
  488.7 4.1 grad_home.11
  494.2 2.7 fold.20
  496.9 7.8 %collective-permute-done.30 = bf16[1,1,96,2304]{3,2,1,0:T(8,128)(2,1)} collective-permute-done((bf16[1,1,96,2304]{3,2,1,0:T(8,128)(2,1)}, bf16[1,1,96,2304]{3,2,1,0:T(8,128)(2,1)}, u32[]{:S(2)}, u32[]{:S(2)}) %collective-permute-start.30) | collective-permute-done | bytes 442400 | tf_op jit(solution)/shard_map/ppermute | solution.py:765
  507.6 2.3 join_rows.1
  510.9 2.5 fold.21
  513.4 2.4 collective-permute-start.32
  515.8 5.5 collective-permute-done.35
  521.3 2.5 fold.22
  523.8 2.8 weave.3
  526.6 7.1 %collective-permute-done.33 = bf16[1,1,128,2048]{3,2,1,0:T(8,128)(2,1)} collective-permute-done((bf16[1,1,128,2048]{3,2,1,0:T(8,128)(2,1)}, bf16[1,1,128,2048]{3,2,1,0:T(8,128)(2,1)}, u32[]{:S(2)}, u32[]{:S(2)}) %collective-permute-start.33) | collective-permute-done | bytes 524320 | tf_op jit(solution)/shard_map/ppermute | solution.py:765
  533.8 2.1 settle.9
  535.9 3.6 collective-permute-start.39
  540.5 2.3 fold.23
  542.8 2.4 add_convert_fusion
  545.9 5.4 collective-permute-done.36
  555.4 2.4 join_columns.3
  560.5 4.6 collective-permute-done.37.got_ref
  565.0 2.3 join_columns.4
  (290 shorter events, 88.5 us)
Async XLA Ops:
  7.2 115.0 %all-gather.5.cloned.1.call-start = ((), (), s32[]{:S(2)}) async-start(), calls=%async_computation.1 | async-start | bytes 22282240 | tf_op jit(solution)/shard_map/all_gather | solution.py:843
  9.9 224.7 %all-gather.7.cloned.1.call-start = ((), (), s32[]{:S(2)}) async-start(), calls=%async_computation.2 | async-start | bytes 22560768 | tf_op jit(solution)/shard_map/all_gather | solution.py:835
  10.0 38.7 %collective-permute-start = (bf16[256,1536]{1,0:T(8,128)(2,1)S(1)}, bf16[256,1536]{1,0:T(8,128)(2,1)}, u32[]{:S(2)}, u32[]{:S(2)}) collective-permute-start(bf16[256,1536]{1,0:T(8,128)(2,1)S(1)} %copy-done.3), channel_id=1, source_target_pairs={{0,16},{16,0},{1,17},{17,1},{2,18},{18,2},{3,19},{19,3},{4,20},{20... | collective-permute-start | bytes 2359304 | tf_op jit(solution)/shard_map/ppermute | solution.py:733
  13.0 41.0 %collective-permute-start.1 = (bf16[256,1536]{1,0:T(8,128)(2,1)S(1)}, bf16[256,1536]{1,0:T(8,128)(2,1)}, u32[]{:S(2)}, u32[]{:S(2)}) collective-permute-start(bf16[256,1536]{1,0:T(8,128)(2,1)S(1)} %copy-done.6), channel_id=1, source_target_pairs={{0,16},{16,0},{1,17},{17,1},{2,18},{18,2},{3,19},{19,3},{4,20},{20... | collective-permute-start | bytes 2359304 | tf_op jit(solution)/shard_map/ppermute | solution.py:733
  24.5 520.7 %all-reduce.6.cloned.1.call-start = ((), (), s32[]{:S(2)}) async-start(), calls=%async_computation | async-start | bytes 131072 | tf_op jit(solution)/shard_map/psum | solution.py:960
  131.8 25.5 %copy-start.42 = (bf16[2,256,1024]{2,1,0:T(8,128)(2,1)}, bf16[2,256,1024]{2,1,0:T(8,128)(2,1)S(1)}, u32[]{:S(2)}) copy-start(bf16[2,256,1024]{2,1,0:T(8,128)(2,1)S(1)} %fusion.32) | copy-start | bytes 3145732
  131.8 25.4 %collective-permute-start.2 = (bf16[512,1024]{1,0:T(8,128)(2,1)S(1)}, bf16[512,1024]{1,0:T(8,128)(2,1)S(1)}, u32[]{:S(2)}, u32[]{:S(2)}) collective-permute-start(bf16[512,1024]{1,0:T(8,128)(2,1)S(1)} %bitcast.153), channel_id=1, source_target_pairs={{0,16},{16,0},{1,17},{17,1},{2,18},{18,2},{3,19},{19,3},{4,20},{20... | collective-permute-start | bytes 3145736 | tf_op jit(solution)/shard_map/ppermute | solution.py:733
  133.4 62.1 %copy-start.60 = (f32[1536]{0:T(1024)}, f32[1536]{0:T(1024)S(1)}, u32[]{:S(2)}) copy-start(f32[1536]{0:T(1024)S(1)} %reshape.325) | copy-start | bytes 18436
  165.1 15.0 %copy-start.44 = (bf16[512,1024]{1,0:T(8,128)(2,1)S(1)}, bf16[512,1024]{1,0:T(8,128)(2,1)}, u32[]{:S(2)}) copy-start(bf16[512,1024]{1,0:T(8,128)(2,1)} %copy-done.43) | copy-start | bytes 3145732
  178.5 13.4 %collective-permute-start.3 = (bf16[256,1024]{1,0:T(8,128)(2,1)S(1)}, bf16[256,1024]{1,0:T(8,128)(2,1)S(1)}, u32[]{:S(2)}, u32[]{:S(2)}) collective-permute-start(bf16[256,1024]{1,0:T(8,128)(2,1)S(1)} %slice.172), channel_id=1, source_target_pairs={{0,16},{16,0},{1,17},{17,1},{2,18},{18,2},{3,19},{19,3},{4,20},{20... | collective-permute-start | bytes 1572872 | tf_op jit(solution)/shard_map/ppermute | solution.py:733
  180.2 11.7 %copy-start.55 = (bf16[512,1024]{1,0:T(8,128)(2,1)S(1)}, bf16[512,1024]{1,0:T(8,128)(2,1)}, u32[]{:S(2)}) copy-start(bf16[512,1024]{1,0:T(8,128)(2,1)} %get-tuple-element.189) | copy-start | bytes 3145732
  180.2 13.3 %copy-start.49 = (bf16[16,128,512]{2,1,0:T(8,128)(2,1)S(1)}, bf16[16,128,512]{2,1,0:T(8,128)(2,1)}, u32[]{:S(2)}) copy-start(bf16[16,128,512]{2,1,0:T(8,128)(2,1)} %get-tuple-element.360) | copy-start | bytes 6291460
  180.3 13.3 %copy-start.50 = (bf16[16,128,512]{2,1,0:T(8,128)(2,1)S(1)}, bf16[16,128,512]{2,1,0:T(8,128)(2,1)}, u32[]{:S(2)}) copy-start(bf16[16,128,512]{2,1,0:T(8,128)(2,1)} %get-tuple-element.361) | copy-start | bytes 6291460
  180.3 13.3 %copy-start.51 = (bf16[16,128,512]{2,1,0:T(8,128)(2,1)S(1)}, bf16[16,128,512]{2,1,0:T(8,128)(2,1)}, u32[]{:S(2)}) copy-start(bf16[16,128,512]{2,1,0:T(8,128)(2,1)} %get-tuple-element.362) | copy-start | bytes 6291460
  181.7 11.8 %copy-start.16 = (bf16[2048,512]{1,0:T(8,128)(2,1)}, bf16[2048,512]{1,0:T(8,128)(2,1)S(1)}, u32[]{:S(2)}) copy-start(bf16[2048,512]{1,0:T(8,128)(2,1)S(1)} %flip.5) | copy-start | bytes 6291460
  181.8 11.8 %copy-start.4 = (bf16[256,1536]{1,0:T(8,128)(2,1)S(1)}, bf16[256,1536]{1,0:T(8,128)(2,1)}, u32[]{:S(2)}) copy-start(bf16[256,1536]{1,0:T(8,128)(2,1)} %v_ref.1) | copy-start | bytes 2359300
  192.1 14.9 %collective-permute-start.5 = (bf16[256,1024]{1,0:T(8,128)(2,1)S(1)}, bf16[256,1024]{1,0:T(8,128)(2,1)S(1)}, u32[]{:S(2)}, u32[]{:S(2)}) collective-permute-start(bf16[256,1024]{1,0:T(8,128)(2,1)S(1)} %get-tuple-element.376), channel_id=1, source_target_pairs={{0,16},{16,0},{1,17},{17,1},{2,18},{18,2},{3,19},{19,3},{4,20},{20... | collective-permute-start | bytes 1572872 | tf_op jit(solution)/shard_map/ppermute | solution.py:733
  195.5 11.6 %copy-start = (f32[256,1536]{1,0:T(8,128)}, f32[256,1536]{1,0:T(8,128)S(1)}, u32[]{:S(2)}) copy-start(f32[256,1536]{1,0:T(8,128)S(1)} %get-tuple-element.400.v_ref) | copy-start | bytes 4718596
  195.7 25.8 %collective-permute-start.4 = (bf16[256,1536]{1,0:T(8,128)(2,1)S(1)}, bf16[256,1536]{1,0:T(8,128)(2,1)S(1)}, u32[]{:S(2)}, u32[]{:S(2)}) collective-permute-start(bf16[256,1536]{1,0:T(8,128)(2,1)S(1)} %multiply_convert_fusion), channel_id=1, source_target_pairs={{0,16},{16,0},{1,17},{17,1},{2,18},{18,2},{3,19},{19,3},{4,20},{20... | collective-permute-start | bytes 2359304 | tf_op jit(solution)/shard_map/ppermute | solution.py:733
  234.6 32.8 %copy-start.26 = (bf16[1536,512]{1,0:T(8,128)(2,1)S(1)}, bf16[1536,512]{1,0:T(8,128)(2,1)}, u32[]{:S(2)}) copy-start(bf16[1536,512]{1,0:T(8,128)(2,1)} %copy-done.25) | copy-start | bytes 4718596
  265.9 20.1 %collective-permute-start.7 = (bf16[256,1536]{1,0:T(8,128)(2,1)}, bf16[256,1536]{1,0:T(8,128)(2,1)}, u32[]{:S(2)}, u32[]{:S(2)}) collective-permute-start(bf16[256,1536]{1,0:T(8,128)(2,1)} %get-tuple-element.201), channel_id=1, source_target_pairs={{0,16},{16,0},{1,17},{17,1},{2,18},{18,2},{3,19},{19,3},{4,20},{20... | collective-permute-start | bytes 2359304 | tf_op jit(solution)/shard_map/ppermute | solution.py:733
  273.6 17.7 %collective-permute-start.6 = (bf16[8,96,2304]{2,1,0:T(8,128)(2,1)}, bf16[8,96,2304]{2,1,0:T(8,128)(2,1)}, u32[]{:S(2)}, u32[]{:S(2)}) collective-permute-start(bf16[8,96,2304]{2,1,0:T(8,128)(2,1)} %grad_away.6), channel_id=1, source_target_pairs={{0,1},{1,0},{2,3},{3,2},{4,5},{5,4},{6,7},{7,6},{8,9},{9,8},{10,11... | collective-permute-start | bytes 10616840 | tf_op jit(solution)/shard_map/ppermute | solution.py:765
  273.6 12.3 %copy-start.61 = (f32[1536]{0:T(1024)S(1)}, f32[1536]{0:T(1024)}, u32[]{:S(2)}) copy-start(f32[1536]{0:T(1024)} %copy-done.60) | copy-start | bytes 18436
  273.6 12.3 %copy-start.1 = (f32[256,1536]{1,0:T(8,128)S(1)}, f32[256,1536]{1,0:T(8,128)}, u32[]{:S(2)}) copy-start(f32[256,1536]{1,0:T(8,128)} %copy-done) | copy-start | bytes 4718596
  278.9 20.1 %collective-permute-start.10 = (bf16[8,144,1536]{2,1,0:T(8,128)(2,1)}, bf16[8,144,1536]{2,1,0:T(8,128)(2,1)}, u32[]{:S(2)}, u32[]{:S(2)}) collective-permute-start(bf16[8,144,1536]{2,1,0:T(8,128)(2,1)} %grad_away.7), channel_id=1, source_target_pairs={{0,1},{1,0},{2,3},{3,2},{4,5},{5,4},{6,7},{7,6},{8,9},{9,8},{10,11... | collective-permute-start | bytes 10616840 | tf_op jit(solution)/shard_map/ppermute | solution.py:765
  289.8 21.1 %collective-permute-start.9 = (bf16[256,1536]{1,0:T(8,128)(2,1)}, bf16[256,1536]{1,0:T(8,128)(2,1)}, u32[]{:S(2)}, u32[]{:S(2)}) collective-permute-start(bf16[256,1536]{1,0:T(8,128)(2,1)} %get-tuple-element.219.own_ref), channel_id=1, source_target_pairs={{0,16},{16,0},{1,17},{17,1},{2,18},{18,2},{3,19},{19,3},{4,20},{20... | collective-permute-start | bytes 2359304 | tf_op jit(solution)/shard_map/ppermute | solution.py:733
  297.4 40.0 %collective-permute-start.8 = (bf16[2,2,96,2304]{3,2,1,0:T(8,128)(2,1)}, bf16[2,2,96,2304]{3,2,1,0:T(8,128)(2,1)}, u32[]{:S(2)}, u32[]{:S(2)}) collective-permute-start(bf16[2,2,96,2304]{3,2,1,0:T(8,128)(2,1)} %get-tuple-element.212), channel_id=1, source_target_pairs={{0,4},{1,5},{2,6},{3,7},{4,0},{5,1},{6,2},{7,3},{8,12},{9,13},{10,... | collective-permute-start | bytes 5308424 | tf_op jit(solution)/shard_map/ppermute | solution.py:765
  305.0 41.9 %collective-permute-start.15 = (bf16[4,1,144,1536]{3,2,1,0:T(8,128)(2,1)}, bf16[4,1,144,1536]{3,2,1,0:T(8,128)(2,1)}, u32[]{:S(2)}, u32[]{:S(2)}) collective-permute-start(bf16[4,1,144,1536]{3,2,1,0:T(8,128)(2,1)} %get-tuple-element.217), channel_id=1, source_target_pairs={{0,2},{1,3},{2,0},{3,1},{4,6},{5,7},{6,4},{7,5},{8,10},{9,11},{10,... | collective-permute-start | bytes 5308424 | tf_op jit(solution)/shard_map/ppermute | solution.py:765
  310.9 39.7 %collective-permute-start.14 = (bf16[8,96,2304]{2,1,0:T(8,128)(2,1)}, bf16[8,96,2304]{2,1,0:T(8,128)(2,1)}, u32[]{:S(2)}, u32[]{:S(2)}) collective-permute-start(bf16[8,96,2304]{2,1,0:T(8,128)(2,1)} %grad_away.8), channel_id=1, source_target_pairs={{0,1},{1,0},{2,3},{3,2},{4,5},{5,4},{6,7},{7,6},{8,9},{9,8},{10,11... | collective-permute-start | bytes 10616840 | tf_op jit(solution)/shard_map/ppermute | solution.py:765
  310.9 18.9 %copy-start.17 = (bf16[2048,512]{1,0:T(8,128)(2,1)S(1)}, bf16[2048,512]{1,0:T(8,128)(2,1)}, u32[]{:S(2)}) copy-start(bf16[2048,512]{1,0:T(8,128)(2,1)} %copy-done.16) | copy-start | bytes 6291460
  329.2 37.9 %collective-permute-start.12 = (bf16[512,1024]{1,0:T(8,128)(2,1)}, bf16[512,1024]{1,0:T(8,128)(2,1)}, u32[]{:S(2)}, u32[]{:S(2)}) collective-permute-start(bf16[512,1024]{1,0:T(8,128)(2,1)} %get-tuple-element.230), channel_id=1, source_target_pairs={{0,16},{16,0},{1,17},{17,1},{2,18},{18,2},{3,19},{19,3},{4,20},{20... | collective-permute-start | bytes 3145736 | tf_op jit(solution)/shard_map/ppermute | solution.py:733
  334.4 24.8 %collective-permute-start.13 = (bf16[8,128,2048]{2,1,0:T(8,128)(2,1)}, bf16[8,128,2048]{2,1,0:T(8,128)(2,1)}, u32[]{:S(2)}, u32[]{:S(2)}) collective-permute-start(bf16[8,128,2048]{2,1,0:T(8,128)(2,1)} %grad_away.9), channel_id=1, source_target_pairs={{0,1},{1,0},{2,3},{3,2},{4,5},{5,4},{6,7},{7,6},{8,9},{9,8},{10,11... | collective-permute-start | bytes 12582920 | tf_op jit(solution)/shard_map/ppermute | solution.py:765
  340.7 36.0 %collective-permute-start.11 = (bf16[2,1,96,2304]{3,2,0,1:T(8,128)(2,1)}, bf16[2,1,96,2304]{3,2,0,1:T(8,128)(2,1)}, u32[]{:S(2)}, u32[]{:S(2)}) collective-permute-start(bf16[2,1,96,2304]{3,2,0,1:T(8,128)(2,1)} %bitcast.188), channel_id=1, source_target_pairs={{0,2},{1,3},{2,0},{3,1},{4,6},{5,7},{6,4},{7,5},{8,10},{9,11},{10,... | collective-permute-start | bytes 2654216 | tf_op jit(solution)/shard_map/ppermute | solution.py:765
  350.4 32.3 %collective-permute-start.17 = (bf16[2,1,144,1536]{3,2,0,1:T(8,128)(2,1)}, bf16[2,1,144,1536]{3,2,0,1:T(8,128)(2,1)}, u32[]{:S(2)}, u32[]{:S(2)}) collective-permute-start(bf16[2,1,144,1536]{3,2,0,1:T(8,128)(2,1)} %bitcast.189), channel_id=1, source_target_pairs={{0,4},{1,5},{2,6},{3,7},{4,0},{5,1},{6,2},{7,3},{8,12},{9,13},{10,... | collective-permute-start | bytes 2654216 | tf_op jit(solution)/shard_map/ppermute | solution.py:765
  350.6 8.6 %copy-start.33 = (bf16[2,512,1024]{2,1,0:T(8,128)(2,1)S(1)}, bf16[2,512,1024]{2,1,0:T(8,128)(2,1)}, u32[]{:S(2)}) copy-start(bf16[2,512,1024]{2,1,0:T(8,128)(2,1)} %copy-done.32) | copy-start | bytes 6291460
  357.9 64.3 %collective-permute-start.23 = (bf16[4,1,96,2304]{3,2,1,0:T(8,128)(2,1)}, bf16[4,1,96,2304]{3,2,1,0:T(8,128)(2,1)}, u32[]{:S(2)}, u32[]{:S(2)}) collective-permute-start(bf16[4,1,96,2304]{3,2,1,0:T(8,128)(2,1)} %get-tuple-element.244), channel_id=1, source_target_pairs={{0,2},{1,3},{2,0},{3,1},{4,6},{5,7},{6,4},{7,5},{8,10},{9,11},{10,... | collective-permute-start | bytes 5308424 | tf_op jit(solution)/shard_map/ppermute | solution.py:765
  359.1 8.0 %copy-start.31 = (f32[512,1024]{1,0:T(8,128)S(1)}, f32[512,1024]{1,0:T(8,128)}, u32[]{:S(2)}) copy-start(f32[512,1024]{1,0:T(8,128)} %copy-done.30) | copy-start | bytes 6291460
  376.7 8.6 %copy-start.35 = (bf16[2,512,1024]{2,1,0:T(8,128)(2,1)}, bf16[2,512,1024]{2,1,0:T(8,128)(2,1)S(1)}, u32[]{:S(2)}) copy-start(bf16[2,512,1024]{2,1,0:T(8,128)(2,1)S(1)} %get-tuple-element.276.right_ref) | copy-start | bytes 6291460
  380.0 18.4 %collective-permute-start.16 = (bf16[1,1,96,2304]{3,2,1,0:T(8,128)(2,1)}, bf16[1,1,96,2304]{3,2,1,0:T(8,128)(2,1)}, u32[]{:S(2)}, u32[]{:S(2)}) collective-permute-start(bf16[1,1,96,2304]{3,2,1,0:T(8,128)(2,1)} %get-tuple-element.259), channel_id=1, source_target_pairs={{0,8},{1,9},{2,10},{3,11},{4,12},{5,13},{6,14},{7,15},{8,0},{9,1},... | collective-permute-start | bytes 1327112 | tf_op jit(solution)/shard_map/ppermute | solution.py:765
  389.2 21.1 %collective-permute-start.19 = (bf16[8,96,2048]{2,1,0:T(8,128)(2,1)}, bf16[8,96,2048]{2,1,0:T(8,128)(2,1)}, u32[]{:S(2)}, u32[]{:S(2)}) collective-permute-start(bf16[8,96,2048]{2,1,0:T(8,128)(2,1)} %grad_away.10), channel_id=1, source_target_pairs={{0,1},{1,0},{2,3},{3,2},{4,5},{5,4},{6,7},{7,6},{8,9},{9,8},{10,11... | collective-permute-start | bytes 9437192 | tf_op jit(solution)/shard_map/ppermute | solution.py:765
  389.3 64.4 %collective-permute-start.22 = (bf16[2,2,128,2048]{3,2,1,0:T(8,128)(2,1)}, bf16[2,2,128,2048]{3,2,1,0:T(8,128)(2,1)}, u32[]{:S(2)}, u32[]{:S(2)}) collective-permute-start(bf16[2,2,128,2048]{3,2,1,0:T(8,128)(2,1)} %get-tuple-element.248), channel_id=1, source_target_pairs={{0,4},{1,5},{2,6},{3,7},{4,0},{5,1},{6,2},{7,3},{8,12},{9,13},{10,... | collective-permute-start | bytes 6291464 | tf_op jit(solution)/shard_map/ppermute | solution.py:765
  390.0 27.1 %collective-permute-start.24 = (bf16[256,1536]{1,0:T(8,128)(2,1)}, bf16[256,1536]{1,0:T(8,128)(2,1)}, u32[]{:S(2)}, u32[]{:S(2)}) collective-permute-start(bf16[256,1536]{1,0:T(8,128)(2,1)} %get-tuple-element.254), channel_id=1, source_target_pairs={{0,16},{16,0},{1,17},{17,1},{2,18},{18,2},{3,19},{19,3},{4,20},{20... | collective-permute-start | bytes 2359304 | tf_op jit(solution)/shard_map/ppermute | solution.py:733
  398.4 85.4 %collective-permute-start.26 = (bf16[1,1,144,1536]{3,2,1,0:T(8,128)(2,1)}, bf16[1,1,144,1536]{3,2,1,0:T(8,128)(2,1)}, u32[]{:S(2)}, u32[]{:S(2)}) collective-permute-start(bf16[1,1,144,1536]{3,2,1,0:T(8,128)(2,1)} %get-tuple-element.265), channel_id=1, source_target_pairs={{0,8},{1,9},{2,10},{3,11},{4,12},{5,13},{6,14},{7,15},{8,0},{9,1},... | collective-permute-start | bytes 1327112 | tf_op jit(solution)/shard_map/ppermute | solution.py:765
  400.5 10.9 %copy-start.24 = (bf16[1536,512]{1,0:T(8,128)(2,1)S(1)}, bf16[1536,512]{1,0:T(8,128)(2,1)}, u32[]{:S(2)}) copy-start(bf16[1536,512]{1,0:T(8,128)(2,1)} %copy-done.22) | copy-start | bytes 4718596
  400.5 10.9 %copy-start.36 = (bf16[2,512,1024]{2,1,0:T(8,128)(2,1)S(1)}, bf16[2,512,1024]{2,1,0:T(8,128)(2,1)}, u32[]{:S(2)}) copy-start(bf16[2,512,1024]{2,1,0:T(8,128)(2,1)} %copy-done.35) | copy-start | bytes 6291460
  410.3 132.5 %collective-permute-start.18 = (bf16[256,1536]{1,0:T(8,128)(2,1)}, bf16[256,1536]{1,0:T(8,128)(2,1)}, u32[]{:S(2)}, u32[]{:S(2)}) collective-permute-start(bf16[256,1536]{1,0:T(8,128)(2,1)} %get-tuple-element.275), channel_id=1, source_target_pairs={{0,16},{16,0},{1,17},{17,1},{2,18},{18,2},{3,19},{19,3},{4,20},{20... | collective-permute-start | bytes 2359304 | tf_op jit(solution)/shard_map/ppermute | solution.py:733
  417.1 40.1 %collective-permute-start.21 = (bf16[96,2304]{1,0:T(8,128)(2,1)}, bf16[96,2304]{1,0:T(8,128)(2,1)}, u32[]{:S(2)}, u32[]{:S(2)}) collective-permute-start(bf16[96,2304]{1,0:T(8,128)(2,1)} %get-tuple-element.272), channel_id=1, source_target_pairs={{0,16},{16,0},{1,17},{17,1},{2,18},{18,2},{3,19},{19,3},{4,20},{20... | collective-permute-start | bytes 1327112 | tf_op jit(solution)/shard_map/ppermute | solution.py:733
  422.1 39.0 %collective-permute-start.20 = (bf16[4,1,96,2048]{3,2,1,0:T(8,128)(2,1)}, bf16[4,1,96,2048]{3,2,1,0:T(8,128)(2,1)}, u32[]{:S(2)}, u32[]{:S(2)}) collective-permute-start(bf16[4,1,96,2048]{3,2,1,0:T(8,128)(2,1)} %get-tuple-element.279), channel_id=1, source_target_pairs={{0,2},{1,3},{2,0},{3,1},{4,6},{5,7},{6,4},{7,5},{8,10},{9,11},{10,... | collective-permute-start | bytes 4718600 | tf_op jit(solution)/shard_map/ppermute | solution.py:765
  422.9 30.8 %copy-start.19 = (bf16[2,2,128,2048]{3,2,1,0:T(8,128)(2,1)S(1)}, bf16[2,2,128,2048]{3,2,1,0:T(8,128)(2,1)}, u32[]{:S(2)}) copy-start(bf16[2,2,128,2048]{3,2,1,0:T(8,128)(2,1)} %copy-done.18) | copy-start | bytes 6291460
  457.3 22.4 %collective-permute-start.27 = (bf16[2,1,96,2304]{3,2,0,1:T(8,128)(2,1)}, bf16[2,1,96,2304]{3,2,0,1:T(8,128)(2,1)}, u32[]{:S(2)}, u32[]{:S(2)}) collective-permute-start(bf16[2,1,96,2304]{3,2,0,1:T(8,128)(2,1)} %bitcast.61), channel_id=1, source_target_pairs={{0,4},{1,5},{2,6},{3,7},{4,0},{5,1},{6,2},{7,3},{8,12},{9,13},{10,... | collective-permute-start | bytes 2654216 | tf_op jit(solution)/shard_map/ppermute | solution.py:765
  457.3 35.5 %collective-permute-start.31 = (bf16[2,1,128,2048]{3,2,0,1:T(8,128)(2,1)}, bf16[2,1,128,2048]{3,2,0,1:T(8,128)(2,1)}, u32[]{:S(2)}, u32[]{:S(2)}) collective-permute-start(bf16[2,1,128,2048]{3,2,0,1:T(8,128)(2,1)} %bitcast.187), channel_id=1, source_target_pairs={{0,2},{1,3},{2,0},{3,1},{4,6},{5,7},{6,4},{7,5},{8,10},{9,11},{10,... | collective-permute-start | bytes 3145736 | tf_op jit(solution)/shard_map/ppermute | solution.py:765
  467.0 19.8 %collective-permute-start.25 = (bf16[8,128,768]{2,1,0:T(8,128)(2,1)}, bf16[8,128,768]{2,1,0:T(8,128)(2,1)}, u32[]{:S(2)}, u32[]{:S(2)}) collective-permute-start(bf16[8,128,768]{2,1,0:T(8,128)(2,1)} %grad_away.11), channel_id=1, source_target_pairs={{0,1},{1,0},{2,3},{3,2},{4,5},{5,4},{6,7},{7,6},{8,9},{9,8},{10,11... | collective-permute-start | bytes 4718600 | tf_op jit(solution)/shard_map/ppermute | solution.py:765
  482.3 22.3 %collective-permute-start.30 = (bf16[1,1,96,2304]{3,2,1,0:T(8,128)(2,1)}, bf16[1,1,96,2304]{3,2,1,0:T(8,128)(2,1)}, u32[]{:S(2)}, u32[]{:S(2)}) collective-permute-start(bf16[1,1,96,2304]{3,2,1,0:T(8,128)(2,1)} %get-tuple-element.301), channel_id=1, source_target_pairs={{0,8},{1,9},{2,10},{3,11},{4,12},{5,13},{6,14},{7,15},{8,0},{9,1},... | collective-permute-start | bytes 1327112 | tf_op jit(solution)/shard_map/ppermute | solution.py:765
  485.8 20.8 %collective-permute-start.29 = (bf16[144,1536]{1,0:T(8,128)(2,1)}, bf16[144,1536]{1,0:T(8,128)(2,1)}, u32[]{:S(2)}, u32[]{:S(2)}) collective-permute-start(bf16[144,1536]{1,0:T(8,128)(2,1)} %get-tuple-element.305), channel_id=1, source_target_pairs={{0,16},{16,0},{1,17},{17,1},{2,18},{18,2},{3,19},{19,3},{4,20},{20... | collective-permute-start | bytes 1327112 | tf_op jit(solution)/shard_map/ppermute | solution.py:733
  486.8 34.4 %collective-permute-start.35 = (bf16[2,1,96,2048]{3,2,0,1:T(8,128)(2,1)}, bf16[2,1,96,2048]{3,2,0,1:T(8,128)(2,1)}, u32[]{:S(2)}, u32[]{:S(2)}) collective-permute-start(bf16[2,1,96,2048]{3,2,0,1:T(8,128)(2,1)} %bitcast.74), channel_id=1, source_target_pairs={{0,4},{1,5},{2,6},{3,7},{4,0},{5,1},{6,2},{7,3},{8,12},{9,13},{10,... | collective-permute-start | bytes 2359304 | tf_op jit(solution)/shard_map/ppermute | solution.py:765
  492.7 18.1 %collective-permute-start.28 = (bf16[4,1,128,768]{3,2,1,0:T(8,128)(2,1)}, bf16[4,1,128,768]{3,2,1,0:T(8,128)(2,1)}, u32[]{:S(2)}, u32[]{:S(2)}) collective-permute-start(bf16[4,1,128,768]{3,2,1,0:T(8,128)(2,1)} %get-tuple-element.309), channel_id=1, source_target_pairs={{0,2},{1,3},{2,0},{3,1},{4,6},{5,7},{6,4},{7,5},{8,10},{9,11},{10,... | collective-permute-start | bytes 2359304 | tf_op jit(solution)/shard_map/ppermute | solution.py:765
  504.6 29.1 %collective-permute-start.33 = (bf16[1,1,128,2048]{3,2,1,0:T(8,128)(2,1)}, bf16[1,1,128,2048]{3,2,1,0:T(8,128)(2,1)}, u32[]{:S(2)}, u32[]{:S(2)}) collective-permute-start(bf16[1,1,128,2048]{3,2,1,0:T(8,128)(2,1)} %get-tuple-element.313), channel_id=1, source_target_pairs={{0,8},{1,9},{2,10},{3,11},{4,12},{5,13},{6,14},{7,15},{8,0},{9,1},... | collective-permute-start | bytes 1572872 | tf_op jit(solution)/shard_map/ppermute | solution.py:765
  506.6 17.3 %collective-permute-start.34 = (bf16[96,2304]{1,0:T(8,128)(2,1)}, bf16[96,2304]{1,0:T(8,128)(2,1)}, u32[]{:S(2)}, u32[]{:S(2)}) collective-permute-start(bf16[96,2304]{1,0:T(8,128)(2,1)} %get-tuple-element.317), channel_id=1, source_target_pairs={{0,16},{16,0},{1,17},{17,1},{2,18},{18,2},{3,19},{19,3},{4,20},{20... | collective-permute-start | bytes 1327112 | tf_op jit(solution)/shard_map/ppermute | solution.py:733
  513.4 27.1 %collective-permute-start.32 = (bf16[2,1,128,768]{3,2,0,1:T(8,128)(2,1)}, bf16[2,1,128,768]{3,2,0,1:T(8,128)(2,1)}, u32[]{:S(2)}, u32[]{:S(2)}) collective-permute-start(bf16[2,1,128,768]{3,2,0,1:T(8,128)(2,1)} %bitcast.190), channel_id=1, source_target_pairs={{0,4},{1,5},{2,6},{3,7},{4,0},{5,1},{6,2},{7,3},{8,12},{9,13},{10,... | collective-permute-start | bytes 1179656 | tf_op jit(solution)/shard_map/ppermute | solution.py:765
  523.8 27.5 %collective-permute-start.36 = (bf16[1,1,96,2048]{3,2,1,0:T(8,128)(2,1)}, bf16[1,1,96,2048]{3,2,1,0:T(8,128)(2,1)}, u32[]{:S(2)}, u32[]{:S(2)}) collective-permute-start(bf16[1,1,96,2048]{3,2,1,0:T(8,128)(2,1)} %get-tuple-element.327), channel_id=1, source_target_pairs={{0,8},{1,9},{2,10},{3,11},{4,12},{5,13},{6,14},{7,15},{8,0},{9,1},... | collective-permute-start | bytes 1179656 | tf_op jit(solution)/shard_map/ppermute | solution.py:765
  535.9 19.5 %collective-permute-start.39 = (bf16[128,2048]{1,0:T(8,128)(2,1)}, bf16[128,2048]{1,0:T(8,128)(2,1)}, u32[]{:S(2)}, u32[]{:S(2)}) collective-permute-start(bf16[128,2048]{1,0:T(8,128)(2,1)} %get-tuple-element.333), channel_id=1, source_target_pairs={{0,16},{16,0},{1,17},{17,1},{2,18},{18,2},{3,19},{19,3},{4,20},{20... | collective-permute-start | bytes 1572872 | tf_op jit(solution)/shard_map/ppermute | solution.py:733
  542.8 15.1 %collective-permute-start.38 = (bf16[1,1,128,768]{3,2,1,0:T(8,128)(2,1)}, bf16[1,1,128,768]{3,2,1,0:T(8,128)(2,1)}, u32[]{:S(2)}, u32[]{:S(2)}) collective-permute-start(bf16[1,1,128,768]{3,2,1,0:T(8,128)(2,1)} %get-tuple-element.337), channel_id=1, source_target_pairs={{0,8},{1,9},{2,10},{3,11},{4,12},{5,13},{6,14},{7,15},{8,0},{9,1},... | collective-permute-start | bytes 589832 | tf_op jit(solution)/shard_map/ppermute | solution.py:765
  553.8 11.2 %collective-permute-start.37 = (bf16[96,2048]{1,0:T(8,128)(2,1)}, bf16[96,2048]{1,0:T(8,128)(2,1)}, u32[]{:S(2)}, u32[]{:S(2)}) collective-permute-start(bf16[96,2048]{1,0:T(8,128)(2,1)} %get-tuple-element.344), channel_id=1, source_target_pairs={{0,16},{16,0},{1,17},{17,1},{2,18},{18,2},{3,19},{19,3},{4,20},{20... | collective-permute-start | bytes 1179656 | tf_op jit(solution)/shard_map/ppermute | solution.py:733
  559.5 10.0 %collective-permute-start.40 = (bf16[128,768]{1,0:T(8,128)(2,1)}, bf16[128,768]{1,0:T(8,128)(2,1)S(1)}, u32[]{:S(2)}, u32[]{:S(2)}) collective-permute-start(bf16[128,768]{1,0:T(8,128)(2,1)} %get-tuple-element.352), channel_id=1, source_target_pairs={{0,16},{16,0},{1,17},{17,1},{2,18},{18,2},{3,19},{19,3},{4,20},{20... | collective-permute-start | bytes 589832 | tf_op jit(solution)/shard_map/ppermute | solution.py:733
  (51 other events, 222.4 us)
Sparse Core Ops, SparseCore 0:
  10.2 111.9 all-gather.4
  124.3 110.2 all-gather.6
  398.6 140.5 all-reduce.5

commit v7 on v6

--- a/solution.py
+++ b/solution.py
@@ -20,10 +20,10 @@
 MORE = 50 << 20
 PARTS = 2
 STEPS = (
-    "turn", "ffn_in", "away_u", "away_d", "norm_two", "home_u", "home_d", "away_g", "mixer", "away_r", "two_u",
-    "two_d", "home_g", "home_r", "conv_in", "fold_u", "fold_d", "away_b", "small", "settle_u", "down", "home_b",
+    "turn", "ffn_in", "away_d", "away_u", "norm_two", "home_u", "home_d", "away_g", "mixer", "away_r", "two_u",
+    "two_d", "home_g", "home_r", "fold_u", "conv_in", "fold_d", "away_b", "small", "settle_u", "down", "home_b",
     "norm_one", "two_g", "two_r", "join_u", "two_b", "away_o", "fold_g", "settle_d", "home_o", "fold_r", "settle_g",
-    "join_d", "two_o", "fold_b", "join_g", "settle_r", "fold_o", "result", "small_end", "settle_b", "join_r",
+    "join_d", "two_o", "fold_b", "join_g", "settle_r", "fold_o", "result", "settle_b", "small_end", "join_r",
     "settle_o", "join_b", "join_o",
 )
 HINT = pl.CostEstimate(flops=100000000000, bytes_accessed=1024, transcendentals=0)

time: 589 us -> 581 us (0.986)
    unnamed x155 -> x153, local copies, waits for them, and re-layouts: 18.6 us -> 19.3 us
  transfers between devices with their start and end apart: 44 -> 44, of which waited for: 18 -> 17; matrix products, arithmetic and copies ran while one was open for 9% -> 9% of each run, Pallas kernels for 32% -> 32%
where the time goes in v7:
time: 581 us; the launch traced here: 569 us
  Pallas kernels  216 us (37%)
  waiting for transfers between devices  213 us (37%)
  local copies, waits for them, and re-layouts  41 us (7%)
  starting transfers between devices  35.9 us (6%)
  blocking collectives  22.7 us (4%)
  between operations  15.1 us (3%)
  other arithmetic  13.7 us (2%)
  matrix products  11.7 us (2%)
    ppermute x24, waiting for transfers between devices, cross(): return lax.ppermute(v, 'shard', [(i, i ^ 1 << bit) for i in range(shards)])  79.4 us
    all_gather x1, waiting for transfers between devices, body(): lax.all_gather(pack(here_side, [branch_proj, lruin_proj, recur_proj, admi...  66 us
    ppermute x17, waiting for transfers between devices, swap(): return lax.ppermute(v, 'rep', [(i, i ^ 1) for i in range(groups)])  56.8 us
    pallas_call x12, Pallas kernels, fold(): pl.pallas_call(functools.partial(fold_kernel, bit), grid_spec=pltpu.Prefe...  36.2 us
    pallas_call x6, Pallas kernels, grad_home(): pl.pallas_call(functools.partial(home_kernel, bit), grid_spec=pltpu.Prefe...  32.9 us
    pallas_call x1, Pallas kernels, ffn_pass(): pl.pallas_call(ffn_kernel, grid=(tiles,), in_specs=[fixed, fixed, pl.Bloc...  31.2 us
    pallas_call x6, Pallas kernels, grad_away(): pl.pallas_call(away_kernel, grid_spec=pltpu.PrefetchScalarGridSpec(num_sc...  25.4 us
    all_gather x1, blocking collectives, body(): lax.all_gather(vectors, 'shard', axis=0).reshape(shards, -1)[:, :count]  22.7 us
  transfers between devices with their start and end apart: 44, of which 17 were waited for; matrix products, arithmetic and copies ran while one was open for 9% of the time, Pallas kernels for 32%

profile of v7, /device:TPU:0, one launch (start us, length us, event | category | flops | bytes accessed | tf_op | source)
XLA Modules:
  0.0 569.4 jit_solution(15633393351262740023)
XLA Ops:
  7.3 2.6 pack.1
  10.0 3.0 collective-permute-start
  24.7 22.7 %all_gather.15 = bf16[16,10,128]{2,1,0:T(8,128)(2,1)S(1)} all-gather(bf16[1,10,128]{2,1,0:T(8,128)(2,1)S(1)} %pad_bitcast_fusion), channel_id=1, replica_groups=mesh['rep'=2,'shard'=16] {'shard'}, dimensions={0}, use_global_device_ids=true | all-gather | bytes 43520 | tf_op jit(solution)/shard_map/all_gather | solution.py:820
  54.1 2.1 constant_dynamic-update-slice_fusion.cot_ref
  56.2 66.0 %all-gather.5.cloned.1.call-done = bf16[20480,512]{1,0:T(8,128)(2,1)} async-done(((bf16[1280,512]{1,0:T(8,128)(2,1)}), bf16[20480,512]{1,0:T(8,128)(2,1)}) %all-gather.5.cloned.1.call-update) | async-done | bytes 20971536 | tf_op jit(solution)/shard_map/all_gather | solution.py:843
  122.1 3.2 fusion.45
  125.4 3.4 fusion.8.pre_ref.lru_ref
  134.3 8.3 %fusion.44 = (bf16[16,128,512]{2,1,0:T(8,128)(2,1)S(1)}, bf16[16,128,512]{2,1,0:T(8,128)(2,1)}, bf16[16,128,512]{2,1,0:T(8,128)(2,1)}, bf16[16,128,512]{2,1,0:T(...) fusion(bf16[16,1280,512]{2,1,0:T(8,128)(2,1)} %bitcast.145), kind=kLoop, calls=%fused_computation.96 | loop fusion | bytes 29360128 | tf_op jit(solution)/shard_map/slice | solution.py:839
  142.6 14.6 %collective-permute-done.2 = bf16[512,1024]{1,0:T(8,128)(2,1)S(1)} collective-permute-done((bf16[512,1024]{1,0:T(8,128)(2,1)S(1)}, bf16[512,1024]{1,0:T(8,128)(2,1)S(1)}, u32[]{:S(2)}, u32[]{:S(2)}) %collective-permute-start.2) | collective-permute-done | bytes 1048608 | tf_op jit(solution)/shard_map/ppermute | solution.py:733
  158.7 6.4 %fusion.gates_r_ref.gates_i_ref = f32[512,2048]{1,0:T(8,128)} fusion(bf16[2048,512]{1,0:T(8,128)(2,1)S(1)} %bitcast.164, bf16[2048,512]{1,0:T(8,128)(2,1)S(1)} %bitcast.165, bf16[2048,512]{1,0:T(8,128)(2,1)S(1)} %bitcast.166, bf16[2048,512]{1,0:T(8,128)(2,1)S(1)} %bitcast.163, bf16[512,1024]{1,0:T(8,128)(2,1)S(1)} %get-tuple-element.371, ...), kind=kOutput, calls=%fused_computation | convolution fusion | flops 4332716032 | bytes 14680064 | tf_op jit(solution)/shard_map/dot_general | solution.py:40
  165.1 12.3 %recurrence_forward.1 = (bf16[512,1024]{1,0:T(8,128)(2,1)}, f32[512,1024]{1,0:T(8,128)}, f32[512,1024]{1,0:T(8,128)}, f32[512,1024]{1,0:T(8,128)}, f32[512,1024]...) custom-call(f32[512,2048]{1,0:T(8,128)} %copy-done.40, ...), custom_call_target="tpu_custom_call" | custom-call | flops 31457280 | bytes 10485760 | tf_op jit(solution)/shard_map/recurrence_forward/pallas_call | solution.py:435
  181.8 10.2 %collective-permute-done.3 = bf16[256,1024]{1,0:T(8,128)(2,1)S(1)} collective-permute-done((bf16[256,1024]{1,0:T(8,128)(2,1)S(1)}, bf16[256,1024]{1,0:T(8,128)(2,1)S(1)}, u32[]{:S(2)}, u32[]{:S(2)}) %collective-permute-start.3) | collective-permute-done | bytes 524320 | tf_op jit(solution)/shard_map/ppermute | solution.py:733
  196.4 10.6 %collective-permute-done.5 = bf16[256,1024]{1,0:T(8,128)(2,1)S(1)} collective-permute-done((bf16[256,1024]{1,0:T(8,128)(2,1)S(1)}, bf16[256,1024]{1,0:T(8,128)(2,1)S(1)}, u32[]{:S(2)}, u32[]{:S(2)}) %collective-permute-start.5) | collective-permute-done | bytes 524320 | tf_op jit(solution)/shard_map/ppermute | solution.py:733
  210.0 11.5 %collective-permute-done.4 = bf16[256,1536]{1,0:T(8,128)(2,1)S(1)} collective-permute-done((bf16[256,1536]{1,0:T(8,128)(2,1)S(1)}, bf16[256,1536]{1,0:T(8,128)(2,1)S(1)}, u32[]{:S(2)}, u32[]{:S(2)}) %collective-permute-start.4) | collective-permute-done | bytes 786464 | tf_op jit(solution)/shard_map/ppermute | solution.py:733
  223.8 10.8 %all-gather.7.cloned.1.call-done = bf16[13824,768]{1,0:T(8,128)(2,1)} async-done(((bf16[864,768]{1,0:T(8,128)(2,1)}), bf16[13824,768]{1,0:T(8,128)(2,1)}) %all-gather.7.cloned.1.call-update) | async-done | bytes 21233680 | tf_op jit(solution)/shard_map/all_gather | solution.py:835
  234.6 31.2 %ffn_pass.1 = (bf16[512,2304]{1,0:T(8,128)(2,1)}, bf16[2304,512]{1,0:T(8,128)(2,1)}, bf16[512,2304]{1,0:T(8,128)(2,1)}, bf16[512,2304]{1,0:T(8,128)(2,1)}, f32[2...) custom-call(bf16[512,1536]{1,0:T(8,128)(2,1)S(1)} %pad_maximum_fusion.2.x_ref, ...), custom_call_target="tpu_custom_call" | custom-call | flops 99999997952 | bytes 1024 | tf_op jit(solution)/shard_map/ffn_pass/pallas_call | solution.py:513
  269.1 5.5 grad_away.6
  274.6 4.5 grad_away.7
  279.6 6.4 %collective-permute-done.7.far_ref = bf16[256,1536]{1,0:T(8,128)(2,1)} collective-permute-done((bf16[256,1536]{1,0:T(8,128)(2,1)}, bf16[256,1536]{1,0:T(8,128)(2,1)}, u32[]{:S(2)}, u32[]{:S(2)}) %collective-permute-start.7) | collective-permute-done | bytes 786464 | tf_op jit(solution)/shard_map/ppermute | solution.py:733
  286.0 3.7 norm_back.2
  291.1 4.7 grad_home.6
  297.3 6.2 %grad_home.7 = (bf16[4,1,144,1536]{3,2,1,0:T(8,128)(2,1)S(1)}, bf16[4,1,144,1536]{3,2,1,0:T(8,128)(2,1)}) custom-call(s32[5]{0:T(128)S(1)} %stack.24.at_ref, bf16[8,2,144,512]{3,2,1,0:T(8,128)(2,1)S(1)} %bitcast.113, bf16[1,512,1536]{2,1,0:T(8,128)(2,1)} %bitcast.36.right_ref, bf16[8,144,1536]{2,1,0:T(8,128)(2,1)} %collective-permute-done.10.got_ref), custom_call_target="tpu_custom_call" | custom-call | flops 99999997952 | bytes 1024 | tf_op jit(solution)/shard_map/grad_home/pallas_call | solution.py:638
  304.8 4.4 grad_away.8
  309.3 18.2 %chain_back.1 = (bf16[512,1024]{1,0:T(8,128)(2,1)S(1)}, bf16[2,512,1024]{2,1,0:T(8,128)(2,1)S(1)}, f32[512,1024]{1,0:T(8,128)S(1)}, f32[48,1024]{1,0:T(8,128)S(1...) custom-call(s32[1]{0:T(128)} %bitcast.2.side_ref, bf16[256,1536]{1,0:T(8,128)(2,1)S(1)} %copy-done.7, ...), custom_call_target="tpu_custom_call" | custom-call | flops 99999997952 | bytes 1024 | tf_op jit(solution)/shard_map/chain_back/pallas_call | solution.py:175
  328.6 4.6 grad_away.9
  335.9 3.3 fold.12
  340.3 5.1 collective-permute-done.14
  345.4 3.6 fold.13
  349.0 6.1 %grad_home.8 = (bf16[4,1,96,2304]{3,2,1,0:T(8,128)(2,1)S(1)}, bf16[4,1,96,2304]{3,2,1,0:T(8,128)(2,1)}) custom-call(s32[5]{0:T(128)S(1)} %stack.24.at_ref, bf16[8,2,96,512]{3,2,1,0:T(8,128)(2,1)S(1)} %bitcast.129, bf16[1,512,2304]{2,1,0:T(8,128)(2,1)S(1)} %bitcast.111, bf16[8,96,2304]{2,1,0:T(8,128)(2,1)} %collective-permute-done.13.got_ref), custom_call_target="tpu_custom_call" | custom-call | flops 99999997952 | bytes 1024 | tf_op jit(solution)/shard_map/grad_home/pallas_call | solution.py:638
  357.6 6.3 %grad_home.9 = (bf16[2,2,128,2048]{3,2,1,0:T(8,128)(2,1)S(1)}, bf16[2,2,128,2048]{3,2,1,0:T(8,128)(2,1)}) custom-call(s32[5]{0:T(128)S(1)} %stack.24.at_ref, bf16[8,2,128,512]{3,2,1,0:T(8,128)(2,1)S(1)} %bitcast.119, bf16[2,512,1024]{2,1,0:T(8,128)(2,1)S(1)} %get-tuple-element.244.right_ref, bf16[8,128,2048]{2,1,0:T(8,128)(2,1)} %collective-permute-done.12.got_ref), custom_call_target="tpu_custom_call" | custom-call | flops 99999997952 | bytes 1024 | tf_op jit(solution)/shard_map/grad_home/pallas_call | solution.py:638
  365.1 2.9 fold.14
  368.0 2.7 collective-permute-start.15
  370.7 9.6 %conv_back.1 = (bf16[2,512,1024]{2,1,0:T(8,128)(2,1)S(1)}, f32[8,1024]{1,0:T(8,128)S(1)}, f32[256,1536]{1,0:T(8,128)S(1)}, bf16[256,1536]{1,0:T(8,128)(2,1)}) custom-call(f32[512,1024]{1,0:T(8,128)S(1)} %copy-done.30, f32[512,1024]{1,0:T(8,128)S(1)} %copy-done.32, bf16[512,1024]{1,0:T(8,128)(2,1)} %collective-permute-done.16.far_in_ref, ...), custom_call_target="tpu_custom_call" | custom-call | flops 99999997952 | bytes 1024 | tf_op jit(solution)/shard_map/conv_back/pallas_call | solution.py:248
  380.3 3.8 fold.15
  384.2 3.8 grad_away.10
  391.7 2.1 settle.6
  393.8 9.8 %down_pass.1 = (f32[256,1536]{1,0:T(8,128)S(1)}, bf16[256,1536]{1,0:T(8,128)(2,1)}) custom-call(bf16[512,2304]{1,0:T(8,128)(2,1)S(1)} %copy-done.33, bf16[16,864,768]{2,1,0:T(8,128)(2,1)} %bitcast.185, bf16[16,864,768]{2,1,0:T(8,128)(2,1)} %bitcast.186), custom_call_target="tpu_custom_call" | custom-call | flops 99999997952 | bytes 1024 | tf_op jit(solution)/shard_map/down_pass/pallas_call | solution.py:562
  405.1 5.6 grad_home.10
  411.3 4.1 norm_back.3
  416.2 3.4 fold.16
  419.6 27.4 %collective-permute-done.22 = bf16[2,2,128,2048]{3,2,1,0:T(8,128)(2,1)} collective-permute-done((bf16[2,2,128,2048]{3,2,1,0:T(8,128)(2,1)}, bf16[2,2,128,2048]{3,2,1,0:T(8,128)(2,1)}, u32[]{:S(2)}, u32[]{:S(2)}) %collective-permute-start.22) | collective-permute-done | bytes 2097184 | tf_op jit(solution)/shard_map/ppermute | solution.py:765
  447.0 3.5 fold.17
  451.3 3.1 weave.2
  454.3 3.2 fold.18
  457.6 2.7 grad_away.11
  460.2 12.3 %collective-permute-done.27 = bf16[2,1,96,2304]{3,2,0,1:T(8,128)(2,1)} collective-permute-done((bf16[2,1,96,2304]{3,2,0,1:T(8,128)(2,1)}, bf16[2,1,96,2304]{3,2,0,1:T(8,128)(2,1)}, u32[]{:S(2)}, u32[]{:S(2)}) %collective-permute-start.27) | collective-permute-done | bytes 884768 | tf_op jit(solution)/shard_map/ppermute | solution.py:765
  472.5 2.6 fold.19
  480.0 4.1 grad_home.11
  484.4 2.7 fold.20
  487.1 9.9 %collective-permute-done.30 = bf16[1,1,96,2304]{3,2,1,0:T(8,128)(2,1)} collective-permute-done((bf16[1,1,96,2304]{3,2,1,0:T(8,128)(2,1)}, bf16[1,1,96,2304]{3,2,1,0:T(8,128)(2,1)}, u32[]{:S(2)}, u32[]{:S(2)}) %collective-permute-start.30) | collective-permute-done | bytes 442400 | tf_op jit(solution)/shard_map/ppermute | solution.py:765
  499.4 2.3 join_rows.1
  501.8 2.5 fold.21
  504.4 2.4 collective-permute-start.32
  506.8 5.8 %collective-permute-done.35 = bf16[2,1,96,2048]{3,2,0,1:T(8,128)(2,1)} collective-permute-done((bf16[2,1,96,2048]{3,2,0,1:T(8,128)(2,1)}, bf16[2,1,96,2048]{3,2,0,1:T(8,128)(2,1)}, u32[]{:S(2)}, u32[]{:S(2)}) %collective-permute-start.35) | collective-permute-done | bytes 786464 | tf_op jit(solution)/shard_map/ppermute | solution.py:765
  512.6 2.5 fold.22
  515.1 2.8 weave.3
  518.0 11.6 %collective-permute-done.33 = bf16[1,1,128,2048]{3,2,1,0:T(8,128)(2,1)} collective-permute-done((bf16[1,1,128,2048]{3,2,1,0:T(8,128)(2,1)}, bf16[1,1,128,2048]{3,2,1,0:T(8,128)(2,1)}, u32[]{:S(2)}, u32[]{:S(2)}) %collective-permute-start.33) | collective-permute-done | bytes 524320 | tf_op jit(solution)/shard_map/ppermute | solution.py:765
  529.5 2.1 settle.9
  533.4 2.3 fold.23
  535.7 2.4 add_convert_fusion
  538.1 5.7 %collective-permute-done.36 = bf16[1,1,96,2048]{3,2,1,0:T(8,128)(2,1)} collective-permute-done((bf16[1,1,96,2048]{3,2,1,0:T(8,128)(2,1)}, bf16[1,1,96,2048]{3,2,1,0:T(8,128)(2,1)}, u32[]{:S(2)}, u32[]{:S(2)}) %collective-permute-start.36) | collective-permute-done | bytes 393248 | tf_op jit(solution)/shard_map/ppermute | solution.py:765
  547.9 2.4 join_columns.3
  553.6 3.5 collective-permute-done.37.got_ref
  557.1 2.3 join_columns.4
  (288 shorter events, 83.0 us)
Async XLA Ops:
  7.2 115.0 %all-gather.5.cloned.1.call-start = ((), (), s32[]{:S(2)}) async-start(), calls=%async_computation.1 | async-start | bytes 22282240 | tf_op jit(solution)/shard_map/all_gather | solution.py:843
  9.9 224.7 %all-gather.7.cloned.1.call-start = ((), (), s32[]{:S(2)}) async-start(), calls=%async_computation.2 | async-start | bytes 22560768 | tf_op jit(solution)/shard_map/all_gather | solution.py:835
  10.0 38.7 %collective-permute-start = (bf16[256,1536]{1,0:T(8,128)(2,1)S(1)}, bf16[256,1536]{1,0:T(8,128)(2,1)}, u32[]{:S(2)}, u32[]{:S(2)}) collective-permute-start(bf16[256,1536]{1,0:T(8,128)(2,1)S(1)} %copy-done.3), channel_id=1, source_target_pairs={{0,16},{16,0},{1,17},{17,1},{2,18},{18,2},{3,19},{19,3},{4,20},{20... | collective-permute-start | bytes 2359304 | tf_op jit(solution)/shard_map/ppermute | solution.py:733
  13.0 41.0 %collective-permute-start.1 = (bf16[256,1536]{1,0:T(8,128)(2,1)S(1)}, bf16[256,1536]{1,0:T(8,128)(2,1)}, u32[]{:S(2)}, u32[]{:S(2)}) collective-permute-start(bf16[256,1536]{1,0:T(8,128)(2,1)S(1)} %copy-done.6), channel_id=1, source_target_pairs={{0,16},{16,0},{1,17},{17,1},{2,18},{18,2},{3,19},{19,3},{4,20},{20... | collective-permute-start | bytes 2359304 | tf_op jit(solution)/shard_map/ppermute | solution.py:733
  24.5 521.6 %all-reduce.6.cloned.1.call-start = ((), (), s32[]{:S(2)}) async-start(), calls=%async_computation | async-start | bytes 131072 | tf_op jit(solution)/shard_map/psum | solution.py:960
  131.8 25.5 %copy-start.41 = (bf16[2,256,1024]{2,1,0:T(8,128)(2,1)}, bf16[2,256,1024]{2,1,0:T(8,128)(2,1)S(1)}, u32[]{:S(2)}) copy-start(bf16[2,256,1024]{2,1,0:T(8,128)(2,1)S(1)} %fusion.32) | copy-start | bytes 3145732
  131.8 25.4 %collective-permute-start.2 = (bf16[512,1024]{1,0:T(8,128)(2,1)S(1)}, bf16[512,1024]{1,0:T(8,128)(2,1)S(1)}, u32[]{:S(2)}, u32[]{:S(2)}) collective-permute-start(bf16[512,1024]{1,0:T(8,128)(2,1)S(1)} %bitcast.153), channel_id=1, source_target_pairs={{0,16},{16,0},{1,17},{17,1},{2,18},{18,2},{3,19},{19,3},{4,20},{20... | collective-permute-start | bytes 3145736 | tf_op jit(solution)/shard_map/ppermute | solution.py:733
  133.4 62.1 %copy-start.59 = (f32[1536]{0:T(1024)}, f32[1536]{0:T(1024)S(1)}, u32[]{:S(2)}) copy-start(f32[1536]{0:T(1024)S(1)} %reshape.325) | copy-start | bytes 18436
  165.1 15.0 %copy-start.43 = (bf16[512,1024]{1,0:T(8,128)(2,1)S(1)}, bf16[512,1024]{1,0:T(8,128)(2,1)}, u32[]{:S(2)}) copy-start(bf16[512,1024]{1,0:T(8,128)(2,1)} %copy-done.42) | copy-start | bytes 3145732
  178.5 13.4 %collective-permute-start.3 = (bf16[256,1024]{1,0:T(8,128)(2,1)S(1)}, bf16[256,1024]{1,0:T(8,128)(2,1)S(1)}, u32[]{:S(2)}, u32[]{:S(2)}) collective-permute-start(bf16[256,1024]{1,0:T(8,128)(2,1)S(1)} %slice.172), channel_id=1, source_target_pairs={{0,16},{16,0},{1,17},{17,1},{2,18},{18,2},{3,19},{19,3},{4,20},{20... | collective-permute-start | bytes 1572872 | tf_op jit(solution)/shard_map/ppermute | solution.py:733
  180.3 11.7 %copy-start.54 = (bf16[512,1024]{1,0:T(8,128)(2,1)S(1)}, bf16[512,1024]{1,0:T(8,128)(2,1)}, u32[]{:S(2)}) copy-start(bf16[512,1024]{1,0:T(8,128)(2,1)} %get-tuple-element.189) | copy-start | bytes 3145732
  180.3 13.3 %copy-start.48 = (bf16[16,128,512]{2,1,0:T(8,128)(2,1)S(1)}, bf16[16,128,512]{2,1,0:T(8,128)(2,1)}, u32[]{:S(2)}) copy-start(bf16[16,128,512]{2,1,0:T(8,128)(2,1)} %get-tuple-element.360) | copy-start | bytes 6291460
  180.3 13.3 %copy-start.49 = (bf16[16,128,512]{2,1,0:T(8,128)(2,1)S(1)}, bf16[16,128,512]{2,1,0:T(8,128)(2,1)}, u32[]{:S(2)}) copy-start(bf16[16,128,512]{2,1,0:T(8,128)(2,1)} %get-tuple-element.361) | copy-start | bytes 6291460
  180.3 13.3 %copy-start.50 = (bf16[16,128,512]{2,1,0:T(8,128)(2,1)S(1)}, bf16[16,128,512]{2,1,0:T(8,128)(2,1)}, u32[]{:S(2)}) copy-start(bf16[16,128,512]{2,1,0:T(8,128)(2,1)} %get-tuple-element.362) | copy-start | bytes 6291460
  181.8 11.8 %copy-start.15 = (bf16[2048,512]{1,0:T(8,128)(2,1)}, bf16[2048,512]{1,0:T(8,128)(2,1)S(1)}, u32[]{:S(2)}) copy-start(bf16[2048,512]{1,0:T(8,128)(2,1)S(1)} %flip.5) | copy-start | bytes 6291460
  181.8 11.8 %copy-start.4 = (bf16[256,1536]{1,0:T(8,128)(2,1)S(1)}, bf16[256,1536]{1,0:T(8,128)(2,1)}, u32[]{:S(2)}) copy-start(bf16[256,1536]{1,0:T(8,128)(2,1)} %v_ref.1) | copy-start | bytes 2359300
  192.1 14.9 %collective-permute-start.5 = (bf16[256,1024]{1,0:T(8,128)(2,1)S(1)}, bf16[256,1024]{1,0:T(8,128)(2,1)S(1)}, u32[]{:S(2)}, u32[]{:S(2)}) collective-permute-start(bf16[256,1024]{1,0:T(8,128)(2,1)S(1)} %get-tuple-element.376), channel_id=1, source_target_pairs={{0,16},{16,0},{1,17},{17,1},{2,18},{18,2},{3,19},{19,3},{4,20},{20... | collective-permute-start | bytes 1572872 | tf_op jit(solution)/shard_map/ppermute | solution.py:733
  195.5 11.6 %copy-start = (f32[256,1536]{1,0:T(8,128)}, f32[256,1536]{1,0:T(8,128)S(1)}, u32[]{:S(2)}) copy-start(f32[256,1536]{1,0:T(8,128)S(1)} %get-tuple-element.400.v_ref) | copy-start | bytes 4718596
  195.8 25.8 %collective-permute-start.4 = (bf16[256,1536]{1,0:T(8,128)(2,1)S(1)}, bf16[256,1536]{1,0:T(8,128)(2,1)S(1)}, u32[]{:S(2)}, u32[]{:S(2)}) collective-permute-start(bf16[256,1536]{1,0:T(8,128)(2,1)S(1)} %multiply_convert_fusion), channel_id=1, source_target_pairs={{0,16},{16,0},{1,17},{17,1},{2,18},{18,2},{3,19},{19,3},{4,20},{20... | collective-permute-start | bytes 2359304 | tf_op jit(solution)/shard_map/ppermute | solution.py:733
  265.9 20.1 %collective-permute-start.7 = (bf16[256,1536]{1,0:T(8,128)(2,1)}, bf16[256,1536]{1,0:T(8,128)(2,1)}, u32[]{:S(2)}, u32[]{:S(2)}) collective-permute-start(bf16[256,1536]{1,0:T(8,128)(2,1)} %get-tuple-element.202), channel_id=1, source_target_pairs={{0,16},{16,0},{1,17},{17,1},{2,18},{18,2},{3,19},{19,3},{4,20},{20... | collective-permute-start | bytes 2359304 | tf_op jit(solution)/shard_map/ppermute | solution.py:733
  274.6 22.8 %collective-permute-start.10 = (bf16[8,144,1536]{2,1,0:T(8,128)(2,1)}, bf16[8,144,1536]{2,1,0:T(8,128)(2,1)}, u32[]{:S(2)}, u32[]{:S(2)}) collective-permute-start(bf16[8,144,1536]{2,1,0:T(8,128)(2,1)} %grad_away.6), channel_id=1, source_target_pairs={{0,1},{1,0},{2,3},{3,2},{4,5},{5,4},{6,7},{7,6},{8,9},{9,8},{10,11... | collective-permute-start | bytes 10616840 | tf_op jit(solution)/shard_map/ppermute | solution.py:765
  274.6 11.4 %copy-start.60 = (f32[1536]{0:T(1024)S(1)}, f32[1536]{0:T(1024)}, u32[]{:S(2)}) copy-start(f32[1536]{0:T(1024)} %copy-done.59) | copy-start | bytes 18436
  274.6 11.4 %copy-start.1 = (f32[256,1536]{1,0:T(8,128)S(1)}, f32[256,1536]{1,0:T(8,128)}, u32[]{:S(2)}) copy-start(f32[256,1536]{1,0:T(8,128)} %copy-done) | copy-start | bytes 4718596
  279.1 12.0 %collective-permute-start.6 = (bf16[8,96,2304]{2,1,0:T(8,128)(2,1)}, bf16[8,96,2304]{2,1,0:T(8,128)(2,1)S(1)}, u32[]{:S(2)}, u32[]{:S(2)}) collective-permute-start(bf16[8,96,2304]{2,1,0:T(8,128)(2,1)} %grad_away.7), channel_id=1, source_target_pairs={{0,1},{1,0},{2,3},{3,2},{4,5},{5,4},{6,7},{7,6},{8,9},{9,8},{10,11... | collective-permute-start | bytes 10616840 | tf_op jit(solution)/shard_map/ppermute | solution.py:765
  289.6 19.6 %collective-permute-start.9 = (bf16[256,1536]{1,0:T(8,128)(2,1)}, bf16[256,1536]{1,0:T(8,128)(2,1)}, u32[]{:S(2)}, u32[]{:S(2)}) collective-permute-start(bf16[256,1536]{1,0:T(8,128)(2,1)} %get-tuple-element.219.own_ref), channel_id=1, source_target_pairs={{0,16},{16,0},{1,17},{17,1},{2,18},{18,2},{3,19},{19,3},{4,20},{20... | collective-permute-start | bytes 2359304 | tf_op jit(solution)/shard_map/ppermute | solution.py:733
  291.1 6.2 %copy-start.11 = (bf16[2304,512]{1,0:T(8,128)(2,1)S(1)}, bf16[2304,512]{1,0:T(8,128)(2,1)}, u32[]{:S(2)}) copy-start(bf16[2304,512]{1,0:T(8,128)(2,1)} %get-tuple-element.200) | copy-start | bytes 7077892
  295.9 40.0 %collective-permute-start.8 = (bf16[2,2,96,2304]{3,2,1,0:T(8,128)(2,1)}, bf16[2,2,96,2304]{3,2,1,0:T(8,128)(2,1)}, u32[]{:S(2)}, u32[]{:S(2)}) collective-permute-start(bf16[2,2,96,2304]{3,2,1,0:T(8,128)(2,1)} %get-tuple-element.212), channel_id=1, source_target_pairs={{0,4},{1,5},{2,6},{3,7},{4,0},{5,1},{6,2},{7,3},{8,12},{9,13},{10,... | collective-permute-start | bytes 5308424 | tf_op jit(solution)/shard_map/ppermute | solution.py:765
  297.3 7.5 %copy-start.8 = (bf16[512,2304]{1,0:T(8,128)(2,1)S(1)}, bf16[512,2304]{1,0:T(8,128)(2,1)}, u32[]{:S(2)}) copy-start(bf16[512,2304]{1,0:T(8,128)(2,1)} %get-tuple-element.213) | copy-start | bytes 7077892
  303.5 41.9 %collective-permute-start.14 = (bf16[4,1,144,1536]{3,2,1,0:T(8,128)(2,1)}, bf16[4,1,144,1536]{3,2,1,0:T(8,128)(2,1)}, u32[]{:S(2)}, u32[]{:S(2)}) collective-permute-start(bf16[4,1,144,1536]{3,2,1,0:T(8,128)(2,1)} %get-tuple-element.217), channel_id=1, source_target_pairs={{0,2},{1,3},{2,0},{3,1},{4,6},{5,7},{6,4},{7,5},{8,10},{9,11},{10,... | collective-permute-start | bytes 5308424 | tf_op jit(solution)/shard_map/ppermute | solution.py:765
  309.2 39.8 %collective-permute-start.13 = (bf16[8,96,2304]{2,1,0:T(8,128)(2,1)}, bf16[8,96,2304]{2,1,0:T(8,128)(2,1)}, u32[]{:S(2)}, u32[]{:S(2)}) collective-permute-start(bf16[8,96,2304]{2,1,0:T(8,128)(2,1)} %grad_away.8), channel_id=1, source_target_pairs={{0,1},{1,0},{2,3},{3,2},{4,5},{5,4},{6,7},{7,6},{8,9},{9,8},{10,11... | collective-permute-start | bytes 10616840 | tf_op jit(solution)/shard_map/ppermute | solution.py:765
  309.2 19.3 %copy-start.16 = (bf16[2048,512]{1,0:T(8,128)(2,1)S(1)}, bf16[2048,512]{1,0:T(8,128)(2,1)}, u32[]{:S(2)}) copy-start(bf16[2048,512]{1,0:T(8,128)(2,1)} %copy-done.15) | copy-start | bytes 6291460
  327.4 43.3 %collective-permute-start.16 = (bf16[512,1024]{1,0:T(8,128)(2,1)}, bf16[512,1024]{1,0:T(8,128)(2,1)}, u32[]{:S(2)}, u32[]{:S(2)}) collective-permute-start(bf16[512,1024]{1,0:T(8,128)(2,1)} %get-tuple-element.230), channel_id=1, source_target_pairs={{0,16},{16,0},{1,17},{17,1},{2,18},{18,2},{3,19},{19,3},{4,20},{20... | collective-permute-start | bytes 3145736 | tf_op jit(solution)/shard_map/ppermute | solution.py:733
  333.1 24.4 %collective-permute-start.12 = (bf16[8,128,2048]{2,1,0:T(8,128)(2,1)}, bf16[8,128,2048]{2,1,0:T(8,128)(2,1)}, u32[]{:S(2)}, u32[]{:S(2)}) collective-permute-start(bf16[8,128,2048]{2,1,0:T(8,128)(2,1)} %grad_away.9), channel_id=1, source_target_pairs={{0,1},{1,0},{2,3},{3,2},{4,5},{5,4},{6,7},{7,6},{8,9},{9,8},{10,11... | collective-permute-start | bytes 12582920 | tf_op jit(solution)/shard_map/ppermute | solution.py:765
  339.1 26.0 %collective-permute-start.11 = (bf16[2,1,96,2304]{3,2,0,1:T(8,128)(2,1)}, bf16[2,1,96,2304]{3,2,0,1:T(8,128)(2,1)}, u32[]{:S(2)}, u32[]{:S(2)}) collective-permute-start(bf16[2,1,96,2304]{3,2,0,1:T(8,128)(2,1)} %bitcast.189), channel_id=1, source_target_pairs={{0,2},{1,3},{2,0},{3,1},{4,6},{5,7},{6,4},{7,5},{8,10},{9,11},{10,... | collective-permute-start | bytes 2654216 | tf_op jit(solution)/shard_map/ppermute | solution.py:765
  349.0 31.3 %collective-permute-start.17 = (bf16[2,1,144,1536]{3,2,0,1:T(8,128)(2,1)}, bf16[2,1,144,1536]{3,2,0,1:T(8,128)(2,1)}, u32[]{:S(2)}, u32[]{:S(2)}) collective-permute-start(bf16[2,1,144,1536]{3,2,0,1:T(8,128)(2,1)} %bitcast.188), channel_id=1, source_target_pairs={{0,4},{1,5},{2,6},{3,7},{4,0},{5,1},{6,2},{7,3},{8,12},{9,13},{10,... | collective-permute-start | bytes 2654216 | tf_op jit(solution)/shard_map/ppermute | solution.py:765
  356.3 59.0 %collective-permute-start.23 = (bf16[4,1,96,2304]{3,2,1,0:T(8,128)(2,1)}, bf16[4,1,96,2304]{3,2,1,0:T(8,128)(2,1)}, u32[]{:S(2)}, u32[]{:S(2)}) collective-permute-start(bf16[4,1,96,2304]{3,2,1,0:T(8,128)(2,1)} %get-tuple-element.243), channel_id=1, source_target_pairs={{0,2},{1,3},{2,0},{3,1},{4,6},{5,7},{6,4},{7,5},{8,10},{9,11},{10,... | collective-permute-start | bytes 5308424 | tf_op jit(solution)/shard_map/ppermute | solution.py:765
  368.0 12.3 %copy-start.27 = (bf16[1,1,96,2304]{3,2,1,0:T(8,128)(2,1)}, bf16[1,1,96,2304]{3,2,1,0:T(8,128)(2,1)S(1)}, u32[]{:S(2)}) copy-start(bf16[1,1,96,2304]{3,2,1,0:T(8,128)(2,1)S(1)} %get-tuple-element.269) | copy-start | bytes 1327108
  368.0 21.9 %collective-permute-start.15 = (bf16[1,1,96,2304]{3,2,1,0:T(8,128)(2,1)}, bf16[1,1,96,2304]{3,2,1,0:T(8,128)(2,1)}, u32[]{:S(2)}, u32[]{:S(2)}) collective-permute-start(bf16[1,1,96,2304]{3,2,1,0:T(8,128)(2,1)} %get-tuple-element.251), channel_id=1, source_target_pairs={{0,8},{1,9},{2,10},{3,11},{4,12},{5,13},{6,14},{7,15},{8,0},{9,1},... | collective-permute-start | bytes 1327112 | tf_op jit(solution)/shard_map/ppermute | solution.py:765
  384.2 7.5 %copy-start.28 = (bf16[1,1,96,2304]{3,2,1,0:T(8,128)(2,1)S(1)}, bf16[1,1,96,2304]{3,2,1,0:T(8,128)(2,1)}, u32[]{:S(2)}) copy-start(bf16[1,1,96,2304]{3,2,1,0:T(8,128)(2,1)} %copy-done.27) | copy-start | bytes 1327108
  388.1 15.5 %collective-permute-start.19 = (bf16[8,96,2048]{2,1,0:T(8,128)(2,1)}, bf16[8,96,2048]{2,1,0:T(8,128)(2,1)}, u32[]{:S(2)}, u32[]{:S(2)}) collective-permute-start(bf16[8,96,2048]{2,1,0:T(8,128)(2,1)} %grad_away.10), channel_id=1, source_target_pairs={{0,1},{1,0},{2,3},{3,2},{4,5},{5,4},{6,7},{7,6},{8,9},{9,8},{10,11... | collective-permute-start | bytes 9437192 | tf_op jit(solution)/shard_map/ppermute | solution.py:765
  388.2 58.9 %collective-permute-start.22 = (bf16[2,2,128,2048]{3,2,1,0:T(8,128)(2,1)}, bf16[2,2,128,2048]{3,2,1,0:T(8,128)(2,1)}, u32[]{:S(2)}, u32[]{:S(2)}) collective-permute-start(bf16[2,2,128,2048]{3,2,1,0:T(8,128)(2,1)} %get-tuple-element.247), channel_id=1, source_target_pairs={{0,4},{1,5},{2,6},{3,7},{4,0},{5,1},{6,2},{7,3},{8,12},{9,13},{10,... | collective-permute-start | bytes 6291464 | tf_op jit(solution)/shard_map/ppermute | solution.py:765
  388.7 22.0 %collective-permute-start.24 = (bf16[256,1536]{1,0:T(8,128)(2,1)}, bf16[256,1536]{1,0:T(8,128)(2,1)}, u32[]{:S(2)}, u32[]{:S(2)}) collective-permute-start(bf16[256,1536]{1,0:T(8,128)(2,1)} %get-tuple-element.261), channel_id=1, source_target_pairs={{0,16},{16,0},{1,17},{17,1},{2,18},{18,2},{3,19},{19,3},{4,20},{20... | collective-permute-start | bytes 2359304 | tf_op jit(solution)/shard_map/ppermute | solution.py:733
  389.9 85.9 %collective-permute-start.26 = (bf16[1,1,144,1536]{3,2,1,0:T(8,128)(2,1)}, bf16[1,1,144,1536]{3,2,1,0:T(8,128)(2,1)}, u32[]{:S(2)}, u32[]{:S(2)}) collective-permute-start(bf16[1,1,144,1536]{3,2,1,0:T(8,128)(2,1)} %get-tuple-element.265), channel_id=1, source_target_pairs={{0,8},{1,9},{2,10},{3,11},{4,12},{5,13},{6,14},{7,15},{8,0},{9,1},... | collective-permute-start | bytes 1327112 | tf_op jit(solution)/shard_map/ppermute | solution.py:765
  393.8 11.3 %copy-start.23 = (bf16[1536,512]{1,0:T(8,128)(2,1)S(1)}, bf16[1536,512]{1,0:T(8,128)(2,1)}, u32[]{:S(2)}) copy-start(bf16[1536,512]{1,0:T(8,128)(2,1)} %copy-done.21) | copy-start | bytes 4718596
  393.8 11.3 %copy-start.35 = (bf16[2,512,1024]{2,1,0:T(8,128)(2,1)S(1)}, bf16[2,512,1024]{2,1,0:T(8,128)(2,1)}, u32[]{:S(2)}) copy-start(bf16[2,512,1024]{2,1,0:T(8,128)(2,1)} %copy-done.34) | copy-start | bytes 6291460
  403.6 132.1 %collective-permute-start.18 = (bf16[256,1536]{1,0:T(8,128)(2,1)}, bf16[256,1536]{1,0:T(8,128)(2,1)}, u32[]{:S(2)}, u32[]{:S(2)}) collective-permute-start(bf16[256,1536]{1,0:T(8,128)(2,1)} %get-tuple-element.275), channel_id=1, source_target_pairs={{0,16},{16,0},{1,17},{17,1},{2,18},{18,2},{3,19},{19,3},{4,20},{20... | collective-permute-start | bytes 2359304 | tf_op jit(solution)/shard_map/ppermute | solution.py:733
  410.6 39.9 %collective-permute-start.21 = (bf16[96,2304]{1,0:T(8,128)(2,1)}, bf16[96,2304]{1,0:T(8,128)(2,1)}, u32[]{:S(2)}, u32[]{:S(2)}) collective-permute-start(bf16[96,2304]{1,0:T(8,128)(2,1)} %get-tuple-element.272), channel_id=1, source_target_pairs={{0,16},{16,0},{1,17},{17,1},{2,18},{18,2},{3,19},{19,3},{4,20},{20... | collective-permute-start | bytes 1327112 | tf_op jit(solution)/shard_map/ppermute | solution.py:733
  415.3 39.0 %collective-permute-start.20 = (bf16[4,1,96,2048]{3,2,1,0:T(8,128)(2,1)}, bf16[4,1,96,2048]{3,2,1,0:T(8,128)(2,1)}, u32[]{:S(2)}, u32[]{:S(2)}) collective-permute-start(bf16[4,1,96,2048]{3,2,1,0:T(8,128)(2,1)} %get-tuple-element.279), channel_id=1, source_target_pairs={{0,2},{1,3},{2,0},{3,1},{4,6},{5,7},{6,4},{7,5},{8,10},{9,11},{10,... | collective-permute-start | bytes 4718600 | tf_op jit(solution)/shard_map/ppermute | solution.py:765
  416.2 30.8 %copy-start.18 = (bf16[2,2,128,2048]{3,2,1,0:T(8,128)(2,1)S(1)}, bf16[2,2,128,2048]{3,2,1,0:T(8,128)(2,1)}, u32[]{:S(2)}) copy-start(bf16[2,2,128,2048]{3,2,1,0:T(8,128)(2,1)} %copy-done.17) | copy-start | bytes 6291460
  450.5 22.0 %collective-permute-start.27 = (bf16[2,1,96,2304]{3,2,0,1:T(8,128)(2,1)}, bf16[2,1,96,2304]{3,2,0,1:T(8,128)(2,1)}, u32[]{:S(2)}, u32[]{:S(2)}) collective-permute-start(bf16[2,1,96,2304]{3,2,0,1:T(8,128)(2,1)} %bitcast.61), channel_id=1, source_target_pairs={{0,4},{1,5},{2,6},{3,7},{4,0},{5,1},{6,2},{7,3},{8,12},{9,13},{10,... | collective-permute-start | bytes 2654216 | tf_op jit(solution)/shard_map/ppermute | solution.py:765
  450.5 33.6 %collective-permute-start.31 = (bf16[2,1,128,2048]{3,2,0,1:T(8,128)(2,1)}, bf16[2,1,128,2048]{3,2,0,1:T(8,128)(2,1)}, u32[]{:S(2)}, u32[]{:S(2)}) collective-permute-start(bf16[2,1,128,2048]{3,2,0,1:T(8,128)(2,1)} %bitcast.187), channel_id=1, source_target_pairs={{0,2},{1,3},{2,0},{3,1},{4,6},{5,7},{6,4},{7,5},{8,10},{9,11},{10,... | collective-permute-start | bytes 3145736 | tf_op jit(solution)/shard_map/ppermute | solution.py:765
  460.2 18.0 %collective-permute-start.25 = (bf16[8,128,768]{2,1,0:T(8,128)(2,1)}, bf16[8,128,768]{2,1,0:T(8,128)(2,1)}, u32[]{:S(2)}, u32[]{:S(2)}) collective-permute-start(bf16[8,128,768]{2,1,0:T(8,128)(2,1)} %grad_away.11), channel_id=1, source_target_pairs={{0,1},{1,0},{2,3},{3,2},{4,5},{5,4},{6,7},{7,6},{8,9},{9,8},{10,11... | collective-permute-start | bytes 4718600 | tf_op jit(solution)/shard_map/ppermute | solution.py:765
  475.1 22.0 %collective-permute-start.30 = (bf16[1,1,96,2304]{3,2,1,0:T(8,128)(2,1)}, bf16[1,1,96,2304]{3,2,1,0:T(8,128)(2,1)}, u32[]{:S(2)}, u32[]{:S(2)}) collective-permute-start(bf16[1,1,96,2304]{3,2,1,0:T(8,128)(2,1)} %get-tuple-element.301), channel_id=1, source_target_pairs={{0,8},{1,9},{2,10},{3,11},{4,12},{5,13},{6,14},{7,15},{8,0},{9,1},... | collective-permute-start | bytes 1327112 | tf_op jit(solution)/shard_map/ppermute | solution.py:765
  477.7 21.3 %collective-permute-start.29 = (bf16[144,1536]{1,0:T(8,128)(2,1)}, bf16[144,1536]{1,0:T(8,128)(2,1)}, u32[]{:S(2)}, u32[]{:S(2)}) collective-permute-start(bf16[144,1536]{1,0:T(8,128)(2,1)} %get-tuple-element.305), channel_id=1, source_target_pairs={{0,16},{16,0},{1,17},{17,1},{2,18},{18,2},{3,19},{19,3},{4,20},{20... | collective-permute-start | bytes 1327112 | tf_op jit(solution)/shard_map/ppermute | solution.py:733
  478.3 34.3 %collective-permute-start.35 = (bf16[2,1,96,2048]{3,2,0,1:T(8,128)(2,1)}, bf16[2,1,96,2048]{3,2,0,1:T(8,128)(2,1)}, u32[]{:S(2)}, u32[]{:S(2)}) collective-permute-start(bf16[2,1,96,2048]{3,2,0,1:T(8,128)(2,1)} %bitcast.74), channel_id=1, source_target_pairs={{0,4},{1,5},{2,6},{3,7},{4,0},{5,1},{6,2},{7,3},{8,12},{9,13},{10,... | collective-permute-start | bytes 2359304 | tf_op jit(solution)/shard_map/ppermute | solution.py:765
  484.1 17.7 %collective-permute-start.28 = (bf16[4,1,128,768]{3,2,1,0:T(8,128)(2,1)}, bf16[4,1,128,768]{3,2,1,0:T(8,128)(2,1)}, u32[]{:S(2)}, u32[]{:S(2)}) collective-permute-start(bf16[4,1,128,768]{3,2,1,0:T(8,128)(2,1)} %get-tuple-element.309), channel_id=1, source_target_pairs={{0,2},{1,3},{2,0},{3,1},{4,6},{5,7},{6,4},{7,5},{8,10},{9,11},{10,... | collective-permute-start | bytes 2359304 | tf_op jit(solution)/shard_map/ppermute | solution.py:765
  497.1 32.4 %collective-permute-start.33 = (bf16[1,1,128,2048]{3,2,1,0:T(8,128)(2,1)}, bf16[1,1,128,2048]{3,2,1,0:T(8,128)(2,1)}, u32[]{:S(2)}, u32[]{:S(2)}) collective-permute-start(bf16[1,1,128,2048]{3,2,1,0:T(8,128)(2,1)} %get-tuple-element.313), channel_id=1, source_target_pairs={{0,8},{1,9},{2,10},{3,11},{4,12},{5,13},{6,14},{7,15},{8,0},{9,1},... | collective-permute-start | bytes 1572872 | tf_op jit(solution)/shard_map/ppermute | solution.py:765
  499.0 16.1 %collective-permute-start.34 = (bf16[96,2304]{1,0:T(8,128)(2,1)}, bf16[96,2304]{1,0:T(8,128)(2,1)}, u32[]{:S(2)}, u32[]{:S(2)}) collective-permute-start(bf16[96,2304]{1,0:T(8,128)(2,1)} %get-tuple-element.317), channel_id=1, source_target_pairs={{0,16},{16,0},{1,17},{17,1},{2,18},{18,2},{3,19},{19,3},{4,20},{20... | collective-permute-start | bytes 1327112 | tf_op jit(solution)/shard_map/ppermute | solution.py:733
  504.4 29.0 %collective-permute-start.32 = (bf16[2,1,128,768]{3,2,0,1:T(8,128)(2,1)}, bf16[2,1,128,768]{3,2,0,1:T(8,128)(2,1)}, u32[]{:S(2)}, u32[]{:S(2)}) collective-permute-start(bf16[2,1,128,768]{3,2,0,1:T(8,128)(2,1)} %bitcast.190), channel_id=1, source_target_pairs={{0,4},{1,5},{2,6},{3,7},{4,0},{5,1},{6,2},{7,3},{8,12},{9,13},{10,... | collective-permute-start | bytes 1179656 | tf_op jit(solution)/shard_map/ppermute | solution.py:765
  515.1 28.7 %collective-permute-start.36 = (bf16[1,1,96,2048]{3,2,1,0:T(8,128)(2,1)}, bf16[1,1,96,2048]{3,2,1,0:T(8,128)(2,1)}, u32[]{:S(2)}, u32[]{:S(2)}) collective-permute-start(bf16[1,1,96,2048]{3,2,1,0:T(8,128)(2,1)} %get-tuple-element.327), channel_id=1, source_target_pairs={{0,8},{1,9},{2,10},{3,11},{4,12},{5,13},{6,14},{7,15},{8,0},{9,1},... | collective-permute-start | bytes 1179656 | tf_op jit(solution)/shard_map/ppermute | solution.py:765
  531.7 16.2 %collective-permute-start.39 = (bf16[128,2048]{1,0:T(8,128)(2,1)}, bf16[128,2048]{1,0:T(8,128)(2,1)}, u32[]{:S(2)}, u32[]{:S(2)}) collective-permute-start(bf16[128,2048]{1,0:T(8,128)(2,1)} %get-tuple-element.333), channel_id=1, source_target_pairs={{0,16},{16,0},{1,17},{17,1},{2,18},{18,2},{3,19},{19,3},{4,20},{20... | collective-permute-start | bytes 1572872 | tf_op jit(solution)/shard_map/ppermute | solution.py:733
  535.6 14.7 %collective-permute-start.38 = (bf16[1,1,128,768]{3,2,1,0:T(8,128)(2,1)}, bf16[1,1,128,768]{3,2,1,0:T(8,128)(2,1)}, u32[]{:S(2)}, u32[]{:S(2)}) collective-permute-start(bf16[1,1,128,768]{3,2,1,0:T(8,128)(2,1)} %get-tuple-element.337), channel_id=1, source_target_pairs={{0,8},{1,9},{2,10},{3,11},{4,12},{5,13},{6,14},{7,15},{8,0},{9,1},... | collective-permute-start | bytes 589832 | tf_op jit(solution)/shard_map/ppermute | solution.py:765
  545.6 11.4 %collective-permute-start.37 = (bf16[96,2048]{1,0:T(8,128)(2,1)}, bf16[96,2048]{1,0:T(8,128)(2,1)}, u32[]{:S(2)}, u32[]{:S(2)}) collective-permute-start(bf16[96,2048]{1,0:T(8,128)(2,1)} %get-tuple-element.343), channel_id=1, source_target_pairs={{0,16},{16,0},{1,17},{17,1},{2,18},{18,2},{3,19},{19,3},{4,20},{20... | collective-permute-start | bytes 1179656 | tf_op jit(solution)/shard_map/ppermute | solution.py:733
  552.0 9.6 %collective-permute-start.40 = (bf16[128,768]{1,0:T(8,128)(2,1)}, bf16[128,768]{1,0:T(8,128)(2,1)S(1)}, u32[]{:S(2)}, u32[]{:S(2)}) collective-permute-start(bf16[128,768]{1,0:T(8,128)(2,1)} %get-tuple-element.352), channel_id=1, source_target_pairs={{0,16},{16,0},{1,17},{17,1},{2,18},{18,2},{3,19},{19,3},{4,20},{20... | collective-permute-start | bytes 589832 | tf_op jit(solution)/shard_map/ppermute | solution.py:733
  (50 other events, 193.4 us)
Sparse Core Ops, SparseCore 0:
  10.2 111.9 all-gather.4
  124.3 110.2 all-gather.6
  391.8 139.3 all-reduce.5

commit v8 on v7

--- a/solution.py
+++ b/solution.py
@@ -521,7 +521,7 @@
         ],
         out_specs=[wide, pl.BlockSpec((tile, tokens), lambda j: (j, 0)), wide, wide, half, half],
         out_shape=[
-            low, jax.ShapeDtypeStruct((n, tokens), BF16), low, low,
+            low, sent((n, tokens)), low, low,
             jax.ShapeDtypeStruct((tokens // 2, depth), F32), sent((tokens // 2, depth)),
         ],
         scratch_shapes=[pltpu.VMEM((tokens, depth), F32), pltpu.VMEM((tile, depth), BF16)],

time: 581 us -> 581 us (level)
  no operation moved by 1% of the time
where the time goes in v8:
time: 581 us; the launch traced here: 569 us
  Pallas kernels  216 us (37%)
  waiting for transfers between devices  213 us (37%)
  local copies, waits for them, and re-layouts  41 us (7%)
  starting transfers between devices  35.9 us (6%)
  blocking collectives  22.7 us (4%)
  between operations  15.1 us (3%)
  other arithmetic  13.7 us (2%)
  matrix products  11.7 us (2%)
    ppermute x24, waiting for transfers between devices, cross(): return lax.ppermute(v, 'shard', [(i, i ^ 1 << bit) for i in range(shards)])  79.4 us
    all_gather x1, waiting for transfers between devices, body(): lax.all_gather(pack(here_side, [branch_proj, lruin_proj, recur_proj, admi...  66 us
    ppermute x17, waiting for transfers between devices, swap(): return lax.ppermute(v, 'rep', [(i, i ^ 1) for i in range(groups)])  56.8 us
    pallas_call x12, Pallas kernels, fold(): pl.pallas_call(functools.partial(fold_kernel, bit), grid_spec=pltpu.Prefe...  36.2 us
    pallas_call x6, Pallas kernels, grad_home(): pl.pallas_call(functools.partial(home_kernel, bit), grid_spec=pltpu.Prefe...  32.9 us
    pallas_call x1, Pallas kernels, ffn_pass(): pl.pallas_call(ffn_kernel, grid=(tiles,), in_specs=[fixed, fixed, pl.Bloc...  31.2 us
    pallas_call x6, Pallas kernels, grad_away(): pl.pallas_call(away_kernel, grid_spec=pltpu.PrefetchScalarGridSpec(num_sc...  25.4 us
    all_gather x1, blocking collectives, body(): lax.all_gather(vectors, 'shard', axis=0).reshape(shards, -1)[:, :count]  22.7 us
  transfers between devices with their start and end apart: 44, of which 17 were waited for; matrix products, arithmetic and copies ran while one was open for 9% of the time, Pallas kernels for 32%

profile of v8, /device:TPU:0, one launch (start us, length us, event | category | flops | bytes accessed | tf_op | source)
XLA Modules:
  0.0 569.4 jit_solution(15633393351262740023)
XLA Ops:
  7.3 2.6 pack.1
  10.0 3.0 collective-permute-start
  24.7 22.7 %all_gather.15 = bf16[16,10,128]{2,1,0:T(8,128)(2,1)S(1)} all-gather(bf16[1,10,128]{2,1,0:T(8,128)(2,1)S(1)} %pad_bitcast_fusion), channel_id=1, replica_groups=mesh['rep'=2,'shard'=16] {'shard'}, dimensions={0}, use_global_device_ids=true | all-gather | bytes 43520 | tf_op jit(solution)/shard_map/all_gather | solution.py:820
  54.1 2.1 constant_dynamic-update-slice_fusion.cot_ref
  56.2 66.0 %all-gather.5.cloned.1.call-done = bf16[20480,512]{1,0:T(8,128)(2,1)} async-done(((bf16[1280,512]{1,0:T(8,128)(2,1)}), bf16[20480,512]{1,0:T(8,128)(2,1)}) %all-gather.5.cloned.1.call-update) | async-done | bytes 20971536 | tf_op jit(solution)/shard_map/all_gather | solution.py:843
  122.1 3.2 fusion.45
  125.4 3.4 fusion.8.pre_ref.lru_ref
  134.3 8.3 %fusion.44 = (bf16[16,128,512]{2,1,0:T(8,128)(2,1)S(1)}, bf16[16,128,512]{2,1,0:T(8,128)(2,1)}, bf16[16,128,512]{2,1,0:T(8,128)(2,1)}, bf16[16,128,512]{2,1,0:T(...) fusion(bf16[16,1280,512]{2,1,0:T(8,128)(2,1)} %bitcast.145), kind=kLoop, calls=%fused_computation.96 | loop fusion | bytes 29360128 | tf_op jit(solution)/shard_map/slice | solution.py:839
  142.6 14.6 %collective-permute-done.2 = bf16[512,1024]{1,0:T(8,128)(2,1)S(1)} collective-permute-done((bf16[512,1024]{1,0:T(8,128)(2,1)S(1)}, bf16[512,1024]{1,0:T(8,128)(2,1)S(1)}, u32[]{:S(2)}, u32[]{:S(2)}) %collective-permute-start.2) | collective-permute-done | bytes 1048608 | tf_op jit(solution)/shard_map/ppermute | solution.py:733
  158.7 6.4 %fusion.gates_r_ref.gates_i_ref = f32[512,2048]{1,0:T(8,128)} fusion(bf16[2048,512]{1,0:T(8,128)(2,1)S(1)} %bitcast.164, bf16[2048,512]{1,0:T(8,128)(2,1)S(1)} %bitcast.165, bf16[2048,512]{1,0:T(8,128)(2,1)S(1)} %bitcast.166, bf16[2048,512]{1,0:T(8,128)(2,1)S(1)} %bitcast.163, bf16[512,1024]{1,0:T(8,128)(2,1)S(1)} %get-tuple-element.371, ...), kind=kOutput, calls=%fused_computation | convolution fusion | flops 4332716032 | bytes 14680064 | tf_op jit(solution)/shard_map/dot_general | solution.py:40
  165.1 12.3 %recurrence_forward.1 = (bf16[512,1024]{1,0:T(8,128)(2,1)}, f32[512,1024]{1,0:T(8,128)}, f32[512,1024]{1,0:T(8,128)}, f32[512,1024]{1,0:T(8,128)}, f32[512,1024]...) custom-call(f32[512,2048]{1,0:T(8,128)} %copy-done.40, ...), custom_call_target="tpu_custom_call" | custom-call | flops 31457280 | bytes 10485760 | tf_op jit(solution)/shard_map/recurrence_forward/pallas_call | solution.py:435
  181.8 10.2 %collective-permute-done.3 = bf16[256,1024]{1,0:T(8,128)(2,1)S(1)} collective-permute-done((bf16[256,1024]{1,0:T(8,128)(2,1)S(1)}, bf16[256,1024]{1,0:T(8,128)(2,1)S(1)}, u32[]{:S(2)}, u32[]{:S(2)}) %collective-permute-start.3) | collective-permute-done | bytes 524320 | tf_op jit(solution)/shard_map/ppermute | solution.py:733
  196.4 10.6 %collective-permute-done.5 = bf16[256,1024]{1,0:T(8,128)(2,1)S(1)} collective-permute-done((bf16[256,1024]{1,0:T(8,128)(2,1)S(1)}, bf16[256,1024]{1,0:T(8,128)(2,1)S(1)}, u32[]{:S(2)}, u32[]{:S(2)}) %collective-permute-start.5) | collective-permute-done | bytes 524320 | tf_op jit(solution)/shard_map/ppermute | solution.py:733
  210.0 11.5 %collective-permute-done.4 = bf16[256,1536]{1,0:T(8,128)(2,1)S(1)} collective-permute-done((bf16[256,1536]{1,0:T(8,128)(2,1)S(1)}, bf16[256,1536]{1,0:T(8,128)(2,1)S(1)}, u32[]{:S(2)}, u32[]{:S(2)}) %collective-permute-start.4) | collective-permute-done | bytes 786464 | tf_op jit(solution)/shard_map/ppermute | solution.py:733
  223.8 10.8 %all-gather.7.cloned.1.call-done = bf16[13824,768]{1,0:T(8,128)(2,1)} async-done(((bf16[864,768]{1,0:T(8,128)(2,1)}), bf16[13824,768]{1,0:T(8,128)(2,1)}) %all-gather.7.cloned.1.call-update) | async-done | bytes 21233680 | tf_op jit(solution)/shard_map/all_gather | solution.py:835
  234.6 31.2 %ffn_pass.1 = (bf16[512,2304]{1,0:T(8,128)(2,1)}, bf16[2304,512]{1,0:T(8,128)(2,1)}, bf16[512,2304]{1,0:T(8,128)(2,1)}, bf16[512,2304]{1,0:T(8,128)(2,1)}, f32[2...) custom-call(bf16[512,1536]{1,0:T(8,128)(2,1)S(1)} %pad_maximum_fusion.2.x_ref, ...), custom_call_target="tpu_custom_call" | custom-call | flops 99999997952 | bytes 1024 | tf_op jit(solution)/shard_map/ffn_pass/pallas_call | solution.py:513
  269.1 5.5 grad_away.6
  274.6 4.5 grad_away.7
  279.6 6.4 %collective-permute-done.7.far_ref = bf16[256,1536]{1,0:T(8,128)(2,1)} collective-permute-done((bf16[256,1536]{1,0:T(8,128)(2,1)}, bf16[256,1536]{1,0:T(8,128)(2,1)}, u32[]{:S(2)}, u32[]{:S(2)}) %collective-permute-start.7) | collective-permute-done | bytes 786464 | tf_op jit(solution)/shard_map/ppermute | solution.py:733
  286.0 3.7 norm_back.2
  291.1 4.7 grad_home.6
  297.3 6.2 %grad_home.7 = (bf16[4,1,144,1536]{3,2,1,0:T(8,128)(2,1)S(1)}, bf16[4,1,144,1536]{3,2,1,0:T(8,128)(2,1)}) custom-call(s32[5]{0:T(128)S(1)} %stack.24.at_ref, bf16[8,2,144,512]{3,2,1,0:T(8,128)(2,1)S(1)} %bitcast.113, bf16[1,512,1536]{2,1,0:T(8,128)(2,1)} %bitcast.36.right_ref, bf16[8,144,1536]{2,1,0:T(8,128)(2,1)} %collective-permute-done.10.got_ref), custom_call_target="tpu_custom_call" | custom-call | flops 99999997952 | bytes 1024 | tf_op jit(solution)/shard_map/grad_home/pallas_call | solution.py:638
  304.8 4.4 grad_away.8
  309.3 18.2 %chain_back.1 = (bf16[512,1024]{1,0:T(8,128)(2,1)S(1)}, bf16[2,512,1024]{2,1,0:T(8,128)(2,1)S(1)}, f32[512,1024]{1,0:T(8,128)S(1)}, f32[48,1024]{1,0:T(8,128)S(1...) custom-call(s32[1]{0:T(128)} %bitcast.2.side_ref, bf16[256,1536]{1,0:T(8,128)(2,1)S(1)} %copy-done.7, ...), custom_call_target="tpu_custom_call" | custom-call | flops 99999997952 | bytes 1024 | tf_op jit(solution)/shard_map/chain_back/pallas_call | solution.py:175
  328.6 4.6 grad_away.9
  335.9 3.3 fold.12
  340.3 5.1 collective-permute-done.14
  345.4 3.6 fold.13
  349.0 6.1 %grad_home.8 = (bf16[4,1,96,2304]{3,2,1,0:T(8,128)(2,1)S(1)}, bf16[4,1,96,2304]{3,2,1,0:T(8,128)(2,1)}) custom-call(s32[5]{0:T(128)S(1)} %stack.24.at_ref, bf16[8,2,96,512]{3,2,1,0:T(8,128)(2,1)S(1)} %bitcast.129, bf16[1,512,2304]{2,1,0:T(8,128)(2,1)S(1)} %bitcast.111, bf16[8,96,2304]{2,1,0:T(8,128)(2,1)} %collective-permute-done.13.got_ref), custom_call_target="tpu_custom_call" | custom-call | flops 99999997952 | bytes 1024 | tf_op jit(solution)/shard_map/grad_home/pallas_call | solution.py:638
  357.6 6.3 %grad_home.9 = (bf16[2,2,128,2048]{3,2,1,0:T(8,128)(2,1)S(1)}, bf16[2,2,128,2048]{3,2,1,0:T(8,128)(2,1)}) custom-call(s32[5]{0:T(128)S(1)} %stack.24.at_ref, bf16[8,2,128,512]{3,2,1,0:T(8,128)(2,1)S(1)} %bitcast.119, bf16[2,512,1024]{2,1,0:T(8,128)(2,1)S(1)} %get-tuple-element.244.right_ref, bf16[8,128,2048]{2,1,0:T(8,128)(2,1)} %collective-permute-done.12.got_ref), custom_call_target="tpu_custom_call" | custom-call | flops 99999997952 | bytes 1024 | tf_op jit(solution)/shard_map/grad_home/pallas_call | solution.py:638
  365.1 2.9 fold.14
  368.0 2.7 collective-permute-start.15
  370.7 9.6 %conv_back.1 = (bf16[2,512,1024]{2,1,0:T(8,128)(2,1)S(1)}, f32[8,1024]{1,0:T(8,128)S(1)}, f32[256,1536]{1,0:T(8,128)S(1)}, bf16[256,1536]{1,0:T(8,128)(2,1)}) custom-call(f32[512,1024]{1,0:T(8,128)S(1)} %copy-done.30, f32[512,1024]{1,0:T(8,128)S(1)} %copy-done.32, bf16[512,1024]{1,0:T(8,128)(2,1)} %collective-permute-done.16.far_in_ref, ...), custom_call_target="tpu_custom_call" | custom-call | flops 99999997952 | bytes 1024 | tf_op jit(solution)/shard_map/conv_back/pallas_call | solution.py:248
  380.3 3.8 fold.15
  384.2 3.8 grad_away.10
  391.7 2.1 settle.6
  393.8 9.8 %down_pass.1 = (f32[256,1536]{1,0:T(8,128)S(1)}, bf16[256,1536]{1,0:T(8,128)(2,1)}) custom-call(bf16[512,2304]{1,0:T(8,128)(2,1)S(1)} %copy-done.33, bf16[16,864,768]{2,1,0:T(8,128)(2,1)} %bitcast.185, bf16[16,864,768]{2,1,0:T(8,128)(2,1)} %bitcast.186), custom_call_target="tpu_custom_call" | custom-call | flops 99999997952 | bytes 1024 | tf_op jit(solution)/shard_map/down_pass/pallas_call | solution.py:562
  405.1 5.6 grad_home.10
  411.3 4.1 norm_back.3
  416.2 3.4 fold.16
  419.6 27.4 %collective-permute-done.22 = bf16[2,2,128,2048]{3,2,1,0:T(8,128)(2,1)} collective-permute-done((bf16[2,2,128,2048]{3,2,1,0:T(8,128)(2,1)}, bf16[2,2,128,2048]{3,2,1,0:T(8,128)(2,1)}, u32[]{:S(2)}, u32[]{:S(2)}) %collective-permute-start.22) | collective-permute-done | bytes 2097184 | tf_op jit(solution)/shard_map/ppermute | solution.py:765
  447.0 3.5 fold.17
  451.3 3.1 weave.2
  454.3 3.2 fold.18
  457.6 2.7 grad_away.11
  460.2 12.3 %collective-permute-done.27 = bf16[2,1,96,2304]{3,2,0,1:T(8,128)(2,1)} collective-permute-done((bf16[2,1,96,2304]{3,2,0,1:T(8,128)(2,1)}, bf16[2,1,96,2304]{3,2,0,1:T(8,128)(2,1)}, u32[]{:S(2)}, u32[]{:S(2)}) %collective-permute-start.27) | collective-permute-done | bytes 884768 | tf_op jit(solution)/shard_map/ppermute | solution.py:765
  472.5 2.6 fold.19
  480.0 4.1 grad_home.11
  484.4 2.7 fold.20
  487.1 9.9 %collective-permute-done.30 = bf16[1,1,96,2304]{3,2,1,0:T(8,128)(2,1)} collective-permute-done((bf16[1,1,96,2304]{3,2,1,0:T(8,128)(2,1)}, bf16[1,1,96,2304]{3,2,1,0:T(8,128)(2,1)}, u32[]{:S(2)}, u32[]{:S(2)}) %collective-permute-start.30) | collective-permute-done | bytes 442400 | tf_op jit(solution)/shard_map/ppermute | solution.py:765
  499.4 2.3 join_rows.1
  501.8 2.5 fold.21
  504.4 2.4 collective-permute-start.32
  506.8 5.8 %collective-permute-done.35 = bf16[2,1,96,2048]{3,2,0,1:T(8,128)(2,1)} collective-permute-done((bf16[2,1,96,2048]{3,2,0,1:T(8,128)(2,1)}, bf16[2,1,96,2048]{3,2,0,1:T(8,128)(2,1)}, u32[]{:S(2)}, u32[]{:S(2)}) %collective-permute-start.35) | collective-permute-done | bytes 786464 | tf_op jit(solution)/shard_map/ppermute | solution.py:765
  512.6 2.5 fold.22
  515.1 2.8 weave.3
  518.0 11.6 %collective-permute-done.33 = bf16[1,1,128,2048]{3,2,1,0:T(8,128)(2,1)} collective-permute-done((bf16[1,1,128,2048]{3,2,1,0:T(8,128)(2,1)}, bf16[1,1,128,2048]{3,2,1,0:T(8,128)(2,1)}, u32[]{:S(2)}, u32[]{:S(2)}) %collective-permute-start.33) | collective-permute-done | bytes 524320 | tf_op jit(solution)/shard_map/ppermute | solution.py:765
  529.5 2.1 settle.9
  533.4 2.3 fold.23
  535.7 2.4 add_convert_fusion
  538.1 5.7 %collective-permute-done.36 = bf16[1,1,96,2048]{3,2,1,0:T(8,128)(2,1)} collective-permute-done((bf16[1,1,96,2048]{3,2,1,0:T(8,128)(2,1)}, bf16[1,1,96,2048]{3,2,1,0:T(8,128)(2,1)}, u32[]{:S(2)}, u32[]{:S(2)}) %collective-permute-start.36) | collective-permute-done | bytes 393248 | tf_op jit(solution)/shard_map/ppermute | solution.py:765
  547.9 2.4 join_columns.3
  553.6 3.5 collective-permute-done.37.got_ref
  557.1 2.3 join_columns.4
  (288 shorter events, 83.0 us)
Async XLA Ops:
  7.2 115.0 %all-gather.5.cloned.1.call-start = ((), (), s32[]{:S(2)}) async-start(), calls=%async_computation.1 | async-start | bytes 22282240 | tf_op jit(solution)/shard_map/all_gather | solution.py:843
  9.9 224.7 %all-gather.7.cloned.1.call-start = ((), (), s32[]{:S(2)}) async-start(), calls=%async_computation.2 | async-start | bytes 22560768 | tf_op jit(solution)/shard_map/all_gather | solution.py:835
  10.0 38.7 %collective-permute-start = (bf16[256,1536]{1,0:T(8,128)(2,1)S(1)}, bf16[256,1536]{1,0:T(8,128)(2,1)}, u32[]{:S(2)}, u32[]{:S(2)}) collective-permute-start(bf16[256,1536]{1,0:T(8,128)(2,1)S(1)} %copy-done.3), channel_id=1, source_target_pairs={{0,16},{16,0},{1,17},{17,1},{2,18},{18,2},{3,19},{19,3},{4,20},{20... | collective-permute-start | bytes 2359304 | tf_op jit(solution)/shard_map/ppermute | solution.py:733
  13.0 41.0 %collective-permute-start.1 = (bf16[256,1536]{1,0:T(8,128)(2,1)S(1)}, bf16[256,1536]{1,0:T(8,128)(2,1)}, u32[]{:S(2)}, u32[]{:S(2)}) collective-permute-start(bf16[256,1536]{1,0:T(8,128)(2,1)S(1)} %copy-done.6), channel_id=1, source_target_pairs={{0,16},{16,0},{1,17},{17,1},{2,18},{18,2},{3,19},{19,3},{4,20},{20... | collective-permute-start | bytes 2359304 | tf_op jit(solution)/shard_map/ppermute | solution.py:733
  24.5 521.6 %all-reduce.6.cloned.1.call-start = ((), (), s32[]{:S(2)}) async-start(), calls=%async_computation | async-start | bytes 131072 | tf_op jit(solution)/shard_map/psum | solution.py:960
  131.8 25.5 %copy-start.41 = (bf16[2,256,1024]{2,1,0:T(8,128)(2,1)}, bf16[2,256,1024]{2,1,0:T(8,128)(2,1)S(1)}, u32[]{:S(2)}) copy-start(bf16[2,256,1024]{2,1,0:T(8,128)(2,1)S(1)} %fusion.32) | copy-start | bytes 3145732
  131.8 25.4 %collective-permute-start.2 = (bf16[512,1024]{1,0:T(8,128)(2,1)S(1)}, bf16[512,1024]{1,0:T(8,128)(2,1)S(1)}, u32[]{:S(2)}, u32[]{:S(2)}) collective-permute-start(bf16[512,1024]{1,0:T(8,128)(2,1)S(1)} %bitcast.153), channel_id=1, source_target_pairs={{0,16},{16,0},{1,17},{17,1},{2,18},{18,2},{3,19},{19,3},{4,20},{20... | collective-permute-start | bytes 3145736 | tf_op jit(solution)/shard_map/ppermute | solution.py:733
  133.4 62.1 %copy-start.59 = (f32[1536]{0:T(1024)}, f32[1536]{0:T(1024)S(1)}, u32[]{:S(2)}) copy-start(f32[1536]{0:T(1024)S(1)} %reshape.325) | copy-start | bytes 18436
  165.1 15.0 %copy-start.43 = (bf16[512,1024]{1,0:T(8,128)(2,1)S(1)}, bf16[512,1024]{1,0:T(8,128)(2,1)}, u32[]{:S(2)}) copy-start(bf16[512,1024]{1,0:T(8,128)(2,1)} %copy-done.42) | copy-start | bytes 3145732
  178.5 13.4 %collective-permute-start.3 = (bf16[256,1024]{1,0:T(8,128)(2,1)S(1)}, bf16[256,1024]{1,0:T(8,128)(2,1)S(1)}, u32[]{:S(2)}, u32[]{:S(2)}) collective-permute-start(bf16[256,1024]{1,0:T(8,128)(2,1)S(1)} %slice.172), channel_id=1, source_target_pairs={{0,16},{16,0},{1,17},{17,1},{2,18},{18,2},{3,19},{19,3},{4,20},{20... | collective-permute-start | bytes 1572872 | tf_op jit(solution)/shard_map/ppermute | solution.py:733
  180.3 11.7 %copy-start.54 = (bf16[512,1024]{1,0:T(8,128)(2,1)S(1)}, bf16[512,1024]{1,0:T(8,128)(2,1)}, u32[]{:S(2)}) copy-start(bf16[512,1024]{1,0:T(8,128)(2,1)} %get-tuple-element.189) | copy-start | bytes 3145732
  180.3 13.3 %copy-start.48 = (bf16[16,128,512]{2,1,0:T(8,128)(2,1)S(1)}, bf16[16,128,512]{2,1,0:T(8,128)(2,1)}, u32[]{:S(2)}) copy-start(bf16[16,128,512]{2,1,0:T(8,128)(2,1)} %get-tuple-element.360) | copy-start | bytes 6291460
  180.3 13.3 %copy-start.49 = (bf16[16,128,512]{2,1,0:T(8,128)(2,1)S(1)}, bf16[16,128,512]{2,1,0:T(8,128)(2,1)}, u32[]{:S(2)}) copy-start(bf16[16,128,512]{2,1,0:T(8,128)(2,1)} %get-tuple-element.361) | copy-start | bytes 6291460
  180.3 13.3 %copy-start.50 = (bf16[16,128,512]{2,1,0:T(8,128)(2,1)S(1)}, bf16[16,128,512]{2,1,0:T(8,128)(2,1)}, u32[]{:S(2)}) copy-start(bf16[16,128,512]{2,1,0:T(8,128)(2,1)} %get-tuple-element.362) | copy-start | bytes 6291460
  181.8 11.8 %copy-start.15 = (bf16[2048,512]{1,0:T(8,128)(2,1)}, bf16[2048,512]{1,0:T(8,128)(2,1)S(1)}, u32[]{:S(2)}) copy-start(bf16[2048,512]{1,0:T(8,128)(2,1)S(1)} %flip.5) | copy-start | bytes 6291460
  181.8 11.8 %copy-start.4 = (bf16[256,1536]{1,0:T(8,128)(2,1)S(1)}, bf16[256,1536]{1,0:T(8,128)(2,1)}, u32[]{:S(2)}) copy-start(bf16[256,1536]{1,0:T(8,128)(2,1)} %v_ref.1) | copy-start | bytes 2359300
  192.1 14.9 %collective-permute-start.5 = (bf16[256,1024]{1,0:T(8,128)(2,1)S(1)}, bf16[256,1024]{1,0:T(8,128)(2,1)S(1)}, u32[]{:S(2)}, u32[]{:S(2)}) collective-permute-start(bf16[256,1024]{1,0:T(8,128)(2,1)S(1)} %get-tuple-element.376), channel_id=1, source_target_pairs={{0,16},{16,0},{1,17},{17,1},{2,18},{18,2},{3,19},{19,3},{4,20},{20... | collective-permute-start | bytes 1572872 | tf_op jit(solution)/shard_map/ppermute | solution.py:733
  195.5 11.6 %copy-start = (f32[256,1536]{1,0:T(8,128)}, f32[256,1536]{1,0:T(8,128)S(1)}, u32[]{:S(2)}) copy-start(f32[256,1536]{1,0:T(8,128)S(1)} %get-tuple-element.400.v_ref) | copy-start | bytes 4718596
  195.8 25.8 %collective-permute-start.4 = (bf16[256,1536]{1,0:T(8,128)(2,1)S(1)}, bf16[256,1536]{1,0:T(8,128)(2,1)S(1)}, u32[]{:S(2)}, u32[]{:S(2)}) collective-permute-start(bf16[256,1536]{1,0:T(8,128)(2,1)S(1)} %multiply_convert_fusion), channel_id=1, source_target_pairs={{0,16},{16,0},{1,17},{17,1},{2,18},{18,2},{3,19},{19,3},{4,20},{20... | collective-permute-start | bytes 2359304 | tf_op jit(solution)/shard_map/ppermute | solution.py:733
  265.9 20.1 %collective-permute-start.7 = (bf16[256,1536]{1,0:T(8,128)(2,1)}, bf16[256,1536]{1,0:T(8,128)(2,1)}, u32[]{:S(2)}, u32[]{:S(2)}) collective-permute-start(bf16[256,1536]{1,0:T(8,128)(2,1)} %get-tuple-element.202), channel_id=1, source_target_pairs={{0,16},{16,0},{1,17},{17,1},{2,18},{18,2},{3,19},{19,3},{4,20},{20... | collective-permute-start | bytes 2359304 | tf_op jit(solution)/shard_map/ppermute | solution.py:733
  274.6 22.8 %collective-permute-start.10 = (bf16[8,144,1536]{2,1,0:T(8,128)(2,1)}, bf16[8,144,1536]{2,1,0:T(8,128)(2,1)}, u32[]{:S(2)}, u32[]{:S(2)}) collective-permute-start(bf16[8,144,1536]{2,1,0:T(8,128)(2,1)} %grad_away.6), channel_id=1, source_target_pairs={{0,1},{1,0},{2,3},{3,2},{4,5},{5,4},{6,7},{7,6},{8,9},{9,8},{10,11... | collective-permute-start | bytes 10616840 | tf_op jit(solution)/shard_map/ppermute | solution.py:765
  274.6 11.4 %copy-start.60 = (f32[1536]{0:T(1024)S(1)}, f32[1536]{0:T(1024)}, u32[]{:S(2)}) copy-start(f32[1536]{0:T(1024)} %copy-done.59) | copy-start | bytes 18436
  274.6 11.4 %copy-start.1 = (f32[256,1536]{1,0:T(8,128)S(1)}, f32[256,1536]{1,0:T(8,128)}, u32[]{:S(2)}) copy-start(f32[256,1536]{1,0:T(8,128)} %copy-done) | copy-start | bytes 4718596
  279.1 12.0 %collective-permute-start.6 = (bf16[8,96,2304]{2,1,0:T(8,128)(2,1)}, bf16[8,96,2304]{2,1,0:T(8,128)(2,1)S(1)}, u32[]{:S(2)}, u32[]{:S(2)}) collective-permute-start(bf16[8,96,2304]{2,1,0:T(8,128)(2,1)} %grad_away.7), channel_id=1, source_target_pairs={{0,1},{1,0},{2,3},{3,2},{4,5},{5,4},{6,7},{7,6},{8,9},{9,8},{10,11... | collective-permute-start | bytes 10616840 | tf_op jit(solution)/shard_map/ppermute | solution.py:765
  289.6 19.6 %collective-permute-start.9 = (bf16[256,1536]{1,0:T(8,128)(2,1)}, bf16[256,1536]{1,0:T(8,128)(2,1)}, u32[]{:S(2)}, u32[]{:S(2)}) collective-permute-start(bf16[256,1536]{1,0:T(8,128)(2,1)} %get-tuple-element.219.own_ref), channel_id=1, source_target_pairs={{0,16},{16,0},{1,17},{17,1},{2,18},{18,2},{3,19},{19,3},{4,20},{20... | collective-permute-start | bytes 2359304 | tf_op jit(solution)/shard_map/ppermute | solution.py:733
  291.1 6.2 %copy-start.11 = (bf16[2304,512]{1,0:T(8,128)(2,1)S(1)}, bf16[2304,512]{1,0:T(8,128)(2,1)}, u32[]{:S(2)}) copy-start(bf16[2304,512]{1,0:T(8,128)(2,1)} %get-tuple-element.200) | copy-start | bytes 7077892
  295.9 40.0 %collective-permute-start.8 = (bf16[2,2,96,2304]{3,2,1,0:T(8,128)(2,1)}, bf16[2,2,96,2304]{3,2,1,0:T(8,128)(2,1)}, u32[]{:S(2)}, u32[]{:S(2)}) collective-permute-start(bf16[2,2,96,2304]{3,2,1,0:T(8,128)(2,1)} %get-tuple-element.212), channel_id=1, source_target_pairs={{0,4},{1,5},{2,6},{3,7},{4,0},{5,1},{6,2},{7,3},{8,12},{9,13},{10,... | collective-permute-start | bytes 5308424 | tf_op jit(solution)/shard_map/ppermute | solution.py:765
  297.3 7.5 %copy-start.8 = (bf16[512,2304]{1,0:T(8,128)(2,1)S(1)}, bf16[512,2304]{1,0:T(8,128)(2,1)}, u32[]{:S(2)}) copy-start(bf16[512,2304]{1,0:T(8,128)(2,1)} %get-tuple-element.213) | copy-start | bytes 7077892
  303.5 41.9 %collective-permute-start.14 = (bf16[4,1,144,1536]{3,2,1,0:T(8,128)(2,1)}, bf16[4,1,144,1536]{3,2,1,0:T(8,128)(2,1)}, u32[]{:S(2)}, u32[]{:S(2)}) collective-permute-start(bf16[4,1,144,1536]{3,2,1,0:T(8,128)(2,1)} %get-tuple-element.217), channel_id=1, source_target_pairs={{0,2},{1,3},{2,0},{3,1},{4,6},{5,7},{6,4},{7,5},{8,10},{9,11},{10,... | collective-permute-start | bytes 5308424 | tf_op jit(solution)/shard_map/ppermute | solution.py:765
  309.2 39.8 %collective-permute-start.13 = (bf16[8,96,2304]{2,1,0:T(8,128)(2,1)}, bf16[8,96,2304]{2,1,0:T(8,128)(2,1)}, u32[]{:S(2)}, u32[]{:S(2)}) collective-permute-start(bf16[8,96,2304]{2,1,0:T(8,128)(2,1)} %grad_away.8), channel_id=1, source_target_pairs={{0,1},{1,0},{2,3},{3,2},{4,5},{5,4},{6,7},{7,6},{8,9},{9,8},{10,11... | collective-permute-start | bytes 10616840 | tf_op jit(solution)/shard_map/ppermute | solution.py:765
  309.2 19.3 %copy-start.16 = (bf16[2048,512]{1,0:T(8,128)(2,1)S(1)}, bf16[2048,512]{1,0:T(8,128)(2,1)}, u32[]{:S(2)}) copy-start(bf16[2048,512]{1,0:T(8,128)(2,1)} %copy-done.15) | copy-start | bytes 6291460
  327.4 43.3 %collective-permute-start.16 = (bf16[512,1024]{1,0:T(8,128)(2,1)}, bf16[512,1024]{1,0:T(8,128)(2,1)}, u32[]{:S(2)}, u32[]{:S(2)}) collective-permute-start(bf16[512,1024]{1,0:T(8,128)(2,1)} %get-tuple-element.230), channel_id=1, source_target_pairs={{0,16},{16,0},{1,17},{17,1},{2,18},{18,2},{3,19},{19,3},{4,20},{20... | collective-permute-start | bytes 3145736 | tf_op jit(solution)/shard_map/ppermute | solution.py:733
  333.1 24.4 %collective-permute-start.12 = (bf16[8,128,2048]{2,1,0:T(8,128)(2,1)}, bf16[8,128,2048]{2,1,0:T(8,128)(2,1)}, u32[]{:S(2)}, u32[]{:S(2)}) collective-permute-start(bf16[8,128,2048]{2,1,0:T(8,128)(2,1)} %grad_away.9), channel_id=1, source_target_pairs={{0,1},{1,0},{2,3},{3,2},{4,5},{5,4},{6,7},{7,6},{8,9},{9,8},{10,11... | collective-permute-start | bytes 12582920 | tf_op jit(solution)/shard_map/ppermute | solution.py:765
  339.1 26.0 %collective-permute-start.11 = (bf16[2,1,96,2304]{3,2,0,1:T(8,128)(2,1)}, bf16[2,1,96,2304]{3,2,0,1:T(8,128)(2,1)}, u32[]{:S(2)}, u32[]{:S(2)}) collective-permute-start(bf16[2,1,96,2304]{3,2,0,1:T(8,128)(2,1)} %bitcast.189), channel_id=1, source_target_pairs={{0,2},{1,3},{2,0},{3,1},{4,6},{5,7},{6,4},{7,5},{8,10},{9,11},{10,... | collective-permute-start | bytes 2654216 | tf_op jit(solution)/shard_map/ppermute | solution.py:765
  349.0 31.3 %collective-permute-start.17 = (bf16[2,1,144,1536]{3,2,0,1:T(8,128)(2,1)}, bf16[2,1,144,1536]{3,2,0,1:T(8,128)(2,1)}, u32[]{:S(2)}, u32[]{:S(2)}) collective-permute-start(bf16[2,1,144,1536]{3,2,0,1:T(8,128)(2,1)} %bitcast.188), channel_id=1, source_target_pairs={{0,4},{1,5},{2,6},{3,7},{4,0},{5,1},{6,2},{7,3},{8,12},{9,13},{10,... | collective-permute-start | bytes 2654216 | tf_op jit(solution)/shard_map/ppermute | solution.py:765
  356.3 59.0 %collective-permute-start.23 = (bf16[4,1,96,2304]{3,2,1,0:T(8,128)(2,1)}, bf16[4,1,96,2304]{3,2,1,0:T(8,128)(2,1)}, u32[]{:S(2)}, u32[]{:S(2)}) collective-permute-start(bf16[4,1,96,2304]{3,2,1,0:T(8,128)(2,1)} %get-tuple-element.243), channel_id=1, source_target_pairs={{0,2},{1,3},{2,0},{3,1},{4,6},{5,7},{6,4},{7,5},{8,10},{9,11},{10,... | collective-permute-start | bytes 5308424 | tf_op jit(solution)/shard_map/ppermute | solution.py:765
  368.0 12.3 %copy-start.27 = (bf16[1,1,96,2304]{3,2,1,0:T(8,128)(2,1)}, bf16[1,1,96,2304]{3,2,1,0:T(8,128)(2,1)S(1)}, u32[]{:S(2)}) copy-start(bf16[1,1,96,2304]{3,2,1,0:T(8,128)(2,1)S(1)} %get-tuple-element.269) | copy-start | bytes 1327108
  368.0 21.9 %collective-permute-start.15 = (bf16[1,1,96,2304]{3,2,1,0:T(8,128)(2,1)}, bf16[1,1,96,2304]{3,2,1,0:T(8,128)(2,1)}, u32[]{:S(2)}, u32[]{:S(2)}) collective-permute-start(bf16[1,1,96,2304]{3,2,1,0:T(8,128)(2,1)} %get-tuple-element.251), channel_id=1, source_target_pairs={{0,8},{1,9},{2,10},{3,11},{4,12},{5,13},{6,14},{7,15},{8,0},{9,1},... | collective-permute-start | bytes 1327112 | tf_op jit(solution)/shard_map/ppermute | solution.py:765
  384.2 7.5 %copy-start.28 = (bf16[1,1,96,2304]{3,2,1,0:T(8,128)(2,1)S(1)}, bf16[1,1,96,2304]{3,2,1,0:T(8,128)(2,1)}, u32[]{:S(2)}) copy-start(bf16[1,1,96,2304]{3,2,1,0:T(8,128)(2,1)} %copy-done.27) | copy-start | bytes 1327108
  388.1 15.5 %collective-permute-start.19 = (bf16[8,96,2048]{2,1,0:T(8,128)(2,1)}, bf16[8,96,2048]{2,1,0:T(8,128)(2,1)}, u32[]{:S(2)}, u32[]{:S(2)}) collective-permute-start(bf16[8,96,2048]{2,1,0:T(8,128)(2,1)} %grad_away.10), channel_id=1, source_target_pairs={{0,1},{1,0},{2,3},{3,2},{4,5},{5,4},{6,7},{7,6},{8,9},{9,8},{10,11... | collective-permute-start | bytes 9437192 | tf_op jit(solution)/shard_map/ppermute | solution.py:765
  388.2 58.9 %collective-permute-start.22 = (bf16[2,2,128,2048]{3,2,1,0:T(8,128)(2,1)}, bf16[2,2,128,2048]{3,2,1,0:T(8,128)(2,1)}, u32[]{:S(2)}, u32[]{:S(2)}) collective-permute-start(bf16[2,2,128,2048]{3,2,1,0:T(8,128)(2,1)} %get-tuple-element.247), channel_id=1, source_target_pairs={{0,4},{1,5},{2,6},{3,7},{4,0},{5,1},{6,2},{7,3},{8,12},{9,13},{10,... | collective-permute-start | bytes 6291464 | tf_op jit(solution)/shard_map/ppermute | solution.py:765
  388.7 22.0 %collective-permute-start.24 = (bf16[256,1536]{1,0:T(8,128)(2,1)}, bf16[256,1536]{1,0:T(8,128)(2,1)}, u32[]{:S(2)}, u32[]{:S(2)}) collective-permute-start(bf16[256,1536]{1,0:T(8,128)(2,1)} %get-tuple-element.261), channel_id=1, source_target_pairs={{0,16},{16,0},{1,17},{17,1},{2,18},{18,2},{3,19},{19,3},{4,20},{20... | collective-permute-start | bytes 2359304 | tf_op jit(solution)/shard_map/ppermute | solution.py:733
  389.9 85.9 %collective-permute-start.26 = (bf16[1,1,144,1536]{3,2,1,0:T(8,128)(2,1)}, bf16[1,1,144,1536]{3,2,1,0:T(8,128)(2,1)}, u32[]{:S(2)}, u32[]{:S(2)}) collective-permute-start(bf16[1,1,144,1536]{3,2,1,0:T(8,128)(2,1)} %get-tuple-element.265), channel_id=1, source_target_pairs={{0,8},{1,9},{2,10},{3,11},{4,12},{5,13},{6,14},{7,15},{8,0},{9,1},... | collective-permute-start | bytes 1327112 | tf_op jit(solution)/shard_map/ppermute | solution.py:765
  393.8 11.3 %copy-start.23 = (bf16[1536,512]{1,0:T(8,128)(2,1)S(1)}, bf16[1536,512]{1,0:T(8,128)(2,1)}, u32[]{:S(2)}) copy-start(bf16[1536,512]{1,0:T(8,128)(2,1)} %copy-done.21) | copy-start | bytes 4718596
  393.8 11.3 %copy-start.35 = (bf16[2,512,1024]{2,1,0:T(8,128)(2,1)S(1)}, bf16[2,512,1024]{2,1,0:T(8,128)(2,1)}, u32[]{:S(2)}) copy-start(bf16[2,512,1024]{2,1,0:T(8,128)(2,1)} %copy-done.34) | copy-start | bytes 6291460
  403.6 132.1 %collective-permute-start.18 = (bf16[256,1536]{1,0:T(8,128)(2,1)}, bf16[256,1536]{1,0:T(8,128)(2,1)}, u32[]{:S(2)}, u32[]{:S(2)}) collective-permute-start(bf16[256,1536]{1,0:T(8,128)(2,1)} %get-tuple-element.275), channel_id=1, source_target_pairs={{0,16},{16,0},{1,17},{17,1},{2,18},{18,2},{3,19},{19,3},{4,20},{20... | collective-permute-start | bytes 2359304 | tf_op jit(solution)/shard_map/ppermute | solution.py:733
  410.6 39.9 %collective-permute-start.21 = (bf16[96,2304]{1,0:T(8,128)(2,1)}, bf16[96,2304]{1,0:T(8,128)(2,1)}, u32[]{:S(2)}, u32[]{:S(2)}) collective-permute-start(bf16[96,2304]{1,0:T(8,128)(2,1)} %get-tuple-element.272), channel_id=1, source_target_pairs={{0,16},{16,0},{1,17},{17,1},{2,18},{18,2},{3,19},{19,3},{4,20},{20... | collective-permute-start | bytes 1327112 | tf_op jit(solution)/shard_map/ppermute | solution.py:733
  415.3 39.0 %collective-permute-start.20 = (bf16[4,1,96,2048]{3,2,1,0:T(8,128)(2,1)}, bf16[4,1,96,2048]{3,2,1,0:T(8,128)(2,1)}, u32[]{:S(2)}, u32[]{:S(2)}) collective-permute-start(bf16[4,1,96,2048]{3,2,1,0:T(8,128)(2,1)} %get-tuple-element.279), channel_id=1, source_target_pairs={{0,2},{1,3},{2,0},{3,1},{4,6},{5,7},{6,4},{7,5},{8,10},{9,11},{10,... | collective-permute-start | bytes 4718600 | tf_op jit(solution)/shard_map/ppermute | solution.py:765
  416.2 30.8 %copy-start.18 = (bf16[2,2,128,2048]{3,2,1,0:T(8,128)(2,1)S(1)}, bf16[2,2,128,2048]{3,2,1,0:T(8,128)(2,1)}, u32[]{:S(2)}) copy-start(bf16[2,2,128,2048]{3,2,1,0:T(8,128)(2,1)} %copy-done.17) | copy-start | bytes 6291460
  450.5 22.0 %collective-permute-start.27 = (bf16[2,1,96,2304]{3,2,0,1:T(8,128)(2,1)}, bf16[2,1,96,2304]{3,2,0,1:T(8,128)(2,1)}, u32[]{:S(2)}, u32[]{:S(2)}) collective-permute-start(bf16[2,1,96,2304]{3,2,0,1:T(8,128)(2,1)} %bitcast.61), channel_id=1, source_target_pairs={{0,4},{1,5},{2,6},{3,7},{4,0},{5,1},{6,2},{7,3},{8,12},{9,13},{10,... | collective-permute-start | bytes 2654216 | tf_op jit(solution)/shard_map/ppermute | solution.py:765
  450.5 33.6 %collective-permute-start.31 = (bf16[2,1,128,2048]{3,2,0,1:T(8,128)(2,1)}, bf16[2,1,128,2048]{3,2,0,1:T(8,128)(2,1)}, u32[]{:S(2)}, u32[]{:S(2)}) collective-permute-start(bf16[2,1,128,2048]{3,2,0,1:T(8,128)(2,1)} %bitcast.187), channel_id=1, source_target_pairs={{0,2},{1,3},{2,0},{3,1},{4,6},{5,7},{6,4},{7,5},{8,10},{9,11},{10,... | collective-permute-start | bytes 3145736 | tf_op jit(solution)/shard_map/ppermute | solution.py:765
  460.2 18.0 %collective-permute-start.25 = (bf16[8,128,768]{2,1,0:T(8,128)(2,1)}, bf16[8,128,768]{2,1,0:T(8,128)(2,1)}, u32[]{:S(2)}, u32[]{:S(2)}) collective-permute-start(bf16[8,128,768]{2,1,0:T(8,128)(2,1)} %grad_away.11), channel_id=1, source_target_pairs={{0,1},{1,0},{2,3},{3,2},{4,5},{5,4},{6,7},{7,6},{8,9},{9,8},{10,11... | collective-permute-start | bytes 4718600 | tf_op jit(solution)/shard_map/ppermute | solution.py:765
  475.1 22.0 %collective-permute-start.30 = (bf16[1,1,96,2304]{3,2,1,0:T(8,128)(2,1)}, bf16[1,1,96,2304]{3,2,1,0:T(8,128)(2,1)}, u32[]{:S(2)}, u32[]{:S(2)}) collective-permute-start(bf16[1,1,96,2304]{3,2,1,0:T(8,128)(2,1)} %get-tuple-element.301), channel_id=1, source_target_pairs={{0,8},{1,9},{2,10},{3,11},{4,12},{5,13},{6,14},{7,15},{8,0},{9,1},... | collective-permute-start | bytes 1327112 | tf_op jit(solution)/shard_map/ppermute | solution.py:765
  477.7 21.3 %collective-permute-start.29 = (bf16[144,1536]{1,0:T(8,128)(2,1)}, bf16[144,1536]{1,0:T(8,128)(2,1)}, u32[]{:S(2)}, u32[]{:S(2)}) collective-permute-start(bf16[144,1536]{1,0:T(8,128)(2,1)} %get-tuple-element.305), channel_id=1, source_target_pairs={{0,16},{16,0},{1,17},{17,1},{2,18},{18,2},{3,19},{19,3},{4,20},{20... | collective-permute-start | bytes 1327112 | tf_op jit(solution)/shard_map/ppermute | solution.py:733
  478.3 34.3 %collective-permute-start.35 = (bf16[2,1,96,2048]{3,2,0,1:T(8,128)(2,1)}, bf16[2,1,96,2048]{3,2,0,1:T(8,128)(2,1)}, u32[]{:S(2)}, u32[]{:S(2)}) collective-permute-start(bf16[2,1,96,2048]{3,2,0,1:T(8,128)(2,1)} %bitcast.74), channel_id=1, source_target_pairs={{0,4},{1,5},{2,6},{3,7},{4,0},{5,1},{6,2},{7,3},{8,12},{9,13},{10,... | collective-permute-start | bytes 2359304 | tf_op jit(solution)/shard_map/ppermute | solution.py:765
  484.1 17.7 %collective-permute-start.28 = (bf16[4,1,128,768]{3,2,1,0:T(8,128)(2,1)}, bf16[4,1,128,768]{3,2,1,0:T(8,128)(2,1)}, u32[]{:S(2)}, u32[]{:S(2)}) collective-permute-start(bf16[4,1,128,768]{3,2,1,0:T(8,128)(2,1)} %get-tuple-element.309), channel_id=1, source_target_pairs={{0,2},{1,3},{2,0},{3,1},{4,6},{5,7},{6,4},{7,5},{8,10},{9,11},{10,... | collective-permute-start | bytes 2359304 | tf_op jit(solution)/shard_map/ppermute | solution.py:765
  497.1 32.4 %collective-permute-start.33 = (bf16[1,1,128,2048]{3,2,1,0:T(8,128)(2,1)}, bf16[1,1,128,2048]{3,2,1,0:T(8,128)(2,1)}, u32[]{:S(2)}, u32[]{:S(2)}) collective-permute-start(bf16[1,1,128,2048]{3,2,1,0:T(8,128)(2,1)} %get-tuple-element.313), channel_id=1, source_target_pairs={{0,8},{1,9},{2,10},{3,11},{4,12},{5,13},{6,14},{7,15},{8,0},{9,1},... | collective-permute-start | bytes 1572872 | tf_op jit(solution)/shard_map/ppermute | solution.py:765
  499.0 16.1 %collective-permute-start.34 = (bf16[96,2304]{1,0:T(8,128)(2,1)}, bf16[96,2304]{1,0:T(8,128)(2,1)}, u32[]{:S(2)}, u32[]{:S(2)}) collective-permute-start(bf16[96,2304]{1,0:T(8,128)(2,1)} %get-tuple-element.317), channel_id=1, source_target_pairs={{0,16},{16,0},{1,17},{17,1},{2,18},{18,2},{3,19},{19,3},{4,20},{20... | collective-permute-start | bytes 1327112 | tf_op jit(solution)/shard_map/ppermute | solution.py:733
  504.4 29.0 %collective-permute-start.32 = (bf16[2,1,128,768]{3,2,0,1:T(8,128)(2,1)}, bf16[2,1,128,768]{3,2,0,1:T(8,128)(2,1)}, u32[]{:S(2)}, u32[]{:S(2)}) collective-permute-start(bf16[2,1,128,768]{3,2,0,1:T(8,128)(2,1)} %bitcast.190), channel_id=1, source_target_pairs={{0,4},{1,5},{2,6},{3,7},{4,0},{5,1},{6,2},{7,3},{8,12},{9,13},{10,... | collective-permute-start | bytes 1179656 | tf_op jit(solution)/shard_map/ppermute | solution.py:765
  515.1 28.7 %collective-permute-start.36 = (bf16[1,1,96,2048]{3,2,1,0:T(8,128)(2,1)}, bf16[1,1,96,2048]{3,2,1,0:T(8,128)(2,1)}, u32[]{:S(2)}, u32[]{:S(2)}) collective-permute-start(bf16[1,1,96,2048]{3,2,1,0:T(8,128)(2,1)} %get-tuple-element.327), channel_id=1, source_target_pairs={{0,8},{1,9},{2,10},{3,11},{4,12},{5,13},{6,14},{7,15},{8,0},{9,1},... | collective-permute-start | bytes 1179656 | tf_op jit(solution)/shard_map/ppermute | solution.py:765
  531.7 16.2 %collective-permute-start.39 = (bf16[128,2048]{1,0:T(8,128)(2,1)}, bf16[128,2048]{1,0:T(8,128)(2,1)}, u32[]{:S(2)}, u32[]{:S(2)}) collective-permute-start(bf16[128,2048]{1,0:T(8,128)(2,1)} %get-tuple-element.333), channel_id=1, source_target_pairs={{0,16},{16,0},{1,17},{17,1},{2,18},{18,2},{3,19},{19,3},{4,20},{20... | collective-permute-start | bytes 1572872 | tf_op jit(solution)/shard_map/ppermute | solution.py:733
  535.6 14.7 %collective-permute-start.38 = (bf16[1,1,128,768]{3,2,1,0:T(8,128)(2,1)}, bf16[1,1,128,768]{3,2,1,0:T(8,128)(2,1)}, u32[]{:S(2)}, u32[]{:S(2)}) collective-permute-start(bf16[1,1,128,768]{3,2,1,0:T(8,128)(2,1)} %get-tuple-element.337), channel_id=1, source_target_pairs={{0,8},{1,9},{2,10},{3,11},{4,12},{5,13},{6,14},{7,15},{8,0},{9,1},... | collective-permute-start | bytes 589832 | tf_op jit(solution)/shard_map/ppermute | solution.py:765
  545.6 11.4 %collective-permute-start.37 = (bf16[96,2048]{1,0:T(8,128)(2,1)}, bf16[96,2048]{1,0:T(8,128)(2,1)}, u32[]{:S(2)}, u32[]{:S(2)}) collective-permute-start(bf16[96,2048]{1,0:T(8,128)(2,1)} %get-tuple-element.343), channel_id=1, source_target_pairs={{0,16},{16,0},{1,17},{17,1},{2,18},{18,2},{3,19},{19,3},{4,20},{20... | collective-permute-start | bytes 1179656 | tf_op jit(solution)/shard_map/ppermute | solution.py:733
  552.0 9.6 %collective-permute-start.40 = (bf16[128,768]{1,0:T(8,128)(2,1)}, bf16[128,768]{1,0:T(8,128)(2,1)S(1)}, u32[]{:S(2)}, u32[]{:S(2)}) collective-permute-start(bf16[128,768]{1,0:T(8,128)(2,1)} %get-tuple-element.352), channel_id=1, source_target_pairs={{0,16},{16,0},{1,17},{17,1},{2,18},{18,2},{3,19},{19,3},{4,20},{20... | collective-permute-start | bytes 589832 | tf_op jit(solution)/shard_map/ppermute | solution.py:733
  (50 other events, 193.4 us)
Sparse Core Ops, SparseCore 0:
  10.2 111.9 all-gather.4
  124.3 110.2 all-gather.6
  391.8 139.3 all-reduce.5
